TPU v7x, 32 devices: a whole 2x2x4 slice. The times are simulated.
32 devices in a mesh: dp: 4 (over y, core), row: 2 (over x), col: 4 (over z).
Axes of the slice: x: 2, y: 2, z: 4, core: 2. Of those that a mesh axis runs over, the one named last changes fastest.
Arguments:
- layer_input: bfloat16 [12288, 1536], P(('dp', 'col'), 'row'), may hold values from -6 to 6
- attn_gain: float32 [1536], P('row'), may hold values from 0.25 to 1.75
- qkv_weight: bfloat16 [1536, 4608], P('row', 'col'), may hold values from -0.15625 to 0.15625
- forget_weight: bfloat16 [1536, 24], P('row', 'col'), may hold values from -0.15625 to 0.15625
- forget_bias: float32 [24], P('col'), may hold values from 2.5 to 7
- out_weight: bfloat16 [1536, 1536], P('col', 'row'), may hold values from -0.625 to 0.625
- ffn_gain: float32 [1536], P('row'), may hold values from 0.25 to 1.75
- gate_weight: bfloat16 [1536, 4096], P('row', 'col'), may hold values from -0.15625 to 0.15625
- up_weight: bfloat16 [1536, 4096], P('row', 'col'), may hold values from -0.15625 to 0.15625
- down_weight: bfloat16 [4096, 1536], P('col', 'row'), may hold values from -0.09375 to 0.09375
- prompt_doc: int32 [8, 1024], P(('dp', 'row')), may hold values from 0 to 3, never falling along the last dimension, each value on 1 to 512 neighbouring positions
- branch_seg: int32 [8, 512], P(('dp', 'row')), may hold values from 0 to 3, never falling along the last dimension, each value on 1 to 256 neighbouring positions
- branch_doc: int32 [8, 4], P(('dp', 'row')), may hold values from 0 to 3
- out_cotangent: bfloat16 [12288, 1536], P(('dp', 'col'), 'row'), may hold values from -6 to 6
Outputs:
- layer_output: bfloat16 [12288, 1536], P(('dp', 'col'), 'row')
- input_grad: bfloat16 [12288, 1536], P(('dp', 'col'), 'row')
- attn_gain_grad: float32 [1536], P('row')
- qkv_grad: float32 [1536, 4608], P('row', 'col')
- forget_grad: float32 [1536, 24], P('row', 'col')
- forget_bias_grad: float32 [24], P('col')
- out_grad: float32 [1536, 1536], P('col', 'row')
- ffn_gain_grad: float32 [1536], P('row')
- gate_grad: float32 [1536, 4096], P('row', 'col')
- up_grad: float32 [1536, 4096], P('row', 'col')
- down_grad: float32 [4096, 1536], P('col', 'row')
Inputs may be any that keep to these rules, and one draw needn't show every extreme that they name: `prompt_doc`: in each group the prompt's documents are numbered 0 to 3 in order, every one present, each of 1 to 512 tokens, one of exactly 512. `branch_seg`: in each group the continuations are numbered 0 to 3 in order, every one present, each of 1 to 256 tokens, one of exactly 256.
All inputs are finite; a program needn't handle non-finite values.
Results may differ from a plain program's by a relative error of at most 0.023.
Values may be sent and summed in bfloat16 or wider, within the bound.
A program may use at most 192 MiB of HBM per device.

v0:
```python
import jax
import jax.numpy as jnp
from jax import lax
from jax.sharding import PartitionSpec as P

D = 1536
DH = 64
DOCS = 4
QBLK = 512


EPS = 1e-06
MASKED = -1e30


def visible(row_start, doc_query, branch_query, doc_key, branch_key):
    pos_query = row_start + jnp.arange(doc_query.shape[0], dtype=jnp.int32)
    pos_key = jnp.arange(doc_key.shape[0], dtype=jnp.int32)
    causal = pos_key[None, :] <= pos_query[:, None]
    same_doc = doc_query[:, None] == doc_key[None, :]
    same_branch = (branch_key[None, :] < 0) | (branch_query[:, None] == branch_key[None, :])
    return causal & same_doc & same_branch


def decay_sums(log_rates, prompt_ids, branch_ids, branch_docs):
    prompt_len = prompt_ids.shape[0]
    prompt_part = log_rates[:prompt_len]
    branch_part = log_rates[prompt_len:]
    prompt_sums = jnp.cumsum(prompt_part, axis=0)
    doc_range = jnp.arange(DOCS, dtype=jnp.int32)
    doc_last = jnp.sum((prompt_ids[None, :] <= doc_range[:, None]).astype(jnp.int32), axis=1) - 1
    at_last = jnp.arange(prompt_len, dtype=jnp.int32)[None, :] == doc_last[:, None]
    doc_totals = jnp.sum(jnp.where(at_last[:, :, None], prompt_sums[None], 0.0), axis=1)
    branch_range = jnp.arange(branch_docs.shape[0], dtype=jnp.int32)
    picked = branch_docs[:, None] == doc_range[None, :]
    branch_start = jnp.sum(jnp.where(picked[:, :, None], doc_totals[None], 0.0), axis=1)
    earlier = branch_ids[None, :] < branch_range[:, None]
    skipped = jnp.sum(jnp.where(earlier[:, :, None], branch_part[None], 0.0), axis=1)
    member = branch_ids[:, None] == branch_range[None, :]
    offsets = jnp.sum(jnp.where(member[:, :, None], (branch_start - skipped)[None], 0.0), axis=1)
    decay_sum = jnp.concatenate([prompt_sums, jnp.cumsum(branch_part, axis=0) + offsets], axis=0)
    branch_doc_ids = jnp.sum(jnp.where(member, branch_docs[None, :], 0), axis=1)
    doc_ids = jnp.concatenate([prompt_ids, branch_doc_ids])
    branch_tags = jnp.concatenate([jnp.full((prompt_len,), -1, jnp.int32), branch_ids])
    return (decay_sum, doc_ids, branch_tags)


def block_scores(query_block, key_rows, decay_query, decay_key, allowed):
    raw_scores = jnp.einsum(
        "qhd,khd->hqk", query_block, key_rows, preferred_element_type=jnp.float32
    )
    scores = raw_scores * DH ** (-0.5) + decay_query.T[:, :, None] - decay_key.T[:, None, :]
    return jnp.where(allowed[None], scores, MASKED)


def contract_rows(left, right):
    return lax.dot_general(
        left, right, (((0,), (0,)), ((), ())), preferred_element_type=jnp.float32
    )


def contract_cols(left, right):
    return lax.dot_general(
        left, right, (((1,), (1,)), ((), ())), preferred_element_type=jnp.float32
    )


def row_stat(values):
    return lax.psum(values, "row")


def gather_tokens(token_rows):
    return lax.all_gather(token_rows, "col", axis=0, tiled=True)


def sum_tokens(partial_value):
    return lax.psum_scatter(
        partial_value.astype(jnp.bfloat16), "col", scatter_dimension=0, tiled=True
    ).astype(jnp.float32)


def gather_group(group_rows):
    return lax.all_gather(group_rows, "row", axis=0, tiled=True)


def sum_group(partial_value):
    return lax.psum_scatter(
        partial_value.astype(jnp.bfloat16), "row", scatter_dimension=0, tiled=True
    ).astype(jnp.float32)


def sum_pair(first, second):
    return (
        lax.psum_scatter(first, "row", scatter_dimension=0, tiled=True),
        lax.psum_scatter(second, "row", scatter_dimension=0, tiled=True),
    )


def gather_pair(first, second):
    return (
        lax.all_gather(first, "row", axis=0, tiled=True),
        lax.all_gather(second, "row", axis=0, tiled=True),
    )


def shards(
    layer_input,
    attn_gain,
    qkv_weight,
    forget_weight,
    forget_bias,
    out_weight,
    ffn_gain,
    gate_weight,
    up_weight,
    down_weight,
    prompt_doc,
    branch_seg,
    branch_doc,
    out_cotangent,
):
    score_scale = DH ** (-0.5)
    stream = layer_input.astype(jnp.float32)
    rms_a = lax.rsqrt(row_stat(jnp.sum(stream * stream, axis=1)) / D + EPS)[:, None]
    normed_a = (stream * rms_a * attn_gain).astype(jnp.bfloat16)
    normed_a_all = gather_tokens(normed_a)
    projected, forget_sum = sum_pair(
        jnp.dot(normed_a_all, qkv_weight, preferred_element_type=jnp.float32),
        jnp.dot(normed_a_all, forget_weight, preferred_element_type=jnp.float32),
    )
    group_len = projected.shape[0]
    heads = forget_weight.shape[1]
    qkv = projected.astype(jnp.bfloat16).reshape(group_len, heads, 3, DH)
    forget_logit = forget_sum + forget_bias
    log_rate = jax.nn.log_sigmoid(forget_logit)
    prompt_ids = prompt_doc[0]
    branch_ids = branch_seg[0]
    branch_docs = branch_doc[0]
    decay_sum, doc_ids, branch_tags = decay_sums(log_rate, prompt_ids, branch_ids, branch_docs)
    queries = qkv[:, :, 0]
    key_rows = qkv[:, :, 1]
    value_rows = qkv[:, :, 2]
    blocks = jnp.arange(group_len // QBLK, dtype=jnp.int32)

    def block_view(block_index):
        row_start = block_index * QBLK
        query_block = lax.dynamic_slice_in_dim(queries, row_start, QBLK, 0)
        decay_query = lax.dynamic_slice_in_dim(decay_sum, row_start, QBLK, 0)
        doc_query = lax.dynamic_slice_in_dim(doc_ids, row_start, QBLK, 0)
        branch_query = lax.dynamic_slice_in_dim(branch_tags, row_start, QBLK, 0)
        allowed = visible(row_start, doc_query, branch_query, doc_ids, branch_tags)
        scores = block_scores(query_block, key_rows, decay_query, decay_sum, allowed)
        return (row_start, query_block, scores)

    def forward_block(block_index):
        row_start, query_block, scores = block_view(block_index)
        row_max = jnp.max(scores, axis=2, keepdims=True)
        expo = jnp.exp(scores - row_max)
        row_total = jnp.sum(expo, axis=2, keepdims=True)
        probs = (expo / row_total).astype(jnp.bfloat16)
        attended_block = jnp.einsum(
            "hqk,khd->qhd", probs, value_rows, preferred_element_type=jnp.float32
        ).astype(jnp.bfloat16)
        return (attended_block, (row_max + jnp.log(row_total))[:, :, 0])

    attended_blocks, lse_blocks = lax.map(forward_block, blocks)
    attended = attended_blocks.reshape(group_len, heads * DH)
    attended_all = gather_group(attended)
    branch_out = sum_tokens(jnp.dot(attended_all, out_weight, preferred_element_type=jnp.float32))
    resid = stream + branch_out
    rms_b = lax.rsqrt(row_stat(jnp.sum(resid * resid, axis=1)) / D + EPS)[:, None]
    normed_b = (resid * rms_b * ffn_gain).astype(jnp.bfloat16)
    normed_b_all = gather_tokens(normed_b)
    gate_pre, up_pre = sum_pair(
        jnp.dot(normed_b_all, gate_weight, preferred_element_type=jnp.float32),
        jnp.dot(normed_b_all, up_weight, preferred_element_type=jnp.float32),
    )
    gate_sig = jax.nn.sigmoid(gate_pre)
    gate_act = gate_pre * gate_sig
    hidden = (gate_act * up_pre).astype(jnp.bfloat16)
    hidden_all = gather_group(hidden)
    layer_output = (
        resid + sum_tokens(jnp.dot(hidden_all, down_weight, preferred_element_type=jnp.float32))
    ).astype(jnp.bfloat16)
    cotangent = out_cotangent.astype(jnp.float32)
    cotangent_all = gather_tokens(out_cotangent)
    down_grad = contract_rows(hidden_all, cotangent_all)
    grad_hidden = sum_group(contract_cols(cotangent_all, down_weight))
    grad_gate = (grad_hidden * up_pre * gate_sig * (1.0 + gate_pre * (1.0 - gate_sig))).astype(
        jnp.bfloat16
    )
    grad_up = (grad_hidden * gate_act).astype(jnp.bfloat16)
    grad_gate_all, grad_up_all = gather_pair(grad_gate, grad_up)
    gate_grad = contract_rows(normed_b_all, grad_gate_all)
    up_grad = contract_rows(normed_b_all, grad_up_all)
    grad_normed_b = sum_tokens(
        contract_cols(grad_gate_all, gate_weight) + contract_cols(grad_up_all, up_weight)
    )
    gained_b = ffn_gain * grad_normed_b
    inner_b = row_stat(jnp.sum(resid * gained_b, axis=1))[:, None]
    ffn_gain_part = jnp.sum(grad_normed_b * resid * rms_b, axis=0)
    grad_resid = cotangent + rms_b * gained_b - resid * (rms_b * rms_b * rms_b) * inner_b / D
    grad_branch = grad_resid.astype(jnp.bfloat16)
    grad_branch_all = gather_tokens(grad_branch)
    out_grad = contract_rows(attended_all, grad_branch_all)
    attended_part = contract_cols(grad_branch_all, out_weight)
    grad_attended = sum_group(attended_part).astype(jnp.bfloat16).reshape(group_len, heads, DH)

    def back_block(carry, block_index):
        key_acc, value_acc, decay_keys = carry
        row_start, query_block, scores = block_view(block_index)
        grad_block = lax.dynamic_slice_in_dim(grad_attended, row_start, QBLK, 0)
        lse_block = lax.dynamic_index_in_dim(lse_blocks, block_index, 0, keepdims=False)
        probs_star = jnp.exp(scores - lse_block[:, :, None])
        grad_probs = jnp.einsum(
            "qhd,khd->hqk", grad_block, value_rows, preferred_element_type=jnp.float32
        )
        row_delta = jnp.sum(probs_star * grad_probs, axis=2, keepdims=True)
        grad_scores = (probs_star * (grad_probs - row_delta)).astype(jnp.bfloat16)
        grad_query = (
            jnp.einsum("hqk,khd->qhd", grad_scores, key_rows, preferred_element_type=jnp.float32)
            * score_scale
        )
        key_acc = key_acc + jnp.einsum(
            "hqk,qhd->khd", grad_scores, query_block, preferred_element_type=jnp.float32
        )
        value_acc = value_acc + jnp.einsum(
            "hqk,qhd->khd",
            probs_star.astype(jnp.bfloat16),
            grad_block,
            preferred_element_type=jnp.float32,
        )
        decay_rows = jnp.sum(grad_scores, axis=2, dtype=jnp.float32)
        decay_keys = decay_keys - jnp.sum(grad_scores, axis=1, dtype=jnp.float32)
        return ((key_acc, value_acc, decay_keys), (grad_query, decay_rows))

    zero_rows = jnp.zeros((group_len, heads, DH), jnp.float32)
    carried, stacked = lax.scan(
        back_block, (zero_rows, zero_rows, jnp.zeros((heads, group_len), jnp.float32)), blocks
    )
    key_acc, value_acc, decay_keys = carried
    query_blocks, decay_blocks = stacked
    grad_query = query_blocks.reshape(group_len, heads, DH)
    grad_decay = jnp.transpose(decay_blocks, (0, 2, 1)).reshape(group_len, heads) + decay_keys.T
    grad_qkv = (
        jnp.stack([grad_query, key_acc * score_scale, value_acc], axis=2)
        .astype(jnp.bfloat16)
        .reshape(group_len, heads * 3 * DH)
    )
    unused, pullback = jax.vjp(
        lambda log_rates: decay_sums(log_rates, prompt_ids, branch_ids, branch_docs)[0], log_rate
    )
    grad_log_rate = pullback(grad_decay)[0]
    grad_forget = (grad_log_rate * jax.nn.sigmoid(-forget_logit)).astype(jnp.bfloat16)
    grad_qkv_all, grad_forget_all = gather_pair(grad_qkv, grad_forget)
    qkv_grad = contract_rows(normed_a_all, grad_qkv_all)
    forget_grad = contract_rows(normed_a_all, grad_forget_all)
    forget_bias_grad = jnp.sum(grad_forget_all, axis=0, dtype=jnp.float32)
    grad_normed_a = sum_tokens(
        contract_cols(grad_qkv_all, qkv_weight) + contract_cols(grad_forget_all, forget_weight)
    )
    gained_a = attn_gain * grad_normed_a
    inner_a = row_stat(jnp.sum(stream * gained_a, axis=1))[:, None]
    attn_gain_part = jnp.sum(grad_normed_a * stream * rms_a, axis=0)
    input_grad = (
        grad_resid + rms_a * gained_a - stream * (rms_a * rms_a * rms_a) * inner_a / D
    ).astype(jnp.bfloat16)
    attn_gain_grad, ffn_gain_grad = lax.psum((attn_gain_part, ffn_gain_part), ("dp", "col"))
    summed = (
        lax.psum(qkv_grad.astype(jnp.bfloat16), "dp").astype(jnp.float32),
        lax.psum(forget_grad.astype(jnp.bfloat16), "dp").astype(jnp.float32),
        lax.psum(forget_bias_grad.astype(jnp.bfloat16), "dp").astype(jnp.float32),
        lax.psum(out_grad.astype(jnp.bfloat16), "dp").astype(jnp.float32),
        lax.psum(gate_grad.astype(jnp.bfloat16), "dp").astype(jnp.float32),
        lax.psum(up_grad.astype(jnp.bfloat16), "dp").astype(jnp.float32),
        lax.psum(down_grad.astype(jnp.bfloat16), "dp").astype(jnp.float32),
    )
    return (
        layer_output,
        input_grad,
        attn_gain_grad,
        summed[0],
        summed[1],
        summed[2],
        summed[3],
        ffn_gain_grad,
        summed[4],
        summed[5],
        summed[6],
    )


def solution(mesh):
    in_specs = (
        P(("dp", "col"), "row"),
        P("row"),
        P("row", "col"),
        P("row", "col"),
        P("col"),
        P("col", "row"),
        P("row"),
        P("row", "col"),
        P("row", "col"),
        P("col", "row"),
        P(("dp", "row"), None),
        P(("dp", "row"), None),
        P(("dp", "row"), None),
        P(("dp", "col"), "row"),
    )
    out_specs = (
        P(("dp", "col"), "row"),
        P(("dp", "col"), "row"),
        P("row"),
        P("row", "col"),
        P("row", "col"),
        P("col"),
        P("col", "row"),
        P("row"),
        P("row", "col"),
        P("row", "col"),
        P("col", "row"),
    )
    return jax.shard_map(shards, mesh=mesh, in_specs=in_specs, out_specs=out_specs, check_vma=False)
```

profile of v0, /device:TPU:1, one launch (start us, length us, event | category | flops | bytes accessed | tf_op | source)
XLA Modules:
  0.0 2115.1 jit_solution(11031045359977941894)
XLA Ops:
  17.2 92.3 %all-gather.10.cloned.1.call-done = bf16[3072,768]{1,0:T(8,128)(2,1)} async-done(((bf16[768,768]{1,0:T(8,128)(2,1)}), bf16[3072,768]{1,0:T(8,128)(2,1)}) %all-gather.10.cloned.1.call-update) | async-done | bytes 4718608 | tf_op jit(solution)/shard_map/all_gather | solution.py:73
  113.8 11.1 fusion.65
  132.1 154.1 %reduce-scatter.11.cloned.1.call-done = f32[1536,1152]{1,0:T(8,128)} async-done(((f32[3072,1152]{1,0:T(8,128)}), f32[1536,1152]{1,0:T(8,128)}) %reduce-scatter.11.cloned.1.call-update) | async-done | bytes 7077904 | tf_op jit(solution)/shard_map/reduce_scatter | solution.py:94
  286.2 5.2 convert_element_type.142
  291.3 5.7 copy.48
  301.0 77.4 %while.31 = (s32[]{:T(128)}, bf16[3,512,6,64]{1,3,2,0:T(8,128)(2,1)}, f32[3,6,512]{2,1,0:T(8,128)S(1)}, s32[3]{0:T(128)S(1)}, s32[1536]{0:T(1024)S(1)}, /*index=...) while((s32[]{:T(128)}, ...), condition=%wide.region_17.18_spmd, body=%wide.region_14.17_spmd.sunk | while | flops 1297808384 | bytes 66381052 | solution.py:166
  304.3 7.2 fusion.137
  311.6 6.5 fusion.138
  318.1 8.9 fusion.139
  329.9 7.2 fusion.137
  337.2 6.5 fusion.138
  343.7 8.9 fusion.139
  355.5 7.2 fusion.137
  362.8 6.5 fusion.138
  369.3 8.9 fusion.139
  382.2 36.2 %all-gather.12.cloned.1.call-done = bf16[3072,384]{0,1:T(8,128)(2,1)} async-done(((bf16[1536,384]{0,1:T(8,128)(2,1)}), bf16[3072,384]{0,1:T(8,128)(2,1)}) %all-gather.12.cloned.1.call-update) | async-done | bytes 2359312 | tf_op jit(solution)/shard_map/all_gather | solution.py:83
  418.3 6.4 convolution_convert_fusion.2
  425.5 84.8 %reduce-scatter.15.cloned.1.call-done = bf16[768,768]{1,0:T(8,128)(2,1)} async-done(((bf16[3072,768]{1,0:T(8,128)(2,1)}), bf16[768,768]{1,0:T(8,128)(2,1)}) %reduce-scatter.15.cloned.1.call-update) | async-done | bytes 1179664 | tf_op jit(solution)/shard_map/reduce_scatter | solution.py:77
  518.6 83.1 %all-gather.18.cloned.1.call-done = bf16[3072,768]{1,0:T(8,128)(2,1)} async-done(((bf16[768,768]{1,0:T(8,128)(2,1)}), bf16[3072,768]{1,0:T(8,128)(2,1)}) %all-gather.18.cloned.1.call-update) | async-done | bytes 4718608 | tf_op jit(solution)/shard_map/all_gather | solution.py:73
  601.7 9.7 convolution_convert_fusion
  611.4 80.3 %all-gather.14.cloned.1.call-done = bf16[3072,768]{1,0:T(8,128)(2,1)} async-done(((bf16[768,768]{1,0:T(8,128)(2,1)}), bf16[3072,768]{1,0:T(8,128)(2,1)}) %all-gather.14.cloned.1.call-update) | async-done | bytes 4718608 | tf_op jit(solution)/shard_map/all_gather | solution.py:73
  691.7 10.0 fusion.68
  701.8 10.4 fusion.67
  712.3 57.2 %reduce-scatter.23.cloned.1.call-done = bf16[1536,1024]{1,0:T(8,128)(2,1)} async-done(((bf16[3072,1024]{1,0:T(8,128)(2,1)}), bf16[1536,1024]{1,0:T(8,128)(2,1)}) %reduce-scatter.23.cloned.1.call-update) | async-done | bytes 3145744 | tf_op jit(solution)/shard_map/reduce_scatter | solution.py:87
  769.5 146.9 %reduce-scatter.19.cloned.1.call-done = f32[1536,1024]{1,0:T(8,128)} async-done(((f32[3072,1024]{1,0:T(8,128)}), f32[1536,1024]{1,0:T(8,128)}) %reduce-scatter.19.cloned.1.call-update) | async-done | bytes 6291472 | tf_op jit(solution)/shard_map/reduce_scatter | solution.py:95
  916.4 146.8 %reduce-scatter.17.cloned.1.call-done = f32[1536,1024]{1,0:T(8,128)} async-done(((f32[3072,1024]{1,0:T(8,128)}), f32[1536,1024]{1,0:T(8,128)}) %reduce-scatter.17.cloned.1.call-update) | async-done | bytes 6291472 | tf_op jit(solution)/shard_map/reduce_scatter | solution.py:94
  1063.2 9.9 fusion.37
  1073.8 79.9 %all-gather.20.cloned.1.call-done = bf16[3072,1024]{1,0:T(8,128)(2,1)} async-done(((bf16[1536,1024]{1,0:T(8,128)(2,1)}), bf16[3072,1024]{1,0:T(8,128)(2,1)}) %all-gather.20.cloned.1.call-update) | async-done | bytes 6291472 | tf_op jit(solution)/shard_map/all_gather | solution.py:101
  1153.7 10.0 fusion.69
  1163.7 72.4 %all-gather.22.cloned.1.call-done = bf16[3072,1024]{1,0:T(8,128)(2,1)} async-done(((bf16[1536,1024]{1,0:T(8,128)(2,1)}), bf16[3072,1024]{1,0:T(8,128)(2,1)}) %all-gather.22.cloned.1.call-update) | async-done | bytes 6291472 | tf_op jit(solution)/shard_map/all_gather | solution.py:102
  1236.1 10.6 add_convert_fusion.1
  1246.8 85.4 %reduce-scatter.25.cloned.1.call-done = bf16[768,768]{1,0:T(8,128)(2,1)} async-done(((bf16[3072,768]{1,0:T(8,128)(2,1)}), bf16[768,768]{1,0:T(8,128)(2,1)}) %reduce-scatter.25.cloned.1.call-update) | async-done | bytes 1179664 | tf_op jit(solution)/shard_map/reduce_scatter | solution.py:77
  1343.3 91.2 %all-gather.24.cloned.1.call-done = bf16[3072,768]{1,0:T(8,128)(2,1)} async-done(((bf16[768,768]{1,0:T(8,128)(2,1)}), bf16[3072,768]{1,0:T(8,128)(2,1)}) %all-gather.24.cloned.1.call-update) | async-done | bytes 4718608 | tf_op jit(solution)/shard_map/all_gather | solution.py:73
  1434.5 6.5 convolution_convert_fusion.3
  1441.9 32.4 %reduce-scatter.27.cloned.1.call-done = bf16[1536,384]{1,0:T(8,128)(2,1)} async-done(((bf16[3072,384]{1,0:T(8,128)(2,1)}), bf16[1536,384]{1,0:T(8,128)(2,1)}) %reduce-scatter.27.cloned.1.call-update) | async-done | bytes 1179664 | tf_op jit(solution)/shard_map/reduce_scatter | solution.py:87
  1476.7 203.5 %while.32 = (s32[]{:T(128)}, f32[1536,6,64]{0,2,1:T(8,128)}, f32[1536,6,64]{0,2,1:T(8,128)}, f32[6,1536]{1,0:T(8,128)S(1)}, bf16[3,512,6,64]{1,3,2,0:T(8,128)(2,...) while((s32[]{:T(128)}, f32[1536,6,64]{0,2,1:T(8,128)}, ...), condition=%wide.region_33.34_spmd.clone, body=%wide.region_29.33_spmd.clone.sunk | while | flops 3093238784 | bytes 276796800 | solution.py:238
  1481.6 10.8 fusion.149
  1492.4 15.3 multiply_reduce_fusion.3
  1507.7 16.3 convert_reduce_fusion.4
  1532.6 7.8 fusion.153
  1549.5 9.2 fusion.149
  1558.6 15.2 multiply_reduce_fusion.3
  1573.8 16.3 convert_reduce_fusion.4
  1594.4 5.2 fusion.152
  1599.6 7.8 fusion.153
  1617.3 9.2 fusion.149
  1626.4 15.2 multiply_reduce_fusion.3
  1641.6 16.3 convert_reduce_fusion.4
  1667.4 7.8 fusion.153
  1690.9 9.6 convolution_convert_fusion.6
  1700.5 10.5 convolution_convert_fusion.7
  1711.0 9.6 convolution_convert_fusion.5
  1720.7 5.2 convolution_convert_fusion.8
  1726.4 7.4 reduce-window.36
  1734.2 46.3 %all-gather.26.cloned.1.call-done = bf16[3072,1152]{0,1:T(8,128)(2,1)} async-done(((bf16[1536,1152]{0,1:T(8,128)(2,1)}), bf16[3072,1152]{0,1:T(8,128)(2,1)}) %all-gather.26.cloned.1.call-update) | async-done | bytes 7077904 | tf_op jit(solution)/shard_map/all_gather | solution.py:101
  1780.5 11.2 convolution_convert_fusion.4
  1791.8 7.7 reduce-window.34
  1803.9 8.7 fusion.70
  1817.6 9.5 convolution_convert_fusion.1
  1830.3 11.9 all-reduce.4
  1843.4 81.6 %all-reduce.8.cloned.1.call-done = (bf16[768,1152]{1,0:T(8,128)(2,1)}, bf16[384,768]{1,0:T(8,128)(2,1)}, bf16[768,1024]{1,0:T(8,128)(2,1)}, bf16[768,1024]{1,0:T(8,128)(2,1)}, bf16[1024,768]{1,0:T(8,128)(2,1)}) async-done(((bf16[768,1152]{1,0:T(8,128)(2,1)}, bf16[384,768]{1,0:T(8,128)(2,1)}, bf16[768,1024]{1,0:T(8,128)(2,1)}, bf16[768,1024]{1,0:T(8,128)(2,1)}, bf16[1024,768]{1,0:T(8,128)(2,1)}), ...) | async-done | bytes 7077904 | tf_op jit(solution)/shard_map/psum | solution.py:270
  1935.3 77.7 %reduce-scatter.29.cloned.1.call-done = bf16[768,768]{1,0:T(8,128)(2,1)} async-done(((bf16[3072,768]{1,0:T(8,128)(2,1)}), bf16[768,768]{1,0:T(8,128)(2,1)}) %reduce-scatter.29.cloned.1.call-update) | async-done | bytes 1179664 | tf_op jit(solution)/shard_map/reduce_scatter | solution.py:77
  2015.5 34.9 %all-reduce.3 = (f32[768]{0:T(1024)}, f32[768]{0:T(1024)}) all-reduce(f32[768]{0:T(1024)S(1)} %get-tuple-element.219, f32[768]{0:T(1024)S(1)} %copy-done.35), channel_id=1, replica_groups=mesh['dp'=4,'row'=2,'col'=4] {'dp','col'}, use_global_device_ids=true, to_apply=%region_46.47 | all-reduce | flops 1536 | bytes 12288 | tf_op jit(solution)/shard_map/psum | solution.py:268
  2054.5 48.7 %reduce-scatter.21.cloned.1.call-done = bf16[768,768]{1,0:T(8,128)(2,1)} async-done(((bf16[3072,768]{1,0:T(8,128)(2,1)}), bf16[768,768]{1,0:T(8,128)(2,1)}) %reduce-scatter.21.cloned.1.call-update) | async-done | bytes 1179664 | tf_op jit(solution)/shard_map/reduce_scatter | solution.py:77
  (311 shorter events, 149.9 us)
Async XLA Ops:
  7.2 106.7 %copy-start = (bf16[768,1152]{1,0:T(8,128)(2,1)S(1)}, bf16[768,1152]{1,0:T(8,128)(2,1)}, u32[]{:S(2)}) copy-start(bf16[768,1152]{1,0:T(8,128)(2,1)} %param.20) | copy-start | bytes 5308420
  7.2 102.3 %copy-start.20 = (bf16[768,6]{0,1:T(8,128)(2,1)S(1)}, bf16[768,6]{0,1:T(8,128)(2,1)}, u32[]{:S(2)}) copy-start(bf16[768,6]{0,1:T(8,128)(2,1)} %param.21) | copy-start | bytes 27652
  7.2 102.3 %all-gather.10.cloned.1.call-start = ((), (), s32[]{:S(2)}) async-start(), calls=%async_computation.10 | async-start | bytes 5898240 | tf_op jit(solution)/shard_map/all_gather | solution.py:73
  17.1 108.9 %reduce-scatter.13.cloned.1.call-start = ((), (), s32[]{:S(2)}) async-start(), calls=%async_computation.12 | async-start | bytes 147456 | tf_op jit(solution)/shard_map/reduce_scatter | solution.py:95
  113.8 172.4 %reduce-scatter.11.cloned.1.call-start = ((), (), s32[]{:S(2)}) async-start(), calls=%async_computation.11 | async-start | bytes 21233664 | tf_op jit(solution)/shard_map/reduce_scatter | solution.py:94
  125.0 293.4 %all-gather.12.cloned.1.call-start = ((), (), s32[]{:S(2)}) async-start(), calls=%async_computation.13 | async-start | bytes 3538944 | tf_op jit(solution)/shard_map/all_gather | solution.py:83
  125.9 165.4 %copy-start.39 = (pred[4,4]{1,0:T(4,128)(4,1)}, pred[4,4]{1,0:T(4,128)(4,1)S(1)}, u32[]{:S(2)}) copy-start(pred[4,4]{1,0:T(4,128)(4,1)S(1)} %iota_compare_fusion.6) | copy-start | bytes 52
  125.9 3.7 copy-start.30
  126.0 6.0 copy-start.32
  126.1 3.6 copy-start.23
  304.3 7.3 copy-start.3
  329.9 7.3 copy-start.3
  355.5 7.3 copy-start.3
  380.7 37.6 %copy-start.44 = (bf16[384,768]{1,0:T(8,128)(2,1)S(1)}, bf16[384,768]{1,0:T(8,128)(2,1)}, u32[]{:S(2)}) copy-start(bf16[384,768]{1,0:T(8,128)(2,1)} %param.23) | copy-start | bytes 1769476
  382.1 128.2 %reduce-scatter.15.cloned.1.call-start = ((), (), s32[]{:S(2)}) async-start(), calls=%async_computation.14 | async-start | bytes 5898240 | tf_op jit(solution)/shard_map/reduce_scatter | solution.py:77
  424.8 85.5 %copy-start.4 = (bf16[768,768]{1,0:T(8,128)(2,1)S(1)}, bf16[768,768]{1,0:T(8,128)(2,1)}, u32[]{:S(2)}) copy-start(bf16[768,768]{1,0:T(8,128)(2,1)} %param.18) | copy-start | bytes 3538948
  424.8 91.0 %copy-start.18 = (f32[768]{0:T(1024)S(1)}, f32[768]{0:T(1024)}, u32[]{:S(2)}) copy-start(f32[768]{0:T(1024)} %param.24) | copy-start | bytes 9220
  424.8 176.9 %all-gather.18.cloned.1.call-start = ((), (), s32[]{:S(2)}) async-start(), calls=%async_computation.20 | async-start | bytes 5898240 | tf_op jit(solution)/shard_map/all_gather | solution.py:73
  425.4 266.3 %all-gather.14.cloned.1.call-start = ((), (), s32[]{:S(2)}) async-start(), calls=%async_computation.15 | async-start | bytes 5898240 | tf_op jit(solution)/shard_map/all_gather | solution.py:73
  515.8 823.4 %copy-start.14 = (f32[768]{0:T(1024)}, f32[768]{0:T(1024)S(1)}, u32[]{:S(2)}) copy-start(f32[768]{0:T(1024)S(1)} %get-tuple-element.300) | copy-start | bytes 9220
  515.8 823.4 %copy-start.25 = (f32[768]{0:T(1024)}, f32[768]{0:T(1024)S(1)}, u32[]{:S(2)}) copy-start(f32[768]{0:T(1024)S(1)} %get-tuple-element.299) | copy-start | bytes 9220
  518.6 250.9 %reduce-scatter.23.cloned.1.call-start = ((), (), s32[]{:S(2)}) async-start(), calls=%async_computation.21 | async-start | bytes 9437184 | tf_op jit(solution)/shard_map/reduce_scatter | solution.py:87
  611.4 305.0 %reduce-scatter.19.cloned.1.call-start = ((), (), s32[]{:S(2)}) async-start(), calls=%async_computation.17 | async-start | bytes 18874368 | tf_op jit(solution)/shard_map/reduce_scatter | solution.py:95
  701.8 361.4 %reduce-scatter.17.cloned.1.call-start = ((), (), s32[]{:S(2)}) async-start(), calls=%async_computation.16 | async-start | bytes 18874368 | tf_op jit(solution)/shard_map/reduce_scatter | solution.py:94
  712.3 441.4 %all-gather.20.cloned.1.call-start = ((), (), s32[]{:S(2)}) async-start(), calls=%async_computation.22 | async-start | bytes 9437184 | tf_op jit(solution)/shard_map/all_gather | solution.py:101
  1073.1 163.0 %all-gather.22.cloned.1.call-start = ((), (), s32[]{:S(2)}) async-start(), calls=%async_computation.23 | async-start | bytes 9437184 | tf_op jit(solution)/shard_map/all_gather | solution.py:102
  1073.7 258.5 %reduce-scatter.25.cloned.1.call-start = ((), (), s32[]{:S(2)}) async-start(), calls=%async_computation.24 | async-start | bytes 5898240 | tf_op jit(solution)/shard_map/reduce_scatter | solution.py:77
  1246.7 187.8 %all-gather.24.cloned.1.call-start = ((), (), s32[]{:S(2)}) async-start(), calls=%async_computation.25 | async-start | bytes 5898240 | tf_op jit(solution)/shard_map/all_gather | solution.py:73
  1339.2 4.0 copy-start.27
  1343.2 131.0 %reduce-scatter.27.cloned.1.call-start = ((), (), s32[]{:S(2)}) async-start(), calls=%async_computation.26 | async-start | bytes 3538944 | tf_op jit(solution)/shard_map/reduce_scatter | solution.py:87
  1441.1 269.9 %all-gather.16.cloned.1.call-start = ((), (), s32[]{:S(2)}) async-start(), calls=%async_computation.18 | async-start | bytes 9437184 | tf_op jit(solution)/shard_map/all_gather | solution.py:83
  1441.2 35.5 %copy-start.6 = (bf16[1536,6,64]{0,2,1:T(8,128)(2,1)S(1)}, bf16[1536,6,64]{0,2,1:T(8,128)(2,1)}, u32[]{:S(2)}) copy-start(bf16[1536,6,64]{0,2,1:T(8,128)(2,1)} %get-tuple-element.600) | copy-start | bytes 3538948
  1441.7 338.9 %all-gather.26.cloned.1.call-start = ((), (), s32[]{:S(2)}) async-start(), calls=%async_computation.27 | async-start | bytes 10616832 | tf_op jit(solution)/shard_map/all_gather | solution.py:101
  1481.5 10.8 copy-start.12
  1507.7 20.6 copy-start.1
  1532.6 7.8 copy-start.2
  1549.5 9.2 copy-start.12
  1573.8 20.6 copy-start.1
  1599.6 7.8 copy-start.2
  1617.2 9.2 copy-start.12
  1641.6 20.6 copy-start.1
  1667.4 7.8 copy-start.2
  1685.5 2.9 copy-start.7
  1690.9 234.1 %all-reduce.8.cloned.1.call-start = ((), (), s32[]{:S(2)}) async-start(), calls=%async_computation.29 | async-start | bytes 14155776 | tf_op jit(solution)/shard_map/psum | solution.py:270
  1711.0 9.6 copy-start.42
  1720.7 5.2 copy-start.33
  1720.7 5.4 copy-start.40
  1720.7 5.6 copy-start.24
  1791.7 8.2 copy-start.31
  1791.7 8.4 copy-start.13
  1791.7 8.4 copy-start.38
  1791.7 221.4 %reduce-scatter.29.cloned.1.call-start = ((), (), s32[]{:S(2)}) async-start(), calls=%async_computation.28 | async-start | bytes 5898240 | tf_op jit(solution)/shard_map/reduce_scatter | solution.py:77
  1803.9 8.7 copy-start.21
  1816.2 287.0 %reduce-scatter.21.cloned.1.call-start = ((), (), s32[]{:S(2)}) async-start(), calls=%async_computation.19 | async-start | bytes 5898240 | tf_op jit(solution)/shard_map/reduce_scatter | solution.py:77
  1925.0 2.3 copy-start.8
  1933.4 79.7 %copy-start.5 = (bf16[768,768]{1,0:T(8,128)(2,1)S(1)}, bf16[768,768]{1,0:T(8,128)(2,1)}, u32[]{:S(2)}) copy-start(bf16[768,768]{1,0:T(8,128)(2,1)} %param.18) | copy-start | bytes 3538948
  1933.4 79.7 %copy-start.17 = (f32[768]{0:T(1024)S(1)}, f32[768]{0:T(1024)}, u32[]{:S(2)}) copy-start(f32[768]{0:T(1024)} %copy-done.16) | copy-start | bytes 9220
  1933.4 79.7 %copy-start.22 = (f32[768]{0:T(1024)S(1)}, f32[768]{0:T(1024)}, u32[]{:S(2)}) copy-start(f32[768]{0:T(1024)} %param.19) | copy-start | bytes 9220
  1935.3 80.1 %copy-start.35 = (f32[768]{0:T(1024)S(1)}, f32[768]{0:T(1024)}, u32[]{:S(2)}) copy-start(f32[768]{0:T(1024)} %get-tuple-element.217) | copy-start | bytes 9220
  1935.3 167.9 %copy-start.15 = (f32[768]{0:T(1024)S(1)}, f32[768]{0:T(1024)}, u32[]{:S(2)}) copy-start(f32[768]{0:T(1024)} %copy-done.14) | copy-start | bytes 9220
  1935.3 167.9 %copy-start.19 = (f32[768]{0:T(1024)S(1)}, f32[768]{0:T(1024)}, u32[]{:S(2)}) copy-start(f32[768]{0:T(1024)} %param.24) | copy-start | bytes 9220
  1935.3 167.9 %copy-start.26 = (f32[768]{0:T(1024)S(1)}, f32[768]{0:T(1024)}, u32[]{:S(2)}) copy-start(f32[768]{0:T(1024)} %copy-done.25) | copy-start | bytes 9220
  1935.3 167.9 %copy-start.28 = (f32[768]{0:T(1024)S(1)}, f32[768]{0:T(1024)}, u32[]{:S(2)}) copy-start(f32[768]{0:T(1024)} %copy-done.27) | copy-start | bytes 9220
  1935.3 167.9 %copy-start.34 = (f32[768]{0:T(1024)S(1)}, f32[768]{0:T(1024)}, u32[]{:S(2)}) copy-start(f32[768]{0:T(1024)} %get-tuple-element.297) | copy-start | bytes 9220
  (9 other events, 11.4 us)
Sparse Core Ops, SparseCore 0:
  17.3 92.1 all-gather.9
  113.9 8.1 reduce-scatter.12
  125.1 161.0 reduce-scatter.10
  382.2 36.0 all-gather.11
  424.9 85.3 reduce-scatter.14
  511.7 89.9 all-gather.17
  603.8 87.8 all-gather.13
  694.0 75.4 reduce-scatter.22
  771.9 144.4 reduce-scatter.18
  918.7 144.4 reduce-scatter.16
  1073.3 80.3 all-gather.19
  1155.7 80.3 all-gather.21
  1246.8 85.3 reduce-scatter.24
  1343.4 91.1 all-gather.23
  1441.2 33.0 reduce-scatter.26
  1476.3 80.3 all-gather.15
  1691.0 89.4 all-gather.25
  1791.8 133.0 all-reduce.7
  1927.3 85.7 reduce-scatter.28
  2015.2 87.9 reduce-scatter.20
where the time goes:
time: 2120 us
  waiting for transfers between devices  1500 us (71%)
  matrix products  325 us (15%)
  other arithmetic  153 us (7%)
  blocking collectives  66.6 us (3%)
  local copies, waits for them, and re-layouts  44.4 us (2%)
    all_gather x4, waiting for transfers between devices, gather_tokens(): return lax.all_gather(token_rows, 'col', axis=0, tiled=True)  347 us
    reduce_scatter x2, waiting for transfers between devices, sum_pair(): lax.psum_scatter(first, 'row', scatter_dimension=0, tiled=True)  301 us
    reduce_scatter x4, waiting for transfers between devices, sum_tokens(): lax.psum_scatter(partial_value.astype(jnp.bfloat16), 'col', scatter_dimen...  297 us
    reduce_scatter x2, waiting for transfers between devices, sum_pair(): lax.psum_scatter(second, 'row', scatter_dimension=0, tiled=True)  147 us
    all_gather x2, waiting for transfers between devices, gather_pair(): lax.all_gather(first, 'row', axis=0, tiled=True)  126 us
    reduce_scatter x2, waiting for transfers between devices, sum_group(): lax.psum_scatter(partial_value.astype(jnp.bfloat16), 'row', scatter_dimen...  89.6 us
    psum x1, waiting for transfers between devices, shards(): lax.psum(qkv_grad.astype(jnp.bfloat16), 'dp').astype(jnp.float32)  81.6 us
    all_gather x1, waiting for transfers between devices, gather_pair(): lax.all_gather(second, 'row', axis=0, tiled=True)  72.4 us
  transfers between devices with their start and end apart: 20, of which 18 were waited for; matrix products, arithmetic and copies ran while one was open for 16% of the time, Pallas kernels for 0%

commit v1 on v0

v1 whole, which is shorter than its diff:
```python
import jax
import jax.numpy as jnp
from jax import lax
from jax.sharding import Mesh, PartitionSpec as P

D = 1536
DH = 64
DOCS = 4
QBLK = 512
EPS = 1e-06
MASKED = -1e30
LANES = 128
BF16 = jnp.bfloat16
F32 = jnp.float32


def swap(value, axis):
    return lax.ppermute(value, axis, [(0, 1), (1, 0)])


def xor_swap(value, axis, size, bit):
    return lax.ppermute(value, axis, [(i, i ^ bit) for i in range(size)])


def kxh(k, x, h):
    return (k * 2 + x) * 2 + h


def fetch_home_away(value):
    pairs = []
    for k in range(2):
        for x in range(2):
            for h in range(2):
                target = (k, 1 - x, h) if k == h else (1 - k, x, 1 - h)
                pairs.append((kxh(k, x, h), kxh(*target)))
    return lax.ppermute(value, ("k", "x", "h"), pairs)


def fetch_away(value):
    pairs = [
        (kxh(k, x, 1 - k), kxh(k, 1 - x, 1 - k)) for k in range(2) for x in range(2)
    ]
    return lax.ppermute(value, ("k", "x", "h"), pairs)


def gather_weight(shard, home, axis):
    first = fetch_home_away(shard)
    second = fetch_away(first)
    mine = jnp.where(home, shard, first)
    other = jnp.where(home, first, second)
    return jnp.concatenate([mine, other], axis=axis)


def reduce_weight(own, other, home, home_steps):
    total = own + swap(other.astype(BF16), "x").astype(F32)
    moved = lax.ppermute(
        total.astype(BF16), ("k", "h"), [(0 * 2 + 1, 0 * 2 + 0), (1 * 2 + 0, 1 * 2 + 1)]
    )
    total = (total + moved.astype(F32)).astype(BF16)
    for size, bit in home_steps:
        pairs = []
        for o in range(size):
            for k in range(2):
                pairs.append(((o * 2 + k) * 2 + k, ((o ^ bit) * 2 + k) * 2 + k))
        moved = lax.ppermute(total, ("o", "k", "h"), pairs)
        total = (total.astype(F32) + moved.astype(F32)).astype(BF16)
    moved = lax.ppermute(total, ("k", "h"), [(0, 2), (3, 1)])
    return jnp.where(home, total, moved).astype(F32)


def take_half(value, index):
    half = value.shape[0] // 2
    return lax.dynamic_slice_in_dim(value, index * half, half, 0)


def kx(k, x):
    return k * 2 + x


SPREAD_A = []
SPREAD_B = []
for _k in range(2):
    for _x in range(2):
        if _k == _x:
            SPREAD_A.append((kx(_k, _x), kx(1 - _k, _x)))
        else:
            SPREAD_A.append((kx(_k, _x), kx(_k, 1 - _x)))
            SPREAD_B.append((kx(_k, _x), kx(1 - _k, 1 - _x)))


def spread_tokens(block, core, same):
    near = take_half(block, core)
    far = take_half(block, 1 - core)
    first = lax.ppermute(jnp.where(same, far, near), ("k", "x"), SPREAD_A)
    second = lax.ppermute(far, ("k", "x"), SPREAD_B)
    own = jnp.where(same, near, first)
    other = jnp.where(same, first, second)
    return jnp.concatenate([own, other], axis=1)


def unspread_tokens(rows, core, same):
    half = rows.shape[1] // 2
    own, other = rows[:, :half], rows[:, half:]
    first = lax.ppermute(
        jnp.where(same, other, own), ("k", "x"), [(b, a) for a, b in SPREAD_A]
    )
    second = lax.ppermute(other, ("k", "x"), [(b, a) for a, b in SPREAD_B])
    near = jnp.where(same, own, first)
    far = jnp.where(same, first, second)
    low = jnp.where(core == 0, near, far)
    high = jnp.where(core == 0, far, near)
    return jnp.concatenate([low, high], axis=0)


def gather_blocks(block, psize):
    blocks = []
    for bit in range(psize):
        moved = block if bit == 0 else xor_swap(block, "p", psize, bit)
        blocks += [moved, swap(moved, "k")]
    return jnp.concatenate(blocks, axis=0)


def sum_blocks(partial, psize):
    size = partial.shape[0] // (2 * psize)
    parts = [partial[i * size : (i + 1) * size] for i in range(2 * psize)]
    total = None
    for bit in reversed(range(psize)):
        pair = parts[2 * bit] + swap(parts[2 * bit + 1].astype(BF16), "k").astype(F32)
        if bit:
            pair = xor_swap(pair.astype(BF16), "p", psize, bit).astype(F32)
        total = pair if total is None else total + pair
    return total


def reorder(rows, me, count):
    parts = rows.reshape((count, rows.shape[0] // count) + rows.shape[1:])
    taken = [lax.dynamic_index_in_dim(parts, j ^ me, 0, keepdims=False) for j in range(count)]
    return jnp.concatenate(taken, axis=0)


def contract_rows(left, right):
    return lax.dot_general(
        left, right, (((0,), (0,)), ((), ())), preferred_element_type=F32
    )


def contract_cols(left, right):
    return lax.dot_general(
        left, right, (((1,), (1,)), ((), ())), preferred_element_type=F32
    )


def matmul(left, right):
    return jnp.dot(left, right, preferred_element_type=F32)


def split3(value):
    high = lax.reduce_precision(value, 8, 7)
    rest = value - high
    mid = lax.reduce_precision(rest, 8, 7)
    return jnp.concatenate([high, mid, rest - mid], axis=1).astype(BF16)


def sum3(value):
    n = value.shape[1] // 3
    return value[:, :n] + value[:, n : 2 * n] + value[:, 2 * n :]


def visible(row_start, doc_query, branch_query, doc_key, branch_key):
    pos_query = row_start + jnp.arange(doc_query.shape[0], dtype=jnp.int32)
    pos_key = jnp.arange(doc_key.shape[0], dtype=jnp.int32)
    causal = pos_key[None, :] <= pos_query[:, None]
    same_doc = doc_query[:, None] == doc_key[None, :]
    same_branch = (branch_key[None, :] < 0) | (branch_query[:, None] == branch_key[None, :])
    return causal & same_doc & same_branch


def block_scores(query_block, key_rows, decay_query, decay_key, allowed):
    raw_scores = jnp.einsum(
        "qhd,khd->hqk", query_block, key_rows, preferred_element_type=jnp.float32
    )
    scores = raw_scores * DH ** (-0.5) + decay_query.T[:, :, None] - decay_key.T[:, None, :]
    return jnp.where(allowed[None], scores, MASKED)


def attention(qkv, decay_sum, doc_ids, branch_tags):
    group_len, heads = qkv.shape[0], qkv.shape[1]
    queries, key_rows, value_rows = qkv[:, :, 0], qkv[:, :, 1], qkv[:, :, 2]
    blocks = jnp.arange(group_len // QBLK, dtype=jnp.int32)

    def block_view(block_index):
        row_start = block_index * QBLK
        query_block = lax.dynamic_slice_in_dim(queries, row_start, QBLK, 0)
        decay_query = lax.dynamic_slice_in_dim(decay_sum, row_start, QBLK, 0)
        doc_query = lax.dynamic_slice_in_dim(doc_ids, row_start, QBLK, 0)
        branch_query = lax.dynamic_slice_in_dim(branch_tags, row_start, QBLK, 0)
        allowed = visible(row_start, doc_query, branch_query, doc_ids, branch_tags)
        scores = block_scores(query_block, key_rows, decay_query, decay_sum, allowed)
        return (row_start, query_block, scores)

    def forward_block(block_index):
        row_start, query_block, scores = block_view(block_index)
        row_max = jnp.max(scores, axis=2, keepdims=True)
        expo = jnp.exp(scores - row_max)
        row_total = jnp.sum(expo, axis=2, keepdims=True)
        probs = (expo / row_total).astype(BF16)
        attended_block = jnp.einsum(
            "hqk,khd->qhd", probs, value_rows, preferred_element_type=jnp.float32
        ).astype(BF16)
        return (attended_block, (row_max + jnp.log(row_total))[:, :, 0])

    attended_blocks, lse_blocks = lax.map(forward_block, blocks)
    attended = attended_blocks.reshape(group_len, heads * DH)

    def backward(grad_attended):
        def back_block(carry, block_index):
            key_acc, value_acc, decay_keys = carry
            row_start, query_block, scores = block_view(block_index)
            grad_block = lax.dynamic_slice_in_dim(grad_attended, row_start, QBLK, 0)
            lse_block = lax.dynamic_index_in_dim(lse_blocks, block_index, 0, keepdims=False)
            probs_star = jnp.exp(scores - lse_block[:, :, None])
            grad_probs = jnp.einsum(
                "qhd,khd->hqk", grad_block, value_rows, preferred_element_type=jnp.float32
            )
            row_delta = jnp.sum(probs_star * grad_probs, axis=2, keepdims=True)
            grad_scores = (probs_star * (grad_probs - row_delta)).astype(BF16)
            grad_query = jnp.einsum(
                "hqk,khd->qhd", grad_scores, key_rows, preferred_element_type=jnp.float32
            ) * DH ** (-0.5)
            key_acc = key_acc + jnp.einsum(
                "hqk,qhd->khd", grad_scores, query_block, preferred_element_type=jnp.float32
            )
            value_acc = value_acc + jnp.einsum(
                "hqk,qhd->khd", probs_star.astype(BF16), grad_block, preferred_element_type=F32
            )
            decay_rows = jnp.sum(grad_scores, axis=2, dtype=F32)
            decay_keys = decay_keys - jnp.sum(grad_scores, axis=1, dtype=F32)
            return ((key_acc, value_acc, decay_keys), (grad_query, decay_rows))

        zero_rows = jnp.zeros((group_len, heads, DH), F32)
        carried, stacked = lax.scan(
            back_block, (zero_rows, zero_rows, jnp.zeros((heads, group_len), F32)), blocks
        )
        key_acc, value_acc, decay_keys = carried
        query_blocks, decay_blocks = stacked
        grad_query = query_blocks.reshape(group_len, heads, DH)
        grad_decay = jnp.transpose(decay_blocks, (0, 2, 1)).reshape(group_len, heads) + decay_keys.T
        grad_qkv = (
            jnp.stack([grad_query, key_acc * DH ** (-0.5), value_acc], axis=2)
            .astype(BF16)
            .reshape(group_len, heads * 3 * DH)
        )
        return grad_qkv, grad_decay

    return attended, backward


def make_shards(osize, psize):
    count = 2 * psize
    home_steps = []
    bit = 1
    while bit < osize:
        home_steps.append((osize, bit))
        bit *= 2

    def shards(
        layer_input,
        attn_gain,
        qkv_weight,
        forget_weight,
        forget_bias,
        out_weight,
        ffn_gain,
        gate_weight,
        up_weight,
        down_weight,
        prompt_doc,
        branch_seg,
        branch_doc,
        out_cotangent,
    ):
        core, xpos = lax.axis_index("k"), lax.axis_index("x")
        hpos, ppos = lax.axis_index("h"), lax.axis_index("p")
        home = core == hpos
        same = core == xpos
        me = ppos * 2 + core
        heads = forget_weight.shape[1]

        prompt_len, branch_len = prompt_doc.shape[1], branch_seg.shape[1]
        packed = jnp.concatenate([prompt_doc[0], branch_seg[0], branch_doc[0]])
        sibling = swap(packed, "k")
        of_x = jnp.where(core == xpos, packed, sibling)
        of_peer = jnp.where(core == xpos, sibling, packed)
        from_peer = swap(of_peer, "x")
        packed = jnp.where(hpos == xpos, of_x, from_peer)
        prompt_ids = packed[:prompt_len]
        branch_ids = packed[prompt_len : prompt_len + branch_len]
        branch_docs = packed[prompt_len + branch_len :]

        gains = jnp.stack([attn_gain, ffn_gain])
        gains = jnp.concatenate([gains, swap(gains, "x")], axis=1)
        gain_a, gain_b = gains[0], gains[1]

        lane_pad = LANES - heads
        w_forget = gather_weight(
            jnp.concatenate([forget_weight, jnp.zeros((forget_weight.shape[0], lane_pad), BF16)], 1),
            home,
            0,
        )
        bias = jnp.where(home, forget_bias, lax.ppermute(forget_bias, ("k", "h"), [(1, 2), (2, 1)]))
        w_qkv = jnp.concatenate([gather_weight(qkv_weight, home, 0), w_forget], axis=1)
        w_out = gather_weight(out_weight, home, 1)
        w_gate = gather_weight(gate_weight, home, 0)
        w_up = gather_weight(up_weight, home, 0)
        w_down = gather_weight(down_weight, home, 1)

        stream = spread_tokens(layer_input, core, same).astype(F32)
        cot = spread_tokens(out_cotangent, core, same)
        cot_all = gather_blocks(cot, psize)
        cotangent = cot.astype(F32)

        rms_a = lax.rsqrt(jnp.sum(stream * stream, axis=1) / D + EPS)[:, None]
        normed_a_all = gather_blocks((stream * rms_a * gain_a).astype(BF16), psize)
        projected = reorder(matmul(normed_a_all, w_qkv), me, count)
        group_len = projected.shape[0]
        width = heads * 3 * DH
        qkv = projected[:, :width].astype(BF16).reshape(group_len, heads, 3, DH)
        forget_logit = projected[:, width : width + heads] + bias
        log_rate = jax.nn.log_sigmoid(forget_logit)

        member = branch_ids[:, None] == jnp.arange(branch_docs.shape[0])[None, :]
        branch_doc_ids = jnp.sum(jnp.where(member, branch_docs[None, :], 0), axis=1)
        doc_ids = jnp.concatenate([prompt_ids, branch_doc_ids])
        branch_tags = jnp.concatenate([jnp.full((prompt_len,), -1, jnp.int32), branch_ids])
        pos = jnp.arange(group_len, dtype=jnp.int32)
        key_prompt = branch_tags[None, :] < 0
        query_prompt = branch_tags[:, None] < 0
        causal = pos[None, :] <= pos[:, None]
        sums = jnp.where(
            query_prompt,
            causal,
            jnp.where(
                key_prompt,
                doc_ids[None, :] <= doc_ids[:, None],
                causal & (branch_tags[None, :] == branch_tags[:, None]),
            ),
        ).astype(BF16)
        decay_sum = sum3(matmul(sums, split3(log_rate)))

        attended, attention_back = attention(qkv, decay_sum, doc_ids, branch_tags)
        attended = reorder(attended, me, count)
        resid = stream + sum_blocks(matmul(attended, w_out), psize)
        rms_b = lax.rsqrt(jnp.sum(resid * resid, axis=1) / D + EPS)[:, None]
        normed_b_all = gather_blocks((resid * rms_b * gain_b).astype(BF16), psize)
        gate_pre = matmul(normed_b_all, w_gate)
        up_pre = matmul(normed_b_all, w_up)
        gate_sig = jax.nn.sigmoid(gate_pre)
        gate_act = gate_pre * gate_sig
        hidden = (gate_act * up_pre).astype(BF16)
        layer_output = (resid + sum_blocks(matmul(hidden, w_down), psize)).astype(BF16)
        layer_output = unspread_tokens(layer_output, core, same)

        feat = D // 2

        def reduce_rows(grad):
            return reduce_weight(grad[:feat], grad[feat:], home, home_steps)

        def reduce_cols(grad):
            return reduce_weight(grad[:, :feat], grad[:, feat:], home, home_steps)

        down_grad = reduce_cols(contract_rows(hidden, cot_all))
        grad_hidden = contract_cols(cot_all, w_down)
        grad_gate = (grad_hidden * up_pre * gate_sig * (1.0 + gate_pre * (1.0 - gate_sig))).astype(BF16)
        grad_up = (grad_hidden * gate_act).astype(BF16)
        gate_grad = reduce_rows(contract_rows(normed_b_all, grad_gate))
        up_grad = reduce_rows(contract_rows(normed_b_all, grad_up))
        grad_normed_b = sum_blocks(
            contract_cols(grad_gate, w_gate) + contract_cols(grad_up, w_up), psize
        )
        gained_b = gain_b * grad_normed_b
        inner_b = jnp.sum(resid * gained_b, axis=1)[:, None]
        ffn_gain_part = jnp.sum(grad_normed_b * resid * rms_b, axis=0)
        grad_resid = cotangent + rms_b * gained_b - resid * (rms_b * rms_b * rms_b) * inner_b / D
        grad_branch_all = gather_blocks(grad_resid.astype(BF16), psize)
        out_grad = reduce_cols(contract_rows(attended, grad_branch_all))
        grad_attended = reorder(contract_cols(grad_branch_all, w_out).astype(BF16), me, count)
        grad_qkv, grad_decay = attention_back(grad_attended.reshape(group_len, heads, DH))
        grad_log_rate = sum3(contract_rows(sums, split3(grad_decay)))
        grad_forget = (grad_log_rate * jax.nn.sigmoid(-forget_logit)).astype(BF16)
        forget_bias_part = jnp.sum(grad_forget, axis=0, dtype=F32)
        grad_proj = reorder(
            jnp.concatenate(
                [grad_qkv, grad_forget, jnp.zeros((group_len, lane_pad), BF16)], axis=1
            ),
            me,
            count,
        )
        proj_grad = reduce_rows(contract_rows(normed_a_all, grad_proj))
        qkv_grad, forget_grad = proj_grad[:, :width], proj_grad[:, width : width + heads]
        grad_normed_a = sum_blocks(contract_cols(grad_proj, w_qkv), psize)
        gained_a = gain_a * grad_normed_a
        inner_a = jnp.sum(stream * gained_a, axis=1)[:, None]
        attn_gain_part = jnp.sum(grad_normed_a * stream * rms_a, axis=0)
        input_grad = (
            grad_resid + rms_a * gained_a - stream * (rms_a * rms_a * rms_a) * inner_a / D
        ).astype(BF16)
        input_grad = unspread_tokens(input_grad, core, same)

        slots = jnp.where(
            (jnp.arange(2 * psize) == core * psize + ppos)[:, None], forget_bias_part[None, :], 0.0
        ).reshape(-1)
        small = jnp.concatenate([attn_gain_part[:feat], ffn_gain_part[:feat], slots])
        sent = jnp.concatenate([attn_gain_part[feat:], ffn_gain_part[feat:], slots])
        small = small + swap(sent, "x")
        small = lax.psum(small, ("o", "k", "h", "p"))
        bias_all = small[2 * feat :].reshape(2 * psize, heads)
        forget_bias_grad = lax.dynamic_index_in_dim(bias_all, hpos * psize + ppos, 0, keepdims=False)

        return (
            layer_output,
            input_grad,
            small[:feat],
            qkv_grad,
            forget_grad,
            forget_bias_grad,
            out_grad,
            small[feat : 2 * feat],
            gate_grad,
            up_grad,
            down_grad,
        )

    return shards


def solution(mesh):
    dp, row, col = mesh.shape["dp"], mesh.shape["row"], mesh.shape["col"]
    osize, psize = dp // 2, col // 2
    assert row == 2
    split = Mesh(mesh.devices.reshape(osize, 2, row, 2, psize), ("o", "k", "x", "h", "p"))
    tokens = P(("o", "k", "h", "p"), "x")
    rows_first = P("x", ("h", "p"))
    cols_first = P(("h", "p"), "x")
    groups = P(("o", "k", "x"), None)
    in_specs = (
        tokens,
        P("x"),
        rows_first,
        rows_first,
        P(("h", "p")),
        cols_first,
        P("x"),
        rows_first,
        rows_first,
        cols_first,
        groups,
        groups,
        groups,
        tokens,
    )
    out_specs = (
        tokens,
        tokens,
        P("x"),
        rows_first,
        rows_first,
        P(("h", "p")),
        cols_first,
        P("x"),
        rows_first,
        rows_first,
        cols_first,
    )
    return jax.shard_map(
        make_shards(osize, psize), mesh=split, in_specs=in_specs, out_specs=out_specs, check_vma=False
    )
```

time: 2120 us -> 1130 us (0.53)
  waiting for transfers between devices: 1500 us -> 288 us
  starting transfers between devices: 1 us -> 170 us
  local copies, waits for them, and re-layouts: 44.4 us -> 136 us
  blocking collectives: 66.6 us -> 28.7 us
  other arithmetic: 153 us -> 176 us
    reduce_scatter x10 -> x0, waiting for transfers between devices: 834 us -> none  [the longest x2 301 us: sum_pair(): lax.psum_scatter(first, 'row', scatter_dimension=0, tiled=True)]
    all_gather x9 -> x0, waiting for transfers between devices: 582 us -> none  [the longest x4 347 us: gather_tokens(): return lax.all_gather(token_rows, 'col', axis=0, tiled=True)]
    ppermute x0 -> x69, waiting for transfers between devices: none -> 288 us  [the longest x6 79.6 us: fetch_home_away(): return lax.ppermute(value, ('k', 'x', 'h'), pairs)]
    ppermute x0 -> x69, starting transfers between devices: none -> 170 us  [the longest x5 50.6 us: reduce_weight(): lax.ppermute(total.astype(BF16), ('k', 'h'), [(0 * 2 + 1, 0 * 2 + 0), (1...]
    psum x1 -> x0, waiting for transfers between devices: 81.6 us -> none  [shards(): lax.psum(qkv_grad.astype(jnp.bfloat16), 'dp').astype(jnp.float32)]
    dynamic_slice x6 -> x26, local copies, waits for them, and re-layouts: 3.51 us -> 66.7 us  [the longest x20 61 us: reorder(): lax.dynamic_index_in_dim(parts, j ^ me, 0, keepdims=False)]
    psum x6 -> x1, blocking collectives: 62.9 us -> 28.7 us  [shards(): small = lax.psum(small, ('o', 'k', 'h', 'p'))]
    convert_element_type x13 -> x27, other arithmetic: 35.9 us -> 46.5 us  [the longest x5 11.7 us: reduce_weight(): total = (total + moved.astype(F32)).astype(BF16)]
  transfers between devices with their start and end apart: 20 -> 69, of which waited for: 18 -> 21; matrix products, arithmetic and copies ran while one was open for 16% -> 39% of each run, Pallas kernels for 0% -> 0%
where the time goes in v1:
time: 1130 us; the launch traced here: 1120 us
  matrix products  312 us (28%)
  waiting for transfers between devices  288 us (25%)
  other arithmetic  176 us (16%)
  starting transfers between devices  170 us (15%)
  local copies, waits for them, and re-layouts  136 us (12%)
  blocking collectives  28.7 us (3%)
    ppermute x6, waiting for transfers between devices, fetch_home_away(): return lax.ppermute(value, ('k', 'x', 'h'), pairs)  79.6 us
    ppermute x8, waiting for transfers between devices, xor_swap(): return lax.ppermute(value, axis, [(i, i ^ bit) for i in range(size)])  76.5 us
    ppermute x25, waiting for transfers between devices, swap(): return lax.ppermute(value, axis, [(0, 1), (1, 0)])  69.4 us
    dot_general x6, matrix products, block_scores(): jnp.einsum('qhd,khd->hqk', query_block, key_rows, preferred_element_type=...  67.5 us
    dynamic_slice x20, local copies, waits for them, and re-layouts, reorder(): lax.dynamic_index_in_dim(parts, j ^ me, 0, keepdims=False)  61 us
    dot_general x5, matrix products, contract_cols(): lax.dot_general(left, right, (((1,), (1,)), ((), ())), preferred_element_...  51.7 us
    ppermute x5, starting transfers between devices, reduce_weight(): lax.ppermute(total.astype(BF16), ('k', 'h'), [(0 * 2 + 1, 0 * 2 + 0), (1...  50.6 us
    reduce_sum x3, other arithmetic, back_block(): decay_rows = jnp.sum(grad_scores, axis=2, dtype=F32)  50.2 us
  transfers between devices with their start and end apart: 69, of which 21 were waited for; matrix products, arithmetic and copies ran while one was open for 39% of the time, Pallas kernels for 0%

profile of v1, /device:TPU:1, one launch (start us, length us, event | category | flops | bytes accessed | tf_op | source)
XLA Modules:
  0.0 1124.5 jit_solution(10222361121342258962)
XLA Ops:
  14.1 20.0 %collective-permute-done.4 = f32[2,768]{1,0:T(2,128)} collective-permute-done((f32[2,768]{1,0:T(2,128)}, f32[2,768]{1,0:T(2,128)}, u32[]{:S(2)}, u32[]{:S(2)}) %collective-permute-start.4) | collective-permute-done | bytes 6176 | tf_op jit(solution)/shard_map/ppermute | solution.py:18
  52.9 19.7 %collective-permute-done.3 = s32[1540]{0:T(1024)S(1)} collective-permute-done((s32[1540]{0:T(1024)S(1)}, s32[1540]{0:T(1024)S(1)}, u32[]{:S(2)}, u32[]{:S(2)}) %collective-permute-start.3) | collective-permute-done | bytes 6192 | tf_op jit(solution)/shard_map/ppermute | solution.py:18
  90.6 9.8 fusion.73
  124.5 71.8 %while.31 = (s32[]{:T(128)}, bf16[3,512,6,64]{1,3,2,0:T(8,128)(2,1)}, f32[3,6,512]{2,1,0:T(8,128)S(1)}, s32[3]{0:T(128)S(1)}, s32[1536]{0:T(1024)S(1)}, /*index=...) while((s32[]{:T(128)}, ...), condition=%wide.region_5.6_spmd, body=%wide.region_2.5_spmd.sunk | while | flops 1297808384 | bytes 63235796 | solution.py:212
  127.6 7.0 fusion.164
  134.5 6.5 fusion.165
  141.1 7.5 fusion.166
  151.4 7.0 fusion.164
  158.4 6.5 fusion.165
  165.0 7.5 fusion.166
  175.3 7.0 fusion.164
  182.3 6.5 fusion.165
  188.8 7.5 fusion.166
  234.9 8.0 collective-permute-done.33
  249.5 28.2 %collective-permute-done.23 = bf16[768,1024]{1,0:T(8,128)(2,1)} collective-permute-done((bf16[768,1024]{1,0:T(8,128)(2,1)S(1)}, bf16[768,1024]{1,0:T(8,128)(2,1)}, u32[]{:S(2)}, u32[]{:S(2)}) %collective-permute-start.23) | collective-permute-done | bytes 1572896 | tf_op jit(solution)/shard_map/ppermute | solution.py:36
  277.7 34.5 %collective-permute-done.25 = bf16[1024,768]{1,0:T(8,128)(2,1)S(1)} collective-permute-done((bf16[1024,768]{1,0:T(8,128)(2,1)S(1)}, bf16[1024,768]{1,0:T(8,128)(2,1)S(1)}, u32[]{:S(2)}, u32[]{:S(2)}) %collective-permute-start.25) | collective-permute-done | bytes 1572896 | tf_op jit(solution)/shard_map/ppermute | solution.py:36
  316.9 12.3 %collective-permute-done.21 = bf16[768,1024]{1,0:T(8,128)(2,1)} collective-permute-done((bf16[768,1024]{1,0:T(8,128)(2,1)}, bf16[768,1024]{1,0:T(8,128)(2,1)}, u32[]{:S(2)}, u32[]{:S(2)}) %collective-permute-start.21) | collective-permute-done | bytes 1572896 | tf_op jit(solution)/shard_map/ppermute | solution.py:36
  341.2 10.7 collective-permute-done.26
  352.2 16.3 %collective-permute-done.22 = bf16[768,1024]{1,0:T(8,128)(2,1)S(1)} collective-permute-done((bf16[768,1024]{1,0:T(8,128)(2,1)}, bf16[768,1024]{1,0:T(8,128)(2,1)S(1)}, u32[]{:S(2)}, u32[]{:S(2)}) %collective-permute-start.22) | collective-permute-done | bytes 1572896 | tf_op jit(solution)/shard_map/ppermute | solution.py:43
  371.8 9.9 fusion.64
  381.8 7.8 fusion.67
  389.6 15.1 %multiply_convert_fusion.2 = (bf16[1536,1024]{1,0:T(8,128)(2,1)}, bf16[1536,1024]{1,0:T(8,128)(2,1)}, bf16[1536,1024]{1,0:T(8,128)(2,1)}) fusion(f32[1536,1024]{1,0:T(8,128)} %fusion.64, f32[1536,1024]{1,0:T(8,128)} %fusion.67, bf16[768,1024]{1,0:T(8,128)(2,1)} %get-tuple-element.351, bf16[768,1024]{1,0:T(8,128)(2,1)S(1)} %get-tuple-element.350, ...), kind=kOutput, calls=%fused_computation.61 | convolution fusion | flops 4880596992 | bytes 29884416 | tf_op jit(solution)/shard_map/dot_general | solution.py:154
  404.8 9.9 fusion.126
  414.7 6.5 fusion.110
  425.4 10.8 fusion.66
  436.2 7.5 fusion.111
  448.2 11.6 %fusion.125 = (bf16[1536,1536]{1,0:T(8,128)(2,1)}, f32[1536,1536]{1,0:T(8,128)}) fusion(f32[1536,1536]{1,0:T(8,128)} %fusion.66, bf16[1536,1024]{1,0:T(8,128)(2,1)} %get-tuple-element.319, bf16[768,1024]{1,0:T(8,128)(2,1)} %get-tuple-element.351, bf16[768,1024]{1,0:T(8,128)(2,1)S(1)} %get-tuple-element.350), kind=kOutput, calls=%fused_computation.300 | convolution fusion | flops 4842848256 | bytes 29884416 | tf_op jit(solution)/shard_map/dot_general | solution.py:148
  462.8 7.1 fusion.112
  477.8 14.6 %collective-permute-done.61 = bf16[768,1024]{1,0:T(8,128)(2,1)S(1)} collective-permute-done((bf16[768,1024]{1,0:T(8,128)(2,1)}, bf16[768,1024]{1,0:T(8,128)(2,1)S(1)}, u32[]{:S(2)}, u32[]{:S(2)}) %collective-permute-start.61) | collective-permute-done | bytes 1572896 | tf_op jit(solution)/shard_map/ppermute | solution.py:18
  494.0 7.7 collective-permute-start.66
  501.7 22.3 %collective-permute-start.62 = (bf16[768,1024]{1,0:T(8,128)(2,1)S(1)}, bf16[768,1024]{1,0:T(8,128)(2,1)}, u32[]{:S(2)}, u32[]{:S(2)}) collective-permute-start(bf16[768,1024]{1,0:T(8,128)(2,1)S(1)} %fusion.70), channel_id=1, source_target_pairs={{2,0},{8,10},{3,1},{9,11},{6,4},{12,14},{7,5},{13,15},{18,16},{24,... | collective-permute-start | bytes 4718600 | tf_op jit(solution)/shard_map/ppermute | solution.py:56
  526.7 21.1 %collective-permute-done.28 = bf16[384,1536]{1,0:T(8,128)(2,1)S(1)} collective-permute-done((bf16[384,1536]{1,0:T(8,128)(2,1)S(1)}, bf16[384,1536]{1,0:T(8,128)(2,1)S(1)}, u32[]{:S(2)}, u32[]{:S(2)}) %collective-permute-start.28) | collective-permute-done | bytes 1179680 | tf_op jit(solution)/shard_map/ppermute | solution.py:22
  548.8 4.9 fusion.114
  564.9 5.5 collective-permute-done.31
  571.6 41.7 %collective-permute-done.41 = bf16[384,1536]{1,0:T(8,128)(2,1)} collective-permute-done((bf16[384,1536]{1,0:T(8,128)(2,1)S(1)}, bf16[384,1536]{1,0:T(8,128)(2,1)}, u32[]{:S(2)}, u32[]{:S(2)}) %collective-permute-start.41) | collective-permute-done | bytes 1179680 | tf_op jit(solution)/shard_map/ppermute | solution.py:22
  643.3 211.9 %while.32 = (s32[]{:T(128)}, f32[1536,6,64]{0,2,1:T(8,128)}, f32[1536,6,64]{0,2,1:T(8,128)S(1)}, f32[6,1536]{1,0:T(8,128)}, bf16[3,512,6,64]{1,3,2,0:T(8,128)(2,...) while((s32[]{:T(128)}, f32[1536,6,64]{0,2,1:T(8,128)}, ...), condition=%wide.region_12.13_spmd.clone, body=%wide.region_8.12_spmd.clone.sunk | while | flops 3093238784 | bytes 211241008 | solution.py:241
  648.0 8.9 fusion.176
  660.9 15.5 %multiply_reduce_fusion.5 = (f32[6,512]{1,0:T(8,128)S(1)}, f32[6,512,1536]{2,1,0:T(8,128)}) fusion(f32[6,512,1536]{2,1,0:T(8,128)} %fusion.176, f32[6,512]{1,0:T(8,128)S(1)} %dynamic-slice_bitcast_fusion.7, f32[6,1536]{1,0:T(8,128)} %bitcast.165, f32[6,512]{1,0:T(8,128)} %dynamic-slice_bitcast_fusion.8, ...), kind=kOutput, calls=%fused_computation.24.clone.1 | convolution fusion | flops 637006848 | bytes 40198148 | tf_op jit(solution)/shard_map/while/body/eval_jaxpr/qhd,khd->hqk/dot_general | solution.py:179
  676.5 16.7 %convert_reduce_fusion.4 = (f32[6,512]{1,0:T(8,128)}, f32[6,1536]{1,0:T(8,128)}, bf16[6,512,1536]{2,1,0:T(8,128)(2,1)}) fusion(f32[6,512,1536]{2,1,0:T(8,128)} %get-tuple-element.560, f32[6,512,1536]{2,1,0:T(8,128)} %fusion.176, f32[6,512]{1,0:T(8,128)S(1)} %get-tuple-element.561), kind=kLoop, calls=%fused_computation.21.clone.1 | loop fusion | flops 28299264 | bytes 47247360 | tf_op jit(solution)/shard_map/while/body/eval_jaxpr/reduce_sum | solution.py:236
  693.2 7.1 fusion.178
  705.2 8.6 fusion.179
  718.1 8.9 fusion.176
  731.0 15.6 %multiply_reduce_fusion.5 = (f32[6,512]{1,0:T(8,128)S(1)}, f32[6,512,1536]{2,1,0:T(8,128)}) fusion(f32[6,512,1536]{2,1,0:T(8,128)} %fusion.176, f32[6,512]{1,0:T(8,128)S(1)} %dynamic-slice_bitcast_fusion.7, f32[6,1536]{1,0:T(8,128)} %bitcast.165, f32[6,512]{1,0:T(8,128)} %dynamic-slice_bitcast_fusion.8, ...), kind=kOutput, calls=%fused_computation.24.clone.1 | convolution fusion | flops 637006848 | bytes 40198148 | tf_op jit(solution)/shard_map/while/body/eval_jaxpr/qhd,khd->hqk/dot_general | solution.py:179
  746.5 16.7 %convert_reduce_fusion.4 = (f32[6,512]{1,0:T(8,128)}, f32[6,1536]{1,0:T(8,128)}, bf16[6,512,1536]{2,1,0:T(8,128)(2,1)}) fusion(f32[6,512,1536]{2,1,0:T(8,128)} %get-tuple-element.560, f32[6,512,1536]{2,1,0:T(8,128)} %fusion.176, f32[6,512]{1,0:T(8,128)S(1)} %get-tuple-element.561), kind=kLoop, calls=%fused_computation.21.clone.1 | loop fusion | flops 28299264 | bytes 47247360 | tf_op jit(solution)/shard_map/while/body/eval_jaxpr/reduce_sum | solution.py:236
  763.3 7.7 fusion.178
  775.9 8.6 fusion.179
  788.8 8.9 fusion.176
  801.7 15.6 %multiply_reduce_fusion.5 = (f32[6,512]{1,0:T(8,128)S(1)}, f32[6,512,1536]{2,1,0:T(8,128)}) fusion(f32[6,512,1536]{2,1,0:T(8,128)} %fusion.176, f32[6,512]{1,0:T(8,128)S(1)} %dynamic-slice_bitcast_fusion.7, f32[6,1536]{1,0:T(8,128)} %bitcast.165, f32[6,512]{1,0:T(8,128)} %dynamic-slice_bitcast_fusion.8, ...), kind=kOutput, calls=%fused_computation.24.clone.1 | convolution fusion | flops 637006848 | bytes 40198148 | tf_op jit(solution)/shard_map/while/body/eval_jaxpr/qhd,khd->hqk/dot_general | solution.py:179
  817.2 16.7 %convert_reduce_fusion.4 = (f32[6,512]{1,0:T(8,128)}, f32[6,1536]{1,0:T(8,128)}, bf16[6,512,1536]{2,1,0:T(8,128)(2,1)}) fusion(f32[6,512,1536]{2,1,0:T(8,128)} %get-tuple-element.560, f32[6,512,1536]{2,1,0:T(8,128)} %fusion.176, f32[6,512]{1,0:T(8,128)S(1)} %get-tuple-element.561), kind=kLoop, calls=%fused_computation.21.clone.1 | loop fusion | flops 28299264 | bytes 47247360 | tf_op jit(solution)/shard_map/while/body/eval_jaxpr/reduce_sum | solution.py:236
  834.0 7.7 fusion.178
  846.6 8.6 fusion.179
  874.5 8.2 maximum_maximum_fusion
  882.7 9.1 constant_dynamic-slice_fusion.4
  901.6 5.0 copy.100
  910.4 9.4 fusion.75
  929.6 14.7 %fusion.127 = (bf16[1536,1536]{1,0:T(8,128)(2,1)}, f32[1536,1536]{1,0:T(8,128)}) fusion(bf16[1536,128]{1,0:T(8,128)(2,1)} %copy.79, bf16[768,1152]{1,0:T(8,128)(2,1)} %copy-done.34, bf16[768,1152]{1,0:T(8,128)(2,1)} %copy-done.33, bf16[384,1280]{1,0:T(8,128)(2,1)} %bitcast.186, bf16[384,1280]{1,0:T(8,128)(2,1)} %bitcast.184, ...), kind=kOutput, calls=%fused_computation.302 | convolution fusion | flops 6069682176 | bytes 22020096 | tf_op jit(solution)/shard_map/dot_general | solution.py:148
  947.5 15.1 %collective-permute-done.49 = bf16[768,1280]{0,1:T(8,128)(2,1)S(1)} collective-permute-done((bf16[768,1280]{0,1:T(8,128)(2,1)}, bf16[768,1280]{0,1:T(8,128)(2,1)S(1)}, u32[]{:S(2)}, u32[]{:S(2)}) %collective-permute-start.49) | collective-permute-done | bytes 1966112 | tf_op jit(solution)/shard_map/ppermute | solution.py:18
  964.5 13.7 %collective-permute-start.50 = (bf16[768,1280]{0,1:T(8,128)(2,1)}, bf16[768,1280]{0,1:T(8,128)(2,1)}, u32[]{:S(2)}, u32[]{:S(2)}) collective-permute-start(bf16[768,1280]{0,1:T(8,128)(2,1)} %fusion.43), channel_id=1, source_target_pairs={{2,0},{8,10},{3,1},{9,11},{6,4},{12,14},{7,5},{13,15},{18,16},{24,... | collective-permute-start | bytes 5898248 | tf_op jit(solution)/shard_map/ppermute | solution.py:56
  981.1 5.6 collective-permute-start.54
  993.6 11.4 %collective-permute-done.54 = bf16[384,768]{1,0:T(8,128)(2,1)S(1)} collective-permute-done((bf16[384,768]{1,0:T(8,128)(2,1)S(1)}, bf16[384,768]{1,0:T(8,128)(2,1)S(1)}, u32[]{:S(2)}, u32[]{:S(2)}) %collective-permute-start.54) | collective-permute-done | bytes 589856 | tf_op jit(solution)/shard_map/ppermute | solution.py:56
  1007.8 28.1 %collective-permute-start.45 = (bf16[384,1536]{1,0:T(8,128)(2,1)S(1)}, bf16[384,1536]{1,0:T(8,128)(2,1)S(1)}, u32[]{:S(2)}, u32[]{:S(2)}) collective-permute-start(bf16[384,1536]{1,0:T(8,128)(2,1)S(1)} %copy-done.59), channel_id=1, source_target_pairs={{0,8},{8,0},{1,9},{9,1},{2,10},{10,2},{3,11},{11,3},{4,12},{12,4},... | collective-permute-start | bytes 3538952 | tf_op jit(solution)/shard_map/ppermute | solution.py:18
  1050.6 13.7 %collective-permute-done.44 = bf16[384,1536]{1,0:T(8,128)(2,1)S(1)} collective-permute-done((bf16[384,1536]{1,0:T(8,128)(2,1)S(1)}, bf16[384,1536]{1,0:T(8,128)(2,1)S(1)}, u32[]{:S(2)}, u32[]{:S(2)}) %collective-permute-start.44) | collective-permute-done | bytes 1179680 | tf_op jit(solution)/shard_map/ppermute | solution.py:22
  1069.6 12.5 %collective-permute-start.46 = (bf16[384,768]{1,0:T(8,128)(2,1)}, bf16[384,768]{1,0:T(8,128)(2,1)}, u32[]{:S(2)}, u32[]{:S(2)}) collective-permute-start(bf16[384,768]{1,0:T(8,128)(2,1)} %get-tuple-element.355), channel_id=1, source_target_pairs={{8,0},{0,4},{12,8},{4,12},{9,1},{1,5},{13,9},{5,13},{10,2},{2,6},{... | collective-permute-start | bytes 1769480 | tf_op jit(solution)/shard_map/ppermute | solution.py:104
  1086.3 28.7 %psum.7 = f32[1560]{0:T(1024)S(1)} all-reduce(f32[1560]{0:T(1024)S(1)} %fusion.94), channel_id=1, replica_groups=mesh['o'=2,'k'=2,'x'=2,'h'=2,'p'=2] {'o','k','h','p'}, use_global_device_ids=true, to_apply=%region_17.18 | all-reduce | flops 1560 | bytes 12480 | tf_op jit(solution)/shard_map/psum | solution.py:415
  (580 shorter events, 337.4 us)
Async XLA Ops:
  0.7 48.0 %collective-permute-start.8 = (bf16[768,1152]{1,0:T(8,128)(2,1)}, bf16[768,1152]{1,0:T(8,128)(2,1)}, u32[]{:S(2)}, u32[]{:S(2)}) collective-permute-start(bf16[768,1152]{1,0:T(8,128)(2,1)} %param.20), channel_id=1, source_target_pairs={{0,4},{2,8},{4,0},{6,12},{8,2},{10,14},{12,6},{14,10},{1,5},{3,9},... | collective-permute-start | bytes 5308424 | tf_op jit(solution)/shard_map/ppermute | solution.py:36
  6.7 32.7 %collective-permute-start = (bf16[384,768]{1,0:T(8,128)(2,1)}, bf16[384,768]{1,0:T(8,128)(2,1)S(1)}, u32[]{:S(2)}, u32[]{:S(2)}) collective-permute-start(bf16[384,768]{1,0:T(8,128)(2,1)} %get-tuple-element.313), channel_id=1, source_target_pairs={{0,8},{4,0},{8,12},{12,4},{1,9},{5,1},{9,13},{13,5},{2,10},{6,2},{... | collective-permute-start | bytes 1769480 | tf_op jit(solution)/shard_map/ppermute | solution.py:94
  7.9 31.5 %collective-permute-start.1 = (bf16[384,768]{1,0:T(8,128)(2,1)S(1)}, bf16[384,768]{1,0:T(8,128)(2,1)S(1)}, u32[]{:S(2)}, u32[]{:S(2)}) collective-permute-start(bf16[384,768]{1,0:T(8,128)(2,1)S(1)} %get-tuple-element.314), channel_id=1, source_target_pairs={{4,8},{8,4},{5,9},{9,5},{6,10},{10,6},{7,11},{11,7},{20,24},{24,20... | collective-permute-start | bytes 1769480 | tf_op jit(solution)/shard_map/ppermute | solution.py:95
  11.1 23.1 %collective-permute-start.4 = (f32[2,768]{1,0:T(2,128)}, f32[2,768]{1,0:T(2,128)}, u32[]{:S(2)}, u32[]{:S(2)}) collective-permute-start(f32[2,768]{1,0:T(2,128)} %pad_maximum_fusion.40), channel_id=1, source_target_pairs={{0,4},{4,0},{1,5},{5,1},{2,6},{6,2},{3,7},{7,3},{8,12},{12,8},{9,1... | collective-permute-start | bytes 18440 | tf_op jit(solution)/shard_map/ppermute | solution.py:18
  11.8 61.0 %collective-permute-start.10 = (bf16[768,128]{0,1:T(8,128)(2,1)}, bf16[768,128]{0,1:T(8,128)(2,1)}, u32[]{:S(2)}, u32[]{:S(2)}) collective-permute-start(bf16[768,128]{0,1:T(8,128)(2,1)} %concatenate.108), channel_id=1, source_target_pairs={{0,4},{2,8},{4,0},{6,12},{8,2},{10,14},{12,6},{14,10},{1,5},{3,9},... | collective-permute-start | bytes 589832 | tf_op jit(solution)/shard_map/ppermute | solution.py:36
  34.1 18.7 %collective-permute-start.12 = (f32[6]{0:T(128)}, f32[6]{0:T(128)S(1)}, u32[]{:S(2)}, u32[]{:S(2)}) collective-permute-start(f32[6]{0:T(128)} %param.22), channel_id=1, source_target_pairs={{2,8},{8,2},{3,9},{9,3},{6,12},{12,6},{7,13},{13,7},{18,24},{24,18... | collective-permute-start | bytes 80 | tf_op jit(solution)/shard_map/ppermute | solution.py:310
  39.5 35.3 %collective-permute-start.13 = (bf16[384,768]{1,0:T(8,128)(2,1)S(1)}, bf16[384,768]{1,0:T(8,128)(2,1)}, u32[]{:S(2)}, u32[]{:S(2)}) collective-permute-start(bf16[384,768]{1,0:T(8,128)(2,1)S(1)} %copy-done.69), channel_id=1, source_target_pairs={{0,4},{2,8},{4,0},{6,12},{8,2},{10,14},{12,6},{14,10},{1,5},{3,9},... | collective-permute-start | bytes 1769480 | tf_op jit(solution)/shard_map/ppermute | solution.py:36
  42.4 38.5 %collective-permute-start.6 = (bf16[384,1536]{1,0:T(8,128)(2,1)S(1)}, bf16[384,1536]{1,0:T(8,128)(2,1)}, u32[]{:S(2)}, u32[]{:S(2)}) collective-permute-start(bf16[384,1536]{1,0:T(8,128)(2,1)S(1)} %fusion.46), channel_id=1, source_target_pairs={{0,1},{1,0},{2,3},{3,2},{4,5},{5,4},{6,7},{7,6},{8,9},{9,8},{10,11... | collective-permute-start | bytes 3538952 | tf_op jit(solution)/shard_map/ppermute | solution.py:22
  48.7 39.5 %collective-permute-start.9 = (bf16[768,1152]{1,0:T(8,128)(2,1)}, bf16[768,1152]{1,0:T(8,128)(2,1)}, u32[]{:S(2)}, u32[]{:S(2)}) collective-permute-start(bf16[768,1152]{1,0:T(8,128)(2,1)} %collective-permute-done.8), channel_id=1, source_target_pairs={{2,6},{6,2},{8,12},{12,8},{3,7},{7,3},{9,13},{13,9},{18,22},{22,18... | collective-permute-start | bytes 5308424 | tf_op jit(solution)/shard_map/ppermute | solution.py:43
  52.9 19.7 %collective-permute-start.3 = (s32[1540]{0:T(1024)S(1)}, s32[1540]{0:T(1024)S(1)}, u32[]{:S(2)}, u32[]{:S(2)}) collective-permute-start(s32[1540]{0:T(1024)S(1)} %broadcast_select_fusion.28), channel_id=1, source_target_pairs={{0,4},{4,0},{1,5},{5,1},{2,6},{6,2},{3,7},{7,3},{8,12},{12,8},{9,1... | collective-permute-start | bytes 18488 | tf_op jit(solution)/shard_map/ppermute | solution.py:18
  74.7 11.1 collective-permute-start.14
  80.8 9.8 collective-permute-start.5
  80.9 9.7 collective-permute-start.7
  219.3 28.8 %collective-permute-start.15 = (bf16[384,1536]{1,0:T(8,128)(2,1)S(1)}, bf16[384,1536]{1,0:T(8,128)(2,1)S(1)}, u32[]{:S(2)}, u32[]{:S(2)}) collective-permute-start(bf16[384,1536]{1,0:T(8,128)(2,1)S(1)} %get-tuple-element.332), channel_id=1, source_target_pairs={{0,8},{8,0},{1,9},{9,1},{2,10},{10,2},{3,11},{11,3},{4,12},{12,4},... | collective-permute-start | bytes 3538952 | tf_op jit(solution)/shard_map/ppermute | solution.py:18
  220.4 9.8 collective-permute-start.32
  221.7 21.2 %collective-permute-start.33 = (bf16[384,768]{1,0:T(8,128)(2,1)S(1)}, bf16[384,768]{1,0:T(8,128)(2,1)S(1)}, u32[]{:S(2)}, u32[]{:S(2)}) collective-permute-start(bf16[384,768]{1,0:T(8,128)(2,1)S(1)} %get-tuple-element.308), channel_id=1, source_target_pairs={{4,8},{8,4},{5,9},{9,5},{6,10},{10,6},{7,11},{11,7},{20,24},{24,20... | collective-permute-start | bytes 1769480 | tf_op jit(solution)/shard_map/ppermute | solution.py:95
  223.9 53.8 %collective-permute-start.23 = (bf16[768,1024]{1,0:T(8,128)(2,1)S(1)}, bf16[768,1024]{1,0:T(8,128)(2,1)}, u32[]{:S(2)}, u32[]{:S(2)}) collective-permute-start(bf16[768,1024]{1,0:T(8,128)(2,1)S(1)} %copy-done.36), channel_id=1, source_target_pairs={{0,4},{2,8},{4,0},{6,12},{8,2},{10,14},{12,6},{14,10},{1,5},{3,9},... | collective-permute-start | bytes 4718600 | tf_op jit(solution)/shard_map/ppermute | solution.py:36
  225.3 86.9 %collective-permute-start.25 = (bf16[1024,768]{1,0:T(8,128)(2,1)S(1)}, bf16[1024,768]{1,0:T(8,128)(2,1)S(1)}, u32[]{:S(2)}, u32[]{:S(2)}) collective-permute-start(bf16[1024,768]{1,0:T(8,128)(2,1)S(1)} %copy-done.38), channel_id=1, source_target_pairs={{0,4},{2,8},{4,0},{6,12},{8,2},{10,14},{12,6},{14,10},{1,5},{3,9},... | collective-permute-start | bytes 4718600 | tf_op jit(solution)/shard_map/ppermute | solution.py:36
  230.3 99.0 %collective-permute-start.21 = (bf16[768,1024]{1,0:T(8,128)(2,1)}, bf16[768,1024]{1,0:T(8,128)(2,1)}, u32[]{:S(2)}, u32[]{:S(2)}) collective-permute-start(bf16[768,1024]{1,0:T(8,128)(2,1)} %param.25), channel_id=1, source_target_pairs={{0,4},{2,8},{4,0},{6,12},{8,2},{10,14},{12,6},{14,10},{1,5},{3,9},... | collective-permute-start | bytes 4718600 | tf_op jit(solution)/shard_map/ppermute | solution.py:36
  244.3 84.9 %collective-permute-start.35 = (bf16[384,1536]{1,0:T(8,128)(2,1)}, bf16[384,1536]{1,0:T(8,128)(2,1)}, u32[]{:S(2)}, u32[]{:S(2)}) collective-permute-start(bf16[384,1536]{1,0:T(8,128)(2,1)} %pad_maximum_fusion.23), channel_id=1, source_target_pairs={{0,1},{1,0},{2,3},{3,2},{4,5},{5,4},{6,7},{7,6},{8,9},{9,8},{10,11... | collective-permute-start | bytes 3538952 | tf_op jit(solution)/shard_map/ppermute | solution.py:22
  248.1 83.9 %collective-permute-start.17 = (bf16[384,1536]{1,0:T(8,128)(2,1)}, bf16[384,1536]{1,0:T(8,128)(2,1)S(1)}, u32[]{:S(2)}, u32[]{:S(2)}) collective-permute-start(bf16[384,1536]{1,0:T(8,128)(2,1)} %get-tuple-element.333), channel_id=1, source_target_pairs={{0,8},{8,0},{1,9},{9,1},{2,10},{10,2},{3,11},{11,3},{4,12},{12,4},... | collective-permute-start | bytes 3538952 | tf_op jit(solution)/shard_map/ppermute | solution.py:18
  277.7 57.0 %collective-permute-start.16 = (bf16[384,1536]{1,0:T(8,128)(2,1)}, bf16[384,1536]{1,0:T(8,128)(2,1)}, u32[]{:S(2)}, u32[]{:S(2)}) collective-permute-start(bf16[384,1536]{1,0:T(8,128)(2,1)} %fusion.63), channel_id=1, source_target_pairs={{0,1},{1,0},{2,3},{3,2},{4,5},{5,4},{6,7},{7,6},{8,9},{9,8},{10,11... | collective-permute-start | bytes 3538952 | tf_op jit(solution)/shard_map/ppermute | solution.py:22
  313.4 24.4 %collective-permute-start.24 = (bf16[768,1024]{1,0:T(8,128)(2,1)}, bf16[768,1024]{1,0:T(8,128)(2,1)}, u32[]{:S(2)}, u32[]{:S(2)}) collective-permute-start(bf16[768,1024]{1,0:T(8,128)(2,1)} %collective-permute-done.23), channel_id=1, source_target_pairs={{2,6},{6,2},{8,12},{12,8},{3,7},{7,3},{9,13},{13,9},{18,22},{22,18... | collective-permute-start | bytes 4718600 | tf_op jit(solution)/shard_map/ppermute | solution.py:43
  329.2 42.6 %collective-permute-start.34 = (bf16[384,1536]{1,0:T(8,128)(2,1)}, bf16[384,1536]{1,0:T(8,128)(2,1)S(1)}, u32[]{:S(2)}, u32[]{:S(2)}) collective-permute-start(bf16[384,1536]{1,0:T(8,128)(2,1)} %pad_maximum_fusion.23), channel_id=1, source_target_pairs={{0,8},{8,0},{1,9},{9,1},{2,10},{10,2},{3,11},{11,3},{4,12},{12,4},... | collective-permute-start | bytes 3538952 | tf_op jit(solution)/shard_map/ppermute | solution.py:18
  329.2 22.7 %collective-permute-start.26 = (bf16[1024,768]{1,0:T(8,128)(2,1)}, bf16[1024,768]{1,0:T(8,128)(2,1)S(1)}, u32[]{:S(2)}, u32[]{:S(2)}) collective-permute-start(bf16[1024,768]{1,0:T(8,128)(2,1)} %copy-done.40), channel_id=1, source_target_pairs={{2,6},{6,2},{8,12},{12,8},{3,7},{7,3},{9,13},{13,9},{18,22},{22,18... | collective-permute-start | bytes 4718600 | tf_op jit(solution)/shard_map/ppermute | solution.py:43
  332.0 36.4 %collective-permute-start.22 = (bf16[768,1024]{1,0:T(8,128)(2,1)}, bf16[768,1024]{1,0:T(8,128)(2,1)S(1)}, u32[]{:S(2)}, u32[]{:S(2)}) collective-permute-start(bf16[768,1024]{1,0:T(8,128)(2,1)} %collective-permute-done.21), channel_id=1, source_target_pairs={{2,6},{6,2},{8,12},{12,8},{3,7},{7,3},{9,13},{13,9},{18,22},{22,18... | collective-permute-start | bytes 4718600 | tf_op jit(solution)/shard_map/ppermute | solution.py:43
  334.7 37.1 %collective-permute-start.36 = (bf16[384,1536]{1,0:T(8,128)(2,1)}, bf16[384,1536]{1,0:T(8,128)(2,1)S(1)}, u32[]{:S(2)}, u32[]{:S(2)}) collective-permute-start(bf16[384,1536]{1,0:T(8,128)(2,1)} %collective-permute-done.35), channel_id=1, source_target_pairs={{0,8},{8,0},{1,9},{9,1},{2,10},{10,2},{3,11},{11,3},{4,12},{12,4},... | collective-permute-start | bytes 3538952 | tf_op jit(solution)/shard_map/ppermute | solution.py:18
  337.8 33.5 %collective-permute-start.19 = (bf16[384,1536]{1,0:T(8,128)(2,1)S(1)}, bf16[384,1536]{1,0:T(8,128)(2,1)S(1)}, u32[]{:S(2)}, u32[]{:S(2)}) collective-permute-start(bf16[384,1536]{1,0:T(8,128)(2,1)S(1)} %multiply_convert_fusion.5), channel_id=1, source_target_pairs={{0,1},{1,0},{2,3},{3,2},{4,5},{5,4},{6,7},{7,6},{8,9},{9,8},{10,11... | collective-permute-start | bytes 3538952 | tf_op jit(solution)/shard_map/ppermute | solution.py:22
  371.3 10.4 collective-permute-start.18
  371.3 10.4 collective-permute-start.20
  422.6 53.1 %collective-permute-start.65 = (bf16[1024,768]{1,0:T(8,128)(2,1)}, bf16[1024,768]{1,0:T(8,128)(2,1)S(1)}, u32[]{:S(2)}, u32[]{:S(2)}) collective-permute-start(bf16[1024,768]{1,0:T(8,128)(2,1)} %slice.404), channel_id=1, source_target_pairs={{0,4},{4,0},{1,5},{5,1},{2,6},{6,2},{3,7},{7,3},{8,12},{12,8},{9,1... | collective-permute-start | bytes 4718600 | tf_op jit(solution)/shard_map/ppermute | solution.py:18
  445.1 47.2 %collective-permute-start.61 = (bf16[768,1024]{1,0:T(8,128)(2,1)}, bf16[768,1024]{1,0:T(8,128)(2,1)S(1)}, u32[]{:S(2)}, u32[]{:S(2)}) collective-permute-start(bf16[768,1024]{1,0:T(8,128)(2,1)} %slice.405), channel_id=1, source_target_pairs={{0,4},{4,0},{1,5},{5,1},{2,6},{6,2},{3,7},{7,3},{8,12},{12,8},{9,1... | collective-permute-start | bytes 4718600 | tf_op jit(solution)/shard_map/ppermute | solution.py:18
  447.7 25.5 %collective-permute-start.27 = (bf16[384,1536]{1,0:T(8,128)(2,1)}, bf16[384,1536]{1,0:T(8,128)(2,1)}, u32[]{:S(2)}, u32[]{:S(2)}) collective-permute-start(bf16[384,1536]{1,0:T(8,128)(2,1)} %get-tuple-element.330), channel_id=1, source_target_pairs={{0,8},{8,0},{1,9},{9,1},{2,10},{10,2},{3,11},{11,3},{4,12},{12,4},... | collective-permute-start | bytes 3538952 | tf_op jit(solution)/shard_map/ppermute | solution.py:18
  470.2 56.4 %collective-permute-start.29 = (bf16[384,1536]{1,0:T(8,128)(2,1)}, bf16[384,1536]{1,0:T(8,128)(2,1)S(1)}, u32[]{:S(2)}, u32[]{:S(2)}) collective-permute-start(bf16[384,1536]{1,0:T(8,128)(2,1)} %get-tuple-element.331), channel_id=1, source_target_pairs={{0,8},{8,0},{1,9},{9,1},{2,10},{10,2},{3,11},{11,3},{4,12},{12,4},... | collective-permute-start | bytes 3538952 | tf_op jit(solution)/shard_map/ppermute | solution.py:18
  470.7 23.3 %collective-permute-start.39 = (bf16[384,1536]{1,0:T(8,128)(2,1)}, bf16[384,1536]{1,0:T(8,128)(2,1)S(1)}, u32[]{:S(2)}, u32[]{:S(2)}) collective-permute-start(bf16[384,1536]{1,0:T(8,128)(2,1)} %get-tuple-element.329), channel_id=1, source_target_pairs={{0,8},{8,0},{1,9},{9,1},{2,10},{10,2},{3,11},{11,3},{4,12},{12,4},... | collective-permute-start | bytes 3538952 | tf_op jit(solution)/shard_map/ppermute | solution.py:18
  473.3 28.5 %collective-permute-start.38 = (bf16[384,1536]{1,0:T(8,128)(2,1)S(1)}, bf16[384,1536]{1,0:T(8,128)(2,1)S(1)}, u32[]{:S(2)}, u32[]{:S(2)}) collective-permute-start(bf16[384,1536]{1,0:T(8,128)(2,1)S(1)} %fusion.57), channel_id=1, source_target_pairs={{0,1},{1,0},{2,3},{3,2},{4,5},{5,4},{6,7},{7,6},{8,9},{9,8},{10,11... | collective-permute-start | bytes 3538952 | tf_op jit(solution)/shard_map/ppermute | solution.py:22
  475.7 72.1 %collective-permute-start.28 = (bf16[384,1536]{1,0:T(8,128)(2,1)S(1)}, bf16[384,1536]{1,0:T(8,128)(2,1)S(1)}, u32[]{:S(2)}, u32[]{:S(2)}) collective-permute-start(bf16[384,1536]{1,0:T(8,128)(2,1)S(1)} %fusion.61), channel_id=1, source_target_pairs={{0,1},{1,0},{2,3},{3,2},{4,5},{5,4},{6,7},{7,6},{8,9},{9,8},{10,11... | collective-permute-start | bytes 3538952 | tf_op jit(solution)/shard_map/ppermute | solution.py:22
  492.3 62.6 %collective-permute-start.57 = (bf16[768,1024]{1,0:T(8,128)(2,1)S(1)}, bf16[768,1024]{1,0:T(8,128)(2,1)S(1)}, u32[]{:S(2)}, u32[]{:S(2)}) collective-permute-start(bf16[768,1024]{1,0:T(8,128)(2,1)S(1)} %slice.406), channel_id=1, source_target_pairs={{0,4},{4,0},{1,5},{5,1},{2,6},{6,2},{3,7},{7,3},{8,12},{12,8},{9,1... | collective-permute-start | bytes 4718600 | tf_op jit(solution)/shard_map/ppermute | solution.py:18
  494.0 64.8 %collective-permute-start.66 = (bf16[1024,768]{1,0:T(8,128)(2,1)S(1)}, bf16[1024,768]{1,0:T(8,128)(2,1)}, u32[]{:S(2)}, u32[]{:S(2)}) collective-permute-start(bf16[1024,768]{1,0:T(8,128)(2,1)S(1)} %fusion.71), channel_id=1, source_target_pairs={{2,0},{8,10},{3,1},{9,11},{6,4},{12,14},{7,5},{13,15},{18,16},{24,... | collective-permute-start | bytes 4718600 | tf_op jit(solution)/shard_map/ppermute | solution.py:56
  501.7 112.4 %collective-permute-start.62 = (bf16[768,1024]{1,0:T(8,128)(2,1)S(1)}, bf16[768,1024]{1,0:T(8,128)(2,1)}, u32[]{:S(2)}, u32[]{:S(2)}) collective-permute-start(bf16[768,1024]{1,0:T(8,128)(2,1)S(1)} %fusion.70), channel_id=1, source_target_pairs={{2,0},{8,10},{3,1},{9,11},{6,4},{12,14},{7,5},{13,15},{18,16},{24,... | collective-permute-start | bytes 4718600 | tf_op jit(solution)/shard_map/ppermute | solution.py:56
  555.6 63.8 %collective-permute-start.58 = (bf16[768,1024]{1,0:T(8,128)(2,1)S(1)}, bf16[768,1024]{1,0:T(8,128)(2,1)S(1)}, u32[]{:S(2)}, u32[]{:S(2)}) collective-permute-start(bf16[768,1024]{1,0:T(8,128)(2,1)S(1)} %fusion.69), channel_id=1, source_target_pairs={{2,0},{8,10},{3,1},{9,11},{6,4},{12,14},{7,5},{13,15},{18,16},{24,... | collective-permute-start | bytes 4718600 | tf_op jit(solution)/shard_map/ppermute | solution.py:56
  557.0 56.4 %collective-permute-start.41 = (bf16[384,1536]{1,0:T(8,128)(2,1)S(1)}, bf16[384,1536]{1,0:T(8,128)(2,1)}, u32[]{:S(2)}, u32[]{:S(2)}) collective-permute-start(bf16[384,1536]{1,0:T(8,128)(2,1)S(1)} %get-tuple-element.305), channel_id=1, source_target_pairs={{0,1},{1,0},{2,3},{3,2},{4,5},{5,4},{6,7},{7,6},{8,9},{9,8},{10,11... | collective-permute-start | bytes 3538952 | tf_op jit(solution)/shard_map/ppermute | solution.py:22
  558.8 11.6 %collective-permute-start.31 = (bf16[384,768]{1,0:T(8,128)(2,1)S(1)}, bf16[384,768]{1,0:T(8,128)(2,1)S(1)}, u32[]{:S(2)}, u32[]{:S(2)}) collective-permute-start(bf16[384,768]{1,0:T(8,128)(2,1)S(1)} %get-tuple-element.360), channel_id=1, source_target_pairs={{8,4},{4,8},{9,5},{5,9},{10,6},{6,10},{11,7},{7,11},{24,20},{20,24... | collective-permute-start | bytes 1769480 | tf_op jit(solution)/shard_map/ppermute | solution.py:107
  562.9 60.5 %collective-permute-start.67 = (bf16[1024,768]{1,0:T(8,128)(2,1)S(1)}, bf16[1024,768]{1,0:T(8,128)(2,1)S(1)}, u32[]{:S(2)}, u32[]{:S(2)}) collective-permute-start(bf16[1024,768]{1,0:T(8,128)(2,1)S(1)} %add_convert_fusion.3), channel_id=1, source_target_pairs={{0,16},{10,26},{16,0},{26,10},{1,17},{11,27},{17,1},{27,11},{4,20}... | collective-permute-start | bytes 4718600 | tf_op jit(solution)/shard_map/ppermute | solution.py:65
  570.4 55.9 %collective-permute-start.40 = (bf16[384,1536]{1,0:T(8,128)(2,1)S(1)}, bf16[384,1536]{1,0:T(8,128)(2,1)S(1)}, u32[]{:S(2)}, u32[]{:S(2)}) collective-permute-start(bf16[384,1536]{1,0:T(8,128)(2,1)S(1)} %get-tuple-element.305), channel_id=1, source_target_pairs={{0,8},{8,0},{1,9},{9,1},{2,10},{10,2},{3,11},{11,3},{4,12},{12,4},... | collective-permute-start | bytes 3538952 | tf_op jit(solution)/shard_map/ppermute | solution.py:18
  613.3 13.0 %collective-permute-start.42 = (bf16[384,1536]{1,0:T(8,128)(2,1)}, bf16[384,1536]{1,0:T(8,128)(2,1)S(1)}, u32[]{:S(2)}, u32[]{:S(2)}) collective-permute-start(bf16[384,1536]{1,0:T(8,128)(2,1)} %collective-permute-done.41), channel_id=1, source_target_pairs={{0,8},{8,0},{1,9},{9,1},{2,10},{10,2},{3,11},{11,3},{4,12},{12,4},... | collective-permute-start | bytes 3538952 | tf_op jit(solution)/shard_map/ppermute | solution.py:18
  617.6 363.5 %collective-permute-start.63 = (bf16[768,1024]{1,0:T(8,128)(2,1)}, bf16[768,1024]{1,0:T(8,128)(2,1)}, u32[]{:S(2)}, u32[]{:S(2)}) collective-permute-start(bf16[768,1024]{1,0:T(8,128)(2,1)} %add_convert_fusion.5), channel_id=1, source_target_pairs={{0,16},{10,26},{16,0},{26,10},{1,17},{11,27},{17,1},{27,11},{4,20}... | collective-permute-start | bytes 4718600 | tf_op jit(solution)/shard_map/ppermute | solution.py:65
  621.5 368.0 %collective-permute-start.59 = (bf16[768,1024]{1,0:T(8,128)(2,1)}, bf16[768,1024]{1,0:T(8,128)(2,1)}, u32[]{:S(2)}, u32[]{:S(2)}) collective-permute-start(bf16[768,1024]{1,0:T(8,128)(2,1)} %add_convert_fusion.7), channel_id=1, source_target_pairs={{0,16},{10,26},{16,0},{26,10},{1,17},{11,27},{17,1},{27,11},{4,20}... | collective-permute-start | bytes 4718600 | tf_op jit(solution)/shard_map/ppermute | solution.py:65
  625.1 415.5 %collective-permute-start.68 = (bf16[1024,768]{1,0:T(8,128)(2,1)}, bf16[1024,768]{1,0:T(8,128)(2,1)}, u32[]{:S(2)}, u32[]{:S(2)}) collective-permute-start(bf16[1024,768]{1,0:T(8,128)(2,1)} %add_convert_fusion.2), channel_id=1, source_target_pairs={{0,8},{10,2},{1,9},{11,3},{4,12},{14,6},{5,13},{15,7},{16,24},{26,... | collective-permute-start | bytes 4718600 | tf_op jit(solution)/shard_map/ppermute | solution.py:67
  921.4 41.1 %collective-permute-start.49 = (bf16[768,1280]{0,1:T(8,128)(2,1)}, bf16[768,1280]{0,1:T(8,128)(2,1)S(1)}, u32[]{:S(2)}, u32[]{:S(2)}) collective-permute-start(bf16[768,1280]{0,1:T(8,128)(2,1)} %slice.403), channel_id=1, source_target_pairs={{0,4},{4,0},{1,5},{5,1},{2,6},{6,2},{3,7},{7,3},{8,12},{12,8},{9,1... | collective-permute-start | bytes 5898248 | tf_op jit(solution)/shard_map/ppermute | solution.py:18
  929.3 49.0 %collective-permute-start.53 = (bf16[384,768]{1,0:T(8,128)(2,1)}, bf16[384,768]{1,0:T(8,128)(2,1)S(1)}, u32[]{:S(2)}, u32[]{:S(2)}) collective-permute-start(bf16[384,768]{1,0:T(8,128)(2,1)} %slice.407), channel_id=1, source_target_pairs={{0,4},{4,0},{1,5},{5,1},{2,6},{6,2},{3,7},{7,3},{8,12},{12,8},{9,1... | collective-permute-start | bytes 1769480 | tf_op jit(solution)/shard_map/ppermute | solution.py:18
  964.5 71.8 %collective-permute-start.50 = (bf16[768,1280]{0,1:T(8,128)(2,1)}, bf16[768,1280]{0,1:T(8,128)(2,1)}, u32[]{:S(2)}, u32[]{:S(2)}) collective-permute-start(bf16[768,1280]{0,1:T(8,128)(2,1)} %fusion.43), channel_id=1, source_target_pairs={{2,0},{8,10},{3,1},{9,11},{6,4},{12,14},{7,5},{13,15},{18,16},{24,... | collective-permute-start | bytes 5898248 | tf_op jit(solution)/shard_map/ppermute | solution.py:56
  978.3 29.4 %collective-permute-start.43 = (bf16[384,1536]{1,0:T(8,128)(2,1)}, bf16[384,1536]{1,0:T(8,128)(2,1)S(1)}, u32[]{:S(2)}, u32[]{:S(2)}) collective-permute-start(bf16[384,1536]{1,0:T(8,128)(2,1)} %get-tuple-element.326), channel_id=1, source_target_pairs={{0,8},{8,0},{1,9},{9,1},{2,10},{10,2},{3,11},{11,3},{4,12},{12,4},... | collective-permute-start | bytes 3538952 | tf_op jit(solution)/shard_map/ppermute | solution.py:18
  981.1 23.9 %collective-permute-start.54 = (bf16[384,768]{1,0:T(8,128)(2,1)S(1)}, bf16[384,768]{1,0:T(8,128)(2,1)S(1)}, u32[]{:S(2)}, u32[]{:S(2)}) collective-permute-start(bf16[384,768]{1,0:T(8,128)(2,1)S(1)} %fusion.78), channel_id=1, source_target_pairs={{2,0},{8,10},{3,1},{9,11},{6,4},{12,14},{7,5},{13,15},{18,16},{24,... | collective-permute-start | bytes 1769480 | tf_op jit(solution)/shard_map/ppermute | solution.py:56
  989.4 55.2 %collective-permute-start.64 = (bf16[768,1024]{1,0:T(8,128)(2,1)S(1)}, bf16[768,1024]{1,0:T(8,128)(2,1)S(1)}, u32[]{:S(2)}, u32[]{:S(2)}) collective-permute-start(bf16[768,1024]{1,0:T(8,128)(2,1)S(1)} %add_convert_fusion.4), channel_id=1, source_target_pairs={{0,8},{10,2},{1,9},{11,3},{4,12},{14,6},{5,13},{15,7},{16,24},{26,... | collective-permute-start | bytes 4718600 | tf_op jit(solution)/shard_map/ppermute | solution.py:67
  1005.0 42.3 %collective-permute-start.60 = (bf16[768,1024]{1,0:T(8,128)(2,1)S(1)}, bf16[768,1024]{1,0:T(8,128)(2,1)S(1)}, u32[]{:S(2)}, u32[]{:S(2)}) collective-permute-start(bf16[768,1024]{1,0:T(8,128)(2,1)S(1)} %add_convert_fusion.6), channel_id=1, source_target_pairs={{0,8},{10,2},{1,9},{11,3},{4,12},{14,6},{5,13},{15,7},{16,24},{26,... | collective-permute-start | bytes 4718600 | tf_op jit(solution)/shard_map/ppermute | solution.py:67
  1007.8 42.8 %collective-permute-start.45 = (bf16[384,1536]{1,0:T(8,128)(2,1)S(1)}, bf16[384,1536]{1,0:T(8,128)(2,1)S(1)}, u32[]{:S(2)}, u32[]{:S(2)}) collective-permute-start(bf16[384,1536]{1,0:T(8,128)(2,1)S(1)} %copy-done.59), channel_id=1, source_target_pairs={{0,8},{8,0},{1,9},{9,1},{2,10},{10,2},{3,11},{11,3},{4,12},{12,4},... | collective-permute-start | bytes 3538952 | tf_op jit(solution)/shard_map/ppermute | solution.py:18
  1036.3 28.0 %collective-permute-start.44 = (bf16[384,1536]{1,0:T(8,128)(2,1)S(1)}, bf16[384,1536]{1,0:T(8,128)(2,1)S(1)}, u32[]{:S(2)}, u32[]{:S(2)}) collective-permute-start(bf16[384,1536]{1,0:T(8,128)(2,1)S(1)} %fusion.55), channel_id=1, source_target_pairs={{0,1},{1,0},{2,3},{3,2},{4,5},{5,4},{6,7},{7,6},{8,9},{9,8},{10,11... | collective-permute-start | bytes 3538952 | tf_op jit(solution)/shard_map/ppermute | solution.py:22
  1040.6 25.0 %collective-permute-start.51 = (bf16[768,1280]{0,1:T(8,128)(2,1)S(1)}, bf16[768,1280]{0,1:T(8,128)(2,1)S(1)}, u32[]{:S(2)}, u32[]{:S(2)}) collective-permute-start(bf16[768,1280]{0,1:T(8,128)(2,1)S(1)} %add_convert_fusion.1), channel_id=1, source_target_pairs={{0,16},{10,26},{16,0},{26,10},{1,17},{11,27},{17,1},{27,11},{4,20}... | collective-permute-start | bytes 5898248 | tf_op jit(solution)/shard_map/ppermute | solution.py:65
  1049.3 35.9 %collective-permute-start.56 = (bf16[384,768]{1,0:T(8,128)(2,1)S(1)}, bf16[384,768]{1,0:T(8,128)(2,1)S(1)}, u32[]{:S(2)}, u32[]{:S(2)}) collective-permute-start(bf16[384,768]{1,0:T(8,128)(2,1)S(1)} %add_convert_fusion.8), channel_id=1, source_target_pairs={{0,8},{10,2},{1,9},{11,3},{4,12},{14,6},{5,13},{15,7},{16,24},{26,... | collective-permute-start | bytes 1769480 | tf_op jit(solution)/shard_map/ppermute | solution.py:67
  1065.3 21.0 %collective-permute-start.48 = (f32[1560]{0:T(1024)S(1)}, f32[1560]{0:T(1024)S(1)}, u32[]{:S(2)}, u32[]{:S(2)}) collective-permute-start(f32[1560]{0:T(1024)S(1)} %pad_maximum_fusion.38), channel_id=1, source_target_pairs={{0,4},{4,0},{1,5},{5,1},{2,6},{6,2},{3,7},{7,3},{8,12},{12,8},{9,1... | collective-permute-start | bytes 18728 | tf_op jit(solution)/shard_map/ppermute | solution.py:18
  1066.2 52.4 %collective-permute-start.52 = (bf16[768,1280]{0,1:T(8,128)(2,1)S(1)}, bf16[768,1280]{0,1:T(8,128)(2,1)}, u32[]{:S(2)}, u32[]{:S(2)}) collective-permute-start(bf16[768,1280]{0,1:T(8,128)(2,1)S(1)} %add_convert_fusion), channel_id=1, source_target_pairs={{0,8},{10,2},{1,9},{11,3},{4,12},{14,6},{5,13},{15,7},{16,24},{26,... | collective-permute-start | bytes 5898248 | tf_op jit(solution)/shard_map/ppermute | solution.py:67
  1069.6 46.6 %collective-permute-start.46 = (bf16[384,768]{1,0:T(8,128)(2,1)}, bf16[384,768]{1,0:T(8,128)(2,1)}, u32[]{:S(2)}, u32[]{:S(2)}) collective-permute-start(bf16[384,768]{1,0:T(8,128)(2,1)} %get-tuple-element.355), channel_id=1, source_target_pairs={{8,0},{0,4},{12,8},{4,12},{9,1},{1,5},{13,9},{5,13},{10,2},{2,6},{... | collective-permute-start | bytes 1769480 | tf_op jit(solution)/shard_map/ppermute | solution.py:104
  1082.1 34.1 %collective-permute-start.47 = (bf16[384,768]{1,0:T(8,128)(2,1)}, bf16[384,768]{1,0:T(8,128)(2,1)}, u32[]{:S(2)}, u32[]{:S(2)}) collective-permute-start(bf16[384,768]{1,0:T(8,128)(2,1)} %get-tuple-element.354), channel_id=1, source_target_pairs={{8,4},{4,8},{9,5},{5,9},{10,6},{6,10},{11,7},{7,11},{24,20},{20,24... | collective-permute-start | bytes 1769480 | tf_op jit(solution)/shard_map/ppermute | solution.py:107
  (135 other events, 1650.3 us)

commit v2 on v1

--- a/solution.py
+++ b/solution.py
@@ -1,12 +1,16 @@
+import functools
+
 import jax
 import jax.numpy as jnp
 from jax import lax
+from jax.experimental import pallas as pl
+from jax.experimental.pallas import tpu as pltpu
 from jax.sharding import Mesh, PartitionSpec as P
 
 D = 1536
 DH = 64
 DOCS = 4
-QBLK = 512
+TILE = 256
 EPS = 1e-06
 MASKED = -1e30
 LANES = 128
@@ -132,12 +136,6 @@
     return total
 
 
-def reorder(rows, me, count):
-    parts = rows.reshape((count, rows.shape[0] // count) + rows.shape[1:])
-    taken = [lax.dynamic_index_in_dim(parts, j ^ me, 0, keepdims=False) for j in range(count)]
-    return jnp.concatenate(taken, axis=0)
-
-
 def contract_rows(left, right):
     return lax.dot_general(
         left, right, (((0,), (0,)), ((), ())), preferred_element_type=F32
@@ -154,105 +152,378 @@
     return jnp.dot(left, right, preferred_element_type=F32)
 
 
-def split3(value):
-    high = lax.reduce_precision(value, 8, 7)
-    rest = value - high
-    mid = lax.reduce_precision(rest, 8, 7)
-    return jnp.concatenate([high, mid, rest - mid], axis=1).astype(BF16)
-
-
-def sum3(value):
-    n = value.shape[1] // 3
-    return value[:, :n] + value[:, n : 2 * n] + value[:, 2 * n :]
-
-
-def visible(row_start, doc_query, branch_query, doc_key, branch_key):
-    pos_query = row_start + jnp.arange(doc_query.shape[0], dtype=jnp.int32)
-    pos_key = jnp.arange(doc_key.shape[0], dtype=jnp.int32)
-    causal = pos_key[None, :] <= pos_query[:, None]
-    same_doc = doc_query[:, None] == doc_key[None, :]
-    same_branch = (branch_key[None, :] < 0) | (branch_query[:, None] == branch_key[None, :])
-    return causal & same_doc & same_branch
-
-
-def block_scores(query_block, key_rows, decay_query, decay_key, allowed):
-    raw_scores = jnp.einsum(
-        "qhd,khd->hqk", query_block, key_rows, preferred_element_type=jnp.float32
+def dot_nn(left, right):
+    return lax.dot_general(left, right, (((1,), (0,)), ((), ())), preferred_element_type=F32)
+
+
+def dot_nt(left, right):
+    return lax.dot_general(left, right, (((1,), (1,)), ((), ())), preferred_element_type=F32)
+
+
+def tile_mask(qrow, kcol, rows, cols, i, j):
+    key_pos = j * TILE + lax.broadcasted_iota(jnp.int32, (TILE, TILE), 0)
+    query_pos = i * TILE + lax.broadcasted_iota(jnp.int32, (TILE, TILE), 1)
+    code = kcol[pl.ds(pl.multiple_of(j * TILE, TILE), TILE), 0:1]
+    first = qrow[0:1, pl.ds(pl.multiple_of(i * TILE, TILE), TILE)]
+    second = qrow[1:2, pl.ds(pl.multiple_of(i * TILE, TILE), TILE)]
+    seen = (key_pos <= query_pos) & ((code == first) | (code == second))
+    return jnp.where(seen, 0.0, MASKED)
+
+
+def split_parts(value):
+    high = value.astype(BF16)
+    rest = value - high.astype(F32)
+    mid = rest.astype(BF16)
+    low = (rest - mid.astype(F32)).astype(BF16)
+    return high, mid, low
+
+
+def lane(shape):
+    return lax.broadcasted_iota(jnp.int32, shape, 1)
+
+
+def decay_map(pos_a, tag_a, limit_a, pos_b, tag_b, doc_b):
+    adds = ((pos_b <= pos_a) & (tag_a == tag_b)) | (doc_b <= limit_a)
+    return jnp.where(adds, 1.0, 0.0).astype(BF16)
+
+
+def forward_kernel(
+    heads, count, prompt_len, flags, qkv_hbm, logit_hbm, kcol, qrow, att_hbm, ot_hbm, lse_ref,
+    qp_hbm, kp_hbm, vp_hbm, qkv, logit, qp, kp, vp, vt, rates, attended, ot, mask, m_ref, l_ref,
+    in_sem, out_sem, keep_sem,
+):
+    me = lax.axis_index("p") * 2 + lax.axis_index("k")
+    total = qkv.shape[0]
+    size = total // count
+    tiles = total // TILE
+    loads = []
+    for b in range(count):
+        rows = pl.ds(b * size, size)
+        loads.append(pltpu.make_async_copy(logit_hbm.at[b ^ me], logit.at[rows], in_sem.at[b]))
+        loads.append(pltpu.make_async_copy(qkv_hbm.at[b ^ me], qkv.at[rows], in_sem.at[count + b]))
+    for load in loads:
+        load.start()
+    for load in loads[::2]:
+        load.wait()
+    value = logit[...]
+    rate = jnp.minimum(value, 0.0) - jnp.log1p(jnp.exp(-jnp.abs(value)))
+    rate = jnp.where(lane(rate.shape) < heads, rate, 0.0)
+    high, mid, low = split_parts(rate)
+    packed = high.astype(F32) + pltpu.roll(mid.astype(F32), 8, 1) + pltpu.roll(low.astype(F32), 16, 1)
+    rates[...] = packed.astype(BF16)
+    for load in loads[1::2]:
+        load.wait()
+    place_row = lax.broadcasted_iota(jnp.int32, (LANES, LANES), 0)
+    place_col = lax.broadcasted_iota(jnp.int32, (LANES, LANES), 1)
+
+    def prepare(t, carry):
+        rows = pl.ds(pl.multiple_of(t * TILE, TILE), TILE)
+
+        def add_rates(u, acc):
+            others = pl.ds(pl.multiple_of(u * TILE, TILE), TILE)
+            pos_a = t * TILE + lax.broadcasted_iota(jnp.int32, (TILE, TILE), 0)
+            pos_b = u * TILE + lax.broadcasted_iota(jnp.int32, (TILE, TILE), 1)
+            adds = decay_map(
+                pos_a, kcol[rows, 1:2], kcol[rows, 2:3], pos_b, qrow[2:3, others], qrow[3:4, others]
+            )
+            return acc + dot_nn(adds, rates[others, :])
+
+        sums = lax.fori_loop(0, t + 1, add_rates, jnp.zeros((TILE, LANES), F32))
+        decay = sums + pltpu.roll(sums, LANES - 8, 1) + pltpu.roll(sums, LANES - 16, 1)
+        decay = jnp.where(lane(decay.shape) < heads, -decay, 0.0)
+        high, mid, low = split_parts(decay)
+        parts = (
+            high.astype(F32) + pltpu.roll(mid.astype(F32), 8, 1) + pltpu.roll(low.astype(F32), 16, 1)
+        ).astype(BF16)
+        lanes = lane((TILE, LANES))
+        for h in range(heads):
+            base = 3 * DH * h
+            query = qkv[rows, base : base + DH].astype(F32) * DH ** (-0.5)
+            key = qkv[rows, base + DH : base + 2 * DH]
+            worth = qkv[rows, base + 2 * DH : base + 3 * DH]
+            ones = jnp.where((lanes >= DH) & (lanes < DH + 3), 1.0, 0.0)[:, :DH]
+            ones = jnp.where(lane((TILE, DH)) < 3, 1.0, 0.0)
+            qp[h, rows, :] = jnp.concatenate([query, ones], axis=1).astype(BF16)
+            spread = jnp.where(
+                (place_col >= DH) & (place_col < DH + 3) & (place_row == 8 * (place_col - DH) + h), 1.0, 0.0
+            ).astype(BF16)
+            extra = dot_nn(parts, spread)
+            extra = jnp.where(lanes == DH + 3, 1.0, extra)
+            key_wide = jnp.concatenate([key.astype(F32), extra[:, DH:]], axis=1)
+            kp[h, rows, :] = key_wide.astype(BF16)
+            vp[h, rows, :] = worth
+            vt[h, :, rows] = worth.astype(F32).T.astype(BF16)
+        return carry
+
+    lax.fori_loop(0, tiles, prepare, 0)
+    keeps = [
+        pltpu.make_async_copy(qp, qp_hbm, keep_sem.at[0]),
+        pltpu.make_async_copy(kp, kp_hbm, keep_sem.at[1]),
+        pltpu.make_async_copy(vp, vp_hbm, keep_sem.at[2]),
+    ]
+    for keep in keeps:
+        keep.start()
+
+    def query_tile(i, carry):
+        cols = pl.ds(pl.multiple_of(i * TILE, TILE), TILE)
+        m_ref[...] = jnp.full(m_ref.shape, MASKED, F32)
+        l_ref[...] = jnp.zeros(l_ref.shape, F32)
+        ot[:, cols] = jnp.zeros((heads * DH, TILE), F32)
+
+        def key_tile(j, inner):
+            @pl.when(flags[i * tiles + j] > 0)
+            def _():
+                rows = pl.ds(pl.multiple_of(j * TILE, TILE), TILE)
+                mask[...] = tile_mask(qrow, kcol, None, None, i, j)
+                for h in range(heads):
+                    scores = dot_nt(kp[h, rows, :], qp[h, cols, :]) + mask[...]
+                    before = m_ref[h : h + 1, :]
+                    top = jnp.maximum(before, jnp.max(scores, axis=0, keepdims=True))
+                    expo = jnp.exp(scores - top)
+                    shrink = jnp.exp(before - top)
+                    m_ref[h : h + 1, :] = top
+                    l_ref[h : h + 1, :] = l_ref[h : h + 1, :] * shrink + jnp.sum(expo, axis=0, keepdims=True)
+                    part = dot_nn(vt[h, :, rows], expo.astype(BF16))
+                    span = pl.ds(h * DH, DH)
+                    ot[span, cols] = ot[span, cols] * shrink + part
+
+            return inner
+
+        lax.fori_loop(0, i + 1, key_tile, 0)
+        for h in range(heads):
+            span = pl.ds(h * DH, DH)
+            ot[span, cols] = ot[span, cols] / l_ref[h : h + 1, :]
+        lse_ref[:, cols] = m_ref[...] + jnp.log(l_ref[...])
+        attended[cols, :] = ot[:, cols].T.astype(BF16)
+        return carry
+
+    lse_ref[...] = jnp.zeros(lse_ref.shape, F32)
+    lax.fori_loop(0, tiles, query_tile, 0)
+    stores = [pltpu.make_async_copy(ot, ot_hbm, keep_sem.at[3])]
+    for b in range(count):
+        stores.append(
+            pltpu.make_async_copy(attended.at[pl.ds(b * size, size)], att_hbm.at[b ^ me], out_sem.at[b])
+        )
+    for store in stores:
+        store.start()
+    for copy in keeps + stores:
+        copy.wait()
+
+
+def attention_forward(qkv, logit, kcol, qrow, flags, heads, prompt_len):
+    count, size, width = qkv.shape
+    total = count * size
+    any_spec = pl.BlockSpec(memory_space=pl.ANY)
+    vmem = pl.BlockSpec(memory_space=pltpu.VMEM)
+    shape = jax.ShapeDtypeStruct
+    return pl.pallas_call(
+        functools.partial(forward_kernel, heads, count, prompt_len),
+        out_shape=(
+            shape((count, size, heads * DH), BF16),
+            shape((heads * DH, total), F32),
+            shape((8, total), F32),
+            shape((heads, total, LANES), BF16),
+            shape((heads, total, LANES), BF16),
+            shape((heads, total, DH), BF16),
+        ),
+        in_specs=[pl.BlockSpec(memory_space=pltpu.SMEM), any_spec, any_spec, vmem, vmem],
+        out_specs=(any_spec, any_spec, vmem, any_spec, any_spec, any_spec),
+        scratch_shapes=[
+            pltpu.VMEM((total, width), BF16),
+            pltpu.VMEM((total, LANES), F32),
+            pltpu.VMEM((heads, total, LANES), BF16),
+            pltpu.VMEM((heads, total, LANES), BF16),
+            pltpu.VMEM((heads, total, DH), BF16),
+            pltpu.VMEM((heads, DH, total), BF16),
+            pltpu.VMEM((total, LANES), BF16),
+            pltpu.VMEM((total, heads * DH), BF16),
+            pltpu.VMEM((heads * DH, total), F32),
+            pltpu.VMEM((TILE, TILE), F32),
+            pltpu.VMEM((8, TILE), F32),
+            pltpu.VMEM((8, TILE), F32),
+            pltpu.SemaphoreType.DMA((2 * count,)),
+            pltpu.SemaphoreType.DMA((count,)),
+            pltpu.SemaphoreType.DMA((4,)),
+        ],
+        compiler_params=pltpu.CompilerParams(vmem_limit_bytes=48 << 20),
+        cost_estimate=pl.CostEstimate(flops=20_000_000_000, bytes_accessed=30_000_000, transcendentals=0),
+        name="attention_forward",
+    )(flags, qkv, logit, kcol, qrow)
+
+
+def backward_kernel(
+    heads, count, prompt_len, flags, gatt_hbm, ot_ref, lse_ref, qp, kp, vp, logit_hbm, kcol, qrow,
+    grad_hbm, bias_ref, gatt, logit, gout, kt, delta, dqt, dk, dv, mask, decay, grad, in_sem, out_sem,
+):
+    me = lax.axis_index("p") * 2 + lax.axis_index("k")
+    total = gatt.shape[0]
+    size = total // count
+    tiles = total // TILE
+    loads = []
+    for b in range(count):
+        rows = pl.ds(b * size, size)
+        loads.append(pltpu.make_async_copy(gatt_hbm.at[b ^ me], gatt.at[rows], in_sem.at[b]))
+        loads.append(pltpu.make_async_copy(logit_hbm.at[b ^ me], logit.at[rows], in_sem.at[count + b]))
+    for load in loads:
+        load.start()
+    for load in loads:
+        load.wait()
+    dqt[...] = jnp.zeros(dqt.shape, F32)
+    delta[...] = jnp.zeros(delta.shape, F32)
+
+    def prepare(t, carry):
+        rows = pl.ds(pl.multiple_of(t * TILE, TILE), TILE)
+        turned = gatt[rows, :].astype(F32).T * ot_ref[:, rows]
+        for h in range(heads):
+            gout[h, rows, :] = gatt[rows, h * DH : (h + 1) * DH]
+            kt[h, :, rows] = kp[h, rows, :].astype(F32).T[: DH + 8].astype(BF16)
+            delta[h : h + 1, rows] = jnp.sum(turned[h * DH : (h + 1) * DH], axis=0, keepdims=True)
+        return carry
+
+    lax.fori_loop(0, tiles, prepare, 0)
+    lanes = lane((TILE, LANES))
+
+    def key_tile(j, carry):
+        rows = pl.ds(pl.multiple_of(j * TILE, TILE), TILE)
+        dk[...] = jnp.zeros(dk.shape, F32)
+        dv[...] = jnp.zeros(dv.shape, F32)
+
+        def query_tile(i, inner):
+            @pl.when(flags[i * tiles + j] > 0)
+            def _():
+                cols = pl.ds(pl.multiple_of(i * TILE, TILE), TILE)
+                mask[...] = tile_mask(qrow, kcol, None, None, i, j)
+                for h in range(heads):
+                    scores = dot_nt(kp[h, rows, :], qp[h, cols, :]) + mask[...]
+                    probs = jnp.exp(scores - lse_ref[h : h + 1, cols])
+                    grad_probs = dot_nt(vp[h, rows, :], gout[h, cols, :])
+                    grad_scores = (probs * (grad_probs - delta[h : h + 1, cols])).astype(BF16)
+                    dv[h] += dot_nn(probs.astype(BF16), gout[h, cols, :])
+                    dk[h] += dot_nn(grad_scores, qp[h, cols, :])
+                    dqt[h, :, cols] += dot_nn(kt[h, :, rows], grad_scores)
+
+            return inner
+
+        lax.fori_loop(j, tiles, query_tile, 0)
+        keys = jnp.zeros((TILE, LANES), F32)
+        for h in range(heads):
+            grad_key = dk[h]
+            keys += jnp.where(lanes == h, pltpu.roll(grad_key, LANES - DH + h, 1), 0.0)
+            grad[rows, (3 * h + 1) * DH : (3 * h + 3) * DH] = jnp.concatenate(
+                [grad_key[:, :DH], dv[h]], axis=1
+            ).astype(BF16)
+        decay[rows, :] = -keys
+        return carry
+
+    lax.fori_loop(0, tiles, key_tile, 0)
+
+    def finish(t, carry):
+        rows = pl.ds(pl.multiple_of(t * TILE, TILE), TILE)
+        queries = jnp.zeros((TILE, LANES), F32)
+        for h in range(heads):
+            turned = jnp.concatenate([dqt[h, :, rows], jnp.zeros((LANES - DH - 8, TILE), F32)], axis=0).T
+            queries += jnp.where(lanes == h, pltpu.roll(turned, LANES - DH - 3 + h, 1), 0.0)
+            grad[rows, 3 * h * DH : (3 * h + 1) * DH] = (turned[:, :DH] * DH ** (-0.5)).astype(BF16)
+        whole = decay[rows, :] + queries
+        high, mid, low = split_parts(whole)
+        decay[rows, :] = (
+            high.astype(F32) + pltpu.roll(mid.astype(F32), 8, 1) + pltpu.roll(low.astype(F32), 16, 1)
+        )
+        return carry
+
+    lax.fori_loop(0, tiles, finish, 0)
+
+    def rates(t, bias):
+        rows = pl.ds(pl.multiple_of(t * TILE, TILE), TILE)
+
+        def add_decays(u, acc):
+            others = pl.ds(pl.multiple_of(u * TILE, TILE), TILE)
+            pos_b = t * TILE + lax.broadcasted_iota(jnp.int32, (TILE, TILE), 0)
+            pos_a = u * TILE + lax.broadcasted_iota(jnp.int32, (TILE, TILE), 1)
+            adds = decay_map(
+                pos_a, qrow[2:3, others], qrow[4:5, others], pos_b, kcol[rows, 1:2], kcol[rows, 3:4]
+            )
+            return acc + dot_nn(adds, decay[others, :].astype(BF16))
+
+        sums = lax.fori_loop(t, tiles, add_decays, jnp.zeros((TILE, LANES), F32))
+        grad_rate = sums + pltpu.roll(sums, LANES - 8, 1) + pltpu.roll(sums, LANES - 16, 1)
+        value = logit[rows, :]
+        grad_forget = grad_rate / (1.0 + jnp.exp(value))
+        grad_forget = jnp.where(lanes < heads, grad_forget, 0.0).astype(BF16)
+        grad[rows, 3 * DH * heads :] = grad_forget
+        return bias + jnp.sum(grad_forget.astype(F32), axis=0, keepdims=True)
+
+    bias_ref[...] = jnp.broadcast_to(
+        lax.fori_loop(0, tiles, rates, jnp.zeros((1, LANES), F32)), bias_ref.shape
     )
-    scores = raw_scores * DH ** (-0.5) + decay_query.T[:, :, None] - decay_key.T[:, None, :]
-    return jnp.where(allowed[None], scores, MASKED)
-
-
-def attention(qkv, decay_sum, doc_ids, branch_tags):
-    group_len, heads = qkv.shape[0], qkv.shape[1]
-    queries, key_rows, value_rows = qkv[:, :, 0], qkv[:, :, 1], qkv[:, :, 2]
-    blocks = jnp.arange(group_len // QBLK, dtype=jnp.int32)
-
-    def block_view(block_index):
-        row_start = block_index * QBLK
-        query_block = lax.dynamic_slice_in_dim(queries, row_start, QBLK, 0)
-        decay_query = lax.dynamic_slice_in_dim(decay_sum, row_start, QBLK, 0)
-        doc_query = lax.dynamic_slice_in_dim(doc_ids, row_start, QBLK, 0)
-        branch_query = lax.dynamic_slice_in_dim(branch_tags, row_start, QBLK, 0)
-        allowed = visible(row_start, doc_query, branch_query, doc_ids, branch_tags)
-        scores = block_scores(query_block, key_rows, decay_query, decay_sum, allowed)
-        return (row_start, query_block, scores)
-
-    def forward_block(block_index):
-        row_start, query_block, scores = block_view(block_index)
-        row_max = jnp.max(scores, axis=2, keepdims=True)
-        expo = jnp.exp(scores - row_max)
-        row_total = jnp.sum(expo, axis=2, keepdims=True)
-        probs = (expo / row_total).astype(BF16)
-        attended_block = jnp.einsum(
-            "hqk,khd->qhd", probs, value_rows, preferred_element_type=jnp.float32
-        ).astype(BF16)
-        return (attended_block, (row_max + jnp.log(row_total))[:, :, 0])
-
-    attended_blocks, lse_blocks = lax.map(forward_block, blocks)
-    attended = attended_blocks.reshape(group_len, heads * DH)
-
-    def backward(grad_attended):
-        def back_block(carry, block_index):
-            key_acc, value_acc, decay_keys = carry
-            row_start, query_block, scores = block_view(block_index)
-            grad_block = lax.dynamic_slice_in_dim(grad_attended, row_start, QBLK, 0)
-            lse_block = lax.dynamic_index_in_dim(lse_blocks, block_index, 0, keepdims=False)
-            probs_star = jnp.exp(scores - lse_block[:, :, None])
-            grad_probs = jnp.einsum(
-                "qhd,khd->hqk", grad_block, value_rows, preferred_element_type=jnp.float32
-            )
-            row_delta = jnp.sum(probs_star * grad_probs, axis=2, keepdims=True)
-            grad_scores = (probs_star * (grad_probs - row_delta)).astype(BF16)
-            grad_query = jnp.einsum(
-                "hqk,khd->qhd", grad_scores, key_rows, preferred_element_type=jnp.float32
-            ) * DH ** (-0.5)
-            key_acc = key_acc + jnp.einsum(
-                "hqk,qhd->khd", grad_scores, query_block, preferred_element_type=jnp.float32
-            )
-            value_acc = value_acc + jnp.einsum(
-                "hqk,qhd->khd", probs_star.astype(BF16), grad_block, preferred_element_type=F32
-            )
-            decay_rows = jnp.sum(grad_scores, axis=2, dtype=F32)
-            decay_keys = decay_keys - jnp.sum(grad_scores, axis=1, dtype=F32)
-            return ((key_acc, value_acc, decay_keys), (grad_query, decay_rows))
-
-        zero_rows = jnp.zeros((group_len, heads, DH), F32)
-        carried, stacked = lax.scan(
-            back_block, (zero_rows, zero_rows, jnp.zeros((heads, group_len), F32)), blocks
+    stores = []
+    for b in range(count):
+        stores.append(
+            pltpu.make_async_copy(grad.at[pl.ds(b * size, size)], grad_hbm.at[b ^ me], out_sem.at[b])
         )
-        key_acc, value_acc, decay_keys = carried
-        query_blocks, decay_blocks = stacked
-        grad_query = query_blocks.reshape(group_len, heads, DH)
-        grad_decay = jnp.transpose(decay_blocks, (0, 2, 1)).reshape(group_len, heads) + decay_keys.T
-        grad_qkv = (
-            jnp.stack([grad_query, key_acc * DH ** (-0.5), value_acc], axis=2)
-            .astype(BF16)
-            .reshape(group_len, heads * 3 * DH)
-        )
-        return grad_qkv, grad_decay
-
-    return attended, backward
+    for store in stores:
+        store.start()
+    for store in stores:
+        store.wait()
+
+
+def attention_backward(grad_attended, saved, logit, kcol, qrow, flags, heads, prompt_len):
+    ot, lse, qp, kp, vp = saved
+    count, size, width = grad_attended.shape
+    total = count * size
+    any_spec = pl.BlockSpec(memory_space=pl.ANY)
+    vmem = pl.BlockSpec(memory_space=pltpu.VMEM)
+    shape = jax.ShapeDtypeStruct
+    out_width = 3 * DH * heads + LANES
+    return pl.pallas_call(
+        functools.partial(backward_kernel, heads, count, prompt_len),
+        out_shape=(shape((count, size, out_width), BF16), shape((8, LANES), F32)),
+        in_specs=[pl.BlockSpec(memory_space=pltpu.SMEM), any_spec]
+        + [vmem] * 5
+        + [any_spec, vmem, vmem],
+        out_specs=(any_spec, vmem),
+        scratch_shapes=[
+            pltpu.VMEM((total, width), BF16),
+            pltpu.VMEM((total, LANES), F32),
+            pltpu.VMEM((heads, total, DH), BF16),
+            pltpu.VMEM((heads, DH + 8, total), BF16),
+            pltpu.VMEM((8, total), F32),
+            pltpu.VMEM((heads, DH + 8, total), F32),
+            pltpu.VMEM((heads, TILE, LANES), F32),
+            pltpu.VMEM((heads, TILE, DH), F32),
+            pltpu.VMEM((TILE, TILE), F32),
+            pltpu.VMEM((total, LANES), F32),
+            pltpu.VMEM((total, out_width), BF16),
+            pltpu.SemaphoreType.DMA((2 * count,)),
+            pltpu.SemaphoreType.DMA((count,)),
+        ],
+        compiler_params=pltpu.CompilerParams(vmem_limit_bytes=56 << 20),
+        cost_estimate=pl.CostEstimate(flops=50_000_000_000, bytes_accessed=30_000_000, transcendentals=0),
+        name="attention_backward",
+    )(flags, grad_attended, ot, lse, qp, kp, vp, logit, kcol, qrow)
+
+
+def group_codes(prompt_ids, branch_ids, branch_docs):
+    prompt_len = prompt_ids.shape[0]
+    member = branch_ids[:, None] == jnp.arange(branch_docs.shape[0])[None, :]
+    branch_doc_ids = jnp.sum(jnp.where(member, branch_docs[None, :], 0), axis=1)
+    key_code = jnp.concatenate([prompt_ids, DOCS + branch_ids])
+    first = jnp.concatenate([prompt_ids, branch_doc_ids])
+    tag = jnp.concatenate([jnp.full_like(prompt_ids, -1), branch_ids])
+    limit = jnp.concatenate([jnp.full_like(prompt_ids, -1), branch_doc_ids])
+    prompt_code = jnp.concatenate([prompt_ids, jnp.full_like(branch_ids, DOCS)])
+    total = key_code.shape[0]
+    none = jnp.zeros_like(tag)
+    kcol = jnp.stack([key_code, tag, limit, prompt_code] + [none] * 4, axis=1)
+    qrow = jnp.stack([first, key_code, tag, prompt_code, limit] + [none] * 3, axis=0)
+    tiles = total // TILE
+    kinds = jnp.arange(2 * DOCS)
+    key_bits = jnp.any(key_code.reshape(tiles, TILE, 1) == kinds, axis=1)
+    query_bits = key_bits | jnp.any(first.reshape(tiles, TILE, 1) == kinds, axis=1)
+    order = jnp.arange(tiles)
+    meets = jnp.any(query_bits[:, None, :] & key_bits[None, :, :], axis=2)
+    flags = (meets & (order[None, :] <= order[:, None])).astype(jnp.int32).reshape(-1)
+    return kcol, qrow, flags
 
 
 def make_shards(osize, psize):
@@ -308,6 +579,7 @@
             0,
         )
         bias = jnp.where(home, forget_bias, lax.ppermute(forget_bias, ("k", "h"), [(1, 2), (2, 1)]))
+        bias = jnp.concatenate([bias, jnp.zeros((lane_pad,), F32)])
         w_qkv = jnp.concatenate([gather_weight(qkv_weight, home, 0), w_forget], axis=1)
         w_out = gather_weight(out_weight, home, 1)
         w_gate = gather_weight(gate_weight, home, 0)
@@ -321,34 +593,14 @@
 
         rms_a = lax.rsqrt(jnp.sum(stream * stream, axis=1) / D + EPS)[:, None]
         normed_a_all = gather_blocks((stream * rms_a * gain_a).astype(BF16), psize)
-        projected = reorder(matmul(normed_a_all, w_qkv), me, count)
-        group_len = projected.shape[0]
+        projected = matmul(normed_a_all, w_qkv)
         width = heads * 3 * DH
-        qkv = projected[:, :width].astype(BF16).reshape(group_len, heads, 3, DH)
-        forget_logit = projected[:, width : width + heads] + bias
-        log_rate = jax.nn.log_sigmoid(forget_logit)
-
-        member = branch_ids[:, None] == jnp.arange(branch_docs.shape[0])[None, :]
-        branch_doc_ids = jnp.sum(jnp.where(member, branch_docs[None, :], 0), axis=1)
-        doc_ids = jnp.concatenate([prompt_ids, branch_doc_ids])
-        branch_tags = jnp.concatenate([jnp.full((prompt_len,), -1, jnp.int32), branch_ids])
-        pos = jnp.arange(group_len, dtype=jnp.int32)
-        key_prompt = branch_tags[None, :] < 0
-        query_prompt = branch_tags[:, None] < 0
-        causal = pos[None, :] <= pos[:, None]
-        sums = jnp.where(
-            query_prompt,
-            causal,
-            jnp.where(
-                key_prompt,
-                doc_ids[None, :] <= doc_ids[:, None],
-                causal & (branch_tags[None, :] == branch_tags[:, None]),
-            ),
-        ).astype(BF16)
-        decay_sum = sum3(matmul(sums, split3(log_rate)))
-
-        attended, attention_back = attention(qkv, decay_sum, doc_ids, branch_tags)
-        attended = reorder(attended, me, count)
+        qkv = projected[:, :width].astype(BF16).reshape(count, -1, width)
+        logit = projected[:, width:] + bias
+        logit = logit.reshape(count, -1, LANES)
+        kcol, qrow, flags = group_codes(prompt_ids, branch_ids, branch_docs)
+        attended, *saved = attention_forward(qkv, logit, kcol, qrow, flags, heads, prompt_len)
+        attended = attended.reshape(-1, heads * DH)
         resid = stream + sum_blocks(matmul(attended, w_out), psize)
         rms_b = lax.rsqrt(jnp.sum(resid * resid, axis=1) / D + EPS)[:, None]
         normed_b_all = gather_blocks((resid * rms_b * gain_b).astype(BF16), psize)
@@ -383,18 +635,12 @@
         grad_resid = cotangent + rms_b * gained_b - resid * (rms_b * rms_b * rms_b) * inner_b / D
         grad_branch_all = gather_blocks(grad_resid.astype(BF16), psize)
         out_grad = reduce_cols(contract_rows(attended, grad_branch_all))
-        grad_attended = reorder(contract_cols(grad_branch_all, w_out).astype(BF16), me, count)
-        grad_qkv, grad_decay = attention_back(grad_attended.reshape(group_len, heads, DH))
-        grad_log_rate = sum3(contract_rows(sums, split3(grad_decay)))
-        grad_forget = (grad_log_rate * jax.nn.sigmoid(-forget_logit)).astype(BF16)
-        forget_bias_part = jnp.sum(grad_forget, axis=0, dtype=F32)
-        grad_proj = reorder(
-            jnp.concatenate(
-                [grad_qkv, grad_forget, jnp.zeros((group_len, lane_pad), BF16)], axis=1
-            ),
-            me,
-            count,
+        grad_attended = contract_cols(grad_branch_all, w_out).astype(BF16)
+        grad_proj, bias_sums = attention_backward(
+            grad_attended.reshape(count, -1, heads * DH), saved, logit, kcol, qrow, flags, heads, prompt_len
         )
+        grad_proj = grad_proj.reshape(-1, width + LANES)
+        forget_bias_part = bias_sums[0, :heads]
         proj_grad = reduce_rows(contract_rows(normed_a_all, grad_proj))
         qkv_grad, forget_grad = proj_grad[:, :width], proj_grad[:, width : width + heads]
         grad_normed_a = sum_blocks(contract_cols(grad_proj, w_qkv), psize)

time: 1130 us -> 875 us (0.77)
  matrix products: 312 us -> 128 us
  local copies, waits for them, and re-layouts: 136 us -> 37.1 us
  Pallas kernels: 0 us -> 96.1 us
  other arithmetic: 176 us -> 83.9 us
  waiting for transfers between devices: 288 us -> 312 us
    dot_general x21 -> x0, matrix products: 174 us -> none  [the longest x6 67.5 us: block_scores(): jnp.einsum('qhd,khd->hqk', query_block, key_rows, preferred_element_type=...]
    pallas_call x0 -> x2, Pallas kernels: none -> 96.1 us  [the longest x1 51.4 us: attention_backward(): pl.pallas_call(functools.partial(backward_kernel, heads, count, prompt_le...]
    reduce_sum x8 -> x1, other arithmetic: 70.6 us -> 0.09 us  [group_codes(): branch_doc_ids = jnp.sum(jnp.where(member, branch_docs[None, :], 0), axis=1)]
    dynamic_slice x38 -> x0, local copies, waits for them, and re-layouts: 67.6 us -> none  [the longest x20 61 us: reorder(): lax.dynamic_index_in_dim(parts, j ^ me, 0, keepdims=False)]
    ppermute x5, starting transfers between devices: 50.6 us -> 20.4 us  [reduce_weight(): lax.ppermute(total.astype(BF16), ('k', 'h'), [(0 * 2 + 1, 0 * 2 + 0), (1...]
    ppermute x6, waiting for transfers between devices: 79.6 us -> 99.1 us  [fetch_home_away(): return lax.ppermute(value, ('k', 'x', 'h'), pairs)]
    ppermute x25, starting transfers between devices: 36.5 us -> 54.6 us  [swap(): return lax.ppermute(value, axis, [(0, 1), (1, 0)])]
    ppermute x8, starting transfers between devices: 10.7 us -> 28.5 us  [xor_swap(): return lax.ppermute(value, axis, [(i, i ^ bit) for i in range(size)])]
  transfers between devices with their start and end apart: 69 -> 69, of which waited for: 21 -> 20; matrix products, arithmetic and copies ran while one was open for 39% -> 20% of each run, Pallas kernels for 0% -> 6%
where the time goes in v2:
time: 875 us; the launch traced here: 863 us
  waiting for transfers between devices  312 us (36%)
  starting transfers between devices  174 us (20%)
  matrix products  128 us (15%)
  Pallas kernels  96.1 us (11%)
  other arithmetic  83.9 us (10%)
  local copies, waits for them, and re-layouts  37.1 us (4%)
  blocking collectives  28 us (3%)
    ppermute x6, waiting for transfers between devices, fetch_home_away(): return lax.ppermute(value, ('k', 'x', 'h'), pairs)  99.1 us
    ppermute x8, waiting for transfers between devices, xor_swap(): return lax.ppermute(value, axis, [(i, i ^ bit) for i in range(size)])  89 us
    ppermute x25, waiting for transfers between devices, swap(): return lax.ppermute(value, axis, [(0, 1), (1, 0)])  61.5 us
    ppermute x25, starting transfers between devices, swap(): return lax.ppermute(value, axis, [(0, 1), (1, 0)])  54.6 us
    pallas_call x1, Pallas kernels, attention_backward(): pl.pallas_call(functools.partial(backward_kernel, heads, count, prompt_le...  51.4 us
    dot_general x5, matrix products, contract_cols(): lax.dot_general(left, right, (((1,), (1,)), ((), ())), preferred_element_...  48.8 us
    dot_general x5, matrix products, matmul(): return jnp.dot(left, right, preferred_element_type=F32)  45.9 us
    pallas_call x1, Pallas kernels, attention_forward(): pl.pallas_call(functools.partial(forward_kernel, heads, count, prompt_len...  44.7 us
  transfers between devices with their start and end apart: 69, of which 20 were waited for; matrix products, arithmetic and copies ran while one was open for 20% of the time, Pallas kernels for 6%

profile of v2, /device:TPU:1, one launch (start us, length us, event | category | flops | bytes accessed | tf_op | source)
XLA Modules:
  0.0 862.5 jit_solution(17715082786398839242)
XLA Ops:
  0.7 5.7 collective-permute-start.12
  13.4 4.0 collective-permute-start.1
  19.5 16.0 %collective-permute-done.3 = s32[1540]{0:T(1024)S(1)} collective-permute-done((s32[1540]{0:T(1024)S(1)}, s32[1540]{0:T(1024)S(1)}, u32[]{:S(2)}, u32[]{:S(2)}) %collective-permute-start.3) | collective-permute-done | bytes 6192 | tf_op jit(solution)/shard_map/ppermute | solution.py:22
  35.5 6.0 collective-permute-start.13
  47.3 18.8 %collective-permute-done.8 = bf16[768,1152]{1,0:T(8,128)(2,1)} collective-permute-done((bf16[768,1152]{1,0:T(8,128)(2,1)}, bf16[768,1152]{1,0:T(8,128)(2,1)}, u32[]{:S(2)}, u32[]{:S(2)}) %collective-permute-start.8) | collective-permute-done | bytes 1769504 | tf_op jit(solution)/shard_map/ppermute | solution.py:40
  68.7 3.4 collective-permute-start.11
  75.0 17.0 %collective-permute-done.11 = bf16[768,128]{0,1:T(8,128)(2,1)S(1)} collective-permute-done((bf16[768,128]{0,1:T(8,128)(2,1)S(1)}, bf16[768,128]{0,1:T(8,128)(2,1)S(1)}, u32[]{:S(2)}, u32[]{:S(2)}) %collective-permute-start.11) | collective-permute-done | bytes 196640 | tf_op jit(solution)/shard_map/ppermute | solution.py:47
  99.6 2.9 broadcast_select_fusion.1
  102.6 10.0 %fusion.31 = f32[1536,1280]{1,0:T(8,128)S(1)} fusion(bf16[1536,128]{1,0:T(8,128)(2,1)S(1)} %copy-done.51, bf16[768,1152]{1,0:T(8,128)(2,1)S(1)} %get-tuple-element.102, bf16[768,1152]{1,0:T(8,128)(2,1)S(1)} %get-tuple-element.101, bf16[384,1536]{1,0:T(8,128)(2,1)} %collective-permute-done.7, bf16[384,1536]{1,0:T(8,128)(2,1)} %collective-permute-done.6, ...), kind=kOutput, calls=%fused_computation.84 | convolution fusion | flops 6070468608 | bytes 16515072 | tf_op jit(solution)/shard_map/dot_general | solution.py:152
  114.8 44.7 %attention_forward.1 = (bf16[4,384,384]{2,1,0:T(8,128)(2,1)S(1)}, f32[384,1536]{1,0:T(8,128)S(1)}, f32[8,1536]{1,0:T(8,128)S(1)}, bf16[6,1536,128]{2,1,0:T(8,128...) custom-call(s32[36]{0:T(128)S(1)} %reshape.108.flags, bf16[4,384,1152]{2,1,0:T(8,128)(2,1)} %bitcast.28, ...), custom_call_target="tpu_custom_call" | custom-call | flops 20000000000 | bytes 30000000 | tf_op jit(solution)/shard_map/attention_forward/pallas_call | solution.py:319
  164.5 3.1 collective-permute-start.33
  170.3 2.7 collective-permute-done.32
  174.4 11.3 %collective-permute-done.33 = bf16[384,768]{1,0:T(8,128)(2,1)S(1)} collective-permute-done((bf16[384,768]{1,0:T(8,128)(2,1)S(1)}, bf16[384,768]{1,0:T(8,128)(2,1)S(1)}, u32[]{:S(2)}, u32[]{:S(2)}) %collective-permute-start.33) | collective-permute-done | bytes 589856 | tf_op jit(solution)/shard_map/ppermute | solution.py:99
  188.5 37.6 %collective-permute-done.21 = bf16[768,1024]{1,0:T(8,128)(2,1)} collective-permute-done((bf16[768,1024]{1,0:T(8,128)(2,1)S(1)}, bf16[768,1024]{1,0:T(8,128)(2,1)}, u32[]{:S(2)}, u32[]{:S(2)}) %collective-permute-start.21) | collective-permute-done | bytes 1572896 | tf_op jit(solution)/shard_map/ppermute | solution.py:40
  226.1 28.4 %collective-permute-done.23 = bf16[768,1024]{1,0:T(8,128)(2,1)S(1)} collective-permute-done((bf16[768,1024]{1,0:T(8,128)(2,1)S(1)}, bf16[768,1024]{1,0:T(8,128)(2,1)S(1)}, u32[]{:S(2)}, u32[]{:S(2)}) %collective-permute-start.23) | collective-permute-done | bytes 1572896 | tf_op jit(solution)/shard_map/ppermute | solution.py:40
  257.6 13.9 %collective-permute-done.25 = bf16[1024,768]{1,0:T(8,128)(2,1)} collective-permute-done((bf16[1024,768]{1,0:T(8,128)(2,1)}, bf16[1024,768]{1,0:T(8,128)(2,1)}, u32[]{:S(2)}, u32[]{:S(2)}) %collective-permute-start.25) | collective-permute-done | bytes 1572896 | tf_op jit(solution)/shard_map/ppermute | solution.py:40
  273.5 3.5 collective-permute-start.26
  279.6 2.7 multiply_reduce_fusion.2
  284.1 3.9 broadcast_select_fusion.7
  288.0 6.2 collective-permute-done.24
  294.6 16.2 %collective-permute-done.26 = bf16[1024,768]{1,0:T(8,128)(2,1)S(1)} collective-permute-done((bf16[1024,768]{1,0:T(8,128)(2,1)}, bf16[1024,768]{1,0:T(8,128)(2,1)S(1)}, u32[]{:S(2)}, u32[]{:S(2)}) %collective-permute-start.26) | collective-permute-done | bytes 1572896 | tf_op jit(solution)/shard_map/ppermute | solution.py:47
  313.1 10.1 %fusion.22 = f32[1536,1024]{1,0:T(8,128)} fusion(bf16[1024,768]{1,0:T(8,128)(2,1)S(1)} %get-tuple-element.104, bf16[1024,768]{1,0:T(8,128)(2,1)S(1)} %get-tuple-element.103, bf16[384,1536]{1,0:T(8,128)(2,1)S(1)} %collective-permute-done.36, bf16[384,1536]{1,0:T(8,128)(2,1)} %collective-permute-done.35, bf16[384,1536]{1,0:T(8,128)(2,1)S(1)} %collective-permute-done.34, ...), kind=kOutput, calls=%fused_computation.72 | convolution fusion | flops 4861722624 | bytes 14155776 | tf_op jit(solution)/shard_map/dot_general | solution.py:146
  323.3 7.8 fusion.25
  331.2 14.9 %multiply_convert_fusion.1 = (bf16[1536,1024]{1,0:T(8,128)(2,1)}, bf16[1536,1024]{1,0:T(8,128)(2,1)}, bf16[1536,1024]{1,0:T(8,128)(2,1)}) fusion(f32[1536,1024]{1,0:T(8,128)} %fusion.22, f32[1536,1024]{1,0:T(8,128)} %fusion.25, bf16[768,1024]{1,0:T(8,128)(2,1)S(1)} %copy-done.36, bf16[768,1024]{1,0:T(8,128)(2,1)S(1)} %copy-done.35, ...), kind=kOutput, calls=%fused_computation.3 | convolution fusion | flops 4880596992 | bytes 29884416 | tf_op jit(solution)/shard_map/dot_general | solution.py:152
  346.2 10.6 %fusion.70 = (bf16[1536,1536]{1,0:T(8,128)(2,1)}, f32[1536,1536]{1,0:T(8,128)}) fusion(bf16[1536,1024]{1,0:T(8,128)(2,1)} %get-tuple-element.87, bf16[1024,768]{1,0:T(8,128)(2,1)} %copy-done.42, bf16[1024,768]{1,0:T(8,128)(2,1)} %copy-done.41), kind=kOutput, calls=%fused_computation.194 | convolution fusion | flops 4840488960 | bytes 20447232 | tf_op jit(solution)/shard_map/dot_general | solution.py:152
  356.8 6.7 fusion.54
  365.3 8.6 %fusion.24 = f32[1536,1536]{1,0:T(8,128)} fusion(bf16[1536,1024]{1,0:T(8,128)(2,1)S(1)} %copy-done.76, bf16[768,1024]{1,0:T(8,128)(2,1)S(1)} %copy-done.40, bf16[768,1024]{1,0:T(8,128)(2,1)S(1)} %copy-done.38), kind=kOutput, calls=%fused_computation.74 | convolution fusion | flops 4838129664 | bytes 15728640 | tf_op jit(solution)/shard_map/dot_general | solution.py:146
  374.0 12.4 %fusion.69 = (bf16[1536,1536]{1,0:T(8,128)(2,1)}, f32[1536,1536]{1,0:T(8,128)}) fusion(f32[1536,1536]{1,0:T(8,128)} %fusion.24, bf16[1536,1024]{1,0:T(8,128)(2,1)} %get-tuple-element.85, bf16[768,1024]{1,0:T(8,128)(2,1)S(1)} %copy-done.36, bf16[768,1024]{1,0:T(8,128)(2,1)S(1)} %copy-done.35), kind=kOutput, calls=%fused_computation.193 | convolution fusion | flops 4842848256 | bytes 29884416 | tf_op jit(solution)/shard_map/dot_general | solution.py:146
  386.4 2.9 fusion.59
  389.4 3.0 fusion.60
  392.9 5.2 fusion.56
  398.0 7.9 fusion.55
  409.7 3.3 fusion.19
  416.2 25.9 %collective-permute-done.57 = bf16[768,1024]{1,0:T(8,128)(2,1)S(1)} collective-permute-done((bf16[768,1024]{1,0:T(8,128)(2,1)S(1)}, bf16[768,1024]{1,0:T(8,128)(2,1)S(1)}, u32[]{:S(2)}, u32[]{:S(2)}) %collective-permute-start.57) | collective-permute-done | bytes 1572896 | tf_op jit(solution)/shard_map/ppermute | solution.py:22
  443.2 4.1 collective-permute-start.66
  452.5 22.7 %collective-permute-done.28 = bf16[384,1536]{1,0:T(8,128)(2,1)S(1)} collective-permute-done((bf16[384,1536]{1,0:T(8,128)(2,1)}, bf16[384,1536]{1,0:T(8,128)(2,1)S(1)}, u32[]{:S(2)}, u32[]{:S(2)}) %collective-permute-start.28) | collective-permute-done | bytes 1179680 | tf_op jit(solution)/shard_map/ppermute | solution.py:26
  476.2 4.7 fusion.57
  480.9 4.5 collective-permute-start.31
  486.1 4.0 collective-permute-start.62
  490.1 25.5 %collective-permute-start.41 = (bf16[384,1536]{1,0:T(8,128)(2,1)S(1)}, bf16[384,1536]{1,0:T(8,128)(2,1)}, u32[]{:S(2)}, u32[]{:S(2)}) collective-permute-start(bf16[384,1536]{1,0:T(8,128)(2,1)S(1)} %copy-done.43), channel_id=1, source_target_pairs={{0,1},{1,0},{2,3},{3,2},{4,5},{5,4},{6,7},{7,6},{8,9},{9,8},{10,11... | collective-permute-start | bytes 3538952 | tf_op jit(solution)/shard_map/ppermute | solution.py:26
  518.6 5.9 collective-permute-start.40
  526.8 50.4 %collective-permute-done.41 = bf16[384,1536]{1,0:T(8,128)(2,1)} collective-permute-done((bf16[384,1536]{1,0:T(8,128)(2,1)S(1)}, bf16[384,1536]{1,0:T(8,128)(2,1)}, u32[]{:S(2)}, u32[]{:S(2)}) %collective-permute-start.41) | collective-permute-done | bytes 1179680 | tf_op jit(solution)/shard_map/ppermute | solution.py:26
  577.6 3.5 add_convert_fusion.7
  583.0 3.5 add_convert_fusion.5
  591.6 3.9 fusion.33
  598.2 4.9 convolution_convert_fusion
  603.1 51.4 %attention_backward.1 = (bf16[4,384,1280]{2,1,0:T(8,128)(2,1)}, f32[8,128]{1,0:T(8,128)}) custom-call(s32[36]{0:T(128)} %copy-done.5, bf16[4,384,384]{2,1,0:T(8,128)(2,1)} %bitcast.40, f32[384,1536]{1,0:T(8,128)} %copy-done.6, f32[8,1536]{1,0:T(8,128)} %copy-done.7, bf16[6,1536,128]{2,1,0:T(8,128)(2,1)} %get-tuple-element.22.qp, ...), custom_call_target="tpu_custom_call" | custom-call | flops 49999998976 | bytes 30000000 | tf_op jit(solution)/shard_map/attention_backward/pallas_call | solution.py:478
  654.6 9.8 %fusion.32 = f32[1536,1280]{0,1:T(8,128)S(1)} fusion(bf16[1536,1280]{1,0:T(8,128)(2,1)} %bitcast.38, bf16[384,1536]{1,0:T(8,128)(2,1)} %collective-permute-done.7, bf16[384,1536]{1,0:T(8,128)(2,1)} %collective-permute-done.6, bf16[384,1536]{1,0:T(8,128)(2,1)} %collective-permute-done.5, bf16[384,1536]{1,0:T(8,128)(2,1)} %fusion.4), kind=kOutput, calls=%fused_computation.103 | convolution fusion | flops 6058672128 | bytes 16515072 | tf_op jit(solution)/shard_map/dot_general | solution.py:140
  669.4 12.7 %fusion.71 = (bf16[1536,1536]{1,0:T(8,128)(2,1)}, f32[1536,1536]{1,0:T(8,128)}) fusion(bf16[1536,1280]{1,0:T(8,128)(2,1)} %bitcast.39, bf16[1536,128]{1,0:T(8,128)(2,1)S(1)} %copy-done.52, bf16[768,1152]{1,0:T(8,128)(2,1)S(1)} %copy-done.28, bf16[768,1152]{1,0:T(8,128)(2,1)S(1)} %copy-done.26), kind=kOutput, calls=%fused_computation.195 | convolution fusion | flops 6053953536 | bytes 22020096 | tf_op jit(solution)/shard_map/dot_general | solution.py:146
  682.1 3.2 fusion.58
  686.0 19.5 %collective-permute-done.49 = bf16[768,1280]{0,1:T(8,128)(2,1)S(1)} collective-permute-done((bf16[768,1280]{0,1:T(8,128)(2,1)S(1)}, bf16[768,1280]{0,1:T(8,128)(2,1)S(1)}, u32[]{:S(2)}, u32[]{:S(2)}) %collective-permute-start.49) | collective-permute-done | bytes 1966112 | tf_op jit(solution)/shard_map/ppermute | solution.py:22
  707.5 3.0 collective-permute-start.50
  710.6 2.8 collective-permute-start.43
  715.0 6.7 collective-permute-start.54
  721.8 2.7 add_convert_fusion.6
  728.6 8.7 %collective-permute-done.54 = bf16[384,768]{1,0:T(8,128)(2,1)S(1)} collective-permute-done((bf16[384,768]{1,0:T(8,128)(2,1)S(1)}, bf16[384,768]{1,0:T(8,128)(2,1)S(1)}, u32[]{:S(2)}, u32[]{:S(2)}) %collective-permute-start.54) | collective-permute-done | bytes 589856 | tf_op jit(solution)/shard_map/ppermute | solution.py:60
  740.2 36.1 %collective-permute-start.45 = (bf16[384,1536]{1,0:T(8,128)(2,1)}, bf16[384,1536]{1,0:T(8,128)(2,1)S(1)}, u32[]{:S(2)}, u32[]{:S(2)}) collective-permute-start(bf16[384,1536]{1,0:T(8,128)(2,1)} %get-tuple-element.89), channel_id=1, source_target_pairs={{0,8},{8,0},{1,9},{9,1},{2,10},{10,2},{3,11},{11,3},{4,12},{12,4},... | collective-permute-start | bytes 3538952 | tf_op jit(solution)/shard_map/ppermute | solution.py:22
  781.1 3.3 select_convert_fusion.1
  785.1 3.3 select_convert_fusion.3
  788.4 3.4 select_convert_fusion.2
  793.3 11.0 %collective-permute-done.44 = bf16[384,1536]{1,0:T(8,128)(2,1)S(1)} collective-permute-done((bf16[384,1536]{1,0:T(8,128)(2,1)S(1)}, bf16[384,1536]{1,0:T(8,128)(2,1)S(1)}, u32[]{:S(2)}, u32[]{:S(2)}) %collective-permute-start.44) | collective-permute-done | bytes 1179680 | tf_op jit(solution)/shard_map/ppermute | solution.py:26
  809.6 15.2 %collective-permute-start.47 = (bf16[384,768]{1,0:T(8,128)(2,1)S(1)}, bf16[384,768]{1,0:T(8,128)(2,1)S(1)}, u32[]{:S(2)}, u32[]{:S(2)}) collective-permute-start(bf16[384,768]{1,0:T(8,128)(2,1)S(1)} %get-tuple-element.109), channel_id=1, source_target_pairs={{8,4},{4,8},{9,5},{5,9},{10,6},{6,10},{11,7},{7,11},{24,20},{20,24... | collective-permute-start | bytes 1769480 | tf_op jit(solution)/shard_map/ppermute | solution.py:111
  826.0 28.0 %psum.7 = f32[1560]{0:T(1024)S(1)} all-reduce(f32[1560]{0:T(1024)S(1)} %fusion.38), channel_id=1, replica_groups=mesh['o'=2,'k'=2,'x'=2,'h'=2,'p'=2] {'o','k','h','p'}, use_global_device_ids=true, to_apply=%region_10.11 | all-reduce | flops 1560 | bytes 12480 | tf_op jit(solution)/shard_map/psum | solution.py:661
  859.1 2.9 copy.40
  (370 shorter events, 120.7 us)
Async XLA Ops:
  0.7 12.7 %collective-permute-start.12 = (f32[6]{0:T(128)}, f32[6]{0:T(128)S(1)}, u32[]{:S(2)}, u32[]{:S(2)}) collective-permute-start(f32[6]{0:T(128)} %param.18), channel_id=1, source_target_pairs={{2,8},{8,2},{3,9},{9,3},{6,12},{12,6},{7,13},{13,7},{18,24},{24,18... | collective-permute-start | bytes 80 | tf_op jit(solution)/shard_map/ppermute | solution.py:581
  10.6 58.1 %collective-permute-start.10 = (bf16[768,128]{0,1:T(8,128)(2,1)S(1)}, bf16[768,128]{0,1:T(8,128)(2,1)S(1)}, u32[]{:S(2)}, u32[]{:S(2)}) collective-permute-start(bf16[768,128]{0,1:T(8,128)(2,1)S(1)} %concatenate.85), channel_id=1, source_target_pairs={{0,4},{2,8},{4,0},{6,12},{8,2},{10,14},{12,6},{14,10},{1,5},{3,9},... | collective-permute-start | bytes 589832 | tf_op jit(solution)/shard_map/ppermute | solution.py:40
  13.2 28.3 %collective-permute-start = (bf16[384,768]{1,0:T(8,128)(2,1)}, bf16[384,768]{1,0:T(8,128)(2,1)S(1)}, u32[]{:S(2)}, u32[]{:S(2)}) collective-permute-start(bf16[384,768]{1,0:T(8,128)(2,1)} %get-tuple-element.83), channel_id=1, source_target_pairs={{0,8},{4,0},{8,12},{12,4},{1,9},{5,1},{9,13},{13,5},{2,10},{6,2},{... | collective-permute-start | bytes 1769480 | tf_op jit(solution)/shard_map/ppermute | solution.py:98
  13.4 28.9 %collective-permute-start.1 = (bf16[384,768]{1,0:T(8,128)(2,1)S(1)}, bf16[384,768]{1,0:T(8,128)(2,1)S(1)}, u32[]{:S(2)}, u32[]{:S(2)}) collective-permute-start(bf16[384,768]{1,0:T(8,128)(2,1)S(1)} %get-tuple-element.84), channel_id=1, source_target_pairs={{4,8},{8,4},{5,9},{9,5},{6,10},{10,6},{7,11},{11,7},{20,24},{24,20... | collective-permute-start | bytes 1769480 | tf_op jit(solution)/shard_map/ppermute | solution.py:99
  17.5 48.6 %collective-permute-start.8 = (bf16[768,1152]{1,0:T(8,128)(2,1)}, bf16[768,1152]{1,0:T(8,128)(2,1)}, u32[]{:S(2)}, u32[]{:S(2)}) collective-permute-start(bf16[768,1152]{1,0:T(8,128)(2,1)} %param.16), channel_id=1, source_target_pairs={{0,4},{2,8},{4,0},{6,12},{8,2},{10,14},{12,6},{14,10},{1,5},{3,9},... | collective-permute-start | bytes 5308424 | tf_op jit(solution)/shard_map/ppermute | solution.py:40
  17.6 17.9 %collective-permute-start.3 = (s32[1540]{0:T(1024)S(1)}, s32[1540]{0:T(1024)S(1)}, u32[]{:S(2)}, u32[]{:S(2)}) collective-permute-start(s32[1540]{0:T(1024)S(1)} %broadcast_select_fusion.28), channel_id=1, source_target_pairs={{0,4},{4,0},{1,5},{5,1},{2,6},{6,2},{3,7},{7,3},{8,12},{12,8},{9,1... | collective-permute-start | bytes 18488 | tf_op jit(solution)/shard_map/ppermute | solution.py:22
  35.5 36.9 %collective-permute-start.13 = (bf16[384,768]{1,0:T(8,128)(2,1)S(1)}, bf16[384,768]{1,0:T(8,128)(2,1)}, u32[]{:S(2)}, u32[]{:S(2)}) collective-permute-start(bf16[384,768]{1,0:T(8,128)(2,1)S(1)} %copy-done.49), channel_id=1, source_target_pairs={{0,4},{2,8},{4,0},{6,12},{8,2},{10,14},{12,6},{14,10},{1,5},{3,9},... | collective-permute-start | bytes 1769480 | tf_op jit(solution)/shard_map/ppermute | solution.py:40
  46.0 48.6 %collective-permute-start.6 = (bf16[384,1536]{1,0:T(8,128)(2,1)}, bf16[384,1536]{1,0:T(8,128)(2,1)}, u32[]{:S(2)}, u32[]{:S(2)}) collective-permute-start(bf16[384,1536]{1,0:T(8,128)(2,1)} %fusion.4), channel_id=1, source_target_pairs={{0,1},{1,0},{2,3},{3,2},{4,5},{5,4},{6,7},{7,6},{8,9},{9,8},{10,11... | collective-permute-start | bytes 3538952 | tf_op jit(solution)/shard_map/ppermute | solution.py:26
  66.1 33.5 %collective-permute-start.9 = (bf16[768,1152]{1,0:T(8,128)(2,1)}, bf16[768,1152]{1,0:T(8,128)(2,1)}, u32[]{:S(2)}, u32[]{:S(2)}) collective-permute-start(bf16[768,1152]{1,0:T(8,128)(2,1)} %collective-permute-done.8), channel_id=1, source_target_pairs={{2,6},{6,2},{8,12},{12,8},{3,7},{7,3},{9,13},{13,9},{18,22},{22,18... | collective-permute-start | bytes 5308424 | tf_op jit(solution)/shard_map/ppermute | solution.py:47
  68.7 23.4 %collective-permute-start.11 = (bf16[768,128]{0,1:T(8,128)(2,1)S(1)}, bf16[768,128]{0,1:T(8,128)(2,1)S(1)}, u32[]{:S(2)}, u32[]{:S(2)}) collective-permute-start(bf16[768,128]{0,1:T(8,128)(2,1)S(1)} %collective-permute-done.10), channel_id=1, source_target_pairs={{2,6},{6,2},{8,12},{12,8},{3,7},{7,3},{9,13},{13,9},{18,22},{22,18... | collective-permute-start | bytes 589832 | tf_op jit(solution)/shard_map/ppermute | solution.py:47
  72.4 25.7 %collective-permute-start.14 = (bf16[384,768]{1,0:T(8,128)(2,1)}, bf16[384,768]{1,0:T(8,128)(2,1)}, u32[]{:S(2)}, u32[]{:S(2)}) collective-permute-start(bf16[384,768]{1,0:T(8,128)(2,1)} %collective-permute-done.13), channel_id=1, source_target_pairs={{2,6},{6,2},{8,12},{12,8},{3,7},{7,3},{9,13},{13,9},{18,22},{22,18... | collective-permute-start | bytes 1769480 | tf_op jit(solution)/shard_map/ppermute | solution.py:47
  92.1 10.4 %collective-permute-start.5 = (bf16[384,1536]{1,0:T(8,128)(2,1)}, bf16[384,1536]{1,0:T(8,128)(2,1)}, u32[]{:S(2)}, u32[]{:S(2)}) collective-permute-start(bf16[384,1536]{1,0:T(8,128)(2,1)} %fusion.4), channel_id=1, source_target_pairs={{0,8},{8,0},{1,9},{9,1},{2,10},{10,2},{3,11},{11,3},{4,12},{12,4},... | collective-permute-start | bytes 3538952 | tf_op jit(solution)/shard_map/ppermute | solution.py:22
  163.4 23.7 %collective-permute-start.15 = (bf16[384,1536]{1,0:T(8,128)(2,1)S(1)}, bf16[384,1536]{1,0:T(8,128)(2,1)S(1)}, u32[]{:S(2)}, u32[]{:S(2)}) collective-permute-start(bf16[384,1536]{1,0:T(8,128)(2,1)S(1)} %get-tuple-element.94), channel_id=1, source_target_pairs={{0,8},{8,0},{1,9},{9,1},{2,10},{10,2},{3,11},{11,3},{4,12},{12,4},... | collective-permute-start | bytes 3538952 | tf_op jit(solution)/shard_map/ppermute | solution.py:22
  164.5 21.1 %collective-permute-start.33 = (bf16[384,768]{1,0:T(8,128)(2,1)S(1)}, bf16[384,768]{1,0:T(8,128)(2,1)S(1)}, u32[]{:S(2)}, u32[]{:S(2)}) collective-permute-start(bf16[384,768]{1,0:T(8,128)(2,1)S(1)} %get-tuple-element.80), channel_id=1, source_target_pairs={{4,8},{8,4},{5,9},{9,5},{6,10},{10,6},{7,11},{11,7},{20,24},{24,20... | collective-permute-start | bytes 1769480 | tf_op jit(solution)/shard_map/ppermute | solution.py:99
  167.6 58.5 %collective-permute-start.21 = (bf16[768,1024]{1,0:T(8,128)(2,1)S(1)}, bf16[768,1024]{1,0:T(8,128)(2,1)}, u32[]{:S(2)}, u32[]{:S(2)}) collective-permute-start(bf16[768,1024]{1,0:T(8,128)(2,1)S(1)} %copy-done.29), channel_id=1, source_target_pairs={{0,4},{2,8},{4,0},{6,12},{8,2},{10,14},{12,6},{14,10},{1,5},{3,9},... | collective-permute-start | bytes 4718600 | tf_op jit(solution)/shard_map/ppermute | solution.py:40
  167.7 86.9 %collective-permute-start.23 = (bf16[768,1024]{1,0:T(8,128)(2,1)S(1)}, bf16[768,1024]{1,0:T(8,128)(2,1)S(1)}, u32[]{:S(2)}, u32[]{:S(2)}) collective-permute-start(bf16[768,1024]{1,0:T(8,128)(2,1)S(1)} %copy-done.31), channel_id=1, source_target_pairs={{0,4},{2,8},{4,0},{6,12},{8,2},{10,14},{12,6},{14,10},{1,5},{3,9},... | collective-permute-start | bytes 4718600 | tf_op jit(solution)/shard_map/ppermute | solution.py:40
  173.0 98.6 %collective-permute-start.25 = (bf16[1024,768]{1,0:T(8,128)(2,1)}, bf16[1024,768]{1,0:T(8,128)(2,1)}, u32[]{:S(2)}, u32[]{:S(2)}) collective-permute-start(bf16[1024,768]{1,0:T(8,128)(2,1)} %param.23), channel_id=1, source_target_pairs={{0,4},{2,8},{4,0},{6,12},{8,2},{10,14},{12,6},{14,10},{1,5},{3,9},... | collective-permute-start | bytes 4718600 | tf_op jit(solution)/shard_map/ppermute | solution.py:40
  187.1 84.5 %collective-permute-start.35 = (bf16[384,1536]{1,0:T(8,128)(2,1)}, bf16[384,1536]{1,0:T(8,128)(2,1)}, u32[]{:S(2)}, u32[]{:S(2)}) collective-permute-start(bf16[384,1536]{1,0:T(8,128)(2,1)} %pad_maximum_fusion.19), channel_id=1, source_target_pairs={{0,1},{1,0},{2,3},{3,2},{4,5},{5,4},{6,7},{7,6},{8,9},{9,8},{10,11... | collective-permute-start | bytes 3538952 | tf_op jit(solution)/shard_map/ppermute | solution.py:26
  187.1 86.4 %collective-permute-start.17 = (bf16[384,1536]{1,0:T(8,128)(2,1)}, bf16[384,1536]{1,0:T(8,128)(2,1)S(1)}, u32[]{:S(2)}, u32[]{:S(2)}) collective-permute-start(bf16[384,1536]{1,0:T(8,128)(2,1)} %get-tuple-element.95), channel_id=1, source_target_pairs={{0,8},{8,0},{1,9},{9,1},{2,10},{10,2},{3,11},{11,3},{4,12},{12,4},... | collective-permute-start | bytes 3538952 | tf_op jit(solution)/shard_map/ppermute | solution.py:22
  226.1 53.5 %collective-permute-start.16 = (bf16[384,1536]{1,0:T(8,128)(2,1)}, bf16[384,1536]{1,0:T(8,128)(2,1)}, u32[]{:S(2)}, u32[]{:S(2)}) collective-permute-start(bf16[384,1536]{1,0:T(8,128)(2,1)} %fusion.21), channel_id=1, source_target_pairs={{0,1},{1,0},{2,3},{3,2},{4,5},{5,4},{6,7},{7,6},{8,9},{9,8},{10,11... | collective-permute-start | bytes 3538952 | tf_op jit(solution)/shard_map/ppermute | solution.py:26
  255.7 26.9 %collective-permute-start.22 = (bf16[768,1024]{1,0:T(8,128)(2,1)}, bf16[768,1024]{1,0:T(8,128)(2,1)}, u32[]{:S(2)}, u32[]{:S(2)}) collective-permute-start(bf16[768,1024]{1,0:T(8,128)(2,1)} %collective-permute-done.21), channel_id=1, source_target_pairs={{2,6},{6,2},{8,12},{12,8},{3,7},{7,3},{9,13},{13,9},{18,22},{22,18... | collective-permute-start | bytes 4718600 | tf_op jit(solution)/shard_map/ppermute | solution.py:47
  271.5 41.5 %collective-permute-start.34 = (bf16[384,1536]{1,0:T(8,128)(2,1)}, bf16[384,1536]{1,0:T(8,128)(2,1)S(1)}, u32[]{:S(2)}, u32[]{:S(2)}) collective-permute-start(bf16[384,1536]{1,0:T(8,128)(2,1)} %pad_maximum_fusion.19), channel_id=1, source_target_pairs={{0,8},{8,0},{1,9},{9,1},{2,10},{10,2},{3,11},{11,3},{4,12},{12,4},... | collective-permute-start | bytes 3538952 | tf_op jit(solution)/shard_map/ppermute | solution.py:22
  271.5 22.7 %collective-permute-start.24 = (bf16[768,1024]{1,0:T(8,128)(2,1)}, bf16[768,1024]{1,0:T(8,128)(2,1)S(1)}, u32[]{:S(2)}, u32[]{:S(2)}) collective-permute-start(bf16[768,1024]{1,0:T(8,128)(2,1)} %copy-done.33), channel_id=1, source_target_pairs={{2,6},{6,2},{8,12},{12,8},{3,7},{7,3},{9,13},{13,9},{18,22},{22,18... | collective-permute-start | bytes 4718600 | tf_op jit(solution)/shard_map/ppermute | solution.py:47
  273.5 37.3 %collective-permute-start.26 = (bf16[1024,768]{1,0:T(8,128)(2,1)}, bf16[1024,768]{1,0:T(8,128)(2,1)S(1)}, u32[]{:S(2)}, u32[]{:S(2)}) collective-permute-start(bf16[1024,768]{1,0:T(8,128)(2,1)} %collective-permute-done.25), channel_id=1, source_target_pairs={{2,6},{6,2},{8,12},{12,8},{3,7},{7,3},{9,13},{13,9},{18,22},{22,18... | collective-permute-start | bytes 4718600 | tf_op jit(solution)/shard_map/ppermute | solution.py:47
  279.6 33.4 %collective-permute-start.36 = (bf16[384,1536]{1,0:T(8,128)(2,1)}, bf16[384,1536]{1,0:T(8,128)(2,1)S(1)}, u32[]{:S(2)}, u32[]{:S(2)}) collective-permute-start(bf16[384,1536]{1,0:T(8,128)(2,1)} %collective-permute-done.35), channel_id=1, source_target_pairs={{0,8},{8,0},{1,9},{9,1},{2,10},{10,2},{3,11},{11,3},{4,12},{12,4},... | collective-permute-start | bytes 3538952 | tf_op jit(solution)/shard_map/ppermute | solution.py:22
  282.6 29.9 %collective-permute-start.19 = (bf16[384,1536]{1,0:T(8,128)(2,1)S(1)}, bf16[384,1536]{1,0:T(8,128)(2,1)S(1)}, u32[]{:S(2)}, u32[]{:S(2)}) collective-permute-start(bf16[384,1536]{1,0:T(8,128)(2,1)S(1)} %multiply_convert_fusion.3), channel_id=1, source_target_pairs={{0,1},{1,0},{2,3},{3,2},{4,5},{5,4},{6,7},{7,6},{8,9},{9,8},{10,11... | collective-permute-start | bytes 3538952 | tf_op jit(solution)/shard_map/ppermute | solution.py:26
  312.5 10.8 %collective-permute-start.18 = (bf16[384,1536]{1,0:T(8,128)(2,1)S(1)}, bf16[384,1536]{1,0:T(8,128)(2,1)S(1)}, u32[]{:S(2)}, u32[]{:S(2)}) collective-permute-start(bf16[384,1536]{1,0:T(8,128)(2,1)S(1)} %multiply_convert_fusion.3), channel_id=1, source_target_pairs={{0,8},{8,0},{1,9},{9,1},{2,10},{10,2},{3,11},{11,3},{4,12},{12,4},... | collective-permute-start | bytes 3538952 | tf_op jit(solution)/shard_map/ppermute | solution.py:22
  312.6 10.7 %collective-permute-start.20 = (bf16[384,1536]{1,0:T(8,128)(2,1)S(1)}, bf16[384,1536]{1,0:T(8,128)(2,1)S(1)}, u32[]{:S(2)}, u32[]{:S(2)}) collective-permute-start(bf16[384,1536]{1,0:T(8,128)(2,1)S(1)} %collective-permute-done.19), channel_id=1, source_target_pairs={{0,8},{8,0},{1,9},{9,1},{2,10},{10,2},{3,11},{11,3},{4,12},{12,4},... | collective-permute-start | bytes 3538952 | tf_op jit(solution)/shard_map/ppermute | solution.py:22
  363.6 49.4 %collective-permute-start.65 = (bf16[1024,768]{1,0:T(8,128)(2,1)S(1)}, bf16[1024,768]{1,0:T(8,128)(2,1)S(1)}, u32[]{:S(2)}, u32[]{:S(2)}) collective-permute-start(bf16[1024,768]{1,0:T(8,128)(2,1)S(1)} %slice.356), channel_id=1, source_target_pairs={{0,4},{4,0},{1,5},{5,1},{2,6},{6,2},{3,7},{7,3},{8,12},{12,8},{9,1... | collective-permute-start | bytes 4718600 | tf_op jit(solution)/shard_map/ppermute | solution.py:22
  389.3 17.9 %collective-permute-start.37 = (bf16[384,1536]{1,0:T(8,128)(2,1)}, bf16[384,1536]{1,0:T(8,128)(2,1)}, u32[]{:S(2)}, u32[]{:S(2)}) collective-permute-start(bf16[384,1536]{1,0:T(8,128)(2,1)} %get-tuple-element.90), channel_id=1, source_target_pairs={{0,8},{8,0},{1,9},{9,1},{2,10},{10,2},{3,11},{11,3},{4,12},{12,4},... | collective-permute-start | bytes 3538952 | tf_op jit(solution)/shard_map/ppermute | solution.py:22
  392.4 17.2 %collective-permute-start.27 = (bf16[384,1536]{1,0:T(8,128)(2,1)}, bf16[384,1536]{1,0:T(8,128)(2,1)}, u32[]{:S(2)}, u32[]{:S(2)}) collective-permute-start(bf16[384,1536]{1,0:T(8,128)(2,1)} %get-tuple-element.92), channel_id=1, source_target_pairs={{0,8},{8,0},{1,9},{9,1},{2,10},{10,2},{3,11},{11,3},{4,12},{12,4},... | collective-permute-start | bytes 3538952 | tf_op jit(solution)/shard_map/ppermute | solution.py:22
  406.4 35.6 %collective-permute-start.57 = (bf16[768,1024]{1,0:T(8,128)(2,1)S(1)}, bf16[768,1024]{1,0:T(8,128)(2,1)S(1)}, u32[]{:S(2)}, u32[]{:S(2)}) collective-permute-start(bf16[768,1024]{1,0:T(8,128)(2,1)S(1)} %slice.358), channel_id=1, source_target_pairs={{0,4},{4,0},{1,5},{5,1},{2,6},{6,2},{3,7},{7,3},{8,12},{12,8},{9,1... | collective-permute-start | bytes 4718600 | tf_op jit(solution)/shard_map/ppermute | solution.py:22
  406.8 36.5 %collective-permute-start.39 = (bf16[384,1536]{1,0:T(8,128)(2,1)S(1)}, bf16[384,1536]{1,0:T(8,128)(2,1)S(1)}, u32[]{:S(2)}, u32[]{:S(2)}) collective-permute-start(bf16[384,1536]{1,0:T(8,128)(2,1)S(1)} %get-tuple-element.91), channel_id=1, source_target_pairs={{0,8},{8,0},{1,9},{9,1},{2,10},{10,2},{3,11},{11,3},{4,12},{12,4},... | collective-permute-start | bytes 3538952 | tf_op jit(solution)/shard_map/ppermute | solution.py:22
  407.2 45.3 %collective-permute-start.29 = (bf16[384,1536]{1,0:T(8,128)(2,1)S(1)}, bf16[384,1536]{1,0:T(8,128)(2,1)S(1)}, u32[]{:S(2)}, u32[]{:S(2)}) collective-permute-start(bf16[384,1536]{1,0:T(8,128)(2,1)S(1)} %get-tuple-element.93), channel_id=1, source_target_pairs={{0,8},{8,0},{1,9},{9,1},{2,10},{10,2},{3,11},{11,3},{4,12},{12,4},... | collective-permute-start | bytes 3538952 | tf_op jit(solution)/shard_map/ppermute | solution.py:22
  409.6 37.8 %collective-permute-start.38 = (bf16[384,1536]{1,0:T(8,128)(2,1)S(1)}, bf16[384,1536]{1,0:T(8,128)(2,1)S(1)}, u32[]{:S(2)}, u32[]{:S(2)}) collective-permute-start(bf16[384,1536]{1,0:T(8,128)(2,1)S(1)} %fusion.15), channel_id=1, source_target_pairs={{0,1},{1,0},{2,3},{3,2},{4,5},{5,4},{6,7},{7,6},{8,9},{9,8},{10,11... | collective-permute-start | bytes 3538952 | tf_op jit(solution)/shard_map/ppermute | solution.py:26
  413.0 62.1 %collective-permute-start.28 = (bf16[384,1536]{1,0:T(8,128)(2,1)}, bf16[384,1536]{1,0:T(8,128)(2,1)S(1)}, u32[]{:S(2)}, u32[]{:S(2)}) collective-permute-start(bf16[384,1536]{1,0:T(8,128)(2,1)} %fusion.19), channel_id=1, source_target_pairs={{0,1},{1,0},{2,3},{3,2},{4,5},{5,4},{6,7},{7,6},{8,9},{9,8},{10,11... | collective-permute-start | bytes 3538952 | tf_op jit(solution)/shard_map/ppermute | solution.py:26
  442.1 43.4 %collective-permute-start.61 = (bf16[768,1024]{1,0:T(8,128)(2,1)S(1)}, bf16[768,1024]{1,0:T(8,128)(2,1)S(1)}, u32[]{:S(2)}, u32[]{:S(2)}) collective-permute-start(bf16[768,1024]{1,0:T(8,128)(2,1)S(1)} %slice.357), channel_id=1, source_target_pairs={{0,4},{4,0},{1,5},{5,1},{2,6},{6,2},{3,7},{7,3},{8,12},{12,8},{9,1... | collective-permute-start | bytes 4718600 | tf_op jit(solution)/shard_map/ppermute | solution.py:22
  443.2 46.9 %collective-permute-start.66 = (bf16[1024,768]{1,0:T(8,128)(2,1)}, bf16[1024,768]{1,0:T(8,128)(2,1)}, u32[]{:S(2)}, u32[]{:S(2)}) collective-permute-start(bf16[1024,768]{1,0:T(8,128)(2,1)} %fusion.29), channel_id=1, source_target_pairs={{2,0},{8,10},{3,1},{9,11},{6,4},{12,14},{7,5},{13,15},{18,16},{24,... | collective-permute-start | bytes 4718600 | tf_op jit(solution)/shard_map/ppermute | solution.py:60
  447.4 130.2 %collective-permute-start.58 = (bf16[768,1024]{1,0:T(8,128)(2,1)S(1)}, bf16[768,1024]{1,0:T(8,128)(2,1)}, u32[]{:S(2)}, u32[]{:S(2)}) collective-permute-start(bf16[768,1024]{1,0:T(8,128)(2,1)S(1)} %fusion.27), channel_id=1, source_target_pairs={{2,0},{8,10},{3,1},{9,11},{6,4},{12,14},{7,5},{13,15},{18,16},{24,... | collective-permute-start | bytes 4718600 | tf_op jit(solution)/shard_map/ppermute | solution.py:60
  480.9 36.8 %collective-permute-start.31 = (bf16[384,768]{1,0:T(8,128)(2,1)S(1)}, bf16[384,768]{1,0:T(8,128)(2,1)}, u32[]{:S(2)}, u32[]{:S(2)}) collective-permute-start(bf16[384,768]{1,0:T(8,128)(2,1)S(1)} %get-tuple-element.111), channel_id=1, source_target_pairs={{8,4},{4,8},{9,5},{5,9},{10,6},{6,10},{11,7},{7,11},{24,20},{20,24... | collective-permute-start | bytes 1769480 | tf_op jit(solution)/shard_map/ppermute | solution.py:111
  486.1 96.9 %collective-permute-start.62 = (bf16[768,1024]{1,0:T(8,128)(2,1)S(1)}, bf16[768,1024]{1,0:T(8,128)(2,1)}, u32[]{:S(2)}, u32[]{:S(2)}) collective-permute-start(bf16[768,1024]{1,0:T(8,128)(2,1)S(1)} %fusion.28), channel_id=1, source_target_pairs={{2,0},{8,10},{3,1},{9,11},{6,4},{12,14},{7,5},{13,15},{18,16},{24,... | collective-permute-start | bytes 4718600 | tf_op jit(solution)/shard_map/ppermute | solution.py:60
  490.1 28.5 %collective-permute-start.30 = (bf16[384,768]{1,0:T(8,128)(2,1)S(1)}, bf16[384,768]{1,0:T(8,128)(2,1)S(1)}, u32[]{:S(2)}, u32[]{:S(2)}) collective-permute-start(bf16[384,768]{1,0:T(8,128)(2,1)S(1)} %get-tuple-element.112), channel_id=1, source_target_pairs={{8,0},{0,4},{12,8},{4,12},{9,1},{1,5},{13,9},{5,13},{10,2},{2,6},{... | collective-permute-start | bytes 1769480 | tf_op jit(solution)/shard_map/ppermute | solution.py:108
  490.1 87.0 %collective-permute-start.41 = (bf16[384,1536]{1,0:T(8,128)(2,1)S(1)}, bf16[384,1536]{1,0:T(8,128)(2,1)}, u32[]{:S(2)}, u32[]{:S(2)}) collective-permute-start(bf16[384,1536]{1,0:T(8,128)(2,1)S(1)} %copy-done.43), channel_id=1, source_target_pairs={{0,1},{1,0},{2,3},{3,2},{4,5},{5,4},{6,7},{7,6},{8,9},{9,8},{10,11... | collective-permute-start | bytes 3538952 | tf_op jit(solution)/shard_map/ppermute | solution.py:26
  517.8 70.7 %collective-permute-start.67 = (bf16[1024,768]{1,0:T(8,128)(2,1)S(1)}, bf16[1024,768]{1,0:T(8,128)(2,1)S(1)}, u32[]{:S(2)}, u32[]{:S(2)}) collective-permute-start(bf16[1024,768]{1,0:T(8,128)(2,1)S(1)} %add_convert_fusion.3), channel_id=1, source_target_pairs={{0,16},{10,26},{16,0},{26,10},{1,17},{11,27},{17,1},{27,11},{4,20}... | collective-permute-start | bytes 4718600 | tf_op jit(solution)/shard_map/ppermute | solution.py:69
  518.6 73.0 %collective-permute-start.40 = (bf16[384,1536]{1,0:T(8,128)(2,1)S(1)}, bf16[384,1536]{1,0:T(8,128)(2,1)S(1)}, u32[]{:S(2)}, u32[]{:S(2)}) collective-permute-start(bf16[384,1536]{1,0:T(8,128)(2,1)S(1)} %copy-done.43), channel_id=1, source_target_pairs={{0,8},{8,0},{1,9},{9,1},{2,10},{10,2},{3,11},{11,3},{4,12},{12,4},... | collective-permute-start | bytes 3538952 | tf_op jit(solution)/shard_map/ppermute | solution.py:22
  577.1 14.4 %collective-permute-start.42 = (bf16[384,1536]{1,0:T(8,128)(2,1)}, bf16[384,1536]{1,0:T(8,128)(2,1)S(1)}, u32[]{:S(2)}, u32[]{:S(2)}) collective-permute-start(bf16[384,1536]{1,0:T(8,128)(2,1)} %collective-permute-done.41), channel_id=1, source_target_pairs={{0,8},{8,0},{1,9},{9,1},{2,10},{10,2},{3,11},{11,3},{4,12},{12,4},... | collective-permute-start | bytes 3538952 | tf_op jit(solution)/shard_map/ppermute | solution.py:22
  581.1 133.9 %collective-permute-start.59 = (bf16[768,1024]{1,0:T(8,128)(2,1)}, bf16[768,1024]{1,0:T(8,128)(2,1)}, u32[]{:S(2)}, u32[]{:S(2)}) collective-permute-start(bf16[768,1024]{1,0:T(8,128)(2,1)} %add_convert_fusion.7), channel_id=1, source_target_pairs={{0,16},{10,26},{16,0},{26,10},{1,17},{11,27},{17,1},{27,11},{4,20}... | collective-permute-start | bytes 4718600 | tf_op jit(solution)/shard_map/ppermute | solution.py:69
  586.5 138.0 %collective-permute-start.63 = (bf16[768,1024]{1,0:T(8,128)(2,1)}, bf16[768,1024]{1,0:T(8,128)(2,1)}, u32[]{:S(2)}, u32[]{:S(2)}) collective-permute-start(bf16[768,1024]{1,0:T(8,128)(2,1)} %add_convert_fusion.5), channel_id=1, source_target_pairs={{0,16},{10,26},{16,0},{26,10},{1,17},{11,27},{17,1},{27,11},{4,20}... | collective-permute-start | bytes 4718600 | tf_op jit(solution)/shard_map/ppermute | solution.py:69
  590.1 190.2 %collective-permute-start.68 = (bf16[1024,768]{1,0:T(8,128)(2,1)}, bf16[1024,768]{1,0:T(8,128)(2,1)}, u32[]{:S(2)}, u32[]{:S(2)}) collective-permute-start(bf16[1024,768]{1,0:T(8,128)(2,1)} %add_convert_fusion.2), channel_id=1, source_target_pairs={{0,8},{10,2},{1,9},{11,3},{4,12},{14,6},{5,13},{15,7},{16,24},{26,... | collective-permute-start | bytes 4718600 | tf_op jit(solution)/shard_map/ppermute | solution.py:71
  596.9 113.7 %collective-permute-start.53 = (bf16[384,768]{1,0:T(8,128)(2,1)S(1)}, bf16[384,768]{1,0:T(8,128)(2,1)S(1)}, u32[]{:S(2)}, u32[]{:S(2)}) collective-permute-start(bf16[384,768]{1,0:T(8,128)(2,1)S(1)} %slice.359), channel_id=1, source_target_pairs={{0,4},{4,0},{1,5},{5,1},{2,6},{6,2},{3,7},{7,3},{8,12},{12,8},{9,1... | collective-permute-start | bytes 1769480 | tf_op jit(solution)/shard_map/ppermute | solution.py:22
  664.7 40.7 %collective-permute-start.49 = (bf16[768,1280]{0,1:T(8,128)(2,1)S(1)}, bf16[768,1280]{0,1:T(8,128)(2,1)S(1)}, u32[]{:S(2)}, u32[]{:S(2)}) collective-permute-start(bf16[768,1280]{0,1:T(8,128)(2,1)S(1)} %slice.355), channel_id=1, source_target_pairs={{0,4},{4,0},{1,5},{5,1},{2,6},{6,2},{3,7},{7,3},{8,12},{12,8},{9,1... | collective-permute-start | bytes 5898248 | tf_op jit(solution)/shard_map/ppermute | solution.py:22
  707.5 69.2 %collective-permute-start.50 = (bf16[768,1280]{0,1:T(8,128)(2,1)}, bf16[768,1280]{0,1:T(8,128)(2,1)}, u32[]{:S(2)}, u32[]{:S(2)}) collective-permute-start(bf16[768,1280]{0,1:T(8,128)(2,1)} %fusion.1), channel_id=1, source_target_pairs={{2,0},{8,10},{3,1},{9,11},{6,4},{12,14},{7,5},{13,15},{18,16},{24,... | collective-permute-start | bytes 5898248 | tf_op jit(solution)/shard_map/ppermute | solution.py:60
  710.6 29.5 %collective-permute-start.43 = (bf16[384,1536]{1,0:T(8,128)(2,1)}, bf16[384,1536]{1,0:T(8,128)(2,1)S(1)}, u32[]{:S(2)}, u32[]{:S(2)}) collective-permute-start(bf16[384,1536]{1,0:T(8,128)(2,1)} %get-tuple-element.88), channel_id=1, source_target_pairs={{0,8},{8,0},{1,9},{9,1},{2,10},{10,2},{3,11},{11,3},{4,12},{12,4},... | collective-permute-start | bytes 3538952 | tf_op jit(solution)/shard_map/ppermute | solution.py:22
  715.0 22.3 %collective-permute-start.54 = (bf16[384,768]{1,0:T(8,128)(2,1)S(1)}, bf16[384,768]{1,0:T(8,128)(2,1)S(1)}, u32[]{:S(2)}, u32[]{:S(2)}) collective-permute-start(bf16[384,768]{1,0:T(8,128)(2,1)S(1)} %fusion.35), channel_id=1, source_target_pairs={{2,0},{8,10},{3,1},{9,11},{6,4},{12,14},{7,5},{13,15},{18,16},{24,... | collective-permute-start | bytes 1769480 | tf_op jit(solution)/shard_map/ppermute | solution.py:60
  724.5 59.9 %collective-permute-start.60 = (bf16[768,1024]{1,0:T(8,128)(2,1)S(1)}, bf16[768,1024]{1,0:T(8,128)(2,1)}, u32[]{:S(2)}, u32[]{:S(2)}) collective-permute-start(bf16[768,1024]{1,0:T(8,128)(2,1)S(1)} %add_convert_fusion.6), channel_id=1, source_target_pairs={{0,8},{10,2},{1,9},{11,3},{4,12},{14,6},{5,13},{15,7},{16,24},{26,... | collective-permute-start | bytes 4718600 | tf_op jit(solution)/shard_map/ppermute | solution.py:71
  737.4 51.0 %collective-permute-start.64 = (bf16[768,1024]{1,0:T(8,128)(2,1)S(1)}, bf16[768,1024]{1,0:T(8,128)(2,1)}, u32[]{:S(2)}, u32[]{:S(2)}) collective-permute-start(bf16[768,1024]{1,0:T(8,128)(2,1)S(1)} %add_convert_fusion.4), channel_id=1, source_target_pairs={{0,8},{10,2},{1,9},{11,3},{4,12},{14,6},{5,13},{15,7},{16,24},{26,... | collective-permute-start | bytes 4718600 | tf_op jit(solution)/shard_map/ppermute | solution.py:71
  740.2 53.1 %collective-permute-start.45 = (bf16[384,1536]{1,0:T(8,128)(2,1)}, bf16[384,1536]{1,0:T(8,128)(2,1)S(1)}, u32[]{:S(2)}, u32[]{:S(2)}) collective-permute-start(bf16[384,1536]{1,0:T(8,128)(2,1)} %get-tuple-element.89), channel_id=1, source_target_pairs={{0,8},{8,0},{1,9},{9,1},{2,10},{10,2},{3,11},{11,3},{4,12},{12,4},... | collective-permute-start | bytes 3538952 | tf_op jit(solution)/shard_map/ppermute | solution.py:22
  776.7 27.6 %collective-permute-start.44 = (bf16[384,1536]{1,0:T(8,128)(2,1)S(1)}, bf16[384,1536]{1,0:T(8,128)(2,1)S(1)}, u32[]{:S(2)}, u32[]{:S(2)}) collective-permute-start(bf16[384,1536]{1,0:T(8,128)(2,1)S(1)} %fusion.13), channel_id=1, source_target_pairs={{0,1},{1,0},{2,3},{3,2},{4,5},{5,4},{6,7},{7,6},{8,9},{9,8},{10,11... | collective-permute-start | bytes 3538952 | tf_op jit(solution)/shard_map/ppermute | solution.py:26
  780.3 25.1 %collective-permute-start.51 = (bf16[768,1280]{0,1:T(8,128)(2,1)S(1)}, bf16[768,1280]{0,1:T(8,128)(2,1)S(1)}, u32[]{:S(2)}, u32[]{:S(2)}) collective-permute-start(bf16[768,1280]{0,1:T(8,128)(2,1)S(1)} %add_convert_fusion.1), channel_id=1, source_target_pairs={{0,16},{10,26},{16,0},{26,10},{1,17},{11,27},{17,1},{27,11},{4,20}... | collective-permute-start | bytes 5898248 | tf_op jit(solution)/shard_map/ppermute | solution.py:69
  792.0 32.9 %collective-permute-start.56 = (bf16[384,768]{1,0:T(8,128)(2,1)S(1)}, bf16[384,768]{1,0:T(8,128)(2,1)S(1)}, u32[]{:S(2)}, u32[]{:S(2)}) collective-permute-start(bf16[384,768]{1,0:T(8,128)(2,1)S(1)} %add_convert_fusion.8), channel_id=1, source_target_pairs={{0,8},{10,2},{1,9},{11,3},{4,12},{14,6},{5,13},{15,7},{16,24},{26,... | collective-permute-start | bytes 1769480 | tf_op jit(solution)/shard_map/ppermute | solution.py:71
  805.3 20.7 %collective-permute-start.48 = (f32[1560]{0:T(1024)S(1)}, f32[1560]{0:T(1024)S(1)}, u32[]{:S(2)}, u32[]{:S(2)}) collective-permute-start(f32[1560]{0:T(1024)S(1)} %pad_maximum_fusion.29), channel_id=1, source_target_pairs={{0,4},{4,0},{1,5},{5,1},{2,6},{6,2},{3,7},{7,3},{8,12},{12,8},{9,1... | collective-permute-start | bytes 18728 | tf_op jit(solution)/shard_map/ppermute | solution.py:22
  807.2 49.2 %collective-permute-start.52 = (bf16[768,1280]{0,1:T(8,128)(2,1)}, bf16[768,1280]{0,1:T(8,128)(2,1)}, u32[]{:S(2)}, u32[]{:S(2)}) collective-permute-start(bf16[768,1280]{0,1:T(8,128)(2,1)} %add_convert_fusion), channel_id=1, source_target_pairs={{0,8},{10,2},{1,9},{11,3},{4,12},{14,6},{5,13},{15,7},{16,24},{26,... | collective-permute-start | bytes 5898248 | tf_op jit(solution)/shard_map/ppermute | solution.py:71
  809.6 45.6 %collective-permute-start.47 = (bf16[384,768]{1,0:T(8,128)(2,1)S(1)}, bf16[384,768]{1,0:T(8,128)(2,1)S(1)}, u32[]{:S(2)}, u32[]{:S(2)}) collective-permute-start(bf16[384,768]{1,0:T(8,128)(2,1)S(1)} %get-tuple-element.109), channel_id=1, source_target_pairs={{8,4},{4,8},{9,5},{5,9},{10,6},{6,10},{11,7},{7,11},{24,20},{20,24... | collective-permute-start | bytes 1769480 | tf_op jit(solution)/shard_map/ppermute | solution.py:111
  824.8 30.4 %collective-permute-start.46 = (bf16[384,768]{1,0:T(8,128)(2,1)S(1)}, bf16[384,768]{1,0:T(8,128)(2,1)S(1)}, u32[]{:S(2)}, u32[]{:S(2)}) collective-permute-start(bf16[384,768]{1,0:T(8,128)(2,1)S(1)} %get-tuple-element.110), channel_id=1, source_target_pairs={{8,0},{0,4},{12,8},{4,12},{9,1},{1,5},{13,9},{5,13},{10,2},{2,6},{... | collective-permute-start | bytes 1769480 | tf_op jit(solution)/shard_map/ppermute | solution.py:108
  (84 other events, 1763.5 us)

commit v3 on v2

--- a/solution.py
+++ b/solution.py
@@ -47,29 +47,48 @@
     return lax.ppermute(value, ("k", "x", "h"), pairs)
 
 
-def gather_weight(shard, home, axis):
-    first = fetch_home_away(shard)
-    second = fetch_away(first)
+def tie(value, *others):
+    return lax.optimization_barrier((value,) + others)[0]
+
+
+def join_weight(shard, first, second, home, axis):
     mine = jnp.where(home, shard, first)
     other = jnp.where(home, first, second)
     return jnp.concatenate([mine, other], axis=axis)
 
 
-def reduce_weight(own, other, home, home_steps):
-    total = own + swap(other.astype(BF16), "x").astype(F32)
-    moved = lax.ppermute(
-        total.astype(BF16), ("k", "h"), [(0 * 2 + 1, 0 * 2 + 0), (1 * 2 + 0, 1 * 2 + 1)]
-    )
-    total = (total + moved.astype(F32)).astype(BF16)
-    for size, bit in home_steps:
-        pairs = []
-        for o in range(size):
-            for k in range(2):
-                pairs.append(((o * 2 + k) * 2 + k, ((o ^ bit) * 2 + k) * 2 + k))
-        moved = lax.ppermute(total, ("o", "k", "h"), pairs)
-        total = (total.astype(F32) + moved.astype(F32)).astype(BF16)
-    moved = lax.ppermute(total, ("k", "h"), [(0, 2), (3, 1)])
-    return jnp.where(home, total, moved).astype(F32)
+def add_parts(kept, moved):
+    return (kept.astype(F32) + moved.astype(F32)).astype(BF16)
+
+
+def to_home(value):
+    return lax.ppermute(value, ("k", "h"), [(1, 0), (2, 3)])
+
+
+def from_home(value):
+    return lax.ppermute(value, ("k", "h"), [(0, 2), (3, 1)])
+
+
+def home_swap(value, size, bit):
+    pairs = []
+    for o in range(size):
+        for k in range(2):
+            pairs.append(((o * 2 + k) * 2 + k, ((o ^ bit) * 2 + k) * 2 + k))
+    return lax.ppermute(value, ("o", "k", "h"), pairs)
+
+
+def bits_of(size):
+    return [1 << i for i in range(size.bit_length() - 1)]
+
+
+def split_rows(value, high):
+    half = value.shape[0] // 2
+    low_rows, high_rows = value[:half], value[half:]
+    return jnp.where(high, high_rows, low_rows), jnp.where(high, low_rows, high_rows)
+
+
+def merge_rows(kept, moved, high):
+    return jnp.concatenate([jnp.where(high, moved, kept), jnp.where(high, kept, moved)], axis=0)
 
 
 def take_half(value, index):
@@ -102,38 +121,24 @@
     return jnp.concatenate([own, other], axis=1)
 
 
-def unspread_tokens(rows, core, same):
+def unspread_parts(rows, same):
     half = rows.shape[1] // 2
     own, other = rows[:, :half], rows[:, half:]
-    first = lax.ppermute(
-        jnp.where(same, other, own), ("k", "x"), [(b, a) for a, b in SPREAD_A]
-    )
-    second = lax.ppermute(other, ("k", "x"), [(b, a) for a, b in SPREAD_B])
+    return own, jnp.where(same, other, own), other
+
+
+def unspread_moves(near, far):
+    first = lax.ppermute(near, ("k", "x"), [(b, a) for a, b in SPREAD_A])
+    second = lax.ppermute(far, ("k", "x"), [(b, a) for a, b in SPREAD_B])
+    return first, second
+
+
+def unspread_join(own, first, second, core, same):
     near = jnp.where(same, own, first)
     far = jnp.where(same, first, second)
     low = jnp.where(core == 0, near, far)
     high = jnp.where(core == 0, far, near)
     return jnp.concatenate([low, high], axis=0)
-
-
-def gather_blocks(block, psize):
-    blocks = []
-    for bit in range(psize):
-        moved = block if bit == 0 else xor_swap(block, "p", psize, bit)
-        blocks += [moved, swap(moved, "k")]
-    return jnp.concatenate(blocks, axis=0)
-
-
-def sum_blocks(partial, psize):
-    size = partial.shape[0] // (2 * psize)
-    parts = [partial[i * size : (i + 1) * size] for i in range(2 * psize)]
-    total = None
-    for bit in reversed(range(psize)):
-        pair = parts[2 * bit] + swap(parts[2 * bit + 1].astype(BF16), "k").astype(F32)
-        if bit:
-            pair = xor_swap(pair.astype(BF16), "p", psize, bit).astype(F32)
-        total = pair if total is None else total + pair
-    return total
 
 
 def contract_rows(left, right):
@@ -526,13 +531,1034 @@
     return kcol, qrow, flags
 
 
+class Wires:
+    def __init__(self, send_sem, recv_sem, local_sem):
+        self.send_sem, self.recv_sem, self.local_sem = send_sem, recv_sem, local_sem
+        self.used, self.local_used = 0, 0
+        self.k, self.x = lax.axis_index("k"), lax.axis_index("x")
+        self.h, self.p, self.o = lax.axis_index("h"), lax.axis_index("p"), lax.axis_index("o")
+        self.home = self.k == self.h
+        self.same = self.k == self.x
+        self.pending = []
+
+    def slot(self):
+        self.used += 1
+        return self.used - 1
+
+    def copy(self, source, target, device, slot):
+        return pltpu.make_async_remote_copy(
+            src_ref=source,
+            dst_ref=target,
+            send_sem=self.send_sem.at[slot],
+            recv_sem=self.recv_sem.at[slot],
+            device_id=device,
+            device_id_type=pl.DeviceIdType.MESH,
+        )
+
+    def send(self, source, target, device):
+        copy = self.copy(source, target, device, self.slot())
+        copy.start()
+        self.pending.append(copy.wait_send)
+        return copy
+
+    def local(self, source, target):
+        copy = pltpu.make_async_copy(source, target, self.local_sem.at[self.local_used])
+        self.local_used += 1
+        copy.start()
+        return copy
+
+    def greet(self, devices):
+        barrier = pltpu.get_barrier_semaphore()
+        for device in devices:
+            pl.semaphore_signal(
+                barrier, inc=1, device_id=device, device_id_type=pl.DeviceIdType.MESH
+            )
+        pl.semaphore_wait(barrier, len(devices))
+
+    def close(self):
+        for wait in self.pending:
+            wait()
+
+
+def row_spans(total, pieces):
+    size = total // pieces
+    return [pl.ds(i * size, size) for i in range(pieces)]
+
+
+class Fetch:
+    def __init__(self, wires, shard, target, stage, pieces, got=None, keep=None):
+        w = self.wires = wires
+        self.shard, self.target, self.stage, self.got, self.keep = shard, target, stage, got, keep
+        self.count = pieces
+        self.half_rows = shard.shape[0] // 2
+        self.size = self.half_rows // pieces
+        self.by_columns = len(target.shape) == 2
+        self.first = [w.slot() for _ in range(pieces)]
+        self.over = [w.slot() for _ in range(pieces)]
+        self.second = [w.slot() for _ in range(2 * pieces)]
+        self.local_slot = w.local_used
+        w.local_used += 2
+
+    def rows(self, i, mine=True):
+        bit = self.wires.o % 2
+        bit = bit if mine else 1 - bit
+        return pl.ds(pl.multiple_of(bit * self.half_rows + i * self.size, 16), self.size)
+
+    def place(self, half, span):
+        if self.by_columns:
+            width = self.shard.shape[1]
+            return self.target.at[span, pl.ds(half * width, width)]
+        return self.target.at[half, span]
+
+    def first_copy(self, i, home):
+        w, span = self.wires, self.rows(i)
+        if home:
+            return w.copy(self.shard.at[span], self.place(1, span), {"x": 1 - w.x}, self.first[i])
+        device = {"k": 1 - w.k, "h": 1 - w.h}
+        return w.copy(self.shard.at[span], self.place(0, span), device, self.first[i])
+
+    def have(self, i, half):
+        if self.got is None:
+            return self.place(half, self.rows(i))
+        return self.got.at[pl.ds(i * self.size, self.size)]
+
+    def over_copy(self, i, home):
+        w, half = self.wires, 1 if home else 0
+        return w.copy(self.have(i, half), self.place(half, self.rows(i)), {"o": w.o ^ 1}, self.over[i])
+
+    def second_copy(self, i, mine):
+        w, span = self.wires, self.rows(i, mine)
+        source = self.have(i, 0) if mine else self.place(0, span)
+        slot = self.second[i if mine else self.count + i]
+        return w.copy(source, self.place(1, span), {"x": 1 - w.x}, slot)
+
+    def shard_load(self):
+        return pltpu.make_async_copy(self.shard, self.stage, self.wires.local_sem.at[self.local_slot])
+
+    def shard_store(self):
+        whole = pl.ds(0, self.shard.shape[0])
+        return pltpu.make_async_copy(
+            self.stage, self.place(0, whole), self.wires.local_sem.at[self.local_slot]
+        )
+
+    def got_load(self):
+        return pltpu.make_async_copy(self.got, self.keep, self.wires.local_sem.at[self.local_slot + 1])
+
+    def got_store(self, half):
+        bit = self.wires.o % 2
+        span = pl.ds(pl.multiple_of(bit * self.half_rows, 16), self.half_rows)
+        return pltpu.make_async_copy(
+            self.keep, self.place(half, span), self.wires.local_sem.at[self.local_slot + 1]
+        )
+
+    def either(self, at_home, away):
+        pl.when(self.wires.home)(at_home)
+        pl.when(jnp.logical_not(self.wires.home))(away)
+
+    def load(self):
+        pl.when(self.wires.home)(lambda: self.shard_load().start())
+        if self.got is not None:
+            self.got_load().start()
+
+    def start(self):
+        if self.got is not None:
+            for i in range(self.count):
+                self.relay(i)
+            return
+
+        def go(home):
+            for i in range(self.count):
+                self.first_copy(i, home).start()
+
+        self.either(lambda: go(True), lambda: go(False))
+
+    def store(self):
+        def at_home():
+            self.shard_load().wait()
+            self.shard_store().start()
+            if self.got is not None:
+                self.got_load().wait()
+                self.got_store(1).start()
+
+        def away():
+            if self.got is not None:
+                self.got_load().wait()
+                self.got_store(0).start()
+
+        self.either(at_home, away)
+
+    def relay(self, i):
+        def at_home():
+            if self.got is None:
+                self.first_copy(i, True).wait_recv()
+            self.over_copy(i, True).start()
+
+        def away():
+            if self.got is None:
+                self.first_copy(i, False).wait_recv()
+            self.over_copy(i, False).start()
+            self.second_copy(i, True).start()
+
+        self.either(at_home, away)
+
+    def relay_over(self, i):
+        def away():
+            self.over_copy(i, False).wait_recv()
+            self.second_copy(i, False).start()
+
+        pl.when(jnp.logical_not(self.wires.home))(away)
+
+    def wait(self):
+        def at_home():
+            for i in range(self.count):
+                if self.got is None:
+                    self.first_copy(i, True).wait_send()
+                self.over_copy(i, True).wait()
+            self.shard_store().wait()
+            if self.got is not None:
+                self.got_store(1).wait()
+
+        def away():
+            for i in range(self.count):
+                if self.got is None:
+                    self.first_copy(i, False).wait_send()
+                self.over_copy(i, False).wait_send()
+                self.second_copy(i, True).wait()
+                self.second_copy(i, False).wait()
+            if self.got is not None:
+                self.got_store(0).wait()
+
+        self.either(at_home, away)
+
+
+def partners(wires, psize, away=False, peers=True, over_o=0):
+    devices = [{"k": 1 - wires.k}]
+    if peers:
+        devices += [{"p": wires.p ^ bit} for bit in range(1, psize)]
+    devices += [{"x": 1 - wires.x}]
+    devices += [{"k": 1 - wires.k, "x": 1 - wires.x}]
+    if away:
+        devices += [{"k": 1 - wires.k, "h": 1 - wires.h}, {"h": 1 - wires.h}]
+    bit = 1
+    while bit < over_o:
+        devices += [{"o": wires.o ^ bit}]
+        bit *= 2
+    return devices
+
+
+class Share:
+    def __init__(self, wires, psize, own, g, spans):
+        self.wires, self.psize, self.own, self.g, self.spans = wires, psize, own, g, spans
+        self.near, self.far, self.kept, self.passed = [], {}, [], []
+
+    def send(self, i):
+        w, span = self.wires, self.spans[i]
+        for bit in range(1, self.psize):
+            self.far[bit, i] = w.send(self.own.at[span], self.g.at[2 * bit, span], {"p": w.p ^ bit})
+        self.near.append(w.send(self.own.at[span], self.g.at[1, span], {"k": 1 - w.k}))
+        self.kept.append(w.local(self.own.at[span], self.g.at[0, span]))
+
+    def relay(self, i):
+        w, span = self.wires, self.spans[i]
+        for bit in range(1, self.psize):
+            self.far[bit, i].wait_recv()
+            self.passed.append(
+                w.send(self.g.at[2 * bit, span], self.g.at[2 * bit + 1, span], {"k": 1 - w.k})
+            )
+
+    def wait(self):
+        for copy in self.near + self.passed:
+            copy.wait_recv()
+        for copy in self.kept:
+            copy.wait()
+
+
+class Reduce:
+    def __init__(self, wires, psize, part, near, mid, far, spans):
+        self.wires, self.psize, self.part = wires, psize, part
+        self.near, self.mid, self.far, self.spans = near, mid, far, spans
+        self.near_copies, self.far_copies = {}, {}
+
+    def start(self):
+        w = self.wires
+        for bit in reversed(range(self.psize)):
+            for i, span in enumerate(self.spans):
+                self.near_copies[bit, i] = w.send(
+                    self.part.at[2 * bit + 1, span], self.near.at[bit, span], {"k": 1 - w.k}
+                )
+        for bit in reversed(range(1, self.psize)):
+            for i, span in enumerate(self.spans):
+                self.near_copies[bit, i].wait_recv()
+                self.mid[bit - 1, span] = (
+                    self.part[2 * bit, span].astype(F32) + self.near[bit, span].astype(F32)
+                ).astype(BF16)
+                self.far_copies[bit, i] = w.send(
+                    self.mid.at[bit - 1, span], self.far.at[bit - 1, span], {"p": w.p ^ bit}
+                )
+
+    def rows(self, i):
+        span = self.spans[i]
+        self.near_copies[0, i].wait_recv()
+        total = self.part[0, span].astype(F32) + self.near[0, span].astype(F32)
+        for bit in range(1, self.psize):
+            self.far_copies[bit, i].wait_recv()
+            total = total + self.far[bit - 1, span].astype(F32)
+        return total
+
+
+PIECES = 3
+
+
+def inverse_rms(value):
+    return lax.rsqrt(jnp.sum(value * value, axis=1, keepdims=True) / D + EPS)
+
+
+def norm_back(grad, value, base, gain):
+    rms = inverse_rms(value)
+    gained = gain * grad
+    inner = jnp.sum(value * gained, axis=1, keepdims=True)
+    result = base + rms * gained - value * (rms * rms * rms) * inner / D
+    return result, jnp.sum(grad * value * rms, axis=0, keepdims=True)
+
+
+def enter_kernel(
+    psize, x_ref, gain_ref, qkv_shard, forget_shard, out_shard, xin, g, proj, out,
+    own, qkv_stage, forget_stage, out_stage, send_sem, recv_sem, local_sem,
+):
+    w = Wires(send_sem, recv_sem, local_sem)
+    width = qkv_shard.shape[1]
+    qkv = Fetch(w, qkv_shard, proj.at[:, :, pl.ds(0, width)], qkv_stage, 3)
+    forget = Fetch(
+        w, forget_shard, proj.at[:, :, pl.ds(width, forget_shard.shape[1])], forget_stage, 1
+    )
+    out_fetch = Fetch(w, out_shard, out, out_stage, 1)
+    for fetch in (qkv, forget, out_fetch):
+        fetch.load()
+    w.greet(partners(w, psize, away=True, over_o=2))
+    rows, half = own.shape[0], x_ref.shape[1]
+    spans = row_spans(rows, PIECES)
+    size = rows // PIECES
+    def spread(source, target, pieces):
+        count = len(pieces)
+        to_near = [w.slot() for _ in pieces]
+        to_far = [w.slot() for _ in pieces]
+        kept = [w.local_used + i for i in range(count)]
+        w.local_used += count
+
+        def piece(base, i):
+            start, length = pieces[i]
+            return source.at[pl.ds(pl.multiple_of(base * rows + start, 8), length)]
+
+        def span(i):
+            return pl.ds(pieces[i][0], pieces[i][1])
+
+        left, right = pl.ds(0, half), pl.ds(half, half)
+
+        def same_keep(i):
+            return pltpu.make_async_copy(piece(w.k, i), target.at[span(i), left], local_sem.at[kept[i]])
+
+        def same_send(i):
+            return w.copy(piece(1 - w.k, i), target.at[span(i), left], {"k": 1 - w.k}, to_near[i])
+
+        def cross_near(i):
+            return w.copy(piece(w.k, i), target.at[span(i), right], {"x": 1 - w.x}, to_near[i])
+
+        def cross_far(i):
+            return w.copy(
+                piece(1 - w.k, i), target.at[span(i), right], {"k": 1 - w.k, "x": 1 - w.x}, to_far[i]
+            )
+
+        def start():
+            @pl.when(w.same)
+            def _():
+                for i in range(count):
+                    same_send(i).start()
+                    same_keep(i).start()
+
+            @pl.when(jnp.logical_not(w.same))
+            def _():
+                for i in range(count):
+                    cross_near(i).start()
+                    cross_far(i).start()
+
+        def arrive(i):
+            @pl.when(w.same)
+            def _():
+                same_keep(i).wait()
+                same_send(i).wait_recv()
+
+            @pl.when(jnp.logical_not(w.same))
+            def _():
+                cross_near(i).wait_recv()
+                cross_far(i).wait_recv()
+
+        def close():
+            @pl.when(w.same)
+            def _():
+                for i in range(count):
+                    same_send(i).wait_send()
+
+            @pl.when(jnp.logical_not(w.same))
+            def _():
+                for i in range(count):
+                    cross_near(i).wait_send()
+                    cross_far(i).wait_send()
+
+        return start, arrive, close
+
+    start, arrive, close = spread(x_ref, xin, [(i * size, size) for i in range(PIECES)])
+    start()
+    qkv.start()
+    forget.start()
+    share = Share(w, psize, own, g, spans)
+    gain = gain_ref[0:1, :]
+    for i, span in enumerate(spans):
+        arrive(i)
+        value = xin[span, :].astype(F32)
+        own[span, :] = (value * inverse_rms(value) * gain).astype(BF16)
+        share.send(i)
+    close()
+    for fetch in (qkv, forget, out_fetch):
+        fetch.store()
+    for i in range(3):
+        qkv.relay(i)
+    out_fetch.start()
+    forget.relay(0)
+    for i in range(3):
+        qkv.relay_over(i)
+        if i < PIECES:
+            share.relay(i)
+    forget.relay_over(0)
+    out_fetch.relay(0)
+    out_fetch.relay_over(0)
+    share.wait()
+    for fetch in (qkv, forget, out_fetch):
+        fetch.wait()
+    w.close()
+
+
+def forward_exchange_kernel(
+    psize, part, xin, gain_ref, gate_shard, gate_got, up_shard, up_got, down_shard, resid, g, gate, up, down,
+    near, mid, far, own, gate_stage, gate_keep, up_stage, up_keep, down_stage, send_sem, recv_sem, local_sem,
+):
+    w = Wires(send_sem, recv_sem, local_sem)
+    gate_fetch = Fetch(w, gate_shard, gate, gate_stage, 2, gate_got, gate_keep)
+    up_fetch = Fetch(w, up_shard, up, up_stage, 2, up_got, up_keep)
+    down_fetch = Fetch(w, down_shard, down, down_stage, 2)
+    fetches = (gate_fetch, up_fetch, down_fetch)
+    for fetch in fetches:
+        fetch.load()
+    w.greet(partners(w, psize, away=True, over_o=2))
+    spans = row_spans(own.shape[0], PIECES)
+    reduce = Reduce(w, psize, part, near, mid, far, spans)
+    gate_fetch.start()
+    reduce.start()
+    up_fetch.start()
+    down_fetch.start()
+    for fetch in fetches:
+        fetch.store()
+    gate_fetch.relay_over(0)
+    gate_fetch.relay_over(1)
+    share = Share(w, psize, own, g, spans)
+    gain = gain_ref[1:2, :]
+    for i, span in enumerate(spans):
+        value = reduce.rows(i) + xin[span, :].astype(F32)
+        resid[span, :] = value
+        own[span, :] = (value * inverse_rms(value) * gain).astype(BF16)
+        share.send(i)
+    for i in range(2):
+        up_fetch.relay_over(i)
+        down_fetch.relay(i)
+    for i in range(PIECES):
+        share.relay(i)
+    for i in range(2):
+        down_fetch.relay_over(i)
+    share.wait()
+    for fetch in fetches:
+        fetch.wait()
+    w.close()
+
+
+class EarlySum:
+    def __init__(self, wires, part, value, over, across, result, pieces):
+        w = self.wires = wires
+        self.part, self.value, self.over, self.across, self.result = part, value, over, across, result
+        self.count, self.half_rows = pieces, value.shape[1]
+        self.size = self.half_rows // pieces
+        self.over_slots = [[w.slot() for _ in range(pieces)] for _ in range(2)]
+        self.across_slots = [w.slot() for _ in range(pieces)]
+        self.local_slot = w.local_used
+        w.local_used += 2 + pieces
+
+    def span(self, i):
+        return pl.ds(i * self.size, self.size)
+
+    def load_copy(self, half):
+        start = pl.multiple_of((self.wires.o % 2) * self.half_rows, 16)
+        return pltpu.make_async_copy(
+            self.part.at[half, pl.ds(start, self.half_rows)],
+            self.value.at[half],
+            self.wires.local_sem.at[self.local_slot + half],
+        )
+
+    def load(self):
+        for half in range(2):
+            self.load_copy(half).start()
+
+    def over_copy(self, half, i):
+        w = self.wires
+        start = pl.multiple_of((1 - w.o % 2) * self.half_rows + i * self.size, 16)
+        return w.copy(
+            self.part.at[half, pl.ds(start, self.size)],
+            self.over.at[half, self.span(i)],
+            {"o": w.o ^ 1},
+            self.over_slots[half][i],
+        )
+
+    def across_copy(self, i):
+        w = self.wires
+        return w.copy(
+            self.value.at[1, self.span(i)], self.across.at[self.span(i)], {"x": 1 - w.x}, self.across_slots[i]
+        )
+
+    def keep_copy(self, i):
+        return pltpu.make_async_copy(
+            self.value.at[0, self.span(i)],
+            self.result.at[self.span(i)],
+            self.wires.local_sem.at[self.local_slot + 2 + i],
+        )
+
+    def start(self, half):
+        for i in range(self.count):
+            self.over_copy(half, i).start()
+
+    def pass_on(self, i):
+        if i == 0:
+            self.load_copy(1).wait()
+        self.over_copy(1, i).wait_recv()
+        span = self.span(i)
+        self.value[1, span] = (
+            self.value[1, span].astype(F32) + self.over[1, span].astype(F32)
+        ).astype(BF16)
+        self.across_copy(i).start()
+
+    def finish(self, i):
+        if i == 0:
+            self.load_copy(0).wait()
+        self.over_copy(0, i).wait_recv()
+        self.across_copy(i).wait_recv()
+        span = self.span(i)
+        total = self.value[0, span].astype(F32) + self.over[0, span].astype(F32)
+        self.value[0, span] = (total + self.across[span].astype(F32)).astype(BF16)
+        self.keep_copy(i).start()
+
+    def close(self):
+        for i in range(self.count):
+            for half in range(2):
+                self.over_copy(half, i).wait_send()
+            self.across_copy(i).wait_send()
+            self.keep_copy(i).wait()
+
+
+def backward_exchange_kernel(
+    psize, part, resid, cot, gain_ref, down_own, down_other, gate_part, up_part,
+    grad_resid, g, gain_grad, down_sum, gate_sum, up_sum,
+    near, mid, far, own, down_across, gate_val, gate_over, gate_across, up_val, up_over, up_across,
+    send_sem, recv_sem, local_sem,
+):
+    w = Wires(send_sem, recv_sem, local_sem)
+    gate = EarlySum(w, gate_part, gate_val, gate_over, gate_across, gate_sum, 2)
+    up = EarlySum(w, up_part, up_val, up_over, up_across, up_sum, 2)
+    gate.load()
+    up.load()
+    w.greet(partners(w, psize, over_o=2))
+    spans = row_spans(own.shape[0], PIECES)
+    reduce = Reduce(w, psize, part, near, mid, far, spans)
+    down_copy = w.send(down_other, down_across, {"x": 1 - w.x})
+    gate.start(1)
+    up.start(1)
+    reduce.start()
+    gate.start(0)
+    up.start(0)
+    for i in range(2):
+        gate.pass_on(i)
+    share = Share(w, psize, own, g, spans)
+    gain = gain_ref[1:2, :]
+    gain_sum = jnp.zeros((1, D), F32)
+    for i, span in enumerate(spans):
+        grad, gain_part = norm_back(reduce.rows(i), resid[span, :], cot[span, :].astype(F32), gain)
+        grad_resid[span, :] = grad
+        own[span, :] = grad.astype(BF16)
+        gain_sum = gain_sum + gain_part
+        share.send(i)
+    gain_grad[...] = jnp.broadcast_to(gain_sum, gain_grad.shape)
+    for i in range(2):
+        up.pass_on(i)
+    down_copy.wait_recv()
+    down_sum[...] = (down_own[...].astype(F32) + down_across[...].astype(F32)).astype(BF16)
+    share.relay(0)
+    for i in range(2):
+        gate.finish(i)
+    for i in range(1, PIECES):
+        share.relay(i)
+    for i in range(2):
+        up.finish(i)
+    share.wait()
+    gate.close()
+    up.close()
+    w.close()
+
+
+class Spread:
+    def __init__(self, wires, value, result):
+        w = self.wires = wires
+        self.value, self.result = value, result
+        self.over_slot, self.near_slot, self.pass_slot = w.slot(), w.slot(), w.slot()
+        self.local_slot = w.local_used
+        w.local_used += 1
+
+    def rows(self, mine):
+        bit = self.wires.o % 2
+        return self.result.at[bit if mine else 1 - bit]
+
+    def over_copy(self):
+        w = self.wires
+        return w.copy(self.value, self.rows(True), {"o": w.o ^ 1}, self.over_slot)
+
+    def near_copy(self):
+        return self.wires.copy(self.value, self.rows(True), {"k": 1 - self.wires.k}, self.near_slot)
+
+    def pass_copy(self):
+        return self.wires.copy(self.rows(False), self.rows(False), {"k": 1 - self.wires.k}, self.pass_slot)
+
+    def keep_copy(self):
+        return pltpu.make_async_copy(
+            self.value, self.rows(True), self.wires.local_sem.at[self.local_slot]
+        )
+
+    def start(self):
+        @pl.when(self.wires.home)
+        def _():
+            self.over_copy().start()
+            self.near_copy().start()
+            self.keep_copy().start()
+
+    def relay(self):
+        @pl.when(self.wires.home)
+        def _():
+            self.over_copy().wait_recv()
+            self.pass_copy().start()
+
+    def wait(self):
+        @pl.when(self.wires.home)
+        def _():
+            self.over_copy().wait_send()
+            self.near_copy().wait_send()
+            self.pass_copy().wait_send()
+            self.keep_copy().wait()
+
+        @pl.when(jnp.logical_not(self.wires.home))
+        def _():
+            self.near_copy().wait_recv()
+            self.pass_copy().wait_recv()
+
+
+class SmallSum:
+    def __init__(self, wires, psize, osize, value, other, buffers):
+        w = self.wires = wires
+        self.value, self.other, self.buffers = value, other, buffers
+        self.devices = [{"x": 1 - w.x}, {"k": 1 - w.k}]
+        self.devices += [{"p": w.p ^ bit} for bit in bits_of(psize)]
+        self.devices += [{"h": 1 - w.h}]
+        self.devices += [{"o": w.o ^ bit} for bit in bits_of(osize)]
+        self.slots = [w.slot() for _ in self.devices]
+
+    def copy(self, step):
+        source = self.other if step == 0 else self.value
+        return self.wires.copy(source, self.buffers.at[step], self.devices[step], self.slots[step])
+
+    def start(self):
+        self.copy(0).start()
+
+    def step(self, step):
+        self.copy(step).wait()
+        self.value[...] = self.value[...] + self.buffers[step]
+        if step + 1 < len(self.devices):
+            self.copy(step + 1).start()
+
+
+class Chain:
+    def __init__(self, wires, osize, value, stages, buffers, result, pieces):
+        self.wires, self.value, self.stages, self.result = wires, value, stages, result
+        self.buffers = buffers
+        self.spans = row_spans(value.shape[0], pieces)
+        self.slots = [[wires.slot() for _ in self.spans] for _ in stages]
+        self.kept = [wires.local_used + i for i in range(pieces)]
+        wires.local_used += pieces
+        self.other = None
+
+    def copy(self, stage, i):
+        w, span = self.wires, self.spans[i]
+        kind, slot = self.stages[stage], self.slots[stage][i]
+        if kind == "x":
+            return w.copy(self.other.at[span], self.buffers[stage].at[span], {"x": 1 - w.x}, slot)
+        if kind == "h":
+            return w.copy(self.value.at[span], self.buffers[stage].at[span], {"h": 1 - w.h}, slot)
+        if kind == "k":
+            return w.copy(self.value.at[span], self.result.at[span], {"k": 1 - w.k}, slot)
+        return w.copy(self.value.at[span], self.buffers[stage].at[span], {"o": w.o ^ kind}, slot)
+
+    def keep(self, i):
+        span = self.spans[i]
+        return pltpu.make_async_copy(
+            self.value.at[span], self.result.at[span], self.wires.local_sem.at[self.kept[i]]
+        )
+
+    def start(self, stage, i):
+        w, kind = self.wires, self.stages[stage]
+        if kind == "x":
+            self.copy(stage, i).start()
+        elif kind == "h":
+            @pl.when(jnp.logical_not(w.home))
+            def _():
+                self.copy(stage, i).start()
+        else:
+            @pl.when(w.home)
+            def _():
+                self.copy(stage, i).start()
+                if kind == "k":
+                    self.keep(i).start()
+
+    def add(self, stage, i):
+        span = self.spans[i]
+        self.value[span, :] = (
+            self.value[span, :].astype(F32) + self.buffers[stage][span, :].astype(F32)
+        ).astype(BF16)
+
+    def end(self, stage, i):
+        w, kind = self.wires, self.stages[stage]
+        if kind == "x":
+            self.copy(stage, i).wait_recv()
+            self.add(stage, i)
+        elif kind == "h":
+            @pl.when(w.home)
+            def _():
+                self.copy(stage, i).wait_recv()
+                self.add(stage, i)
+        elif kind == "k":
+            @pl.when(w.home)
+            def _():
+                self.copy(stage, i).wait_send()
+                self.keep(i).wait()
+
+            @pl.when(jnp.logical_not(w.home))
+            def _():
+                self.copy(stage, i).wait_recv()
+        else:
+            @pl.when(w.home)
+            def _():
+                self.copy(stage, i).wait()
+                self.add(stage, i)
+
+    def close(self):
+        w = self.wires
+        for stage, kind in enumerate(self.stages):
+            for i in range(len(self.spans)):
+                if kind == "x":
+                    self.copy(stage, i).wait_send()
+                elif kind == "h":
+                    @pl.when(jnp.logical_not(w.home))
+                    def _():
+                        self.copy(stage, i).wait_send()
+
+    def step(self, stage, i):
+        self.end(stage, i)
+        if stage + 1 < len(self.stages):
+            self.start(stage + 1, i)
+
+    def order(self, first=0):
+        return [(stage, i) for stage in range(first, len(self.stages)) for i in range(len(self.spans))]
+
+    def run(self, first=0):
+        for stage, i in self.order(first):
+            self.step(stage, i)
+
+
+def leave_kernel(
+    psize, osize, proj_pieces, part, stream, base, gain_ref, small_in, proj_own, proj_other, out_own, out_other,
+    up_in, gate_in, down_in, block, small, proj_sum, out_sum, up_sum, gate_sum, down_sum,
+    near, mid, far, kept, proj_val, out_val, up_val, gate_val, down_val, proj_bufs, out_bufs, small_other, small_bufs,
+    send_sem, recv_sem, local_sem,
+):
+    w = Wires(send_sem, recv_sem, local_sem)
+    loads = [
+        w.local(source, target)
+        for source, target in (
+            (up_in, up_val), (gate_in, gate_val), (down_in, down_val), (out_own, out_val), (proj_own, proj_val)
+        )
+    ]
+    w.greet(partners(w, psize, away=True, over_o=osize))
+    rows, half = kept.shape[1], kept.shape[2]
+    spans = row_spans(rows, PIECES)
+    size = rows // PIECES
+    bits = bits_of(osize)
+
+    proj = Chain(
+        w, osize, proj_val, ["x", "h"] + bits + ["k"], [proj_bufs.at[i] for i in range(2 + len(bits))],
+        proj_sum, proj_pieces,
+    )
+    proj.other = proj_other
+    out = Chain(w, osize, out_val, ["x", "h"] + bits[1:], [out_bufs.at[i] for i in range(1 + len(bits))], None, 1)
+    out.other = out_other
+    out_spread = Spread(w, out_val, out_sum)
+    spreads = [Spread(w, up_val, up_sum), Spread(w, gate_val, gate_sum), Spread(w, down_val, down_sum)]
+    reduce = Reduce(w, psize, part, near, mid, far, spans)
+    out.start(0, 0)
+    for i in range(proj_pieces):
+        proj.start(0, i)
+    for load in loads:
+        load.wait()
+    for spread in spreads:
+        spread.start()
+    reduce.start()
+
+    near_slots = [w.slot() for _ in spans]
+    far_slots = [w.slot() for _ in spans]
+    keep_slots = [w.local_used + i for i in range(PIECES)]
+    w.local_used += PIECES
+
+    def target(i):
+        return block.at[pl.ds(pl.multiple_of(w.k * rows + i * size, 8), size)]
+
+    def same_keep(i):
+        return pltpu.make_async_copy(kept.at[0, spans[i]], target(i), local_sem.at[keep_slots[i]])
+
+    def same_send(i):
+        return w.copy(kept.at[1, spans[i]], target(i), {"x": 1 - w.x}, near_slots[i])
+
+    def cross_near(i):
+        return w.copy(kept.at[0, spans[i]], target(i), {"k": 1 - w.k}, near_slots[i])
+
+    def cross_far(i):
+        return w.copy(kept.at[1, spans[i]], target(i), {"k": 1 - w.k, "x": 1 - w.x}, far_slots[i])
+
+    out.step(0, 0)
+    for i in range(proj_pieces):
+        proj.step(0, i)
+    gain = gain_ref[0:1, :]
+    gain_sum = jnp.zeros((1, D), F32)
+    for i, span in enumerate(spans):
+        grad, gain_part = norm_back(reduce.rows(i), stream[span, :].astype(F32), base[span, :], gain)
+        gain_sum = gain_sum + gain_part
+        kept[0, span, :] = grad[:, :half].astype(BF16)
+        kept[1, span, :] = grad[:, half:].astype(BF16)
+
+        @pl.when(w.same)
+        def _():
+            same_send(i).start()
+            same_keep(i).start()
+
+        @pl.when(jnp.logical_not(w.same))
+        def _():
+            cross_near(i).start()
+            cross_far(i).start()
+
+    row = lax.broadcasted_iota(jnp.int32, (8, half), 0)
+    small[...] = jnp.where(row == 0, gain_sum[:, :half], small_in[:, :half])
+    small_other[...] = jnp.where(row == 0, gain_sum[:, half:], small_in[:, half:])
+    total = SmallSum(w, psize, osize, small, small_other, small_bufs)
+    total.start()
+    out.run(1)
+    out_spread.start()
+    for spread in spreads:
+        spread.relay()
+    smalls = list(range(len(total.devices)))
+    for n, (stage, i) in enumerate(proj.order(1)):
+        proj.step(stage, i)
+        if n % 2 and smalls:
+            total.step(smalls.pop(0))
+    for step in smalls:
+        total.step(step)
+    out_spread.relay()
+    for spread in spreads + [out_spread]:
+        spread.wait()
+    for i in range(PIECES):
+        @pl.when(w.same)
+        def _():
+            same_keep(i).wait()
+            same_send(i).wait_send()
+            cross_near(i).wait_recv()
+
+        @pl.when(jnp.logical_not(w.same))
+        def _():
+            cross_near(i).wait_send()
+            cross_far(i).wait()
+            same_send(i).wait_recv()
+
+    proj.close()
+    out.close()
+    w.close()
+
+
+ANY = pl.BlockSpec(memory_space=pl.ANY)
+VMEM = pl.BlockSpec(memory_space=pltpu.VMEM)
+SLOTS = 128
+
+
+def exchange_call(kernel, name, collective_id, outs, out_specs, in_specs, scratch, args):
+    return pl.pallas_call(
+        kernel,
+        out_shape=outs,
+        in_specs=in_specs,
+        out_specs=out_specs,
+        scratch_shapes=scratch
+        + [
+            pltpu.SemaphoreType.DMA((SLOTS,)),
+            pltpu.SemaphoreType.DMA((SLOTS,)),
+            pltpu.SemaphoreType.DMA((SLOTS // 2,)),
+        ],
+        compiler_params=pltpu.CompilerParams(
+            collective_id=collective_id, has_side_effects=True, vmem_limit_bytes=56 << 20
+        ),
+        name=name,
+    )(*args)
+
+
+def sds(shape, dtype):
+    return jax.ShapeDtypeStruct(shape, dtype)
+
+
+def sum_scratch(psize, rows):
+    far = max(psize - 1, 1)
+    return [
+        pltpu.VMEM((psize, rows, D), BF16),
+        pltpu.VMEM((far, rows, D), BF16),
+        pltpu.VMEM((far, rows, D), BF16),
+    ]
+
+
+def enter(psize, layer_input, gains, qkv_weight, forget_weight, out_weight):
+    rows = layer_input.shape[0] // 2
+    half, width = qkv_weight.shape
+    columns = width + forget_weight.shape[1]
+    return exchange_call(
+        functools.partial(enter_kernel, psize),
+        "enter",
+        1,
+        (
+            sds((rows, D), BF16),
+            sds((2 * psize, rows, D), BF16),
+            sds((2, half, columns), BF16),
+            sds((out_weight.shape[0], 2 * half), BF16),
+        ),
+        (VMEM, ANY, ANY, ANY),
+        [ANY, VMEM, ANY, ANY, ANY],
+        [pltpu.VMEM((rows, D), BF16)]
+        + [pltpu.VMEM(value.shape, BF16) for value in (qkv_weight, forget_weight, out_weight)],
+        (layer_input, gains, qkv_weight, forget_weight, out_weight),
+    )
+
+
+def forward_exchange(psize, part, xin, gains, gate_weight, gate_got, up_weight, up_got, down_weight):
+    rows = xin.shape[0]
+    return exchange_call(
+        functools.partial(forward_exchange_kernel, psize),
+        "forward_exchange",
+        2,
+        (
+            sds((rows, D), F32),
+            sds((2 * psize, rows, D), BF16),
+            sds((2,) + gate_weight.shape, BF16),
+            sds((2,) + up_weight.shape, BF16),
+            sds((down_weight.shape[0], D), BF16),
+        ),
+        (VMEM, ANY, ANY, ANY, ANY),
+        [VMEM, VMEM, VMEM, ANY, ANY, ANY, ANY, ANY],
+        sum_scratch(psize, rows)
+        + [pltpu.VMEM((rows, D), BF16)]
+        + [
+            pltpu.VMEM(value.shape, BF16)
+            for value in (gate_weight, gate_got, up_weight, up_got, down_weight)
+        ],
+        (part, xin, gains, gate_weight, gate_got, up_weight, up_got, down_weight),
+    )
+
+
+def backward_exchange(psize, part, resid, cot, gains, down_own, down_other, gate_part, up_part):
+    rows = resid.shape[0]
+
+    def early(value):
+        half_rows = value.shape[1] // 2
+        shape = (half_rows, value.shape[2])
+        return [
+            pltpu.VMEM((2,) + shape, BF16),
+            pltpu.VMEM((2,) + shape, BF16),
+            pltpu.VMEM(shape, BF16),
+        ]
+
+    def kept(value):
+        return sds((value.shape[1] // 2, value.shape[2]), BF16)
+
+    return exchange_call(
+        functools.partial(backward_exchange_kernel, psize),
+        "backward_exchange",
+        3,
+        (
+            sds((rows, D), F32),
+            sds((2 * psize, rows, D), BF16),
+            sds((8, D), F32),
+            sds(down_own.shape, BF16),
+            kept(gate_part),
+            kept(up_part),
+        ),
+        (VMEM, ANY, VMEM, VMEM, ANY, ANY),
+        [VMEM, VMEM, VMEM, VMEM, VMEM, ANY, ANY, ANY],
+        sum_scratch(psize, rows)
+        + [pltpu.VMEM((rows, D), BF16), pltpu.VMEM(down_own.shape, BF16)]
+        + early(gate_part)
+        + early(up_part),
+        (part, resid, cot, gains, down_own, down_other, gate_part, up_part),
+    )
+
+
+def leave(psize, osize, part, stream, base, gains, small, proj_own, proj_other, out_own, out_other, up, gate, down):
+    rows = stream.shape[0]
+    bits = len(bits_of(osize))
+    half = D // 2
+
+    def buffers(count, value):
+        return pltpu.VMEM((count,) + value.shape, BF16)
+
+    def both(value):
+        return sds((2,) + value.shape, BF16)
+
+    return exchange_call(
+        functools.partial(leave_kernel, psize, osize, 6),
+        "leave",
+        4,
+        (
+            sds((2 * rows, half), BF16),
+            sds((8, half), F32),
+            sds(proj_own.shape, BF16),
+            both(out_own),
+            both(up),
+            both(gate),
+            both(down),
+        ),
+        (ANY, VMEM, ANY, ANY, ANY, ANY, ANY),
+        [VMEM] * 5 + [ANY] * 7,
+        sum_scratch(psize, rows)
+        + [pltpu.VMEM((2, rows, half), BF16)]
+        + [pltpu.VMEM(value.shape, BF16) for value in (proj_own, out_own, up, gate, down)]
+        + [buffers(2 + bits, proj_own), buffers(1 + bits, out_own)]
+        + [pltpu.VMEM((8, half), F32), pltpu.VMEM((3 + len(bits_of(psize)) + bits, 8, half), F32)],
+        (part, stream, base, gains, small, proj_own, proj_other, out_own, out_other, up, gate, down),
+    )
+
+
 def make_shards(osize, psize):
     count = 2 * psize
-    home_steps = []
-    bit = 1
-    while bit < osize:
-        home_steps.append((osize, bit))
-        bit *= 2
+    obits = bits_of(osize)
 
     def shards(
         layer_input,
@@ -551,11 +1577,37 @@
         out_cotangent,
     ):
         core, xpos = lax.axis_index("k"), lax.axis_index("x")
-        hpos, ppos = lax.axis_index("h"), lax.axis_index("p")
+        hpos, ppos, opos = lax.axis_index("h"), lax.axis_index("p"), lax.axis_index("o")
         home = core == hpos
         same = core == xpos
-        me = ppos * 2 + core
         heads = forget_weight.shape[1]
+        width = heads * 3 * DH
+        lane_pad = LANES - heads
+        feat = D // 2
+
+        def far_blocks(block):
+            return [xor_swap(block, "p", psize, bit) for bit in range(1, psize)]
+
+        def all_blocks(block, far):
+            blocks = []
+            for near in [block] + far:
+                blocks += [near, swap(near, "k")]
+            return jnp.concatenate(blocks, axis=0)
+
+        def near_sums(partial):
+            size = partial.shape[0] // count
+            parts = [partial[i * size : (i + 1) * size] for i in range(count)]
+            moved = [swap(parts[i + 1], "k") for i in range(0, count, 2)]
+            return [add_parts(parts[i], moved[i // 2]) for i in range(0, count, 2)]
+
+        def far_sums(sums):
+            return [xor_swap(sums[bit], "p", psize, bit) for bit in range(1, psize)]
+
+        def total_of(near, far):
+            total = near.astype(F32)
+            for value in far:
+                total = total + value.astype(F32)
+            return total
 
         prompt_len, branch_len = prompt_doc.shape[1], branch_seg.shape[1]
         packed = jnp.concatenate([prompt_doc[0], branch_seg[0], branch_doc[0]])
@@ -567,113 +1619,150 @@
         prompt_ids = packed[:prompt_len]
         branch_ids = packed[prompt_len : prompt_len + branch_len]
         branch_docs = packed[prompt_len + branch_len :]
-
         gains = jnp.stack([attn_gain, ffn_gain])
         gains = jnp.concatenate([gains, swap(gains, "x")], axis=1)
         gain_a, gain_b = gains[0], gains[1]
-
-        lane_pad = LANES - heads
-        w_forget = gather_weight(
-            jnp.concatenate([forget_weight, jnp.zeros((forget_weight.shape[0], lane_pad), BF16)], 1),
-            home,
-            0,
-        )
         bias = jnp.where(home, forget_bias, lax.ppermute(forget_bias, ("k", "h"), [(1, 2), (2, 1)]))
         bias = jnp.concatenate([bias, jnp.zeros((lane_pad,), F32)])
-        w_qkv = jnp.concatenate([gather_weight(qkv_weight, home, 0), w_forget], axis=1)
-        w_out = gather_weight(out_weight, home, 1)
-        w_gate = gather_weight(gate_weight, home, 0)
-        w_up = gather_weight(up_weight, home, 0)
-        w_down = gather_weight(down_weight, home, 1)
-
-        stream = spread_tokens(layer_input, core, same).astype(F32)
-        cot = spread_tokens(out_cotangent, core, same)
-        cot_all = gather_blocks(cot, psize)
-        cotangent = cot.astype(F32)
-
-        rms_a = lax.rsqrt(jnp.sum(stream * stream, axis=1) / D + EPS)[:, None]
-        normed_a_all = gather_blocks((stream * rms_a * gain_a).astype(BF16), psize)
-        projected = matmul(normed_a_all, w_qkv)
-        width = heads * 3 * DH
+        kcol, qrow, flags = group_codes(prompt_ids, branch_ids, branch_docs)
+
+        gains8 = jnp.concatenate([gains, jnp.zeros((6, D), F32)])
+        forget_wide = jnp.concatenate(
+            [forget_weight, jnp.zeros((forget_weight.shape[0], lane_pad), BF16)], axis=1
+        )
+        first_part, second_part = qkv_weight, forget_wide
+        if width % LANES:
+            spare = jnp.zeros((qkv_weight.shape[0], LANES - width % LANES), BF16)
+            first_part = jnp.concatenate([qkv_weight, forget_wide, spare], axis=1)
+        xin, normed_a_all, w_proj, w_out = enter(
+            psize, layer_input, gains8, first_part, second_part, out_weight
+        )
+        normed_a_all = normed_a_all.reshape(-1, D)
+        w_proj = w_proj.reshape(D, -1)[:, : width + LANES]
+
+        projected = matmul(normed_a_all, w_proj)
         qkv = projected[:, :width].astype(BF16).reshape(count, -1, width)
-        logit = projected[:, width:] + bias
-        logit = logit.reshape(count, -1, LANES)
-        kcol, qrow, flags = group_codes(prompt_ids, branch_ids, branch_docs)
+        logit = (projected[:, width:] + bias).reshape(count, -1, LANES)
+        qkv, logit = lax.optimization_barrier((qkv, logit))
+        gate_got = fetch_home_away(tie(take_half(gate_weight, opos % 2), qkv))
+        up_got = fetch_home_away(tie(take_half(up_weight, opos % 2), qkv))
+        cot = spread_tokens(tie(out_cotangent, qkv), core, same)
         attended, *saved = attention_forward(qkv, logit, kcol, qrow, flags, heads, prompt_len)
-        attended = attended.reshape(-1, heads * DH)
-        resid = stream + sum_blocks(matmul(attended, w_out), psize)
-        rms_b = lax.rsqrt(jnp.sum(resid * resid, axis=1) / D + EPS)[:, None]
-        normed_b_all = gather_blocks((resid * rms_b * gain_b).astype(BF16), psize)
+        attended = tie(attended.reshape(-1, heads * DH), gate_got, up_got, cot)
+        part = matmul(attended, w_out).astype(BF16).reshape(count, -1, D)
+        resid, normed_b_all, w_gate, w_up, w_down = forward_exchange(
+            psize, part, xin, gains8, gate_weight, gate_got, up_weight, up_got, down_weight
+        )
+        normed_b_all = normed_b_all.reshape(-1, D)
+        w_gate, w_up = w_gate.reshape(D, -1), w_up.reshape(D, -1)
+        cot_far = far_blocks(tie(cot, normed_b_all))
         gate_pre = matmul(normed_b_all, w_gate)
         up_pre = matmul(normed_b_all, w_up)
         gate_sig = jax.nn.sigmoid(gate_pre)
         gate_act = gate_pre * gate_sig
         hidden = (gate_act * up_pre).astype(BF16)
-        layer_output = (resid + sum_blocks(matmul(hidden, w_down), psize)).astype(BF16)
-        layer_output = unspread_tokens(layer_output, core, same)
-
-        feat = D // 2
-
-        def reduce_rows(grad):
-            return reduce_weight(grad[:feat], grad[feat:], home, home_steps)
-
-        def reduce_cols(grad):
-            return reduce_weight(grad[:, :feat], grad[:, feat:], home, home_steps)
-
-        down_grad = reduce_cols(contract_rows(hidden, cot_all))
-        grad_hidden = contract_cols(cot_all, w_down)
+        hidden = tie(hidden, *cot_far)
+        cot_all = all_blocks(cot, cot_far)
+
+        def finish(total, axis_bits):
+            for bit in axis_bits:
+                total = add_parts(total, home_swap(total, osize, bit))
+            return total
+
+        high = opos % 2 == 1
+        down_part = contract_rows(hidden, cot_all).astype(BF16)
+        down_keep, down_give = split_rows(down_part, high)
+        down_moved = xor_swap(down_give, "o", osize, 1)
+        out_sums = near_sums(matmul(hidden, w_down).astype(BF16))
+        out_far = far_sums(out_sums)
+        grad_hidden = contract_cols(tie(cot_all, out_sums[0]), w_down)
         grad_gate = (grad_hidden * up_pre * gate_sig * (1.0 + gate_pre * (1.0 - gate_sig))).astype(BF16)
         grad_up = (grad_hidden * gate_act).astype(BF16)
-        gate_grad = reduce_rows(contract_rows(normed_b_all, grad_gate))
-        up_grad = reduce_rows(contract_rows(normed_b_all, grad_up))
-        grad_normed_b = sum_blocks(
-            contract_cols(grad_gate, w_gate) + contract_cols(grad_up, w_up), psize
-        )
-        gained_b = gain_b * grad_normed_b
-        inner_b = jnp.sum(resid * gained_b, axis=1)[:, None]
-        ffn_gain_part = jnp.sum(grad_normed_b * resid * rms_b, axis=0)
-        grad_resid = cotangent + rms_b * gained_b - resid * (rms_b * rms_b * rms_b) * inner_b / D
-        grad_branch_all = gather_blocks(grad_resid.astype(BF16), psize)
-        out_grad = reduce_cols(contract_rows(attended, grad_branch_all))
+        gate_part = contract_rows(normed_b_all, grad_gate).astype(BF16)
+        up_part = contract_rows(normed_b_all, grad_up).astype(BF16)
+        part = (contract_cols(grad_gate, w_gate) + contract_cols(grad_up, w_up)).astype(BF16)
+        part = tie(part, *out_far)
+        layer_output = (resid + total_of(out_sums[0], out_far)).astype(BF16)
+        down_total = add_parts(down_keep, down_moved)
+        grad_resid, grad_branch_all, ffn_gain_part, down_total, gate_total, up_total = backward_exchange(
+            psize,
+            part.reshape(count, -1, D),
+            resid,
+            cot,
+            gains8,
+            down_total[:, :feat],
+            down_total[:, feat:],
+            gate_part.reshape(2, feat, -1),
+            up_part.reshape(2, feat, -1),
+        )
+        grad_branch_all = grad_branch_all.reshape(-1, D)
         grad_attended = contract_cols(grad_branch_all, w_out).astype(BF16)
+        out_part = contract_rows(attended, grad_branch_all).astype(BF16)
+        out_keep, out_give = split_rows(out_part, high)
+        grad_attended, out_keep, out_give, *totals = lax.optimization_barrier(
+            (grad_attended, out_keep, out_give, down_total, gate_total, up_total) + unspread_parts(layer_output, same)
+        )
+        totals, (own_part, near_part, far_part) = totals[:3], totals[3:]
+        moved = [to_home(value) for value in totals]
+        out_moved = xor_swap(out_give, "o", osize, 1)
+        near_moved, far_moved = unspread_moves(near_part, far_part)
         grad_proj, bias_sums = attention_backward(
             grad_attended.reshape(count, -1, heads * DH), saved, logit, kcol, qrow, flags, heads, prompt_len
         )
+        grad_proj, bias_sums, out_moved, near_moved, far_moved, *moved = lax.optimization_barrier(
+            (grad_proj, bias_sums, out_moved, near_moved, far_moved, *moved)
+        )
+        layer_output = unspread_join(own_part, near_moved, far_moved, core, same)
         grad_proj = grad_proj.reshape(-1, width + LANES)
-        forget_bias_part = bias_sums[0, :heads]
-        proj_grad = reduce_rows(contract_rows(normed_a_all, grad_proj))
+        proj_part = contract_rows(normed_a_all, grad_proj).astype(BF16)
+        part = contract_cols(grad_proj, w_proj).astype(BF16).reshape(count, -1, D)
+        down_total, gate_total, up_total = (
+            finish(add_parts(value, other), obits[1:]) for value, other in zip(totals, moved)
+        )
+        out_total = add_parts(out_keep, out_moved)
+
+        slots = jnp.where(
+            (jnp.arange(2 * psize) == core * psize + ppos)[:, None], bias_sums[:1, :heads], 0.0
+        ).reshape(-1)
+        slots = jnp.concatenate([slots, jnp.zeros((feat - slots.shape[0],), F32)])
+        small = jnp.stack([jnp.zeros((D,), F32), ffn_gain_part[0], jnp.concatenate([slots, slots])])
+        small = jnp.concatenate([small, jnp.zeros((5, D), F32)])
+        input_grad, small, proj_grad, out_both, up_both, gate_both, down_both = leave(
+            psize,
+            osize,
+            part,
+            xin,
+            grad_resid,
+            gains8,
+            small,
+            proj_part[:feat],
+            proj_part[feat:],
+            out_total[:, :feat],
+            out_total[:, feat:],
+            up_total,
+            gate_total,
+            down_total,
+        )
+        proj_grad = proj_grad.astype(F32)
         qkv_grad, forget_grad = proj_grad[:, :width], proj_grad[:, width : width + heads]
-        grad_normed_a = sum_blocks(contract_cols(grad_proj, w_qkv), psize)
-        gained_a = gain_a * grad_normed_a
-        inner_a = jnp.sum(stream * gained_a, axis=1)[:, None]
-        attn_gain_part = jnp.sum(grad_normed_a * stream * rms_a, axis=0)
-        input_grad = (
-            grad_resid + rms_a * gained_a - stream * (rms_a * rms_a * rms_a) * inner_a / D
-        ).astype(BF16)
-        input_grad = unspread_tokens(input_grad, core, same)
-
-        slots = jnp.where(
-            (jnp.arange(2 * psize) == core * psize + ppos)[:, None], forget_bias_part[None, :], 0.0
-        ).reshape(-1)
-        small = jnp.concatenate([attn_gain_part[:feat], ffn_gain_part[:feat], slots])
-        sent = jnp.concatenate([attn_gain_part[feat:], ffn_gain_part[feat:], slots])
-        small = small + swap(sent, "x")
-        small = lax.psum(small, ("o", "k", "h", "p"))
-        bias_all = small[2 * feat :].reshape(2 * psize, heads)
+        bias_all = small[2, : 2 * psize * heads].reshape(2 * psize, heads)
         forget_bias_grad = lax.dynamic_index_in_dim(bias_all, hpos * psize + ppos, 0, keepdims=False)
+
+        def whole(halves):
+            return halves.reshape(-1, halves.shape[2]).astype(F32)
 
         return (
             layer_output,
             input_grad,
-            small[:feat],
+            small[0],
             qkv_grad,
             forget_grad,
             forget_bias_grad,
-            out_grad,
-            small[feat : 2 * feat],
-            gate_grad,
-            up_grad,
-            down_grad,
+            whole(out_both),
+            small[1],
+            whole(gate_both),
+            whole(up_both),
+            whole(down_both),
         )
 
     return shards

time: 875 us -> 672 us (0.77)
  Pallas kernels: 96.1 us -> 431 us
  waiting for transfers between devices: 312 us -> 23.3 us
  starting transfers between devices: 174 us -> 29 us
  other arithmetic: 83.9 us -> 33.1 us
  blocking collectives: 28 us -> 0 us
  matrix products: 128 us -> 118 us
  local copies, waits for them, and re-layouts: 37.1 us -> 27.6 us
    pallas_call x0 -> x4, Pallas kernels: none -> 332 us  [exchange_call(): pl.pallas_call(kernel, out_shape=outs, in_specs=in_specs, out_specs=out_s...]
    ppermute x6 -> x2, waiting for transfers between devices: 99.1 us -> 0.01 us  [fetch_home_away(): return lax.ppermute(value, ('k', 'x', 'h'), pairs)]
    ppermute x8 -> x4, waiting for transfers between devices: 89 us -> 18.2 us  [xor_swap(): return lax.ppermute(value, axis, [(i, i ^ bit) for i in range(size)])]
    ppermute x25 -> x5, starting transfers between devices: 67.5 us -> 10.8 us  [the longest x3 7.72 us: to_home(): return lax.ppermute(value, ('k', 'h'), [(1, 0), (2, 3)])]
    ppermute x25 -> x7, waiting for transfers between devices: 61.5 us -> 5.05 us  [swap(): return lax.ppermute(value, axis, [(0, 1), (1, 0)])]
    ppermute x25 -> x7, starting transfers between devices: 54.6 us -> 4.26 us  [swap(): return lax.ppermute(value, axis, [(0, 1), (1, 0)])]
    ppermute x25 -> x5, waiting for transfers between devices: 48.6 us -> 0.01 us  [the longest x3 0.01 us: to_home(): return lax.ppermute(value, ('k', 'h'), [(1, 0), (2, 3)])]
    convert_element_type x28 -> x11, other arithmetic: 56 us -> 16.7 us  [the longest x4 7.45 us: whole(): return halves.reshape(-1, halves.shape[2]).astype(F32)]
  transfers between devices with their start and end apart: 69 -> 21, of which waited for: 20 -> 5; matrix products, arithmetic and copies ran while one was open for 20% -> 16% of each run, Pallas kernels for 6% -> 25%
where the time goes in v3:
time: 672 us; the launch traced here: 664 us
  Pallas kernels  431 us (64%)
  matrix products  118 us (18%)
  other arithmetic  33.1 us (5%)
  starting transfers between devices  29 us (4%)
  local copies, waits for them, and re-layouts  27.6 us (4%)
  waiting for transfers between devices  23.3 us (3%)
    pallas_call x4, Pallas kernels, exchange_call(): pl.pallas_call(kernel, out_shape=outs, in_specs=in_specs, out_specs=out_s...  332 us
    pallas_call x1, Pallas kernels, attention_backward(): pl.pallas_call(functools.partial(backward_kernel, heads, count, prompt_le...  53.5 us
    dot_general x5, matrix products, contract_cols(): lax.dot_general(left, right, (((1,), (1,)), ((), ())), preferred_element_...  46.4 us
    pallas_call x1, Pallas kernels, attention_forward(): pl.pallas_call(functools.partial(forward_kernel, heads, count, prompt_len...  45.9 us
    dot_general x5, matrix products, contract_rows(): lax.dot_general(left, right, (((0,), (0,)), ((), ())), preferred_element_...  36.6 us
    dot_general x5, matrix products, matmul(): return jnp.dot(left, right, preferred_element_type=F32)  34.7 us
    ppermute x4, waiting for transfers between devices, xor_swap(): return lax.ppermute(value, axis, [(i, i ^ bit) for i in range(size)])  18.2 us
  transfers between devices with their start and end apart: 21, of which 5 were waited for; matrix products, arithmetic and copies ran while one was open for 16% of the time, Pallas kernels for 25%

profile of v3, /device:TPU:1, one launch (start us, length us, event | category | flops | bytes accessed | tf_op | source)
XLA Modules:
  0.0 663.6 jit_solution(7199795785634623037)
XLA Ops:
  0.7 5.6 collective-permute-start.1
  7.7 1.3 collective-permute-start
  9.7 0.9 copy.40
  11.3 2.7 constant_dynamic-slice_fusion.1
  14.6 64.0 %enter.1 = (bf16[384,1536]{1,0:T(8,128)(2,1)}, bf16[4,384,1536]{2,1,0:T(8,128)(2,1)}, bf16[2,768,1280]{2,1,0:T(8,128)(2,1)}, bf16[384,1536]{1,0:T(8,128)(2,1)}) custom-call(bf16[768,768]{1,0:T(8,128)(2,1)} %x_ref.1, f32[8,1536]{1,0:T(8,128)} %select_maximum_fusion.gain_ref, bf16[768,1152]{1,0:T(8,128)(2,1)} %qkv_shard.1, ...), custom_call_target="tpu_custom_call" | custom-call | tf_op jit(solution)/shard_map/enter/pallas_call | solution.py:1409
  78.7 9.3 %fusion.13 = f32[1536,1280]{1,0:T(8,128)S(1)} fusion(bf16[1536,1536]{1,0:T(8,128)(2,1)} %bitcast.88, bf16[1536,1280]{1,0:T(8,128)(2,1)} %bitcast.97), kind=kOutput, calls=%fused_computation.84 | convolution fusion | flops 6039797760 | bytes 16515072 | tf_op jit(solution)/shard_map/dot_general | solution.py:157
  88.1 2.2 slice.161
  90.2 2.0 collective-permute-start.7
  92.9 2.0 collective-permute-start.6
  94.9 1.2 broadcast_select_fusion.8
  96.1 2.2 collective-permute-start.3
  99.7 45.9 %attention_forward.1 = (bf16[4,384,384]{2,1,0:T(8,128)(2,1)S(1)}, f32[384,1536]{1,0:T(8,128)S(1)}, f32[8,1536]{1,0:T(8,128)S(1)}, bf16[6,1536,128]{2,1,0:T(8,128...) custom-call(s32[36]{0:T(128)S(1)} %reshape.128.flags, bf16[4,384,1152]{2,1,0:T(8,128)(2,1)} %bitcast.76, ...), custom_call_target="tpu_custom_call" | custom-call | flops 20000000000 | bytes 30000000 | tf_op jit(solution)/shard_map/attention_forward/pallas_call | solution.py:324
  145.7 2.4 broadcast_select_fusion.7
  148.1 1.1 pad_maximum_fusion.1.cot
  149.2 4.3 convolution_convert_fusion.2
  153.6 95.3 %forward_exchange.1 = (f32[384,1536]{1,0:T(8,128)}, bf16[4,384,1536]{2,1,0:T(8,128)(2,1)}, bf16[2,768,1024]{2,1,0:T(8,128)(2,1)}, bf16[2,768,1024]{2,1,0:T(8,128)(2,1)}, bf16[1024,1536]{1,0:T(8,128)(2,1)}) custom-call(bf16[4,384,1536]{2,1,0:T(8,128)(2,1)} %bitcast.74, bf16[384,1536]{1,0:T(8,128)(2,1)} %get-tuple-element.78.xin.stream, ...), custom_call_target="tpu_custom_call" | custom-call | tf_op jit(solution)/shard_map/forward_exchange/pallas_call | solution.py:1409
  248.9 8.0 %fusion.14 = f32[1536,1024]{1,0:T(8,128)S(1)} fusion(bf16[1536,1536]{1,0:T(8,128)(2,1)} %bitcast.89, bf16[1536,1024]{1,0:T(8,128)(2,1)} %bitcast.99), kind=kOutput, calls=%fused_computation.85 | convolution fusion | flops 4831838208 | bytes 14155776 | tf_op jit(solution)/shard_map/dot_general | solution.py:157
  257.0 7.3 %multiply_convert_fusion.2 = (bf16[1536,1024]{1,0:T(8,128)(2,1)S(1)}, f32[1536,1024]{1,0:T(8,128)}) fusion(f32[1536,1024]{1,0:T(8,128)S(1)} %fusion.14, bf16[1536,1536]{1,0:T(8,128)(2,1)S(1)} %bitcast.90, bf16[1536,1024]{1,0:T(8,128)(2,1)S(1)} %bitcast.101), kind=kOutput, calls=%fused_computation.9 | convolution fusion | flops 4841275392 | bytes 23592960 | tf_op jit(solution)/shard_map/dot_general | solution.py:157
  264.2 4.1 collective-permute-done.9
  268.3 5.9 convolution_convert_fusion
  274.2 2.2 copy-done.7
  276.4 1.6 fusion.7
  279.0 2.2 collective-permute-done.12
  281.1 1.9 add_convert_fusion.3
  283.3 2.9 collective-permute-done.4
  286.2 8.9 %convolution_convert_fusion.5 = bf16[1024,1536]{1,0:T(8,128)(2,1)S(1)} fusion(bf16[1536,1024]{1,0:T(8,128)(2,1)S(1)} %copy-done.40, bf16[384,1536]{1,0:T(8,128)(2,1)} %collective-permute-done.10, bf16[384,1536]{1,0:T(8,128)(2,1)S(1)} %collective-permute-done.9, bf16[384,1536]{1,0:T(8,128)(2,1)} %collective-permute-done.4, ...), kind=kOutput, calls=%fused_computation.15 | convolution fusion | flops 4857004032 | bytes 11010048 | tf_op jit(solution)/shard_map/dot_general | solution.py:145
  295.4 5.6 pad_maximum_fusion
  301.0 9.6 %collective-permute-done.13 = bf16[384,1536]{1,0:T(8,128)(2,1)S(1)} collective-permute-done((bf16[384,1536]{1,0:T(8,128)(2,1)S(1)}, bf16[384,1536]{1,0:T(8,128)(2,1)S(1)}, u32[]{:S(2)}, u32[]{:S(2)}) %collective-permute-start.13) | collective-permute-done | bytes 1179680 | tf_op jit(solution)/shard_map/ppermute | solution.py:26
  310.5 2.1 add_convert_fusion.2
  312.8 12.5 %multiply_convert_fusion.1 = (bf16[1536,1024]{1,0:T(8,128)(2,1)}, bf16[1536,1024]{1,0:T(8,128)(2,1)}) fusion(f32[1536,1024]{1,0:T(8,128)} %copy-done.36, f32[1536,1024]{1,0:T(8,128)} %get-tuple-element.200, bf16[1536,1536]{1,0:T(8,128)(2,1)S(1)} %pad_maximum_fusion, bf16[1024,1536]{1,0:T(8,128)(2,1)S(1)} %copy-done.33), kind=kOutput, calls=%fused_computation.8 | convolution fusion | flops 4852285440 | bytes 26738688 | tf_op jit(solution)/shard_map/dot_general | solution.py:151
  325.3 9.9 %fusion.15 = f32[1536,1536]{1,0:T(8,128)} fusion(bf16[1536,1024]{1,0:T(8,128)(2,1)} %get-tuple-element.176, bf16[1536,1024]{1,0:T(8,128)(2,1)S(1)} %bitcast.102), kind=kOutput, calls=%fused_computation.86 | convolution fusion | flops 4831838208 | bytes 15728640 | tf_op jit(solution)/shard_map/dot_general | solution.py:151
  335.2 9.4 %add_convert_fusion = bf16[1536,1536]{1,0:T(8,128)(2,1)} fusion(f32[1536,1536]{1,0:T(8,128)} %fusion.15, bf16[1536,1024]{1,0:T(8,128)(2,1)S(1)} %copy-done.38, bf16[1536,1024]{1,0:T(8,128)(2,1)S(1)} %bitcast.100), kind=kOutput, calls=%fused_computation | convolution fusion | flops 4836556800 | bytes 20447232 | tf_op jit(solution)/shard_map/dot_general | solution.py:151
  344.6 6.6 convolution_convert_fusion.4
  351.2 1.2 fusion.10
  352.4 6.8 %convolution_convert_fusion.3 = bf16[1536,1024]{1,0:T(8,128)(2,1)} fusion(bf16[1536,1536]{1,0:T(8,128)(2,1)S(1)} %bitcast.94, bf16[1536,1024]{1,0:T(8,128)(2,1)S(1)} %copy-done.37), kind=kOutput, calls=%fused_computation.13 | convolution fusion | flops 4833411072 | bytes 11010048 | tf_op jit(solution)/shard_map/dot_general | solution.py:145
  359.7 1.2 fusion.9
  361.0 78.2 %backward_exchange.1 = (f32[384,1536]{1,0:T(8,128)}, bf16[4,384,1536]{2,1,0:T(8,128)(2,1)}, f32[8,1536]{1,0:T(8,128)}, bf16[512,768]{1,0:T(8,128)(2,1)}, bf16[38...) custom-call(bf16[4,384,1536]{2,1,0:T(8,128)(2,1)} %bitcast.73, f32[384,1536]{1,0:T(8,128)} %get-tuple-element.87.resid, ...), custom_call_target="tpu_custom_call" | custom-call | tf_op jit(solution)/shard_map/backward_exchange/pallas_call | solution.py:1409
  439.3 4.5 convolution_convert_fusion.6
  443.8 3.7 convolution_convert_fusion.7
  448.4 3.0 collective-permute-start.15
  451.5 1.2 collective-permute-start.16
  452.6 1.9 collective-permute-start.17
  454.5 4.0 collective-permute-start.18
  458.6 1.3 collective-permute-start.19
  459.9 4.6 collective-permute-done.15
  464.5 2.3 collective-permute-start.20
  466.9 53.5 %attention_backward.1 = (bf16[4,384,1280]{2,1,0:T(8,128)(2,1)}, f32[8,128]{1,0:T(8,128)}) custom-call(s32[36]{0:T(128)} %copy-done.3, bf16[4,384,384]{2,1,0:T(8,128)(2,1)} %bitcast.104, f32[384,1536]{1,0:T(8,128)} %copy-done.4, f32[8,1536]{1,0:T(8,128)} %copy-done.5, bf16[6,1536,128]{2,1,0:T(8,128)(2,1)} %get-tuple-element.96.qp, ...), custom_call_target="tpu_custom_call" | custom-call | flops 49999998976 | bytes 30000000 | tf_op jit(solution)/shard_map/attention_backward/pallas_call | solution.py:483
  521.2 9.8 %fusion = bf16[1536,1280]{1,0:T(8,128)(2,1)S(1)} fusion(bf16[4,384,1536]{2,1,0:T(8,128)(2,1)} %get-tuple-element.68, bf16[4,384,1280]{2,1,0:T(8,128)(2,1)} %get-tuple-element.109), kind=kOutput, calls=%fused_computation.3 | convolution fusion | flops 6041763840 | bytes 12582912 | tf_op jit(solution)/shard_map/dot_general | solution.py:145
  531.1 1.1 add_convert_fusion.5.down_in
  532.1 1.2 add_convert_fusion.6.gate_in
  533.3 1.2 add_convert_fusion.7.up_in
  534.5 1.2 add_convert_fusion.8
  536.6 2.2 fusion.8
  539.7 10.9 %convolution_convert_fusion.1 = bf16[1536,1536]{1,0:T(8,128)(2,1)} fusion(bf16[1536,1280]{1,0:T(8,128)(2,1)} %bitcast.103, bf16[1536,1280]{1,0:T(8,128)(2,1)} %bitcast.98), kind=kOutput, calls=%fused_computation.4 | convolution fusion | flops 6042157056 | bytes 12582912 | tf_op jit(solution)/shard_map/dot_general | solution.py:151
  551.3 94.3 %leave.1 = (bf16[768,768]{1,0:T(8,128)(2,1)}, f32[8,768]{1,0:T(8,128)}, bf16[768,1280]{1,0:T(8,128)(2,1)}, bf16[2,192,768]{2,1,0:T(8,128)(2,1)}, bf16[2,384,1024...) custom-call(bf16[4,384,1536]{2,1,0:T(8,128)(2,1)} %bitcast.75, ...), custom_call_target="tpu_custom_call" | custom-call | tf_op jit(solution)/shard_map/leave/pallas_call | solution.py:1409
  646.3 1.4 slice_reduce_fusion
  647.7 1.0 slice.140
  648.7 3.6 slice.139
  653.2 1.1 bitcast_convert_fusion.3
  654.3 2.2 bitcast_convert_fusion.2
  656.5 2.2 bitcast_convert_fusion.1
  658.7 2.0 bitcast_convert_fusion
  660.8 1.1 pad_maximum_fusion.2
  662.4 1.0 copy.47
  (173 shorter events, 14.5 us)
Async XLA Ops:
  0.6 13.3 %copy-start.26 = (f32[6]{0:T(128)S(1)}, f32[6]{0:T(128)}, u32[]{:S(2)}) copy-start(f32[6]{0:T(128)} %param.18) | copy-start | bytes 76
  0.7 13.3 %collective-permute-start.1 = (f32[6]{0:T(128)}, f32[6]{0:T(128)S(1)}, u32[]{:S(2)}, u32[]{:S(2)}) collective-permute-start(f32[6]{0:T(128)} %param.18), channel_id=1, source_target_pairs={{2,8},{8,2},{3,9},{9,3},{6,12},{12,6},{7,13},{13,7},{18,24},{24,18... | collective-permute-start | bytes 80 | tf_op jit(solution)/shard_map/ppermute | solution.py:1625
  7.7 6.3 collective-permute-start
  9.7 83.2 %collective-permute-start.5 = (s32[1540]{0:T(1024)S(1)}, s32[1540]{0:T(1024)S(1)}, u32[]{:S(2)}, u32[]{:S(2)}) collective-permute-start(s32[1540]{0:T(1024)S(1)} %pad_add_fusion.2), channel_id=1, source_target_pairs={{0,8},{8,0},{1,9},{9,1},{2,10},{10,2},{3,11},{11,3},{4,12},{12,4},... | collective-permute-start | bytes 18488 | tf_op jit(solution)/shard_map/ppermute | solution.py:22
  88.0 11.7 %copy-start = (f32[1536,128]{1,0:T(8,128)}, f32[1536,128]{1,0:T(8,128)S(1)}, u32[]{:S(2)}) copy-start(f32[1536,128]{1,0:T(8,128)S(1)} %slice_add_fusion) | copy-start | bytes 2359300
  88.0 4.9 copy-start.22
  88.0 4.9 copy-start.23
  88.1 4.8 copy-start.24
  88.1 6.8 %copy-start.8 = (bf16[768,768]{1,0:T(8,128)(2,1)S(1)}, bf16[768,768]{1,0:T(8,128)(2,1)}, u32[]{:S(2)}) copy-start(bf16[768,768]{1,0:T(8,128)(2,1)} %param.27) | copy-start | bytes 3538948
  88.1 10.3 %copy-start.25 = (pred[1536]{0:T(1024)(128)(4,1)S(1)}, pred[1536]{0:T(1024)(128)(4,1)}, u32[]{:S(2)}) copy-start(pred[1536]{0:T(1024)(128)(4,1)} %constant.63.clone.1) | copy-start | bytes 4612
  90.2 59.0 %collective-permute-start.7 = (bf16[384,1024]{1,0:T(8,128)(2,1)}, bf16[384,1024]{1,0:T(8,128)(2,1)}, u32[]{:S(2)}, u32[]{:S(2)}) collective-permute-start(bf16[384,1024]{1,0:T(8,128)(2,1)} %get-tuple-element.74), channel_id=1, source_target_pairs={{0,4},{2,8},{4,0},{6,12},{8,2},{10,14},{12,6},{14,10},{1,5},{3,9},... | collective-permute-start | bytes 2359304 | tf_op jit(solution)/shard_map/ppermute | solution.py:40
  92.2 57.0 %collective-permute-start.8 = (bf16[384,1024]{1,0:T(8,128)(2,1)}, bf16[384,1024]{1,0:T(8,128)(2,1)}, u32[]{:S(2)}, u32[]{:S(2)}) collective-permute-start(bf16[384,1024]{1,0:T(8,128)(2,1)} %get-tuple-element.75), channel_id=1, source_target_pairs={{0,4},{2,8},{4,0},{6,12},{8,2},{10,14},{12,6},{14,10},{1,5},{3,9},... | collective-permute-start | bytes 2359304 | tf_op jit(solution)/shard_map/ppermute | solution.py:40
  92.9 5.4 collective-permute-start.6
  96.1 49.6 %collective-permute-start.2 = (bf16[384,768]{1,0:T(8,128)(2,1)}, bf16[384,768]{1,0:T(8,128)(2,1)}, u32[]{:S(2)}, u32[]{:S(2)}) collective-permute-start(bf16[384,768]{1,0:T(8,128)(2,1)} %get-tuple-element.173), channel_id=1, source_target_pairs={{0,8},{4,0},{8,12},{12,4},{1,9},{5,1},{9,13},{13,5},{2,10},{6,2},{... | collective-permute-start | bytes 1769480 | tf_op jit(solution)/shard_map/ppermute | solution.py:117
  96.1 49.6 %collective-permute-start.3 = (bf16[384,768]{1,0:T(8,128)(2,1)}, bf16[384,768]{1,0:T(8,128)(2,1)}, u32[]{:S(2)}, u32[]{:S(2)}) collective-permute-start(bf16[384,768]{1,0:T(8,128)(2,1)} %get-tuple-element.174), channel_id=1, source_target_pairs={{4,8},{8,4},{5,9},{9,5},{6,10},{10,6},{7,11},{11,7},{20,24},{24,20... | collective-permute-start | bytes 1769480 | tf_op jit(solution)/shard_map/ppermute | solution.py:118
  99.2 46.4 %copy-start.3 = (s32[36]{0:T(128)}, s32[36]{0:T(128)S(1)}, u32[]{:S(2)}) copy-start(s32[36]{0:T(128)S(1)} %reshape.128.flags) | copy-start | bytes 436
  99.6 46.1 %copy-start.1 = (s32[1536,8]{1,0:T(8,128)}, s32[1536,8]{1,0:T(8,128)S(1)}, u32[]{:S(2)}) copy-start(s32[1536,8]{1,0:T(8,128)S(1)} %copy.41.kcol) | copy-start | bytes 147460
  99.7 45.9 %copy-start.2 = (s32[8,1536]{1,0:T(8,128)}, s32[8,1536]{1,0:T(8,128)S(1)}, u32[]{:S(2)}) copy-start(s32[8,1536]{1,0:T(8,128)S(1)} %stack.66.qrow) | copy-start | bytes 147460
  99.7 46.0 %copy-start.9 = (bf16[768,768]{1,0:T(8,128)(2,1)S(1)}, bf16[768,768]{1,0:T(8,128)(2,1)}, u32[]{:S(2)}) copy-start(bf16[768,768]{1,0:T(8,128)(2,1)} %param.27) | copy-start | bytes 3538948
  145.7 7.9 %copy-start.4 = (f32[384,1536]{1,0:T(8,128)}, f32[384,1536]{1,0:T(8,128)S(1)}, u32[]{:S(2)}) copy-start(f32[384,1536]{1,0:T(8,128)S(1)} %get-tuple-element.94.ot_ref) | copy-start | bytes 7077892
  145.7 7.9 %copy-start.5 = (f32[8,1536]{1,0:T(8,128)}, f32[8,1536]{1,0:T(8,128)S(1)}, u32[]{:S(2)}) copy-start(f32[8,1536]{1,0:T(8,128)S(1)} %get-tuple-element.95.lse_ref) | copy-start | bytes 147460
  145.7 3.5 copy-start.34
  248.8 19.5 %collective-permute-start.9 = (bf16[384,1536]{1,0:T(8,128)(2,1)}, bf16[384,1536]{1,0:T(8,128)(2,1)S(1)}, u32[]{:S(2)}, u32[]{:S(2)}) collective-permute-start(bf16[384,1536]{1,0:T(8,128)(2,1)} %pad_maximum_fusion.1.cot), channel_id=1, source_target_pairs={{0,1},{1,0},{2,3},{3,2},{4,5},{5,4},{6,7},{7,6},{8,9},{9,8},{10,11... | collective-permute-start | bytes 3538952 | tf_op jit(solution)/shard_map/ppermute | solution.py:26
  248.9 8.0 %copy-start.27 = (bf16[4,384,1536]{2,1,0:T(8,128)(2,1)S(1)}, bf16[4,384,1536]{2,1,0:T(8,128)(2,1)}, u32[]{:S(2)}) copy-start(bf16[4,384,1536]{2,1,0:T(8,128)(2,1)} %get-tuple-element.79) | copy-start | bytes 14155780
  248.9 8.0 %copy-start.30 = (bf16[2,768,1024]{2,1,0:T(8,128)(2,1)S(1)}, bf16[2,768,1024]{2,1,0:T(8,128)(2,1)}, u32[]{:S(2)}) copy-start(bf16[2,768,1024]{2,1,0:T(8,128)(2,1)} %get-tuple-element.82) | copy-start | bytes 9437188
  256.9 7.3 %copy-start.36 = (f32[1536,1024]{1,0:T(8,128)}, f32[1536,1024]{1,0:T(8,128)S(1)}, u32[]{:S(2)}) copy-start(f32[1536,1024]{1,0:T(8,128)S(1)} %fusion.14) | copy-start | bytes 18874372
  256.9 11.4 %copy-start.32 = (bf16[1024,1536]{1,0:T(8,128)(2,1)S(1)}, bf16[1024,1536]{1,0:T(8,128)(2,1)}, u32[]{:S(2)}) copy-start(bf16[1024,1536]{1,0:T(8,128)(2,1)} %get-tuple-element.84) | copy-start | bytes 9437188
  264.2 9.9 %copy-start.39 = (bf16[1536,1024]{1,0:T(8,128)(2,1)}, bf16[1536,1024]{1,0:T(8,128)(2,1)S(1)}, u32[]{:S(2)}) copy-start(bf16[1536,1024]{1,0:T(8,128)(2,1)S(1)} %get-tuple-element.83) | copy-start | bytes 9437188
  274.2 2.2 copy-start.7
  277.9 3.2 collective-permute-start.12
  277.9 8.2 %collective-permute-start.4 = (bf16[384,1536]{1,0:T(8,128)(2,1)}, bf16[384,1536]{1,0:T(8,128)(2,1)}, u32[]{:S(2)}, u32[]{:S(2)}) collective-permute-start(bf16[384,1536]{1,0:T(8,128)(2,1)} %pad_maximum_fusion.1.cot), channel_id=1, source_target_pairs={{0,8},{8,0},{1,9},{9,1},{2,10},{10,2},{3,11},{11,3},{4,12},{12,4},... | collective-permute-start | bytes 3538952 | tf_op jit(solution)/shard_map/ppermute | solution.py:22
  278.5 7.7 %collective-permute-start.10 = (bf16[384,1536]{1,0:T(8,128)(2,1)S(1)}, bf16[384,1536]{1,0:T(8,128)(2,1)}, u32[]{:S(2)}, u32[]{:S(2)}) collective-permute-start(bf16[384,1536]{1,0:T(8,128)(2,1)S(1)} %collective-permute-done.9), channel_id=1, source_target_pairs={{0,8},{8,0},{1,9},{9,1},{2,10},{10,2},{3,11},{11,3},{4,12},{12,4},... | collective-permute-start | bytes 3538952 | tf_op jit(solution)/shard_map/ppermute | solution.py:22
  278.5 7.7 %copy-start.40 = (bf16[1536,1024]{1,0:T(8,128)(2,1)S(1)}, bf16[1536,1024]{1,0:T(8,128)(2,1)}, u32[]{:S(2)}) copy-start(bf16[1536,1024]{1,0:T(8,128)(2,1)} %copy-done.39) | copy-start | bytes 9437188
  278.5 22.5 %collective-permute-start.11 = (bf16[384,1536]{1,0:T(8,128)(2,1)}, bf16[384,1536]{1,0:T(8,128)(2,1)S(1)}, u32[]{:S(2)}, u32[]{:S(2)}) collective-permute-start(bf16[384,1536]{1,0:T(8,128)(2,1)} %get-tuple-element.177), channel_id=1, source_target_pairs={{0,8},{8,0},{1,9},{9,1},{2,10},{10,2},{3,11},{11,3},{4,12},{12,4},... | collective-permute-start | bytes 3538952 | tf_op jit(solution)/shard_map/ppermute | solution.py:22
  283.0 27.5 %collective-permute-start.13 = (bf16[384,1536]{1,0:T(8,128)(2,1)S(1)}, bf16[384,1536]{1,0:T(8,128)(2,1)S(1)}, u32[]{:S(2)}, u32[]{:S(2)}) collective-permute-start(bf16[384,1536]{1,0:T(8,128)(2,1)S(1)} %add_convert_fusion.3), channel_id=1, source_target_pairs={{0,1},{1,0},{2,3},{3,2},{4,5},{5,4},{6,7},{7,6},{8,9},{9,8},{10,11... | collective-permute-start | bytes 3538952 | tf_op jit(solution)/shard_map/ppermute | solution.py:26
  295.3 15.2 %copy-start.6 = (f32[384,1536]{1,0:T(8,128)S(1)}, f32[384,1536]{1,0:T(8,128)}, u32[]{:S(2)}) copy-start(f32[384,1536]{1,0:T(8,128)} %get-tuple-element.87.resid) | copy-start | bytes 7077892
  295.3 63.8 %collective-permute-start.14 = (bf16[512,1536]{1,0:T(8,128)(2,1)S(1)}, bf16[512,1536]{1,0:T(8,128)(2,1)S(1)}, u32[]{:S(2)}, u32[]{:S(2)}) collective-permute-start(bf16[512,1536]{1,0:T(8,128)(2,1)S(1)} %broadcast_select_fusion), channel_id=1, source_target_pairs={{0,16},{16,0},{1,17},{17,1},{2,18},{18,2},{3,19},{19,3},{4,20},{20... | collective-permute-start | bytes 4718600 | tf_op jit(solution)/shard_map/ppermute | solution.py:26
  310.5 2.2 copy-start.33
  312.8 12.5 %copy-start.31 = (bf16[2,768,1024]{2,1,0:T(8,128)(2,1)S(1)}, bf16[2,768,1024]{2,1,0:T(8,128)(2,1)}, u32[]{:S(2)}) copy-start(bf16[2,768,1024]{2,1,0:T(8,128)(2,1)} %get-tuple-element.82) | copy-start | bytes 9437188
  325.3 9.9 %copy-start.29 = (bf16[2,768,1024]{2,1,0:T(8,128)(2,1)S(1)}, bf16[2,768,1024]{2,1,0:T(8,128)(2,1)}, u32[]{:S(2)}) copy-start(bf16[2,768,1024]{2,1,0:T(8,128)(2,1)} %get-tuple-element.81) | copy-start | bytes 9437188
  325.3 9.9 %copy-start.38 = (bf16[1536,1024]{1,0:T(8,128)(2,1)S(1)}, bf16[1536,1024]{1,0:T(8,128)(2,1)}, u32[]{:S(2)}) copy-start(bf16[1536,1024]{1,0:T(8,128)(2,1)} %get-tuple-element.175) | copy-start | bytes 9437188
  325.3 19.3 %slice-start = ((s8[4718592]{0:T(1024)(128)(4,1)}), s8[4194304]{0:T(1024)(128)(4,1)S(1)}, s32[]{:S(2)}) async-start(s8[4718592]{0:T(1024)(128)(4,1)} %bitcast.91), calls=%async_computation | async-start | bytes 8388608
  335.2 9.4 %slice-start.1 = ((s8[4718592]{0:T(1024)(128)(4,1)}), s8[524288]{0:T(1024)(128)(4,1)S(1)}, s32[]{:S(2)}) async-start(s8[4718592]{0:T(1024)(128)(4,1)} %bitcast.91), calls=%async_computation.1 | async-start | bytes 1048576
  344.6 7.8 %copy-start.37 = (bf16[1536,1024]{1,0:T(8,128)(2,1)S(1)}, bf16[1536,1024]{1,0:T(8,128)(2,1)}, u32[]{:S(2)}) copy-start(bf16[1536,1024]{1,0:T(8,128)(2,1)} %get-tuple-element.176) | copy-start | bytes 9437188
  439.2 4.5 copy-start.28
  439.2 4.5 copy-start.35
  443.8 10.8 %copy-start.16 = (bf16[512,768]{1,0:T(8,128)(2,1)S(1)}, bf16[512,768]{1,0:T(8,128)(2,1)}, u32[]{:S(2)}) copy-start(bf16[512,768]{1,0:T(8,128)(2,1)} %get-tuple-element.104) | copy-start | bytes 2359300
  443.8 14.8 %copy-start.15 = (bf16[384,1024]{1,0:T(8,128)(2,1)S(1)}, bf16[384,1024]{1,0:T(8,128)(2,1)}, u32[]{:S(2)}) copy-start(bf16[384,1024]{1,0:T(8,128)(2,1)} %get-tuple-element.105) | copy-start | bytes 2359300
  443.8 20.7 %copy-start.14 = (bf16[384,1024]{1,0:T(8,128)(2,1)S(1)}, bf16[384,1024]{1,0:T(8,128)(2,1)}, u32[]{:S(2)}) copy-start(bf16[384,1024]{1,0:T(8,128)(2,1)} %get-tuple-element.106) | copy-start | bytes 2359300
  448.4 16.1 %collective-permute-start.15 = (bf16[192,1536]{1,0:T(8,128)(2,1)}, bf16[192,1536]{1,0:T(8,128)(2,1)}, u32[]{:S(2)}, u32[]{:S(2)}) collective-permute-start(bf16[192,1536]{1,0:T(8,128)(2,1)} %get-tuple-element.101), channel_id=1, source_target_pairs={{0,16},{16,0},{1,17},{17,1},{2,18},{18,2},{3,19},{19,3},{4,20},{20... | collective-permute-start | bytes 1769480 | tf_op jit(solution)/shard_map/ppermute | solution.py:26
  451.5 69.7 %collective-permute-start.16 = (bf16[384,768]{1,0:T(8,128)(2,1)}, bf16[384,768]{1,0:T(8,128)(2,1)S(1)}, u32[]{:S(2)}, u32[]{:S(2)}) collective-permute-start(bf16[384,768]{1,0:T(8,128)(2,1)} %get-tuple-element.102), channel_id=1, source_target_pairs={{8,0},{0,4},{12,8},{4,12},{9,1},{1,5},{13,9},{5,13},{10,2},{2,6},{... | collective-permute-start | bytes 1769480 | tf_op jit(solution)/shard_map/ppermute | solution.py:131
  452.6 68.6 %collective-permute-start.17 = (bf16[384,768]{1,0:T(8,128)(2,1)}, bf16[384,768]{1,0:T(8,128)(2,1)S(1)}, u32[]{:S(2)}, u32[]{:S(2)}) collective-permute-start(bf16[384,768]{1,0:T(8,128)(2,1)} %get-tuple-element.103), channel_id=1, source_target_pairs={{8,4},{4,8},{9,5},{5,9},{10,6},{6,10},{11,7},{7,11},{24,20},{20,24... | collective-permute-start | bytes 1769480 | tf_op jit(solution)/shard_map/ppermute | solution.py:132
  454.5 66.7 %collective-permute-start.18 = (bf16[512,768]{1,0:T(8,128)(2,1)S(1)}, bf16[512,768]{1,0:T(8,128)(2,1)S(1)}, u32[]{:S(2)}, u32[]{:S(2)}) collective-permute-start(bf16[512,768]{1,0:T(8,128)(2,1)S(1)} %copy-done.16), channel_id=1, source_target_pairs={{2,0},{8,10},{3,1},{9,11},{6,4},{12,14},{7,5},{13,15},{18,16},{24,... | collective-permute-start | bytes 2359304 | tf_op jit(solution)/shard_map/ppermute | solution.py:65
  458.6 62.6 %collective-permute-start.19 = (bf16[384,1024]{1,0:T(8,128)(2,1)S(1)}, bf16[384,1024]{1,0:T(8,128)(2,1)S(1)}, u32[]{:S(2)}, u32[]{:S(2)}) collective-permute-start(bf16[384,1024]{1,0:T(8,128)(2,1)S(1)} %copy-done.15), channel_id=1, source_target_pairs={{2,0},{8,10},{3,1},{9,11},{6,4},{12,14},{7,5},{13,15},{18,16},{24,... | collective-permute-start | bytes 2359304 | tf_op jit(solution)/shard_map/ppermute | solution.py:65
  464.5 56.7 %collective-permute-start.20 = (bf16[384,1024]{1,0:T(8,128)(2,1)S(1)}, bf16[384,1024]{1,0:T(8,128)(2,1)S(1)}, u32[]{:S(2)}, u32[]{:S(2)}) collective-permute-start(bf16[384,1024]{1,0:T(8,128)(2,1)S(1)} %copy-done.14), channel_id=1, source_target_pairs={{2,0},{8,10},{3,1},{9,11},{6,4},{12,14},{7,5},{13,15},{18,16},{24,... | collective-permute-start | bytes 2359304 | tf_op jit(solution)/shard_map/ppermute | solution.py:65
  521.2 9.9 %copy-start.18 = (bf16[384,768]{1,0:T(8,128)(2,1)}, bf16[384,768]{1,0:T(8,128)(2,1)S(1)}, u32[]{:S(2)}) copy-start(bf16[384,768]{1,0:T(8,128)(2,1)S(1)} %collective-permute-done.16) | copy-start | bytes 1769476
  521.2 9.9 %copy-start.20 = (bf16[384,768]{1,0:T(8,128)(2,1)}, bf16[384,768]{1,0:T(8,128)(2,1)S(1)}, u32[]{:S(2)}) copy-start(bf16[384,768]{1,0:T(8,128)(2,1)S(1)} %collective-permute-done.17) | copy-start | bytes 1769476
  648.7 4.5 copy-start.17
  648.7 5.6 copy-start.12
  653.2 3.3 copy-start.11
  656.5 2.2 copy-start.10
  658.7 2.0 copy-start.19
  658.7 2.0 copy-start.21
  660.7 1.7 copy-start.13

commit v4 on v3

--- a/solution.py
+++ b/solution.py
@@ -773,6 +773,24 @@
             copy.wait()
 
 
+def by_chunks(span, body):
+    def run(n, carry):
+        body(pl.ds(pl.multiple_of(span.start + n * CHUNK, CHUNK), CHUNK))
+        return carry
+
+    lax.fori_loop(0, span.size // CHUNK, run, 0)
+
+
+def add_into(value, *others):
+    def body(rows):
+        total = value[rows, :].astype(F32)
+        for other in others:
+            total = total + other[rows, :].astype(F32)
+        value[rows, :] = total.astype(BF16)
+
+    by_chunks(pl.ds(0, value.shape[0]), body)
+
+
 class Reduce:
     def __init__(self, wires, psize, part, near, mid, far, spans):
         self.wires, self.psize, self.part = wires, psize, part
@@ -789,23 +807,33 @@
         for bit in reversed(range(1, self.psize)):
             for i, span in enumerate(self.spans):
                 self.near_copies[bit, i].wait_recv()
-                self.mid[bit - 1, span] = (
-                    self.part[2 * bit, span].astype(F32) + self.near[bit, span].astype(F32)
-                ).astype(BF16)
+
+                def add(rows, bit=bit):
+                    self.mid[bit - 1, rows] = (
+                        self.part[2 * bit, rows].astype(F32) + self.near[bit, rows].astype(F32)
+                    ).astype(BF16)
+
+                by_chunks(span, add)
                 self.far_copies[bit, i] = w.send(
                     self.mid.at[bit - 1, span], self.far.at[bit - 1, span], {"p": w.p ^ bit}
                 )
 
-    def rows(self, i):
+    def each(self, i, body):
         span = self.spans[i]
         self.near_copies[0, i].wait_recv()
-        total = self.part[0, span].astype(F32) + self.near[0, span].astype(F32)
         for bit in range(1, self.psize):
             self.far_copies[bit, i].wait_recv()
-            total = total + self.far[bit - 1, span].astype(F32)
-        return total
-
-
+
+        def run(rows):
+            total = self.part[0, rows].astype(F32) + self.near[0, rows].astype(F32)
+            for bit in range(1, self.psize):
+                total = total + self.far[bit - 1, rows].astype(F32)
+            body(rows, total)
+
+        by_chunks(span, run)
+
+
+CHUNK = 32
 PIECES = 3
 
 
@@ -818,11 +846,12 @@
     gained = gain * grad
     inner = jnp.sum(value * gained, axis=1, keepdims=True)
     result = base + rms * gained - value * (rms * rms * rms) * inner / D
-    return result, jnp.sum(grad * value * rms, axis=0, keepdims=True)
+    parts = grad * value * rms
+    return result, sum(parts[n : n + 8] for n in range(0, parts.shape[0], 8))
 
 
 def enter_kernel(
-    psize, x_ref, gain_ref, qkv_shard, forget_shard, out_shard, xin, g, proj, out,
+    psize, x_ref, gain_own, codes_own, qkv_shard, forget_shard, out_shard, xin, g, proj, out, gain_ref, codes,
     own, qkv_stage, forget_stage, out_stage, send_sem, recv_sem, local_sem,
 ):
     w = Wires(send_sem, recv_sem, local_sem)
@@ -906,16 +935,28 @@
 
         return start, arrive, close
 
+    gain_copy = w.send(gain_own, gain_ref.at[:, pl.ds(half, half)], {"x": 1 - w.x})
+    code_copies = [
+        w.send(codes_own, codes.at[1], {"x": 1 - w.x}),
+        w.send(codes_own, codes.at[2], {"k": 1 - w.k}),
+        w.send(codes_own, codes.at[3], {"k": 1 - w.k, "x": 1 - w.x}),
+    ]
+    codes[0] = codes_own[...]
     start, arrive, close = spread(x_ref, xin, [(i * size, size) for i in range(PIECES)])
     start()
     qkv.start()
     forget.start()
     share = Share(w, psize, own, g, spans)
-    gain = gain_ref[0:1, :]
+    gain_ref[:, pl.ds(0, half)] = gain_own[...]
+    gain_copy.wait_recv()
     for i, span in enumerate(spans):
         arrive(i)
-        value = xin[span, :].astype(F32)
-        own[span, :] = (value * inverse_rms(value) * gain).astype(BF16)
+
+        def norm(rows):
+            value = xin[rows, :].astype(F32)
+            own[rows, :] = (value * inverse_rms(value) * gain_ref[0:1, :]).astype(BF16)
+
+        by_chunks(span, norm)
         share.send(i)
     close()
     for fetch in (qkv, forget, out_fetch):
@@ -934,6 +975,8 @@
     share.wait()
     for fetch in (qkv, forget, out_fetch):
         fetch.wait()
+    for copy in code_copies:
+        copy.wait_recv()
     w.close()
 
 
@@ -957,22 +1000,26 @@
     down_fetch.start()
     for fetch in fetches:
         fetch.store()
-    gate_fetch.relay_over(0)
-    gate_fetch.relay_over(1)
+    for i in range(2):
+        gate_fetch.relay_over(i)
+    for i in range(2):
+        down_fetch.relay(i)
+    for i in range(2):
+        up_fetch.relay_over(i)
     share = Share(w, psize, own, g, spans)
-    gain = gain_ref[1:2, :]
-    for i, span in enumerate(spans):
-        value = reduce.rows(i) + xin[span, :].astype(F32)
-        resid[span, :] = value
-        own[span, :] = (value * inverse_rms(value) * gain).astype(BF16)
+    for i in range(PIECES):
+
+        def norm(rows, total):
+            value = total + xin[rows, :].astype(F32)
+            resid[rows, :] = value
+            own[rows, :] = (value * inverse_rms(value) * gain_ref[1:2, :]).astype(BF16)
+
+        reduce.each(i, norm)
         share.send(i)
     for i in range(2):
-        up_fetch.relay_over(i)
-        down_fetch.relay(i)
+        down_fetch.relay_over(i)
     for i in range(PIECES):
         share.relay(i)
-    for i in range(2):
-        down_fetch.relay_over(i)
     share.wait()
     for fetch in fetches:
         fetch.wait()
@@ -980,8 +1027,9 @@
 
 
 class EarlySum:
-    def __init__(self, wires, part, value, over, across, result, pieces):
+    def __init__(self, wires, part, value, over, across, result, pieces, offset=0, got=None):
         w = self.wires = wires
+        self.offset, self.got = offset, got
         self.part, self.value, self.over, self.across, self.result = part, value, over, across, result
         self.count, self.half_rows = pieces, value.shape[1]
         self.size = self.half_rows // pieces
@@ -994,7 +1042,7 @@
         return pl.ds(i * self.size, self.size)
 
     def load_copy(self, half):
-        start = pl.multiple_of((self.wires.o % 2) * self.half_rows, 16)
+        start = pl.multiple_of(self.offset + (self.wires.o % 2) * self.half_rows, 16)
         return pltpu.make_async_copy(
             self.part.at[half, pl.ds(start, self.half_rows)],
             self.value.at[half],
@@ -1007,7 +1055,7 @@
 
     def over_copy(self, half, i):
         w = self.wires
-        start = pl.multiple_of((1 - w.o % 2) * self.half_rows + i * self.size, 16)
+        start = pl.multiple_of(self.offset + (1 - w.o % 2) * self.half_rows + i * self.size, 16)
         return w.copy(
             self.part.at[half, pl.ds(start, self.size)],
             self.over.at[half, self.span(i)],
@@ -1035,11 +1083,12 @@
     def pass_on(self, i):
         if i == 0:
             self.load_copy(1).wait()
-        self.over_copy(1, i).wait_recv()
         span = self.span(i)
-        self.value[1, span] = (
-            self.value[1, span].astype(F32) + self.over[1, span].astype(F32)
-        ).astype(BF16)
+        if self.got is None:
+            self.over_copy(1, i).wait_recv()
+            add_into(self.value.at[1, span], self.over.at[1, span])
+        else:
+            add_into(self.value.at[1, span], self.got.at[span])
         self.across_copy(i).start()
 
     def finish(self, i):
@@ -1048,57 +1097,66 @@
         self.over_copy(0, i).wait_recv()
         self.across_copy(i).wait_recv()
         span = self.span(i)
-        total = self.value[0, span].astype(F32) + self.over[0, span].astype(F32)
-        self.value[0, span] = (total + self.across[span].astype(F32)).astype(BF16)
-        self.keep_copy(i).start()
+        add_into(self.value.at[0, span], self.over.at[0, span], self.across.at[span])
+        if self.result is not None:
+            self.keep_copy(i).start()
 
     def close(self):
         for i in range(self.count):
             for half in range(2):
-                self.over_copy(half, i).wait_send()
+                if half == 0 or self.got is None:
+                    self.over_copy(half, i).wait_send()
             self.across_copy(i).wait_send()
-            self.keep_copy(i).wait()
+            if self.result is not None:
+                self.keep_copy(i).wait()
 
 
 def backward_exchange_kernel(
-    psize, part, resid, cot, gain_ref, down_own, down_other, gate_part, up_part,
-    grad_resid, g, gain_grad, down_sum, gate_sum, up_sum,
+    psize, part, resid, cot, gain_ref, down_own, down_other, gate_part, gate_got, up_part,
+    grad_resid, g, gain_grad, down_sum, pair_sum,
     near, mid, far, own, down_across, gate_val, gate_over, gate_across, up_val, up_over, up_across,
     send_sem, recv_sem, local_sem,
 ):
     w = Wires(send_sem, recv_sem, local_sem)
-    gate = EarlySum(w, gate_part, gate_val, gate_over, gate_across, gate_sum, 2)
-    up = EarlySum(w, up_part, up_val, up_over, up_across, up_sum, 2)
+    gate = EarlySum(w, gate_part, gate_val, gate_over, gate_across, pair_sum.at[0], 2, got=gate_got)
+    up = EarlySum(w, up_part, up_val, up_over, up_across, pair_sum.at[1], 2)
     gate.load()
     up.load()
     w.greet(partners(w, psize, over_o=2))
     spans = row_spans(own.shape[0], PIECES)
     reduce = Reduce(w, psize, part, near, mid, far, spans)
     down_copy = w.send(down_other, down_across, {"x": 1 - w.x})
-    gate.start(1)
+    gate.start(0)
     up.start(1)
-    reduce.start()
-    gate.start(0)
     up.start(0)
     for i in range(2):
         gate.pass_on(i)
+    reduce.start()
     share = Share(w, psize, own, g, spans)
-    gain = gain_ref[1:2, :]
-    gain_sum = jnp.zeros((1, D), F32)
-    for i, span in enumerate(spans):
-        grad, gain_part = norm_back(reduce.rows(i), resid[span, :], cot[span, :].astype(F32), gain)
-        grad_resid[span, :] = grad
-        own[span, :] = grad.astype(BF16)
-        gain_sum = gain_sum + gain_part
+    gain_grad[...] = jnp.zeros(gain_grad.shape, F32)
+
+    def back(rows, total):
+        grad, gain_part = norm_back(total, resid[rows, :], cot[rows, :].astype(F32), gain_ref[1:2, :])
+        grad_resid[rows, :] = grad
+        own[rows, :] = grad.astype(BF16)
+        gain_grad[...] += gain_part
+
+    for i in range(PIECES):
+        reduce.each(i, back)
         share.send(i)
-    gain_grad[...] = jnp.broadcast_to(gain_sum, gain_grad.shape)
     for i in range(2):
         up.pass_on(i)
-    down_copy.wait_recv()
-    down_sum[...] = (down_own[...].astype(F32) + down_across[...].astype(F32)).astype(BF16)
     share.relay(0)
     for i in range(2):
         gate.finish(i)
+    down_copy.wait_recv()
+
+    def add_down(rows):
+        down_sum[rows, :] = (
+            down_own[rows, :].astype(F32) + down_across[rows, :].astype(F32)
+        ).astype(BF16)
+
+    by_chunks(pl.ds(0, down_sum.shape[0]), add_down)
     for i in range(1, PIECES):
         share.relay(i)
     for i in range(2):
@@ -1231,9 +1289,7 @@
 
     def add(self, stage, i):
         span = self.spans[i]
-        self.value[span, :] = (
-            self.value[span, :].astype(F32) + self.buffers[stage][span, :].astype(F32)
-        ).astype(BF16)
+        add_into(self.value.at[span], self.buffers[stage].at[span])
 
     def end(self, stage, i):
         w, kind = self.wires, self.stages[stage]
@@ -1285,16 +1341,21 @@
 
 
 def leave_kernel(
-    psize, osize, proj_pieces, part, stream, base, gain_ref, small_in, proj_own, proj_other, out_own, out_other,
-    up_in, gate_in, down_in, block, small, proj_sum, out_sum, up_sum, gate_sum, down_sum,
-    near, mid, far, kept, proj_val, out_val, up_val, gate_val, down_val, proj_bufs, out_bufs, small_other, small_bufs,
+    psize, osize, pieces, part, stream, base, gain_ref, small_in, proj_in, out_own, out_other,
+    pair_in, down_in, block, small, first_sum, second_sum, out_sum, up_sum, gate_sum, down_sum,
+    near, mid, far, kept, first_val, second_val, out_val, up_val, gate_val, down_val, first_bufs,
+    second_over, second_across, second_bufs, out_bufs, small_other, small_bufs, gain_acc,
     send_sem, recv_sem, local_sem,
 ):
     w = Wires(send_sem, recv_sem, local_sem)
+    split = first_val.shape[0]
+    second = EarlySum(w, proj_in, second_val, second_over, second_across, None, 2, split)
+    second.load()
     loads = [
         w.local(source, target)
         for source, target in (
-            (up_in, up_val), (gate_in, gate_val), (down_in, down_val), (out_own, out_val), (proj_own, proj_val)
+            (pair_in.at[1], up_val), (pair_in.at[0], gate_val), (down_in, down_val), (out_own, out_val),
+            (proj_in.at[0, pl.ds(0, split)], first_val),
         )
     ]
     w.greet(partners(w, psize, away=True, over_o=osize))
@@ -1303,24 +1364,29 @@
     size = rows // PIECES
     bits = bits_of(osize)
 
-    proj = Chain(
-        w, osize, proj_val, ["x", "h"] + bits + ["k"], [proj_bufs.at[i] for i in range(2 + len(bits))],
-        proj_sum, proj_pieces,
+    first = Chain(
+        w, osize, first_val, ["x", "h"] + bits + ["k"], [first_bufs.at[i] for i in range(2 + len(bits))],
+        first_sum, pieces,
     )
-    proj.other = proj_other
+    first.other = proj_in.at[1, pl.ds(0, split)]
+    late = Chain(
+        w, osize, second_val.at[0], ["h"] + bits[1:], [second_bufs.at[i] for i in range(len(bits))], None, 2
+    )
     out = Chain(w, osize, out_val, ["x", "h"] + bits[1:], [out_bufs.at[i] for i in range(1 + len(bits))], None, 1)
     out.other = out_other
-    out_spread = Spread(w, out_val, out_sum)
     spreads = [Spread(w, up_val, up_sum), Spread(w, gate_val, gate_sum), Spread(w, down_val, down_sum)]
+    last_spreads = [Spread(w, out_val, out_sum), Spread(w, second_val.at[0], second_sum)]
     reduce = Reduce(w, psize, part, near, mid, far, spans)
+    second.start(1)
+    for i in range(pieces):
+        first.start(0, i)
     out.start(0, 0)
-    for i in range(proj_pieces):
-        proj.start(0, i)
+    second.start(0)
     for load in loads:
         load.wait()
+    reduce.start()
     for spread in spreads:
         spread.start()
-    reduce.start()
 
     near_slots = [w.slot() for _ in spans]
     far_slots = [w.slot() for _ in spans]
@@ -1342,16 +1408,26 @@
     def cross_far(i):
         return w.copy(kept.at[1, spans[i]], target(i), {"k": 1 - w.k, "x": 1 - w.x}, far_slots[i])
 
+    for i in range(2):
+        second.pass_on(i)
+    first.step(0, 0)
+    for i in range(1, pieces):
+        first.step(0, i)
+        first.step(1, i - 1)
     out.step(0, 0)
-    for i in range(proj_pieces):
-        proj.step(0, i)
-    gain = gain_ref[0:1, :]
-    gain_sum = jnp.zeros((1, D), F32)
-    for i, span in enumerate(spans):
-        grad, gain_part = norm_back(reduce.rows(i), stream[span, :].astype(F32), base[span, :], gain)
-        gain_sum = gain_sum + gain_part
-        kept[0, span, :] = grad[:, :half].astype(BF16)
-        kept[1, span, :] = grad[:, half:].astype(BF16)
+    second.finish(0)
+    late.start(0, 0)
+    first.step(1, pieces - 1)
+    gain_acc[...] = jnp.zeros(gain_acc.shape, F32)
+
+    def back(rows_, total):
+        grad, gain_part = norm_back(total, stream[rows_, :].astype(F32), base[rows_, :], gain_ref[0:1, :])
+        gain_acc[...] += gain_part
+        kept[0, rows_, :] = grad[:, :half].astype(BF16)
+        kept[1, rows_, :] = grad[:, half:].astype(BF16)
+
+    for i in range(PIECES):
+        reduce.each(i, back)
 
         @pl.when(w.same)
         def _():
@@ -1363,24 +1439,29 @@
             cross_near(i).start()
             cross_far(i).start()
 
+        if i == 0:
+            second.finish(1)
+            late.start(0, 1)
+
+    gain_sum = jnp.sum(gain_acc[...], axis=0, keepdims=True)
     row = lax.broadcasted_iota(jnp.int32, (8, half), 0)
     small[...] = jnp.where(row == 0, gain_sum[:, :half], small_in[:, :half])
     small_other[...] = jnp.where(row == 0, gain_sum[:, half:], small_in[:, half:])
     total = SmallSum(w, psize, osize, small, small_other, small_bufs)
     total.start()
     out.run(1)
-    out_spread.start()
-    for spread in spreads:
-        spread.relay()
+    last_spreads[0].start()
+    steps = [lambda a=a: late.step(*a) for a in late.order(0)] + [last_spreads[1].start]
+    steps += [spread.relay for spread in spreads] + [lambda a=a: first.step(*a) for a in first.order(2)]
+    steps += [last_spreads[0].relay, last_spreads[1].relay]
     smalls = list(range(len(total.devices)))
-    for n, (stage, i) in enumerate(proj.order(1)):
-        proj.step(stage, i)
-        if n % 2 and smalls:
+    for n, step in enumerate(steps):
+        step()
+        if n % 2 == 0 and smalls:
             total.step(smalls.pop(0))
     for step in smalls:
         total.step(step)
-    out_spread.relay()
-    for spread in spreads + [out_spread]:
+    for spread in spreads + last_spreads:
         spread.wait()
     for i in range(PIECES):
         @pl.when(w.same)
@@ -1395,8 +1476,8 @@
             cross_far(i).wait()
             same_send(i).wait_recv()
 
-    proj.close()
-    out.close()
+    for chain in (first, second, late, out):
+        chain.close()
     w.close()
 
 
@@ -1437,7 +1518,7 @@
     ]
 
 
-def enter(psize, layer_input, gains, qkv_weight, forget_weight, out_weight):
+def enter(psize, layer_input, gains, codes, qkv_weight, forget_weight, out_weight):
     rows = layer_input.shape[0] // 2
     half, width = qkv_weight.shape
     columns = width + forget_weight.shape[1]
@@ -1450,12 +1531,14 @@
             sds((2 * psize, rows, D), BF16),
             sds((2, half, columns), BF16),
             sds((out_weight.shape[0], 2 * half), BF16),
+            sds((8, D), F32),
+            sds((4,) + codes.shape, jnp.int32),
         ),
-        (VMEM, ANY, ANY, ANY),
-        [ANY, VMEM, ANY, ANY, ANY],
+        (VMEM, ANY, ANY, ANY, VMEM, VMEM),
+        [ANY, VMEM, VMEM, ANY, ANY, ANY],
         [pltpu.VMEM((rows, D), BF16)]
         + [pltpu.VMEM(value.shape, BF16) for value in (qkv_weight, forget_weight, out_weight)],
-        (layer_input, gains, qkv_weight, forget_weight, out_weight),
+        (layer_input, gains, codes, qkv_weight, forget_weight, out_weight),
     )
 
 
@@ -1484,7 +1567,7 @@
     )
 
 
-def backward_exchange(psize, part, resid, cot, gains, down_own, down_other, gate_part, up_part):
+def backward_exchange(psize, part, resid, cot, gains, down_own, down_other, gate_part, gate_got, up_part):
     rows = resid.shape[0]
 
     def early(value):
@@ -1495,9 +1578,6 @@
             pltpu.VMEM((2,) + shape, BF16),
             pltpu.VMEM(shape, BF16),
         ]
-
-    def kept(value):
-        return sds((value.shape[1] // 2, value.shape[2]), BF16)
 
     return exchange_call(
         functools.partial(backward_exchange_kernel, psize),
@@ -1508,51 +1588,66 @@
             sds((2 * psize, rows, D), BF16),
             sds((8, D), F32),
             sds(down_own.shape, BF16),
-            kept(gate_part),
-            kept(up_part),
+            sds((2, gate_part.shape[1] // 2, gate_part.shape[2]), BF16),
         ),
-        (VMEM, ANY, VMEM, VMEM, ANY, ANY),
-        [VMEM, VMEM, VMEM, VMEM, VMEM, ANY, ANY, ANY],
+        (VMEM, ANY, VMEM, VMEM, ANY),
+        [VMEM, VMEM, VMEM, VMEM, VMEM, ANY, ANY, VMEM, ANY],
         sum_scratch(psize, rows)
         + [pltpu.VMEM((rows, D), BF16), pltpu.VMEM(down_own.shape, BF16)]
         + early(gate_part)
         + early(up_part),
-        (part, resid, cot, gains, down_own, down_other, gate_part, up_part),
+        (part, resid, cot, gains, down_own, down_other, gate_part, gate_got, up_part),
     )
 
 
-def leave(psize, osize, part, stream, base, gains, small, proj_own, proj_other, out_own, out_other, up, gate, down):
+def leave(psize, osize, part, stream, base, gains, small, proj, out_own, out_other, pair, down):
     rows = stream.shape[0]
     bits = len(bits_of(osize))
     half = D // 2
-
-    def buffers(count, value):
-        return pltpu.VMEM((count,) + value.shape, BF16)
-
-    def both(value):
-        return sds((2,) + value.shape, BF16)
+    columns = proj.shape[2]
+    split = proj.shape[1] // 2
+
+    def scratch(*shape):
+        return pltpu.VMEM(shape, BF16)
+
+    def both(shape):
+        return sds((2,) + shape, BF16)
 
     return exchange_call(
-        functools.partial(leave_kernel, psize, osize, 6),
+        functools.partial(leave_kernel, psize, osize, 3),
         "leave",
         4,
         (
             sds((2 * rows, half), BF16),
             sds((8, half), F32),
-            sds(proj_own.shape, BF16),
-            both(out_own),
-            both(up),
-            both(gate),
-            both(down),
+            sds((split, columns), BF16),
+            both((split // 2, columns)),
+            both(out_own.shape),
+            both(pair.shape[1:]),
+            both(pair.shape[1:]),
+            both(down.shape),
         ),
-        (ANY, VMEM, ANY, ANY, ANY, ANY, ANY),
-        [VMEM] * 5 + [ANY] * 7,
+        (ANY, VMEM, ANY, ANY, ANY, ANY, ANY, ANY),
+        [VMEM] * 5 + [ANY] * 5,
         sum_scratch(psize, rows)
-        + [pltpu.VMEM((2, rows, half), BF16)]
-        + [pltpu.VMEM(value.shape, BF16) for value in (proj_own, out_own, up, gate, down)]
-        + [buffers(2 + bits, proj_own), buffers(1 + bits, out_own)]
-        + [pltpu.VMEM((8, half), F32), pltpu.VMEM((3 + len(bits_of(psize)) + bits, 8, half), F32)],
-        (part, stream, base, gains, small, proj_own, proj_other, out_own, out_other, up, gate, down),
+        + [
+            scratch(2, rows, half),
+            scratch(split, columns),
+            scratch(2, split // 2, columns),
+            scratch(*out_own.shape),
+            scratch(*pair.shape[1:]),
+            scratch(*pair.shape[1:]),
+            scratch(*down.shape),
+            scratch(2 + bits, split, columns),
+            scratch(2, split // 2, columns),
+            scratch(split // 2, columns),
+            scratch(bits, split // 2, columns),
+            scratch(1 + bits, *out_own.shape),
+            pltpu.VMEM((8, half), F32),
+            pltpu.VMEM((3 + len(bits_of(psize)) + bits, 8, half), F32),
+            pltpu.VMEM((8, D), F32),
+        ],
+        (part, stream, base, gains, small, proj, out_own, out_other, pair, down),
     )
 
 
@@ -1611,22 +1706,12 @@
 
         prompt_len, branch_len = prompt_doc.shape[1], branch_seg.shape[1]
         packed = jnp.concatenate([prompt_doc[0], branch_seg[0], branch_doc[0]])
-        sibling = swap(packed, "k")
-        of_x = jnp.where(core == xpos, packed, sibling)
-        of_peer = jnp.where(core == xpos, sibling, packed)
-        from_peer = swap(of_peer, "x")
-        packed = jnp.where(hpos == xpos, of_x, from_peer)
-        prompt_ids = packed[:prompt_len]
-        branch_ids = packed[prompt_len : prompt_len + branch_len]
-        branch_docs = packed[prompt_len + branch_len :]
-        gains = jnp.stack([attn_gain, ffn_gain])
-        gains = jnp.concatenate([gains, swap(gains, "x")], axis=1)
-        gain_a, gain_b = gains[0], gains[1]
+        code_rows = -(-packed.shape[0] // (8 * LANES)) * 8
+        packed = jnp.pad(packed, (0, code_rows * LANES - packed.shape[0])).reshape(code_rows, LANES)
+        own_gains = jnp.concatenate([jnp.stack([attn_gain, ffn_gain]), jnp.zeros((6, feat), F32)])
         bias = jnp.where(home, forget_bias, lax.ppermute(forget_bias, ("k", "h"), [(1, 2), (2, 1)]))
         bias = jnp.concatenate([bias, jnp.zeros((lane_pad,), F32)])
-        kcol, qrow, flags = group_codes(prompt_ids, branch_ids, branch_docs)
-
-        gains8 = jnp.concatenate([gains, jnp.zeros((6, D), F32)])
+
         forget_wide = jnp.concatenate(
             [forget_weight, jnp.zeros((forget_weight.shape[0], lane_pad), BF16)], axis=1
         )
@@ -1634,35 +1719,62 @@
         if width % LANES:
             spare = jnp.zeros((qkv_weight.shape[0], LANES - width % LANES), BF16)
             first_part = jnp.concatenate([qkv_weight, forget_wide, spare], axis=1)
-        xin, normed_a_all, w_proj, w_out = enter(
-            psize, layer_input, gains8, first_part, second_part, out_weight
-        )
+        xin, normed_a_all, w_proj, w_out, gains8, codes = enter(
+            psize, layer_input, own_gains, packed, first_part, second_part, out_weight
+        )
+        packed = lax.dynamic_index_in_dim(
+            codes, (core ^ xpos) * 2 + (xpos ^ hpos), 0, keepdims=False
+        ).reshape(-1)
+        prompt_ids = packed[:prompt_len]
+        branch_ids = packed[prompt_len : prompt_len + branch_len]
+        branch_docs = packed[prompt_len + branch_len : prompt_len + branch_len + branch_doc.shape[1]]
+        kcol, qrow, flags = group_codes(prompt_ids, branch_ids, branch_docs)
         normed_a_all = normed_a_all.reshape(-1, D)
         w_proj = w_proj.reshape(D, -1)[:, : width + LANES]
 
         projected = matmul(normed_a_all, w_proj)
         qkv = projected[:, :width].astype(BF16).reshape(count, -1, width)
         logit = (projected[:, width:] + bias).reshape(count, -1, LANES)
-        qkv, logit = lax.optimization_barrier((qkv, logit))
-        gate_got = fetch_home_away(tie(take_half(gate_weight, opos % 2), qkv))
-        up_got = fetch_home_away(tie(take_half(up_weight, opos % 2), qkv))
-        cot = spread_tokens(tie(out_cotangent, qkv), core, same)
+        cot_near, cot_far = take_half(out_cotangent, core), take_half(out_cotangent, 1 - core)
+        qkv, logit, kcol, qrow, flags, gate_half, up_half, cot_first, cot_near, cot_far = lax.optimization_barrier(
+            (
+                qkv,
+                logit,
+                kcol,
+                qrow,
+                flags,
+                take_half(gate_weight, opos % 2),
+                take_half(up_weight, opos % 2),
+                jnp.where(same, cot_far, cot_near),
+                cot_near,
+                cot_far,
+            )
+        )
+        gate_got, up_got = fetch_home_away(gate_half), fetch_home_away(up_half)
+        cot_first = lax.ppermute(cot_first, ("k", "x"), SPREAD_A)
+        cot_second = lax.ppermute(cot_far, ("k", "x"), SPREAD_B)
         attended, *saved = attention_forward(qkv, logit, kcol, qrow, flags, heads, prompt_len)
-        attended = tie(attended.reshape(-1, heads * DH), gate_got, up_got, cot)
+        attended, gate_got, up_got, cot_first, cot_second, *saved = lax.optimization_barrier(
+            (attended, gate_got, up_got, cot_first, cot_second, *saved)
+        )
+        attended = attended.reshape(-1, heads * DH)
+        cot = jnp.concatenate(
+            [jnp.where(same, cot_near, cot_first), jnp.where(same, cot_first, cot_second)], axis=1
+        )
         part = matmul(attended, w_out).astype(BF16).reshape(count, -1, D)
         resid, normed_b_all, w_gate, w_up, w_down = forward_exchange(
             psize, part, xin, gains8, gate_weight, gate_got, up_weight, up_got, down_weight
         )
         normed_b_all = normed_b_all.reshape(-1, D)
         w_gate, w_up = w_gate.reshape(D, -1), w_up.reshape(D, -1)
-        cot_far = far_blocks(tie(cot, normed_b_all))
+        cot_others = far_blocks(tie(cot, normed_b_all))
         gate_pre = matmul(normed_b_all, w_gate)
         up_pre = matmul(normed_b_all, w_up)
         gate_sig = jax.nn.sigmoid(gate_pre)
         gate_act = gate_pre * gate_sig
         hidden = (gate_act * up_pre).astype(BF16)
-        hidden = tie(hidden, *cot_far)
-        cot_all = all_blocks(cot, cot_far)
+        hidden = tie(hidden, *cot_others)
+        cot_all = all_blocks(cot, cot_others)
 
         def finish(total, axis_bits):
             for bit in axis_bits:
@@ -1678,13 +1790,17 @@
         grad_hidden = contract_cols(tie(cot_all, out_sums[0]), w_down)
         grad_gate = (grad_hidden * up_pre * gate_sig * (1.0 + gate_pre * (1.0 - gate_sig))).astype(BF16)
         grad_up = (grad_hidden * gate_act).astype(BF16)
-        gate_part = contract_rows(normed_b_all, grad_gate).astype(BF16)
-        up_part = contract_rows(normed_b_all, grad_up).astype(BF16)
+        gate_part = contract_rows(normed_b_all, grad_gate).astype(BF16).reshape(2, feat, -1)
+        gate_got = xor_swap(take_half(gate_part[1], 1 - opos % 2), "o", osize, 1)
+        grad_gate, grad_up = lax.optimization_barrier((grad_gate, grad_up, gate_part))[:2]
+        up_part = contract_rows(normed_b_all, grad_up).astype(BF16).reshape(2, feat, -1)
         part = (contract_cols(grad_gate, w_gate) + contract_cols(grad_up, w_up)).astype(BF16)
-        part = tie(part, *out_far)
+        part, up_part, gate_got, down_moved, *out_far = lax.optimization_barrier(
+            (part, up_part, gate_got, down_moved, *out_far)
+        )
         layer_output = (resid + total_of(out_sums[0], out_far)).astype(BF16)
         down_total = add_parts(down_keep, down_moved)
-        grad_resid, grad_branch_all, ffn_gain_part, down_total, gate_total, up_total = backward_exchange(
+        grad_resid, grad_branch_all, ffn_gain_part, down_total, pair_total = backward_exchange(
             psize,
             part.reshape(count, -1, D),
             resid,
@@ -1692,18 +1808,19 @@
             gains8,
             down_total[:, :feat],
             down_total[:, feat:],
-            gate_part.reshape(2, feat, -1),
-            up_part.reshape(2, feat, -1),
+            gate_part,
+            gate_got,
+            up_part,
         )
         grad_branch_all = grad_branch_all.reshape(-1, D)
         grad_attended = contract_cols(grad_branch_all, w_out).astype(BF16)
         out_part = contract_rows(attended, grad_branch_all).astype(BF16)
         out_keep, out_give = split_rows(out_part, high)
-        grad_attended, out_keep, out_give, *totals = lax.optimization_barrier(
-            (grad_attended, out_keep, out_give, down_total, gate_total, up_total) + unspread_parts(layer_output, same)
-        )
-        totals, (own_part, near_part, far_part) = totals[:3], totals[3:]
-        moved = [to_home(value) for value in totals]
+        grad_attended, out_keep, out_give, down_total, pair_total, *block_parts = lax.optimization_barrier(
+            (grad_attended, out_keep, out_give, down_total, pair_total) + unspread_parts(layer_output, same)
+        )
+        own_part, near_part, far_part = block_parts
+        moved = [to_home(down_total), to_home(pair_total)]
         out_moved = xor_swap(out_give, "o", osize, 1)
         near_moved, far_moved = unspread_moves(near_part, far_part)
         grad_proj, bias_sums = attention_backward(
@@ -1716,8 +1833,9 @@
         grad_proj = grad_proj.reshape(-1, width + LANES)
         proj_part = contract_rows(normed_a_all, grad_proj).astype(BF16)
         part = contract_cols(grad_proj, w_proj).astype(BF16).reshape(count, -1, D)
-        down_total, gate_total, up_total = (
-            finish(add_parts(value, other), obits[1:]) for value, other in zip(totals, moved)
+        down_total, pair_total = (
+            finish(add_parts(value, other), obits[1:])
+            for value, other in zip((down_total, pair_total), moved)
         )
         out_total = add_parts(out_keep, out_moved)
 
@@ -1725,9 +1843,9 @@
             (jnp.arange(2 * psize) == core * psize + ppos)[:, None], bias_sums[:1, :heads], 0.0
         ).reshape(-1)
         slots = jnp.concatenate([slots, jnp.zeros((feat - slots.shape[0],), F32)])
-        small = jnp.stack([jnp.zeros((D,), F32), ffn_gain_part[0], jnp.concatenate([slots, slots])])
+        small = jnp.stack([jnp.zeros((D,), F32), jnp.sum(ffn_gain_part, axis=0), jnp.concatenate([slots, slots])])
         small = jnp.concatenate([small, jnp.zeros((5, D), F32)])
-        input_grad, small, proj_grad, out_both, up_both, gate_both, down_both = leave(
+        input_grad, small, first_rows, second_rows, out_both, up_both, gate_both, down_both = leave(
             psize,
             osize,
             part,
@@ -1735,16 +1853,15 @@
             grad_resid,
             gains8,
             small,
-            proj_part[:feat],
-            proj_part[feat:],
+            proj_part.reshape(2, feat, -1),
             out_total[:, :feat],
             out_total[:, feat:],
-            up_total,
-            gate_total,
+            pair_total,
             down_total,
         )
-        proj_grad = proj_grad.astype(F32)
-        qkv_grad, forget_grad = proj_grad[:, :width], proj_grad[:, width : width + heads]
+        proj_grad = jnp.concatenate([first_rows, second_rows.reshape(first_rows.shape)], axis=0)
+        qkv_grad = proj_grad[:, :width].astype(F32)
+        forget_grad = proj_grad[:, width : width + heads].astype(F32)
         bias_all = small[2, : 2 * psize * heads].reshape(2 * psize, heads)
         forget_bias_grad = lax.dynamic_index_in_dim(bias_all, hpos * psize + ppos, 0, keepdims=False)
 

time: 672 us -> 621 us (0.924)
  Pallas kernels: 431 us -> 382 us
  starting transfers between devices: 29 us -> 38.4 us
  waiting for transfers between devices: 23.3 us -> 15.3 us
    pallas_call x4, Pallas kernels: 332 us -> 286 us  [exchange_call(): pl.pallas_call(kernel, out_shape=outs, in_specs=in_specs, out_specs=out_s...]
    ppermute x4 -> x5, starting transfers between devices: 3.44 us -> 14.7 us  [xor_swap(): return lax.ppermute(value, axis, [(i, i ^ bit) for i in range(size)])]
    slice x5 -> x2, local copies, waits for them, and re-layouts: 7.58 us -> 0.12 us  [the longest x1 0.12 us: shards(): gate_got = xor_swap(take_half(gate_part[1], 1 - opos % 2), 'o', osize, 1)]
    ppermute x4 -> x5, waiting for transfers between devices: 18.2 us -> 15.3 us  [xor_swap(): return lax.ppermute(value, axis, [(i, i ^ bit) for i in range(size)])]
  transfers between devices with their start and end apart: 21 -> 18, of which waited for: 5 -> 3; matrix products, arithmetic and copies ran while one was open for 16% -> 17% of each run, Pallas kernels for 25% -> 38%
where the time goes in v4:
time: 621 us; the launch traced here: 617 us
  Pallas kernels  382 us (62%)
  matrix products  115 us (19%)
  starting transfers between devices  38.4 us (6%)
  other arithmetic  38.1 us (6%)
  local copies, waits for them, and re-layouts  26.6 us (4%)
  waiting for transfers between devices  15.3 us (2%)
    pallas_call x4, Pallas kernels, exchange_call(): pl.pallas_call(kernel, out_shape=outs, in_specs=in_specs, out_specs=out_s...  286 us
    pallas_call x1, Pallas kernels, attention_backward(): pl.pallas_call(functools.partial(backward_kernel, heads, count, prompt_le...  51.6 us
    pallas_call x1, Pallas kernels, attention_forward(): pl.pallas_call(functools.partial(forward_kernel, heads, count, prompt_len...  44.2 us
    dot_general x5, matrix products, contract_cols(): lax.dot_general(left, right, (((1,), (1,)), ((), ())), preferred_element_...  43.8 us
    dot_general x5, matrix products, contract_rows(): lax.dot_general(left, right, (((0,), (0,)), ((), ())), preferred_element_...  36.6 us
    dot_general x5, matrix products, matmul(): return jnp.dot(left, right, preferred_element_type=F32)  34.6 us
    ppermute x5, waiting for transfers between devices, xor_swap(): return lax.ppermute(value, axis, [(i, i ^ bit) for i in range(size)])  15.3 us
    ppermute x5, starting transfers between devices, xor_swap(): return lax.ppermute(value, axis, [(i, i ^ bit) for i in range(size)])  14.7 us
  transfers between devices with their start and end apart: 18, of which 3 were waited for; matrix products, arithmetic and copies ran while one was open for 17% of the time, Pallas kernels for 38%

profile of v4, /device:TPU:1, one launch (start us, length us, event | category | flops | bytes accessed | tf_op | source)
XLA Modules:
  0.0 617.3 jit_solution(2706705070709252774)
XLA Ops:
  0.6 5.6 collective-permute-start
  6.3 0.9 copy.43
  11.4 64.2 %enter.1 = (bf16[384,1536]{1,0:T(8,128)(2,1)}, bf16[4,384,1536]{2,1,0:T(8,128)(2,1)}, bf16[2,768,1280]{2,1,0:T(8,128)(2,1)}, bf16[384,1536]{1,0:T(8,128)(2,1)}, ...) custom-call(bf16[768,768]{1,0:T(8,128)(2,1)} %x_ref.1, f32[8,768]{1,0:T(8,128)} %maximum_maximum_fusion.1.gain_own, ...), custom_call_target="tpu_custom_call" | custom-call | tf_op jit(solution)/shard_map/enter/pallas_call | solution.py:1490
  78.6 9.3 %fusion.17 = f32[1536,1280]{1,0:T(8,128)S(1)} fusion(bf16[1536,1536]{1,0:T(8,128)(2,1)} %bitcast.100, bf16[1536,1280]{1,0:T(8,128)(2,1)} %bitcast.107), kind=kOutput, calls=%fused_computation.89 | convolution fusion | flops 6039797760 | bytes 16515072 | tf_op jit(solution)/shard_map/dot_general | solution.py:157
  87.9 3.2 copy-done.12
  91.1 2.2 slice.160
  94.9 1.3 constant_dynamic-slice_fusion.5
  96.7 1.3 broadcast_select_fusion.8
  98.1 1.2 slice_add_fusion
  99.6 3.5 collective-permute-start.1
  103.2 2.2 collective-permute-start.3
  105.4 2.1 collective-permute-start.4
  107.5 44.2 %attention_forward.1 = (bf16[4,384,384]{2,1,0:T(8,128)(2,1)S(1)}, f32[384,1536]{1,0:T(8,128)S(1)}, f32[8,1536]{1,0:T(8,128)S(1)}, bf16[6,1536,128]{2,1,0:T(8,128...) custom-call(s32[36]{0:T(128)S(1)} %reshape.151.flags, bf16[4,384,1152]{2,1,0:T(8,128)(2,1)} %bitcast.95, ...), custom_call_target="tpu_custom_call" | custom-call | flops 20000000000 | bytes 30000000 | tf_op jit(solution)/shard_map/attention_forward/pallas_call | solution.py:324
  151.9 0.8 copy-done.20
  152.9 1.0 copy-done.33
  153.9 4.4 convolution_convert_fusion.2
  158.3 73.4 %forward_exchange.1 = (f32[384,1536]{1,0:T(8,128)}, bf16[4,384,1536]{2,1,0:T(8,128)(2,1)}, bf16[2,768,1024]{2,1,0:T(8,128)(2,1)}, bf16[2,768,1024]{2,1,0:T(8,128)(2,1)}, bf16[1024,1536]{1,0:T(8,128)(2,1)}) custom-call(bf16[4,384,1536]{2,1,0:T(8,128)(2,1)} %bitcast.90, bf16[384,1536]{1,0:T(8,128)(2,1)} %get-tuple-element.111.xin.stream, ...), custom_call_target="tpu_custom_call" | custom-call | tf_op jit(solution)/shard_map/forward_exchange/pallas_call | solution.py:1490
  231.7 9.1 %collective-permute-start.6 = (bf16[384,1536]{1,0:T(8,128)(2,1)S(1)}, bf16[384,1536]{1,0:T(8,128)(2,1)S(1)}, u32[]{:S(2)}, u32[]{:S(2)}) collective-permute-start(bf16[384,1536]{1,0:T(8,128)(2,1)S(1)} %pad_maximum_fusion.1.cot), channel_id=1, source_target_pairs={{0,1},{1,0},{2,3},{3,2},{4,5},{5,4},{6,7},{7,6},{8,9},{9,8},{10,11... | collective-permute-start | bytes 3538952 | tf_op jit(solution)/shard_map/ppermute | solution.py:26
  240.8 8.0 %fusion.18 = f32[1536,1024]{1,0:T(8,128)S(1)} fusion(bf16[1536,1536]{1,0:T(8,128)(2,1)} %bitcast.101, bf16[1536,1024]{1,0:T(8,128)(2,1)} %bitcast.111), kind=kOutput, calls=%fused_computation.90 | convolution fusion | flops 4831838208 | bytes 14155776 | tf_op jit(solution)/shard_map/dot_general | solution.py:157
  248.8 7.3 %multiply_convert_fusion.2 = (bf16[1536,1024]{1,0:T(8,128)(2,1)S(1)}, f32[1536,1024]{1,0:T(8,128)}) fusion(f32[1536,1024]{1,0:T(8,128)S(1)} %fusion.18, bf16[1536,1536]{1,0:T(8,128)(2,1)S(1)} %bitcast.103, bf16[1536,1024]{1,0:T(8,128)(2,1)S(1)} %bitcast.109), kind=kOutput, calls=%fused_computation.9 | convolution fusion | flops 4841275392 | bytes 23592960 | tf_op jit(solution)/shard_map/dot_general | solution.py:157
  256.1 4.3 collective-permute-done.6
  260.4 5.7 convolution_convert_fusion
  266.9 7.6 %convolution_convert_fusion.3 = bf16[1024,1536]{1,0:T(8,128)(2,1)S(1)} fusion(bf16[1536,1024]{1,0:T(8,128)(2,1)S(1)} %get-tuple-element.119, bf16[384,1536]{1,0:T(8,128)(2,1)S(1)} %collective-permute-done.7, bf16[384,1536]{1,0:T(8,128)(2,1)S(1)} %collective-permute-done.6, bf16[384,1536]{1,0:T(8,128)(2,1)S(1)} %collective-permute-done.5, ...), kind=kOutput, calls=%fused_computation.13 | convolution fusion | flops 4857004032 | bytes 11010048 | tf_op jit(solution)/shard_map/dot_general | solution.py:145
  274.7 4.1 collective-permute-start.10
  278.7 4.3 pad_maximum_fusion
  283.7 12.4 %multiply_convert_fusion = (bf16[1536,1024]{1,0:T(8,128)(2,1)}, bf16[1536,1024]{1,0:T(8,128)(2,1)}) fusion(f32[1536,1024]{1,0:T(8,128)} %copy-done.36, f32[1536,1024]{1,0:T(8,128)} %get-tuple-element.240, bf16[1536,1536]{1,0:T(8,128)(2,1)S(1)} %pad_maximum_fusion, bf16[1024,1536]{1,0:T(8,128)(2,1)} %get-tuple-element.120), kind=kOutput, calls=%fused_computation.7 | convolution fusion | flops 4852285440 | bytes 26738688 | tf_op jit(solution)/shard_map/dot_general | solution.py:151
  296.1 8.5 %convolution_convert_fusion.5 = bf16[1536,1024]{1,0:T(8,128)(2,1)S(1)} fusion(bf16[1536,1536]{1,0:T(8,128)(2,1)} %bitcast.102, bf16[1536,1024]{1,0:T(8,128)(2,1)} %get-tuple-element.122), kind=kOutput, calls=%fused_computation.15 | convolution fusion | flops 4833411072 | bytes 11010048 | tf_op jit(solution)/shard_map/dot_general | solution.py:145
  304.8 2.9 copy-done.31
  307.6 7.6 %fusion.19 = f32[1536,1536]{1,0:T(8,128)} fusion(bf16[1536,1024]{1,0:T(8,128)(2,1)S(1)} %copy-done.37, bf16[1536,1024]{1,0:T(8,128)(2,1)S(1)} %bitcast.112), kind=kOutput, calls=%fused_computation.91 | convolution fusion | flops 4831838208 | bytes 15728640 | tf_op jit(solution)/shard_map/dot_general | solution.py:151
  315.7 9.3 %add_convert_fusion = bf16[1536,1536]{1,0:T(8,128)(2,1)} fusion(f32[1536,1536]{1,0:T(8,128)} %fusion.19, bf16[1536,1024]{1,0:T(8,128)(2,1)S(1)} %copy-done.38, bf16[1536,1024]{1,0:T(8,128)(2,1)S(1)} %bitcast.110), kind=kOutput, calls=%fused_computation | convolution fusion | flops 4836556800 | bytes 20447232 | tf_op jit(solution)/shard_map/dot_general | solution.py:151
  324.9 6.5 %convolution_convert_fusion.4 = bf16[1536,1024]{1,0:T(8,128)(2,1)} fusion(bf16[1536,1536]{1,0:T(8,128)(2,1)S(1)} %bitcast.106, bf16[1536,1024]{1,0:T(8,128)(2,1)S(1)} %copy-done.38), kind=kOutput, calls=%fused_computation.14 | convolution fusion | flops 4833411072 | bytes 11010048 | tf_op jit(solution)/shard_map/dot_general | solution.py:145
  331.5 2.3 collective-permute-done.9.gate_got
  333.8 8.7 %collective-permute-done.12 = bf16[384,1536]{1,0:T(8,128)(2,1)S(1)} collective-permute-done((bf16[384,1536]{1,0:T(8,128)(2,1)S(1)}, bf16[384,1536]{1,0:T(8,128)(2,1)S(1)}, u32[]{:S(2)}, u32[]{:S(2)}) %collective-permute-start.12) | collective-permute-done | bytes 1179680 | tf_op jit(solution)/shard_map/ppermute | solution.py:26
  343.0 1.2 fusion.15
  344.7 1.2 fusion.14
  346.0 68.0 %backward_exchange.1 = (f32[384,1536]{1,0:T(8,128)}, bf16[4,384,1536]{2,1,0:T(8,128)(2,1)}, f32[8,1536]{1,0:T(8,128)}, bf16[512,768]{1,0:T(8,128)(2,1)}, bf16[2,384,1024]{2,1,0:T(8,128)(2,1)}) custom-call(bf16[4,384,1536]{2,1,0:T(8,128)(2,1)} %bitcast.88, f32[384,1536]{1,0:T(8,128)} %get-tuple-element.125.resid, bf16[384,1536]{1,0:T(8,128)(2,1)} %copy-done.8, ...), custom_call_target="tpu_custom_call" | custom-call | tf_op jit(solution)/shard_map/backward_exchange/pallas_call | solution.py:1490
  414.0 4.5 fusion.2
  418.5 0.9 broadcast_select_fusion.1
  419.4 3.7 convolution_convert_fusion.6
  423.1 4.2 collective-permute-start.17
  427.3 2.2 collective-permute-start.16
  429.5 1.2 collective-permute-start.13
  430.8 3.2 collective-permute-start.15
  434.0 51.6 %attention_backward.1 = (bf16[4,384,1280]{2,1,0:T(8,128)(2,1)}, f32[8,128]{1,0:T(8,128)}) custom-call(s32[36]{0:T(128)} %copy-done.3, bf16[4,384,384]{2,1,0:T(8,128)(2,1)} %bitcast.114, f32[384,1536]{1,0:T(8,128)} %copy-done.4, f32[8,1536]{1,0:T(8,128)} %copy-done.5, bf16[6,1536,128]{2,1,0:T(8,128)(2,1)} %get-tuple-element.137.qp, ...), custom_call_target="tpu_custom_call" | custom-call | flops 49999998976 | bytes 30000000 | tf_op jit(solution)/shard_map/attention_backward/pallas_call | solution.py:483
  485.5 0.8 reduce_sum.19
  486.4 2.2 add_convert_fusion.6.down_in
  488.6 3.4 add_convert_fusion.1.pair_in
  492.0 1.2 add_convert_fusion.7
  493.2 0.9 fusion.16
  494.1 9.6 %fusion = bf16[1536,1280]{1,0:T(8,128)(2,1)} fusion(bf16[4,384,1536]{2,1,0:T(8,128)(2,1)} %get-tuple-element.88, bf16[4,384,1280]{2,1,0:T(8,128)(2,1)S(1)} %copy-done.35), kind=kOutput, calls=%fused_computation.3 | convolution fusion | flops 6041763840 | bytes 12582912 | tf_op jit(solution)/shard_map/dot_general | solution.py:145
  504.6 10.8 %convolution_convert_fusion.1 = bf16[1536,1536]{1,0:T(8,128)(2,1)} fusion(bf16[1536,1280]{1,0:T(8,128)(2,1)} %bitcast.113, bf16[1536,1280]{1,0:T(8,128)(2,1)} %bitcast.108), kind=kOutput, calls=%fused_computation.4 | convolution fusion | flops 6042157056 | bytes 12582912 | tf_op jit(solution)/shard_map/dot_general | solution.py:151
  516.1 80.5 %leave.1 = (bf16[768,768]{1,0:T(8,128)(2,1)}, f32[8,768]{1,0:T(8,128)}, bf16[384,1280]{1,0:T(8,128)(2,1)}, bf16[2,192,1280]{2,1,0:T(8,128)(2,1)}, bf16[2,192,768...) custom-call(bf16[4,384,1536]{2,1,0:T(8,128)(2,1)} %bitcast.91, ...), custom_call_target="tpu_custom_call" | custom-call | tf_op jit(solution)/shard_map/leave/pallas_call | solution.py:1490
  596.6 1.0 fusion.5
  597.6 3.5 fusion.4
  601.0 0.8 slice_reduce_fusion.2
  601.9 1.4 slice_reduce_fusion
  603.3 0.8 copy.48
  604.0 3.3 bitcast_convert_fusion
  607.4 2.2 bitcast_convert_fusion.1
  609.5 2.2 bitcast_convert_fusion.2
  611.7 1.1 bitcast_convert_fusion.3
  613.4 1.3 broadcast_select_fusion.10
  614.8 1.1 pad_maximum_fusion.2
  615.9 1.0 copy.52
  (164 shorter events, 15.6 us)
Async XLA Ops:
  0.6 97.5 %collective-permute-start = (f32[6]{0:T(128)}, f32[6]{0:T(128)S(1)}, u32[]{:S(2)}, u32[]{:S(2)}) collective-permute-start(f32[6]{0:T(128)} %param.18), channel_id=1, source_target_pairs={{2,8},{8,2},{3,9},{9,3},{6,12},{12,6},{7,13},{13,7},{18,24},{24,18... | collective-permute-start | bytes 80 | tf_op jit(solution)/shard_map/ppermute | solution.py:1712
  78.6 28.9 %copy-start.3 = (s32[36]{0:T(128)}, s32[36]{0:T(128)S(1)}, u32[]{:S(2)}) copy-start(s32[36]{0:T(128)S(1)} %reshape.151.flags) | copy-start | bytes 436
  87.9 3.2 copy-start.12
  91.0 3.8 copy-start.10
  91.1 3.8 copy-start.11
  94.9 1.8 copy-start.16
  94.9 3.2 copy-start.26
  96.7 6.4 %copy-start.22 = (bf16[384,1024]{1,0:T(8,128)(2,1)S(1)}, bf16[384,1024]{1,0:T(8,128)(2,1)}, u32[]{:S(2)}) copy-start(bf16[384,1024]{1,0:T(8,128)(2,1)} %get-tuple-element.99) | copy-start | bytes 2359300
  98.1 53.6 %copy-start.2 = (s32[8,1536]{1,0:T(8,128)}, s32[8,1536]{1,0:T(8,128)S(1)}, u32[]{:S(2)}) copy-start(s32[8,1536]{1,0:T(8,128)S(1)} %stack.65.qrow) | copy-start | bytes 147460
  99.3 52.4 %copy-start = (f32[1536,128]{1,0:T(8,128)}, f32[1536,128]{1,0:T(8,128)S(1)}, u32[]{:S(2)}) copy-start(f32[1536,128]{1,0:T(8,128)S(1)} %slice_add_fusion) | copy-start | bytes 2359300
  99.6 52.1 %copy-start.1 = (s32[1536,8]{1,0:T(8,128)}, s32[1536,8]{1,0:T(8,128)S(1)}, u32[]{:S(2)}) copy-start(s32[1536,8]{1,0:T(8,128)S(1)} %copy.44.kcol) | copy-start | bytes 147460
  99.6 52.2 %collective-permute-start.1 = (bf16[384,1024]{1,0:T(8,128)(2,1)}, bf16[384,1024]{1,0:T(8,128)(2,1)S(1)}, u32[]{:S(2)}, u32[]{:S(2)}) collective-permute-start(bf16[384,1024]{1,0:T(8,128)(2,1)} %get-tuple-element.98), channel_id=1, source_target_pairs={{0,4},{2,8},{4,0},{6,12},{8,2},{10,14},{12,6},{14,10},{1,5},{3,9},... | collective-permute-start | bytes 2359304 | tf_op jit(solution)/shard_map/ppermute | solution.py:40
  103.1 48.7 %collective-permute-start.2 = (bf16[384,1024]{1,0:T(8,128)(2,1)S(1)}, bf16[384,1024]{1,0:T(8,128)(2,1)S(1)}, u32[]{:S(2)}, u32[]{:S(2)}) collective-permute-start(bf16[384,1024]{1,0:T(8,128)(2,1)S(1)} %copy-done.22), channel_id=1, source_target_pairs={{0,4},{2,8},{4,0},{6,12},{8,2},{10,14},{12,6},{14,10},{1,5},{3,9},... | collective-permute-start | bytes 2359304 | tf_op jit(solution)/shard_map/ppermute | solution.py:40
  103.2 48.6 %collective-permute-start.3 = (bf16[384,768]{1,0:T(8,128)(2,1)}, bf16[384,768]{1,0:T(8,128)(2,1)S(1)}, u32[]{:S(2)}, u32[]{:S(2)}) collective-permute-start(bf16[384,768]{1,0:T(8,128)(2,1)} %get-tuple-element.100), channel_id=1, source_target_pairs={{0,8},{4,0},{8,12},{12,4},{1,9},{5,1},{9,13},{13,5},{2,10},{6,2},{... | collective-permute-start | bytes 1769480 | tf_op jit(solution)/shard_map/ppermute | solution.py:1754
  105.4 46.4 %collective-permute-start.4 = (bf16[384,768]{1,0:T(8,128)(2,1)}, bf16[384,768]{1,0:T(8,128)(2,1)S(1)}, u32[]{:S(2)}, u32[]{:S(2)}) collective-permute-start(bf16[384,768]{1,0:T(8,128)(2,1)} %get-tuple-element.101), channel_id=1, source_target_pairs={{4,8},{8,4},{5,9},{9,5},{6,10},{10,6},{7,11},{11,7},{20,24},{24,20... | collective-permute-start | bytes 1769480 | tf_op jit(solution)/shard_map/ppermute | solution.py:1755
  151.7 6.6 %copy-start.4 = (f32[384,1536]{1,0:T(8,128)}, f32[384,1536]{1,0:T(8,128)S(1)}, u32[]{:S(2)}) copy-start(f32[384,1536]{1,0:T(8,128)S(1)} %get-tuple-element.135.ot_ref) | copy-start | bytes 7077892
  151.7 6.6 %copy-start.5 = (f32[8,1536]{1,0:T(8,128)}, f32[8,1536]{1,0:T(8,128)S(1)}, u32[]{:S(2)}) copy-start(f32[8,1536]{1,0:T(8,128)S(1)} %get-tuple-element.136.lse_ref) | copy-start | bytes 147460
  151.7 2.2 copy-start.33
  151.8 6.5 %copy-start.19 = (bf16[384,1024]{1,0:T(8,128)(2,1)}, bf16[384,1024]{1,0:T(8,128)(2,1)S(1)}, u32[]{:S(2)}) copy-start(bf16[384,1024]{1,0:T(8,128)(2,1)S(1)} %collective-permute-done.1.gate_got) | copy-start | bytes 2359300
  151.8 0.9 copy-start.20
  152.8 79.0 %copy-start.8 = (bf16[384,1536]{1,0:T(8,128)(2,1)}, bf16[384,1536]{1,0:T(8,128)(2,1)S(1)}, u32[]{:S(2)}) copy-start(bf16[384,1536]{1,0:T(8,128)(2,1)S(1)} %pad_maximum_fusion.1.cot) | copy-start | bytes 3538948
  152.8 114.1 %collective-permute-start.5 = (bf16[384,1536]{1,0:T(8,128)(2,1)S(1)}, bf16[384,1536]{1,0:T(8,128)(2,1)S(1)}, u32[]{:S(2)}, u32[]{:S(2)}) collective-permute-start(bf16[384,1536]{1,0:T(8,128)(2,1)S(1)} %pad_maximum_fusion.1.cot), channel_id=1, source_target_pairs={{0,8},{8,0},{1,9},{9,1},{2,10},{10,2},{3,11},{11,3},{4,12},{12,4},... | collective-permute-start | bytes 3538952 | tf_op jit(solution)/shard_map/ppermute | solution.py:22
  231.7 28.7 %collective-permute-start.6 = (bf16[384,1536]{1,0:T(8,128)(2,1)S(1)}, bf16[384,1536]{1,0:T(8,128)(2,1)S(1)}, u32[]{:S(2)}, u32[]{:S(2)}) collective-permute-start(bf16[384,1536]{1,0:T(8,128)(2,1)S(1)} %pad_maximum_fusion.1.cot), channel_id=1, source_target_pairs={{0,1},{1,0},{2,3},{3,2},{4,5},{5,4},{6,7},{7,6},{8,9},{9,8},{10,11... | collective-permute-start | bytes 3538952 | tf_op jit(solution)/shard_map/ppermute | solution.py:26
  240.8 8.0 %copy-start.28 = (bf16[4,384,1536]{2,1,0:T(8,128)(2,1)S(1)}, bf16[4,384,1536]{2,1,0:T(8,128)(2,1)}, u32[]{:S(2)}) copy-start(bf16[4,384,1536]{2,1,0:T(8,128)(2,1)} %get-tuple-element.115) | copy-start | bytes 14155780
  240.8 8.0 %copy-start.29 = (bf16[2,768,1024]{2,1,0:T(8,128)(2,1)S(1)}, bf16[2,768,1024]{2,1,0:T(8,128)(2,1)}, u32[]{:S(2)}) copy-start(bf16[2,768,1024]{2,1,0:T(8,128)(2,1)} %get-tuple-element.118) | copy-start | bytes 9437188
  248.8 7.3 %copy-start.36 = (f32[1536,1024]{1,0:T(8,128)}, f32[1536,1024]{1,0:T(8,128)S(1)}, u32[]{:S(2)}) copy-start(f32[1536,1024]{1,0:T(8,128)S(1)} %fusion.18) | copy-start | bytes 18874372
  248.8 11.6 %copy-start.32 = (bf16[1024,1536]{1,0:T(8,128)(2,1)S(1)}, bf16[1024,1536]{1,0:T(8,128)(2,1)}, u32[]{:S(2)}) copy-start(bf16[1024,1536]{1,0:T(8,128)(2,1)} %get-tuple-element.120) | copy-start | bytes 9437188
  260.4 6.5 %collective-permute-start.7 = (bf16[384,1536]{1,0:T(8,128)(2,1)S(1)}, bf16[384,1536]{1,0:T(8,128)(2,1)S(1)}, u32[]{:S(2)}, u32[]{:S(2)}) collective-permute-start(bf16[384,1536]{1,0:T(8,128)(2,1)S(1)} %collective-permute-done.6), channel_id=1, source_target_pairs={{0,8},{8,0},{1,9},{9,1},{2,10},{10,2},{3,11},{11,3},{4,12},{12,4},... | collective-permute-start | bytes 3538952 | tf_op jit(solution)/shard_map/ppermute | solution.py:22
  266.3 16.7 %collective-permute-start.11 = (bf16[384,1536]{1,0:T(8,128)(2,1)S(1)}, bf16[384,1536]{1,0:T(8,128)(2,1)S(1)}, u32[]{:S(2)}, u32[]{:S(2)}) collective-permute-start(bf16[384,1536]{1,0:T(8,128)(2,1)S(1)} %get-tuple-element.220), channel_id=1, source_target_pairs={{0,8},{8,0},{1,9},{9,1},{2,10},{10,2},{3,11},{11,3},{4,12},{12,4},... | collective-permute-start | bytes 3538952 | tf_op jit(solution)/shard_map/ppermute | solution.py:22
  266.9 16.2 %collective-permute-start.8 = (bf16[384,1536]{1,0:T(8,128)(2,1)S(1)}, bf16[384,1536]{1,0:T(8,128)(2,1)S(1)}, u32[]{:S(2)}, u32[]{:S(2)}) collective-permute-start(bf16[384,1536]{1,0:T(8,128)(2,1)S(1)} %get-tuple-element.221), channel_id=1, source_target_pairs={{0,8},{8,0},{1,9},{9,1},{2,10},{10,2},{3,11},{11,3},{4,12},{12,4},... | collective-permute-start | bytes 3538952 | tf_op jit(solution)/shard_map/ppermute | solution.py:22
  274.7 67.8 %collective-permute-start.10 = (bf16[512,1536]{1,0:T(8,128)(2,1)S(1)}, bf16[512,1536]{1,0:T(8,128)(2,1)S(1)}, u32[]{:S(2)}, u32[]{:S(2)}) collective-permute-start(bf16[512,1536]{1,0:T(8,128)(2,1)S(1)} %broadcast_select_fusion), channel_id=1, source_target_pairs={{0,16},{16,0},{1,17},{17,1},{2,18},{18,2},{3,19},{19,3},{4,20},{20... | collective-permute-start | bytes 4718600 | tf_op jit(solution)/shard_map/ppermute | solution.py:26
  296.1 8.6 %copy-start.37 = (bf16[1536,1024]{1,0:T(8,128)(2,1)S(1)}, bf16[1536,1024]{1,0:T(8,128)(2,1)}, u32[]{:S(2)}) copy-start(bf16[1536,1024]{1,0:T(8,128)(2,1)} %get-tuple-element.122) | copy-start | bytes 9437188
  304.6 10.7 %copy-start.7 = (bf16[1536,1024]{1,0:T(8,128)(2,1)}, bf16[1536,1024]{1,0:T(8,128)(2,1)S(1)}, u32[]{:S(2)}) copy-start(bf16[1536,1024]{1,0:T(8,128)(2,1)S(1)} %convolution_convert_fusion.5) | copy-start | bytes 9437188
  304.6 3.0 copy-start.31
  307.6 8.0 %copy-start.30 = (bf16[2,768,1024]{2,1,0:T(8,128)(2,1)S(1)}, bf16[2,768,1024]{2,1,0:T(8,128)(2,1)}, u32[]{:S(2)}) copy-start(bf16[2,768,1024]{2,1,0:T(8,128)(2,1)} %get-tuple-element.118) | copy-start | bytes 9437188
  307.6 8.0 %copy-start.38 = (bf16[1536,1024]{1,0:T(8,128)(2,1)S(1)}, bf16[1536,1024]{1,0:T(8,128)(2,1)}, u32[]{:S(2)}) copy-start(bf16[1536,1024]{1,0:T(8,128)(2,1)} %get-tuple-element.123) | copy-start | bytes 9437188
  315.4 18.4 %collective-permute-start.9 = (bf16[384,1024]{1,0:T(8,128)(2,1)S(1)}, bf16[384,1024]{1,0:T(8,128)(2,1)S(1)}, u32[]{:S(2)}, u32[]{:S(2)}) collective-permute-start(bf16[384,1024]{1,0:T(8,128)(2,1)S(1)} %constant_dynamic-slice_fusion.2), channel_id=1, source_target_pairs={{0,16},{16,0},{1,17},{17,1},{2,18},{18,2},{3,19},{19,3},{4,20},{20... | collective-permute-start | bytes 2359304 | tf_op jit(solution)/shard_map/ppermute | solution.py:26
  315.7 9.3 %slice-start = ((s8[4718592]{0:T(1024)(128)(4,1)}), s8[4194304]{0:T(1024)(128)(4,1)S(1)}, s32[]{:S(2)}) async-start(s8[4718592]{0:T(1024)(128)(4,1)} %bitcast.104), calls=%async_computation | async-start | bytes 8388608
  315.7 9.3 %slice-start.1 = ((s8[4718592]{0:T(1024)(128)(4,1)}), s8[524288]{0:T(1024)(128)(4,1)S(1)}, s32[]{:S(2)}) async-start(s8[4718592]{0:T(1024)(128)(4,1)} %bitcast.104), calls=%async_computation.1 | async-start | bytes 1048576
  315.7 26.8 %collective-permute-start.12 = (bf16[384,1536]{1,0:T(8,128)(2,1)S(1)}, bf16[384,1536]{1,0:T(8,128)(2,1)S(1)}, u32[]{:S(2)}, u32[]{:S(2)}) collective-permute-start(bf16[384,1536]{1,0:T(8,128)(2,1)S(1)} %get-tuple-element.218), channel_id=1, source_target_pairs={{0,1},{1,0},{2,3},{3,2},{4,5},{5,4},{6,7},{7,6},{8,9},{9,8},{10,11... | collective-permute-start | bytes 3538952 | tf_op jit(solution)/shard_map/ppermute | solution.py:26
  324.9 17.5 %copy-start.6 = (f32[384,1536]{1,0:T(8,128)S(1)}, f32[384,1536]{1,0:T(8,128)}, u32[]{:S(2)}) copy-start(f32[384,1536]{1,0:T(8,128)} %get-tuple-element.125.resid) | copy-start | bytes 7077892
  333.8 10.4 %copy-start.18 = (bf16[384,1024]{1,0:T(8,128)(2,1)}, bf16[384,1024]{1,0:T(8,128)(2,1)S(1)}, u32[]{:S(2)}) copy-start(bf16[384,1024]{1,0:T(8,128)(2,1)S(1)} %collective-permute-done.9.gate_got) | copy-start | bytes 2359300
  414.0 5.4 copy-start.9
  414.0 5.4 copy-start.34
  419.4 3.7 copy-start.13
  419.4 7.9 %copy-start.21 = (bf16[512,768]{1,0:T(8,128)(2,1)S(1)}, bf16[512,768]{1,0:T(8,128)(2,1)}, u32[]{:S(2)}) copy-start(bf16[512,768]{1,0:T(8,128)(2,1)} %get-tuple-element.145) | copy-start | bytes 2359300
  423.1 63.3 %collective-permute-start.17 = (bf16[2,384,1024]{2,1,0:T(8,128)(2,1)S(1)}, bf16[2,384,1024]{2,1,0:T(8,128)(2,1)}, u32[]{:S(2)}, u32[]{:S(2)}) collective-permute-start(bf16[2,384,1024]{2,1,0:T(8,128)(2,1)S(1)} %copy-done.13), channel_id=1, source_target_pairs={{2,0},{8,10},{3,1},{9,11},{6,4},{12,14},{7,5},{13,15},{18,16},{24,... | collective-permute-start | bytes 4718600 | tf_op jit(solution)/shard_map/ppermute | solution.py:65
  427.3 59.1 %collective-permute-start.16 = (bf16[512,768]{1,0:T(8,128)(2,1)S(1)}, bf16[512,768]{1,0:T(8,128)(2,1)}, u32[]{:S(2)}, u32[]{:S(2)}) collective-permute-start(bf16[512,768]{1,0:T(8,128)(2,1)S(1)} %copy-done.21), channel_id=1, source_target_pairs={{2,0},{8,10},{3,1},{9,11},{6,4},{12,14},{7,5},{13,15},{18,16},{24,... | collective-permute-start | bytes 2359304 | tf_op jit(solution)/shard_map/ppermute | solution.py:65
  429.5 56.9 %collective-permute-start.13 = (bf16[192,1536]{1,0:T(8,128)(2,1)}, bf16[192,1536]{1,0:T(8,128)(2,1)}, u32[]{:S(2)}, u32[]{:S(2)}) collective-permute-start(bf16[192,1536]{1,0:T(8,128)(2,1)} %get-tuple-element.142), channel_id=1, source_target_pairs={{0,16},{16,0},{1,17},{17,1},{2,18},{18,2},{3,19},{19,3},{4,20},{20... | collective-permute-start | bytes 1769480 | tf_op jit(solution)/shard_map/ppermute | solution.py:26
  430.8 55.6 %collective-permute-start.14 = (bf16[384,768]{1,0:T(8,128)(2,1)}, bf16[384,768]{1,0:T(8,128)(2,1)}, u32[]{:S(2)}, u32[]{:S(2)}) collective-permute-start(bf16[384,768]{1,0:T(8,128)(2,1)} %get-tuple-element.143), channel_id=1, source_target_pairs={{8,0},{0,4},{12,8},{4,12},{9,1},{1,5},{13,9},{5,13},{10,2},{2,6},{... | collective-permute-start | bytes 1769480 | tf_op jit(solution)/shard_map/ppermute | solution.py:131
  430.8 55.6 %collective-permute-start.15 = (bf16[384,768]{1,0:T(8,128)(2,1)}, bf16[384,768]{1,0:T(8,128)(2,1)}, u32[]{:S(2)}, u32[]{:S(2)}) collective-permute-start(bf16[384,768]{1,0:T(8,128)(2,1)} %get-tuple-element.144), channel_id=1, source_target_pairs={{8,4},{4,8},{9,5},{5,9},{10,6},{6,10},{11,7},{7,11},{24,20},{20,24... | collective-permute-start | bytes 1769480 | tf_op jit(solution)/shard_map/ppermute | solution.py:132
  488.6 5.4 copy-start.35
  494.1 10.2 %copy-start.27 = (pred[4]{0:T(512)(128)(4,1)S(1)}, pred[4]{0:T(512)(128)(4,1)}, u32[]{:S(2)}) copy-start(pred[4]{0:T(512)(128)(4,1)} %iota_compare_fusion.4) | copy-start | bytes 16
  504.6 10.8 %copy-start.24 = (f32[8]{0:T(128)S(1)}, f32[8]{0:T(128)}, u32[]{:S(2)}) copy-start(f32[8]{0:T(128)} %pad.15.clone) | copy-start | bytes 100
  504.6 10.8 %copy-start.25 = (f32[8]{0:T(128)S(1)}, f32[8]{0:T(128)}, u32[]{:S(2)}) copy-start(f32[8]{0:T(128)} %pad.12.clone) | copy-start | bytes 100
  601.0 6.3 %copy-start.15 = (bf16[2,384,1024]{2,1,0:T(8,128)(2,1)S(1)}, bf16[2,384,1024]{2,1,0:T(8,128)(2,1)}, u32[]{:S(2)}) copy-start(bf16[2,384,1024]{2,1,0:T(8,128)(2,1)} %get-tuple-element.163) | copy-start | bytes 4718596
  607.3 2.2 copy-start.14
  609.5 2.2 copy-start.23
  611.7 4.2 copy-start.17

commit v5 on v4

--- a/solution.py
+++ b/solution.py
@@ -187,15 +187,10 @@
     return lax.broadcasted_iota(jnp.int32, shape, 1)
 
 
-def decay_map(pos_a, tag_a, limit_a, pos_b, tag_b, doc_b):
-    adds = ((pos_b <= pos_a) & (tag_a == tag_b)) | (doc_b <= limit_a)
-    return jnp.where(adds, 1.0, 0.0).astype(BF16)
-
-
 def forward_kernel(
-    heads, count, prompt_len, flags, qkv_hbm, logit_hbm, kcol, qrow, att_hbm, ot_hbm, lse_ref,
-    qp_hbm, kp_hbm, vp_hbm, qkv, logit, qp, kp, vp, vt, rates, attended, ot, mask, m_ref, l_ref,
-    in_sem, out_sem, keep_sem,
+    heads, count, prompt_len, flags, proj_hbm, bias_ref, kcol, qrow, att_hbm, ot_hbm, lse_ref,
+    qp_hbm, kp_hbm, vp_hbm, logit, qkv, qp, kp, vp, vt, rates, sums_ref, attended, ot, mask,
+    in_sem, out_sem, keep_sem, *per_head,
 ):
     me = lax.axis_index("p") * 2 + lax.axis_index("k")
     total = qkv.shape[0]
@@ -204,36 +199,57 @@
     loads = []
     for b in range(count):
         rows = pl.ds(b * size, size)
-        loads.append(pltpu.make_async_copy(logit_hbm.at[b ^ me], logit.at[rows], in_sem.at[b]))
-        loads.append(pltpu.make_async_copy(qkv_hbm.at[b ^ me], qkv.at[rows], in_sem.at[count + b]))
+        loads.append(pltpu.make_async_copy(proj_hbm.at[b ^ me], qkv.at[rows], in_sem.at[b]))
     for load in loads:
         load.start()
-    for load in loads[::2]:
+    for load in loads:
         load.wait()
+    logit[...] = qkv[:, 3 * DH * heads :] + bias_ref[...]
     value = logit[...]
     rate = jnp.minimum(value, 0.0) - jnp.log1p(jnp.exp(-jnp.abs(value)))
     rate = jnp.where(lane(rate.shape) < heads, rate, 0.0)
     high, mid, low = split_parts(rate)
     packed = high.astype(F32) + pltpu.roll(mid.astype(F32), 8, 1) + pltpu.roll(low.astype(F32), 16, 1)
     rates[...] = packed.astype(BF16)
-    for load in loads[1::2]:
-        load.wait()
     place_row = lax.broadcasted_iota(jnp.int32, (LANES, LANES), 0)
     place_col = lax.broadcasted_iota(jnp.int32, (LANES, LANES), 1)
 
+    prompt_tiles = prompt_len // TILE
+    wide = (TILE, TILE)
+    row_pos, col_pos = lax.broadcasted_iota(jnp.int32, wide, 0), lax.broadcasted_iota(jnp.int32, wide, 1)
+    below = jnp.where(col_pos <= row_pos, 1.0, 0.0).astype(BF16)
+
+    def prompt_sums(t, before):
+        rows = pl.ds(pl.multiple_of(t * TILE, TILE), TILE)
+        prefix = dot_nn(below, rates[rows, :]) + before
+        sums_ref[rows, :] = prefix
+        return prefix[TILE - 1 : TILE, :]
+
+    lax.fori_loop(0, prompt_tiles, prompt_sums, jnp.zeros((1, LANES), F32))
+    doc_index = lax.broadcasted_iota(jnp.int32, (8, prompt_len), 0)
+    within = jnp.where(qrow[3:4, 0:prompt_len] <= doc_index, 1.0, 0.0).astype(BF16)
+    doc_sums = dot_nn(within, rates[0:prompt_len, :])
+
+    def branch_sums(t, carry):
+        rows = pl.ds(pl.multiple_of(t * TILE, TILE), TILE)
+        limit = kcol[rows, 2:3]
+        start = jnp.zeros((TILE, LANES), F32)
+        for doc in range(DOCS):
+            start = jnp.where(limit == doc, doc_sums[doc : doc + 1, :], start)
+
+        def add_own(u, acc):
+            others = pl.ds(pl.multiple_of(u * TILE, TILE), TILE)
+            own = (u * TILE + col_pos <= t * TILE + row_pos) & (kcol[rows, 1:2] == qrow[2:3, others])
+            return acc + dot_nn(jnp.where(own, 1.0, 0.0).astype(BF16), rates[others, :])
+
+        sums_ref[rows, :] = lax.fori_loop(prompt_tiles, t + 1, add_own, start)
+        return carry
+
+    lax.fori_loop(prompt_tiles, tiles, branch_sums, 0)
+
     def prepare(t, carry):
         rows = pl.ds(pl.multiple_of(t * TILE, TILE), TILE)
-
-        def add_rates(u, acc):
-            others = pl.ds(pl.multiple_of(u * TILE, TILE), TILE)
-            pos_a = t * TILE + lax.broadcasted_iota(jnp.int32, (TILE, TILE), 0)
-            pos_b = u * TILE + lax.broadcasted_iota(jnp.int32, (TILE, TILE), 1)
-            adds = decay_map(
-                pos_a, kcol[rows, 1:2], kcol[rows, 2:3], pos_b, qrow[2:3, others], qrow[3:4, others]
-            )
-            return acc + dot_nn(adds, rates[others, :])
-
-        sums = lax.fori_loop(0, t + 1, add_rates, jnp.zeros((TILE, LANES), F32))
+        sums = sums_ref[rows, :]
         decay = sums + pltpu.roll(sums, LANES - 8, 1) + pltpu.roll(sums, LANES - 16, 1)
         decay = jnp.where(lane(decay.shape) < heads, -decay, 0.0)
         high, mid, low = split_parts(decay)
@@ -243,9 +259,9 @@
         lanes = lane((TILE, LANES))
         for h in range(heads):
             base = 3 * DH * h
-            query = qkv[rows, base : base + DH].astype(F32) * DH ** (-0.5)
+            query = qkv[rows, base : base + DH].astype(BF16).astype(F32) * DH ** (-0.5)
             key = qkv[rows, base + DH : base + 2 * DH]
-            worth = qkv[rows, base + 2 * DH : base + 3 * DH]
+            worth = qkv[rows, base + 2 * DH : base + 3 * DH].astype(BF16)
             ones = jnp.where((lanes >= DH) & (lanes < DH + 3), 1.0, 0.0)[:, :DH]
             ones = jnp.where(lane((TILE, DH)) < 3, 1.0, 0.0)
             qp[h, rows, :] = jnp.concatenate([query, ones], axis=1).astype(BF16)
@@ -254,7 +270,7 @@
             ).astype(BF16)
             extra = dot_nn(parts, spread)
             extra = jnp.where(lanes == DH + 3, 1.0, extra)
-            key_wide = jnp.concatenate([key.astype(F32), extra[:, DH:]], axis=1)
+            key_wide = jnp.concatenate([key, extra[:, DH:]], axis=1)
             kp[h, rows, :] = key_wide.astype(BF16)
             vp[h, rows, :] = worth
             vt[h, :, rows] = worth.astype(F32).T.astype(BF16)
@@ -269,36 +285,39 @@
     for keep in keeps:
         keep.start()
 
+    acc, top_refs, total_refs, score_refs = (per_head[n * heads : (n + 1) * heads] for n in range(4))
+
     def query_tile(i, carry):
         cols = pl.ds(pl.multiple_of(i * TILE, TILE), TILE)
-        m_ref[...] = jnp.full(m_ref.shape, MASKED, F32)
-        l_ref[...] = jnp.zeros(l_ref.shape, F32)
-        ot[:, cols] = jnp.zeros((heads * DH, TILE), F32)
+        for h in range(heads):
+            top_refs[h][...] = jnp.full(top_refs[h].shape, MASKED, F32)
+            total_refs[h][...] = jnp.zeros(total_refs[h].shape, F32)
+            acc[h][...] = jnp.zeros(acc[h].shape, F32)
 
         def key_tile(j, inner):
             @pl.when(flags[i * tiles + j] > 0)
             def _():
                 rows = pl.ds(pl.multiple_of(j * TILE, TILE), TILE)
                 mask[...] = tile_mask(qrow, kcol, None, None, i, j)
+                tops = []
                 for h in range(heads):
                     scores = dot_nt(kp[h, rows, :], qp[h, cols, :]) + mask[...]
-                    before = m_ref[h : h + 1, :]
-                    top = jnp.maximum(before, jnp.max(scores, axis=0, keepdims=True))
-                    expo = jnp.exp(scores - top)
-                    shrink = jnp.exp(before - top)
-                    m_ref[h : h + 1, :] = top
-                    l_ref[h : h + 1, :] = l_ref[h : h + 1, :] * shrink + jnp.sum(expo, axis=0, keepdims=True)
-                    part = dot_nn(vt[h, :, rows], expo.astype(BF16))
-                    span = pl.ds(h * DH, DH)
-                    ot[span, cols] = ot[span, cols] * shrink + part
+                    score_refs[h][...] = scores
+                    tops.append(jnp.maximum(top_refs[h][0:1, :], jnp.max(scores, axis=0, keepdims=True)))
+                for h, top in enumerate(tops):
+                    expo = jnp.exp(score_refs[h][...] - top)
+                    shrink = jnp.exp(top_refs[h][0:1, :] - top)
+                    top_refs[h][0:1, :] = top
+                    total_refs[h][0:1, :] = total_refs[h][0:1, :] * shrink + jnp.sum(expo, axis=0, keepdims=True)
+                    acc[h][...] = acc[h][...] * shrink + dot_nn(vt[h, :, rows], expo.astype(BF16))
 
             return inner
 
         lax.fori_loop(0, i + 1, key_tile, 0)
         for h in range(heads):
-            span = pl.ds(h * DH, DH)
-            ot[span, cols] = ot[span, cols] / l_ref[h : h + 1, :]
-        lse_ref[:, cols] = m_ref[...] + jnp.log(l_ref[...])
+            total = total_refs[h][0:1, :]
+            ot[pl.ds(h * DH, DH), cols] = acc[h][...] / total
+            lse_ref[h : h + 1, cols] = top_refs[h][0:1, :] + jnp.log(total)
         attended[cols, :] = ot[:, cols].T.astype(BF16)
         return carry
 
@@ -315,8 +334,8 @@
         copy.wait()
 
 
-def attention_forward(qkv, logit, kcol, qrow, flags, heads, prompt_len):
-    count, size, width = qkv.shape
+def attention_forward(projected, bias, kcol, qrow, flags, heads, prompt_len):
+    count, size, width = projected.shape
     total = count * size
     any_spec = pl.BlockSpec(memory_space=pl.ANY)
     vmem = pl.BlockSpec(memory_space=pltpu.VMEM)
@@ -330,36 +349,39 @@
             shape((heads, total, LANES), BF16),
             shape((heads, total, LANES), BF16),
             shape((heads, total, DH), BF16),
+            shape((total, LANES), F32),
         ),
-        in_specs=[pl.BlockSpec(memory_space=pltpu.SMEM), any_spec, any_spec, vmem, vmem],
-        out_specs=(any_spec, any_spec, vmem, any_spec, any_spec, any_spec),
+        in_specs=[pl.BlockSpec(memory_space=pltpu.SMEM), any_spec, vmem, vmem, vmem],
+        out_specs=(any_spec, any_spec, vmem, any_spec, any_spec, any_spec, vmem),
         scratch_shapes=[
-            pltpu.VMEM((total, width), BF16),
-            pltpu.VMEM((total, LANES), F32),
+            pltpu.VMEM((total, width), F32),
             pltpu.VMEM((heads, total, LANES), BF16),
             pltpu.VMEM((heads, total, LANES), BF16),
             pltpu.VMEM((heads, total, DH), BF16),
             pltpu.VMEM((heads, DH, total), BF16),
             pltpu.VMEM((total, LANES), BF16),
+            pltpu.VMEM((total, LANES), F32),
             pltpu.VMEM((total, heads * DH), BF16),
             pltpu.VMEM((heads * DH, total), F32),
             pltpu.VMEM((TILE, TILE), F32),
-            pltpu.VMEM((8, TILE), F32),
-            pltpu.VMEM((8, TILE), F32),
-            pltpu.SemaphoreType.DMA((2 * count,)),
+            pltpu.SemaphoreType.DMA((count,)),
             pltpu.SemaphoreType.DMA((count,)),
             pltpu.SemaphoreType.DMA((4,)),
-        ],
+        ]
+        + [pltpu.VMEM((DH, TILE), F32)] * heads
+        + [pltpu.VMEM((8, TILE), F32)] * (2 * heads)
+        + [pltpu.VMEM((TILE, TILE), F32)] * heads,
         compiler_params=pltpu.CompilerParams(vmem_limit_bytes=48 << 20),
         cost_estimate=pl.CostEstimate(flops=20_000_000_000, bytes_accessed=30_000_000, transcendentals=0),
         name="attention_forward",
-    )(flags, qkv, logit, kcol, qrow)
+    )(flags, projected, bias, kcol, qrow)
 
 
 def backward_kernel(
-    heads, count, prompt_len, flags, gatt_hbm, ot_ref, lse_ref, qp, kp, vp, logit_hbm, kcol, qrow,
-    grad_hbm, bias_ref, gatt, logit, gout, kt, delta, dqt, dk, dv, mask, decay, grad, in_sem, out_sem,
+    heads, count, prompt_len, flags, gatt_hbm, ot_ref, lse_ref, qp, kp, vp, logit, kcol, qrow,
+    grad_hbm, bias_ref, gatt, gout, kt, delta, mask, decay, grad, in_sem, out_sem, *per_head,
 ):
+    dqt, dk, dv, prob_refs, score_refs = (per_head[n * heads : (n + 1) * heads] for n in range(5))
     me = lax.axis_index("p") * 2 + lax.axis_index("k")
     total = gatt.shape[0]
     size = total // count
@@ -368,12 +390,12 @@
     for b in range(count):
         rows = pl.ds(b * size, size)
         loads.append(pltpu.make_async_copy(gatt_hbm.at[b ^ me], gatt.at[rows], in_sem.at[b]))
-        loads.append(pltpu.make_async_copy(logit_hbm.at[b ^ me], logit.at[rows], in_sem.at[count + b]))
     for load in loads:
         load.start()
     for load in loads:
         load.wait()
-    dqt[...] = jnp.zeros(dqt.shape, F32)
+    for h in range(heads):
+        dqt[h][...] = jnp.zeros(dqt[h].shape, F32)
     delta[...] = jnp.zeros(delta.shape, F32)
 
     def prepare(t, carry):
@@ -390,8 +412,9 @@
 
     def key_tile(j, carry):
         rows = pl.ds(pl.multiple_of(j * TILE, TILE), TILE)
-        dk[...] = jnp.zeros(dk.shape, F32)
-        dv[...] = jnp.zeros(dv.shape, F32)
+        for h in range(heads):
+            dk[h][...] = jnp.zeros(dk[h].shape, F32)
+            dv[h][...] = jnp.zeros(dv[h].shape, F32)
 
         def query_tile(i, inner):
             @pl.when(flags[i * tiles + j] > 0)
@@ -400,22 +423,26 @@
                 mask[...] = tile_mask(qrow, kcol, None, None, i, j)
                 for h in range(heads):
                     scores = dot_nt(kp[h, rows, :], qp[h, cols, :]) + mask[...]
-                    probs = jnp.exp(scores - lse_ref[h : h + 1, cols])
+                    prob_refs[h][...] = jnp.exp(scores - lse_ref[h : h + 1, cols])
+                for h in range(heads):
+                    probs = prob_refs[h][...]
                     grad_probs = dot_nt(vp[h, rows, :], gout[h, cols, :])
-                    grad_scores = (probs * (grad_probs - delta[h : h + 1, cols])).astype(BF16)
-                    dv[h] += dot_nn(probs.astype(BF16), gout[h, cols, :])
-                    dk[h] += dot_nn(grad_scores, qp[h, cols, :])
-                    dqt[h, :, cols] += dot_nn(kt[h, :, rows], grad_scores)
+                    score_refs[h][...] = (probs * (grad_probs - delta[h : h + 1, cols])).astype(BF16)
+                    dv[h][...] += dot_nn(probs.astype(BF16), gout[h, cols, :])
+                for h in range(heads):
+                    grad_scores = score_refs[h][...]
+                    dk[h][...] += dot_nn(grad_scores, qp[h, cols, :])
+                    dqt[h][:, cols] += dot_nn(kt[h, :, rows], grad_scores)
 
             return inner
 
         lax.fori_loop(j, tiles, query_tile, 0)
         keys = jnp.zeros((TILE, LANES), F32)
         for h in range(heads):
-            grad_key = dk[h]
+            grad_key = dk[h][...]
             keys += jnp.where(lanes == h, pltpu.roll(grad_key, LANES - DH + h, 1), 0.0)
             grad[rows, (3 * h + 1) * DH : (3 * h + 3) * DH] = jnp.concatenate(
-                [grad_key[:, :DH], dv[h]], axis=1
+                [grad_key[:, :DH], dv[h][...]], axis=1
             ).astype(BF16)
         decay[rows, :] = -keys
         return carry
@@ -426,7 +453,7 @@
         rows = pl.ds(pl.multiple_of(t * TILE, TILE), TILE)
         queries = jnp.zeros((TILE, LANES), F32)
         for h in range(heads):
-            turned = jnp.concatenate([dqt[h, :, rows], jnp.zeros((LANES - DH - 8, TILE), F32)], axis=0).T
+            turned = jnp.concatenate([dqt[h][:, rows], jnp.zeros((LANES - DH - 8, TILE), F32)], axis=0).T
             queries += jnp.where(lanes == h, pltpu.roll(turned, LANES - DH - 3 + h, 1), 0.0)
             grad[rows, 3 * h * DH : (3 * h + 1) * DH] = (turned[:, :DH] * DH ** (-0.5)).astype(BF16)
         whole = decay[rows, :] + queries
@@ -438,19 +465,43 @@
 
     lax.fori_loop(0, tiles, finish, 0)
 
+    prompt_tiles = prompt_len // TILE
+    wide = (TILE, TILE)
+    row_pos, col_pos = lax.broadcasted_iota(jnp.int32, wide, 0), lax.broadcasted_iota(jnp.int32, wide, 1)
+    above = jnp.where(col_pos >= row_pos, 1.0, 0.0).astype(BF16)
+    branch_len = total - prompt_len
+    doc_index = lax.broadcasted_iota(jnp.int32, (8, branch_len), 0)
+    chosen = jnp.where(qrow[4:5, prompt_len:total] == doc_index, 1.0, 0.0).astype(BF16)
+    doc_sums = dot_nn(chosen, decay[prompt_len:total, :].astype(BF16))
+
+    def prompt_sums(n, after):
+        t = prompt_tiles - 1 - n
+        rows = pl.ds(pl.multiple_of(t * TILE, TILE), TILE)
+        suffix = dot_nn(above, decay[rows, :].astype(BF16)) + after
+        doc = kcol[rows, 3:4]
+        sums = suffix
+        for d in range(DOCS):
+            sums = sums + jnp.where(doc <= d, doc_sums[d : d + 1, :], 0.0)
+        decay[rows, :] = sums
+        return suffix[0:1, :]
+
+    def branch_sums(t, carry):
+        rows = pl.ds(pl.multiple_of(t * TILE, TILE), TILE)
+
+        def add_own(u, acc):
+            others = pl.ds(pl.multiple_of(u * TILE, TILE), TILE)
+            own = (u * TILE + col_pos >= t * TILE + row_pos) & (kcol[rows, 1:2] == qrow[2:3, others])
+            return acc + dot_nn(jnp.where(own, 1.0, 0.0).astype(BF16), decay[others, :].astype(BF16))
+
+        decay[rows, :] = lax.fori_loop(t, tiles, add_own, jnp.zeros((TILE, LANES), F32))
+        return carry
+
+    lax.fori_loop(0, prompt_tiles, prompt_sums, jnp.zeros((1, LANES), F32))
+    lax.fori_loop(prompt_tiles, tiles, branch_sums, 0)
+
     def rates(t, bias):
         rows = pl.ds(pl.multiple_of(t * TILE, TILE), TILE)
-
-        def add_decays(u, acc):
-            others = pl.ds(pl.multiple_of(u * TILE, TILE), TILE)
-            pos_b = t * TILE + lax.broadcasted_iota(jnp.int32, (TILE, TILE), 0)
-            pos_a = u * TILE + lax.broadcasted_iota(jnp.int32, (TILE, TILE), 1)
-            adds = decay_map(
-                pos_a, qrow[2:3, others], qrow[4:5, others], pos_b, kcol[rows, 1:2], kcol[rows, 3:4]
-            )
-            return acc + dot_nn(adds, decay[others, :].astype(BF16))
-
-        sums = lax.fori_loop(t, tiles, add_decays, jnp.zeros((TILE, LANES), F32))
+        sums = decay[rows, :]
         grad_rate = sums + pltpu.roll(sums, LANES - 8, 1) + pltpu.roll(sums, LANES - 16, 1)
         value = logit[rows, :]
         grad_forget = grad_rate / (1.0 + jnp.exp(value))
@@ -472,8 +523,8 @@
         store.wait()
 
 
-def attention_backward(grad_attended, saved, logit, kcol, qrow, flags, heads, prompt_len):
-    ot, lse, qp, kp, vp = saved
+def attention_backward(grad_attended, saved, kcol, qrow, flags, heads, prompt_len):
+    ot, lse, qp, kp, vp, logit = saved
     count, size, width = grad_attended.shape
     total = count * size
     any_spec = pl.BlockSpec(memory_space=pl.ANY)
@@ -484,24 +535,24 @@
         functools.partial(backward_kernel, heads, count, prompt_len),
         out_shape=(shape((count, size, out_width), BF16), shape((8, LANES), F32)),
         in_specs=[pl.BlockSpec(memory_space=pltpu.SMEM), any_spec]
-        + [vmem] * 5
-        + [any_spec, vmem, vmem],
+        + [vmem] * 8,
         out_specs=(any_spec, vmem),
         scratch_shapes=[
             pltpu.VMEM((total, width), BF16),
-            pltpu.VMEM((total, LANES), F32),
             pltpu.VMEM((heads, total, DH), BF16),
             pltpu.VMEM((heads, DH + 8, total), BF16),
             pltpu.VMEM((8, total), F32),
-            pltpu.VMEM((heads, DH + 8, total), F32),
-            pltpu.VMEM((heads, TILE, LANES), F32),
-            pltpu.VMEM((heads, TILE, DH), F32),
             pltpu.VMEM((TILE, TILE), F32),
             pltpu.VMEM((total, LANES), F32),
             pltpu.VMEM((total, out_width), BF16),
-            pltpu.SemaphoreType.DMA((2 * count,)),
             pltpu.SemaphoreType.DMA((count,)),
-        ],
+            pltpu.SemaphoreType.DMA((count,)),
+        ]
+        + [pltpu.VMEM((DH + 8, total), F32)] * heads
+        + [pltpu.VMEM((TILE, LANES), F32)] * heads
+        + [pltpu.VMEM((TILE, DH), F32)] * heads
+        + [pltpu.VMEM((TILE, TILE), F32)] * heads
+        + [pltpu.VMEM((TILE, TILE), BF16)] * heads,
         compiler_params=pltpu.CompilerParams(vmem_limit_bytes=56 << 20),
         cost_estimate=pl.CostEstimate(flops=50_000_000_000, bytes_accessed=30_000_000, transcendentals=0),
         name="attention_backward",
@@ -1114,7 +1165,7 @@
 def backward_exchange_kernel(
     psize, part, resid, cot, gain_ref, down_own, down_other, gate_part, gate_got, up_part,
     grad_resid, g, gain_grad, down_sum, pair_sum,
-    near, mid, far, own, down_across, gate_val, gate_over, gate_across, up_val, up_over, up_across,
+    near, mid, far, own, down_across, down_moved, gate_val, gate_over, gate_across, up_val, up_over, up_across,
     send_sem, recv_sem, local_sem,
 ):
     w = Wires(send_sem, recv_sem, local_sem)
@@ -1122,7 +1173,7 @@
     up = EarlySum(w, up_part, up_val, up_over, up_across, pair_sum.at[1], 2)
     gate.load()
     up.load()
-    w.greet(partners(w, psize, over_o=2))
+    w.greet(partners(w, psize, away=True, over_o=2))
     spans = row_spans(own.shape[0], PIECES)
     reduce = Reduce(w, psize, part, near, mid, far, spans)
     down_copy = w.send(down_other, down_across, {"x": 1 - w.x})
@@ -1132,6 +1183,20 @@
     for i in range(2):
         gate.pass_on(i)
     reduce.start()
+    down_home = w.copy(down_sum, down_moved, {"h": 1 - w.h}, w.slot())
+    down_copy.wait_recv()
+
+    def add_down(rows):
+        down_sum[rows, :] = (
+            down_own[rows, :].astype(F32) + down_across[rows, :].astype(F32)
+        ).astype(BF16)
+
+    by_chunks(pl.ds(0, down_sum.shape[0]), add_down)
+
+    @pl.when(jnp.logical_not(w.home))
+    def _():
+        down_home.start()
+
     share = Share(w, psize, own, g, spans)
     gain_grad[...] = jnp.zeros(gain_grad.shape, F32)
 
@@ -1149,14 +1214,6 @@
     share.relay(0)
     for i in range(2):
         gate.finish(i)
-    down_copy.wait_recv()
-
-    def add_down(rows):
-        down_sum[rows, :] = (
-            down_own[rows, :].astype(F32) + down_across[rows, :].astype(F32)
-        ).astype(BF16)
-
-    by_chunks(pl.ds(0, down_sum.shape[0]), add_down)
     for i in range(1, PIECES):
         share.relay(i)
     for i in range(2):
@@ -1164,6 +1221,16 @@
     share.wait()
     gate.close()
     up.close()
+
+    @pl.when(jnp.logical_not(w.home))
+    def _():
+        down_home.wait_send()
+
+    @pl.when(w.home)
+    def _():
+        down_home.wait_recv()
+        add_into(down_sum, down_moved)
+
     w.close()
 
 
@@ -1593,7 +1660,8 @@
         (VMEM, ANY, VMEM, VMEM, ANY),
         [VMEM, VMEM, VMEM, VMEM, VMEM, ANY, ANY, VMEM, ANY],
         sum_scratch(psize, rows)
-        + [pltpu.VMEM((rows, D), BF16), pltpu.VMEM(down_own.shape, BF16)]
+        + [pltpu.VMEM((rows, D), BF16)]
+        + [pltpu.VMEM(down_own.shape, BF16)] * 2
         + early(gate_part)
         + early(up_part),
         (part, resid, cot, gains, down_own, down_other, gate_part, gate_got, up_part),
@@ -1732,14 +1800,11 @@
         normed_a_all = normed_a_all.reshape(-1, D)
         w_proj = w_proj.reshape(D, -1)[:, : width + LANES]
 
-        projected = matmul(normed_a_all, w_proj)
-        qkv = projected[:, :width].astype(BF16).reshape(count, -1, width)
-        logit = (projected[:, width:] + bias).reshape(count, -1, LANES)
+        projected = matmul(normed_a_all, w_proj).reshape(count, -1, width + LANES)
         cot_near, cot_far = take_half(out_cotangent, core), take_half(out_cotangent, 1 - core)
-        qkv, logit, kcol, qrow, flags, gate_half, up_half, cot_first, cot_near, cot_far = lax.optimization_barrier(
+        projected, kcol, qrow, flags, gate_half, up_half, cot_first, cot_near, cot_far = lax.optimization_barrier(
             (
-                qkv,
-                logit,
+                projected,
                 kcol,
                 qrow,
                 flags,
@@ -1753,7 +1818,9 @@
         gate_got, up_got = fetch_home_away(gate_half), fetch_home_away(up_half)
         cot_first = lax.ppermute(cot_first, ("k", "x"), SPREAD_A)
         cot_second = lax.ppermute(cot_far, ("k", "x"), SPREAD_B)
-        attended, *saved = attention_forward(qkv, logit, kcol, qrow, flags, heads, prompt_len)
+        attended, *saved = attention_forward(
+            projected, bias[None], kcol, qrow, flags, heads, prompt_len
+        )
         attended, gate_got, up_got, cot_first, cot_second, *saved = lax.optimization_barrier(
             (attended, gate_got, up_got, cot_first, cot_second, *saved)
         )
@@ -1820,23 +1887,21 @@
             (grad_attended, out_keep, out_give, down_total, pair_total) + unspread_parts(layer_output, same)
         )
         own_part, near_part, far_part = block_parts
-        moved = [to_home(down_total), to_home(pair_total)]
+        pair_moved = to_home(pair_total)
         out_moved = xor_swap(out_give, "o", osize, 1)
         near_moved, far_moved = unspread_moves(near_part, far_part)
         grad_proj, bias_sums = attention_backward(
-            grad_attended.reshape(count, -1, heads * DH), saved, logit, kcol, qrow, flags, heads, prompt_len
-        )
-        grad_proj, bias_sums, out_moved, near_moved, far_moved, *moved = lax.optimization_barrier(
-            (grad_proj, bias_sums, out_moved, near_moved, far_moved, *moved)
+            grad_attended.reshape(count, -1, heads * DH), saved, kcol, qrow, flags, heads, prompt_len
+        )
+        grad_proj, bias_sums, out_moved, near_moved, far_moved, pair_moved = lax.optimization_barrier(
+            (grad_proj, bias_sums, out_moved, near_moved, far_moved, pair_moved)
         )
         layer_output = unspread_join(own_part, near_moved, far_moved, core, same)
         grad_proj = grad_proj.reshape(-1, width + LANES)
         proj_part = contract_rows(normed_a_all, grad_proj).astype(BF16)
         part = contract_cols(grad_proj, w_proj).astype(BF16).reshape(count, -1, D)
-        down_total, pair_total = (
-            finish(add_parts(value, other), obits[1:])
-            for value, other in zip((down_total, pair_total), moved)
-        )
+        down_total = finish(down_total, obits[1:])
+        pair_total = finish(add_parts(pair_total, pair_moved), obits[1:])
         out_total = add_parts(out_keep, out_moved)
 
         slots = jnp.where(

time: 621 us -> 592 us (0.953)
  Pallas kernels: 382 us -> 364 us
  starting transfers between devices: 38.4 us -> 31 us
  local copies, waits for them, and re-layouts: 26.6 us -> 19.4 us
    pallas_call x1, Pallas kernels: 44.2 us -> 27.2 us  [attention_forward(): pl.pallas_call(functools.partial(forward_kernel, heads, count, prompt_len...]
    pallas_call x1, Pallas kernels: 51.6 us -> 40.8 us  [attention_backward(): pl.pallas_call(functools.partial(backward_kernel, heads, count, prompt_le...]
    pallas_call x4, Pallas kernels: 286 us -> 296 us  [exchange_call(): pl.pallas_call(kernel, out_shape=outs, in_specs=in_specs, out_specs=out_s...]
  transfers between devices with their start and end apart: 18 -> 17, of which waited for: 3 -> 4; matrix products, arithmetic and copies ran while one was open for 17% -> 18% of each run, Pallas kernels for 38% -> 35%
where the time goes in v5:
time: 592 us; the launch traced here: 587 us
  Pallas kernels  364 us (61%)
  matrix products  117 us (20%)
  other arithmetic  34.5 us (6%)
  starting transfers between devices  31 us (5%)
  local copies, waits for them, and re-layouts  19.4 us (3%)
  waiting for transfers between devices  19.3 us (3%)
    pallas_call x4, Pallas kernels, exchange_call(): pl.pallas_call(kernel, out_shape=outs, in_specs=in_specs, out_specs=out_s...  296 us
    dot_general x5, matrix products, contract_cols(): lax.dot_general(left, right, (((1,), (1,)), ((), ())), preferred_element_...  43.9 us
    pallas_call x1, Pallas kernels, attention_backward(): pl.pallas_call(functools.partial(backward_kernel, heads, count, prompt_le...  40.8 us
    dot_general x5, matrix products, contract_rows(): lax.dot_general(left, right, (((0,), (0,)), ((), ())), preferred_element_...  36.8 us
    dot_general x5, matrix products, matmul(): return jnp.dot(left, right, preferred_element_type=F32)  36.3 us
    pallas_call x1, Pallas kernels, attention_forward(): pl.pallas_call(functools.partial(forward_kernel, heads, count, prompt_len...  27.2 us
    ppermute x5, waiting for transfers between devices, xor_swap(): return lax.ppermute(value, axis, [(i, i ^ bit) for i in range(size)])  17.6 us
  transfers between devices with their start and end apart: 17, of which 4 were waited for; matrix products, arithmetic and copies ran while one was open for 18% of the time, Pallas kernels for 35%

profile of v5, /device:TPU:1, one launch (start us, length us, event | category | flops | bytes accessed | tf_op | source)
XLA Modules:
  0.0 586.7 jit_solution(1134823739113546095)
XLA Ops:
  0.6 5.6 collective-permute-start
  6.3 0.9 copy.43
  7.2 0.7 stack.51
  7.9 0.7 stack.52
  8.6 0.7 pad_add_fusion.2
  9.9 0.7 concatenate.49.forget_shard
  11.4 64.3 %enter.1 = (bf16[384,1536]{1,0:T(8,128)(2,1)}, bf16[4,384,1536]{2,1,0:T(8,128)(2,1)}, bf16[2,768,1280]{2,1,0:T(8,128)(2,1)}, bf16[384,1536]{1,0:T(8,128)(2,1)}, ...) custom-call(bf16[768,768]{1,0:T(8,128)(2,1)} %x_ref.1, f32[8,768]{1,0:T(8,128)} %maximum_maximum_fusion.1.gain_own, ...), custom_call_target="tpu_custom_call" | custom-call | tf_op jit(solution)/shard_map/enter/pallas_call | solution.py:1557
  75.6 0.7 dynamic-slice_bitcast_fusion
  78.6 11.4 %fusion.17.proj_hbm = f32[4,384,1280]{2,1,0:T(8,128)} fusion(bf16[4,384,1536]{2,1,0:T(8,128)(2,1)} %get-tuple-element.88, bf16[1536,1280,1]{1,0,2:T(8,128)(2,1)} %bitcast.104), kind=kOutput, calls=%fused_computation.87 | convolution fusion | flops 6039797760 | bytes 16515072 | tf_op jit(solution)/shard_map/dot_general | solution.py:157
  90.0 1.3 constant_dynamic-slice_fusion.5
  91.7 1.3 broadcast_select_fusion.8
  93.1 3.5 collective-permute-start.1
  96.7 2.2 collective-permute-start.3
  98.9 1.9 collective-permute-start.4
  102.8 27.2 %attention_forward.1 = (bf16[4,384,384]{2,1,0:T(8,128)(2,1)S(1)}, f32[384,1536]{1,0:T(8,128)S(1)}, f32[8,1536]{1,0:T(8,128)S(1)}, bf16[6,1536,128]{2,1,0:T(8,128...) custom-call(s32[36]{0:T(128)S(1)} %reshape.142.flags, ...), custom_call_target="tpu_custom_call" | custom-call | flops 20000000000 | bytes 30000000 | tf_op jit(solution)/shard_map/attention_forward/pallas_call | solution.py:343
  130.1 1.7 collective-permute-done.2.up_got
  131.8 1.6 broadcast_select_fusion.7
  133.6 4.4 convolution_convert_fusion.2
  138.0 74.7 %forward_exchange.1 = (f32[384,1536]{1,0:T(8,128)}, bf16[4,384,1536]{2,1,0:T(8,128)(2,1)}, bf16[2,768,1024]{2,1,0:T(8,128)(2,1)}, bf16[2,768,1024]{2,1,0:T(8,128)(2,1)}, bf16[1024,1536]{1,0:T(8,128)(2,1)}) custom-call(bf16[4,384,1536]{2,1,0:T(8,128)(2,1)} %bitcast.89, bf16[384,1536]{1,0:T(8,128)(2,1)} %get-tuple-element.111.xin.stream, ...), custom_call_target="tpu_custom_call" | custom-call | tf_op jit(solution)/shard_map/forward_exchange/pallas_call | solution.py:1557
  212.7 6.2 %collective-permute-start.6 = (bf16[384,1536]{1,0:T(8,128)(2,1)S(1)}, bf16[384,1536]{1,0:T(8,128)(2,1)S(1)}, u32[]{:S(2)}, u32[]{:S(2)}) collective-permute-start(bf16[384,1536]{1,0:T(8,128)(2,1)S(1)} %pad_maximum_fusion.1.cot), channel_id=1, source_target_pairs={{0,1},{1,0},{2,3},{3,2},{4,5},{5,4},{6,7},{7,6},{8,9},{9,8},{10,11... | collective-permute-start | bytes 3538952 | tf_op jit(solution)/shard_map/ppermute | solution.py:26
  219.0 8.0 %fusion.18 = f32[1536,1024]{1,0:T(8,128)S(1)} fusion(bf16[1536,1536]{1,0:T(8,128)(2,1)} %bitcast.98, bf16[1536,1024]{1,0:T(8,128)(2,1)} %bitcast.108), kind=kOutput, calls=%fused_computation.88 | convolution fusion | flops 4831838208 | bytes 14155776 | tf_op jit(solution)/shard_map/dot_general | solution.py:157
  227.0 7.3 %multiply_convert_fusion.2 = (bf16[1536,1024]{1,0:T(8,128)(2,1)S(1)}, f32[1536,1024]{1,0:T(8,128)}) fusion(f32[1536,1024]{1,0:T(8,128)S(1)} %fusion.18, bf16[1536,1536]{1,0:T(8,128)(2,1)S(1)} %bitcast.100, bf16[1536,1024]{1,0:T(8,128)(2,1)S(1)} %bitcast.106), kind=kOutput, calls=%fused_computation.8 | convolution fusion | flops 4841275392 | bytes 23592960 | tf_op jit(solution)/shard_map/dot_general | solution.py:157
  234.3 7.1 %collective-permute-done.6 = bf16[384,1536]{1,0:T(8,128)(2,1)S(1)} collective-permute-done((bf16[384,1536]{1,0:T(8,128)(2,1)S(1)}, bf16[384,1536]{1,0:T(8,128)(2,1)S(1)}, u32[]{:S(2)}, u32[]{:S(2)}) %collective-permute-start.6) | collective-permute-done | bytes 1179680 | tf_op jit(solution)/shard_map/ppermute | solution.py:26
  241.4 5.3 convolution_convert_fusion
  247.5 8.0 %convolution_convert_fusion.3 = bf16[1024,1536]{1,0:T(8,128)(2,1)S(1)} fusion(bf16[1536,1024]{1,0:T(8,128)(2,1)S(1)} %get-tuple-element.119, bf16[384,1536]{1,0:T(8,128)(2,1)S(1)} %collective-permute-done.7, bf16[384,1536]{1,0:T(8,128)(2,1)S(1)} %collective-permute-done.6, bf16[384,1536]{1,0:T(8,128)(2,1)S(1)} %collective-permute-done.5, ...), kind=kOutput, calls=%fused_computation.12 | convolution fusion | flops 4857004032 | bytes 11010048 | tf_op jit(solution)/shard_map/dot_general | solution.py:145
  256.0 4.3 pad_maximum_fusion
  261.0 12.4 %multiply_convert_fusion = (bf16[1536,1024]{1,0:T(8,128)(2,1)}, bf16[1536,1024]{1,0:T(8,128)(2,1)}) fusion(f32[1536,1024]{1,0:T(8,128)} %copy-done.34, f32[1536,1024]{1,0:T(8,128)} %get-tuple-element.240, bf16[1536,1536]{1,0:T(8,128)(2,1)S(1)} %pad_maximum_fusion, bf16[1024,1536]{1,0:T(8,128)(2,1)} %get-tuple-element.120), kind=kOutput, calls=%fused_computation.6 | convolution fusion | flops 4852285440 | bytes 26738688 | tf_op jit(solution)/shard_map/dot_general | solution.py:151
  273.4 8.3 %convolution_convert_fusion.5 = bf16[1536,1024]{1,0:T(8,128)(2,1)S(1)} fusion(bf16[1536,1536]{1,0:T(8,128)(2,1)} %bitcast.99, bf16[1536,1024]{1,0:T(8,128)(2,1)} %get-tuple-element.122), kind=kOutput, calls=%fused_computation.14 | convolution fusion | flops 4833411072 | bytes 11010048 | tf_op jit(solution)/shard_map/dot_general | solution.py:145
  281.9 2.9 copy-done.29
  284.7 7.8 %fusion.19 = f32[1536,1536]{1,0:T(8,128)} fusion(bf16[1536,1024]{1,0:T(8,128)(2,1)S(1)} %copy-done.35, bf16[1536,1024]{1,0:T(8,128)(2,1)S(1)} %bitcast.109), kind=kOutput, calls=%fused_computation.89 | convolution fusion | flops 4831838208 | bytes 15728640 | tf_op jit(solution)/shard_map/dot_general | solution.py:151
  292.6 1.3 collective-permute-start.9
  294.1 9.3 %add_convert_fusion = bf16[1536,1536]{1,0:T(8,128)(2,1)} fusion(f32[1536,1536]{1,0:T(8,128)} %fusion.19, bf16[1536,1024]{1,0:T(8,128)(2,1)S(1)} %copy-done.36, bf16[1536,1024]{1,0:T(8,128)(2,1)S(1)} %bitcast.107), kind=kOutput, calls=%fused_computation | convolution fusion | flops 4836556800 | bytes 20447232 | tf_op jit(solution)/shard_map/dot_general | solution.py:151
  303.4 6.5 %convolution_convert_fusion.4 = bf16[1536,1024]{1,0:T(8,128)(2,1)} fusion(bf16[1536,1536]{1,0:T(8,128)(2,1)S(1)} %bitcast.103, bf16[1536,1024]{1,0:T(8,128)(2,1)S(1)} %copy-done.36), kind=kOutput, calls=%fused_computation.13 | convolution fusion | flops 4833411072 | bytes 11010048 | tf_op jit(solution)/shard_map/dot_general | solution.py:145
  309.9 1.1 collective-permute-done.9.gate_got
  311.0 9.3 %collective-permute-done.12 = bf16[384,1536]{1,0:T(8,128)(2,1)S(1)} collective-permute-done((bf16[384,1536]{1,0:T(8,128)(2,1)S(1)}, bf16[384,1536]{1,0:T(8,128)(2,1)S(1)}, u32[]{:S(2)}, u32[]{:S(2)}) %collective-permute-start.12) | collective-permute-done | bytes 1179680 | tf_op jit(solution)/shard_map/ppermute | solution.py:26
  320.9 1.2 fusion.15
  322.7 1.2 fusion.14
  323.9 76.2 %backward_exchange.1 = (f32[384,1536]{1,0:T(8,128)}, bf16[4,384,1536]{2,1,0:T(8,128)(2,1)}, f32[8,1536]{1,0:T(8,128)}, bf16[512,768]{1,0:T(8,128)(2,1)}, bf16[2,384,1024]{2,1,0:T(8,128)(2,1)}) custom-call(bf16[4,384,1536]{2,1,0:T(8,128)(2,1)} %bitcast.87, f32[384,1536]{1,0:T(8,128)} %get-tuple-element.125.resid, bf16[384,1536]{1,0:T(8,128)(2,1)} %copy-done.8, ...), custom_call_target="tpu_custom_call" | custom-call | tf_op jit(solution)/shard_map/backward_exchange/pallas_call | solution.py:1557
  400.2 4.5 fusion.2
  404.7 0.9 broadcast_select_fusion.1
  405.6 3.7 convolution_convert_fusion.6
  409.3 4.8 collective-permute-start.16
  414.1 1.0 collective-permute-start.13
  415.1 3.1 collective-permute-start.15
  418.3 40.8 %attention_backward.1 = (bf16[4,384,1280]{2,1,0:T(8,128)(2,1)}, f32[8,128]{1,0:T(8,128)}) custom-call(s32[36]{0:T(128)} %copy-done.2, bf16[4,384,384]{2,1,0:T(8,128)(2,1)} %bitcast.111, f32[384,1536]{1,0:T(8,128)} %copy-done.3, f32[8,1536]{1,0:T(8,128)} %copy-done.5, bf16[6,1536,128]{2,1,0:T(8,128)(2,1)} %get-tuple-element.137.qp, ...), custom_call_target="tpu_custom_call" | custom-call | flops 49999998976 | bytes 30000000 | tf_op jit(solution)/shard_map/attention_backward/pallas_call | solution.py:534
  459.1 3.4 add_convert_fusion.1.pair_in
  462.7 0.9 fusion.16
  463.6 9.5 %fusion = bf16[1536,1280]{1,0:T(8,128)(2,1)} fusion(bf16[4,384,1536]{2,1,0:T(8,128)(2,1)} %get-tuple-element.88, bf16[4,384,1280]{2,1,0:T(8,128)(2,1)S(1)} %copy-done.33), kind=kOutput, calls=%fused_computation.3 | convolution fusion | flops 6041763840 | bytes 12582912 | tf_op jit(solution)/shard_map/dot_general | solution.py:145
  473.1 0.7 slice_bitcast_fusion
  474.1 10.8 %convolution_convert_fusion.1 = bf16[1536,1536]{1,0:T(8,128)(2,1)} fusion(bf16[1536,1280]{1,0:T(8,128)(2,1)} %bitcast.110, bf16[1536,1280]{1,0:T(8,128)(2,1)} %bitcast.105), kind=kOutput, calls=%fused_computation.4 | convolution fusion | flops 6042157056 | bytes 12582912 | tf_op jit(solution)/shard_map/dot_general | solution.py:151
  484.9 0.7 maximum_maximum_fusion.small_in
  485.6 80.6 %leave.1 = (bf16[768,768]{1,0:T(8,128)(2,1)}, f32[8,768]{1,0:T(8,128)}, bf16[384,1280]{1,0:T(8,128)(2,1)}, bf16[2,192,1280]{2,1,0:T(8,128)(2,1)}, bf16[2,192,768...) custom-call(bf16[4,384,1536]{2,1,0:T(8,128)(2,1)} %bitcast.90, ...), custom_call_target="tpu_custom_call" | custom-call | tf_op jit(solution)/shard_map/leave/pallas_call | solution.py:1557
  566.1 1.0 fusion.5
  567.1 3.5 fusion.4
  570.6 0.8 slice_reduce_fusion.2
  571.4 1.4 slice_reduce_fusion
  572.8 0.8 copy.48
  573.6 3.3 bitcast_convert_fusion
  576.9 2.2 bitcast_convert_fusion.1
  579.1 2.2 bitcast_convert_fusion.2
  581.2 1.1 bitcast_convert_fusion.3
  583.0 1.3 broadcast_select_fusion.10
  584.3 1.1 pad_maximum_fusion.2
  585.4 1.0 copy.52
  (155 shorter events, 11.0 us)
Async XLA Ops:
  0.6 102.1 %collective-permute-start = (f32[6]{0:T(128)}, f32[6]{0:T(128)S(1)}, u32[]{:S(2)}, u32[]{:S(2)}) collective-permute-start(f32[6]{0:T(128)} %param.18), channel_id=1, source_target_pairs={{2,8},{8,2},{3,9},{9,3},{6,12},{12,6},{7,13},{13,7},{18,24},{24,18... | collective-permute-start | bytes 80 | tf_op jit(solution)/shard_map/ppermute | solution.py:1780
  78.6 24.2 %copy-start.2 = (s32[36]{0:T(128)}, s32[36]{0:T(128)S(1)}, u32[]{:S(2)}) copy-start(s32[36]{0:T(128)S(1)} %reshape.142.flags) | copy-start | bytes 436
  78.6 11.4 %copy-start.10 = (bf16[768,1024]{1,0:T(8,128)(2,1)S(1)}, bf16[768,1024]{1,0:T(8,128)(2,1)}, u32[]{:S(2)}) copy-start(bf16[768,1024]{1,0:T(8,128)(2,1)} %gate_shard.1) | copy-start | bytes 4718596
  78.6 11.4 %copy-start.11 = (bf16[768,1024]{1,0:T(8,128)(2,1)S(1)}, bf16[768,1024]{1,0:T(8,128)(2,1)}, u32[]{:S(2)}) copy-start(bf16[768,1024]{1,0:T(8,128)(2,1)} %up_shard.1) | copy-start | bytes 4718596
  90.0 1.7 copy-start.15
  90.0 12.8 %copy-start.24 = (f32[6]{0:T(128)S(1)}, f32[6]{0:T(128)}, u32[]{:S(2)}) copy-start(f32[6]{0:T(128)} %param.18) | copy-start | bytes 76
  93.1 36.8 %copy-start.1 = (s32[8,1536]{1,0:T(8,128)}, s32[8,1536]{1,0:T(8,128)S(1)}, u32[]{:S(2)}) copy-start(s32[8,1536]{1,0:T(8,128)S(1)} %stack.65.qrow) | copy-start | bytes 147460
  93.1 36.9 %collective-permute-start.1 = (bf16[384,1024]{1,0:T(8,128)(2,1)}, bf16[384,1024]{1,0:T(8,128)(2,1)S(1)}, u32[]{:S(2)}, u32[]{:S(2)}) collective-permute-start(bf16[384,1024]{1,0:T(8,128)(2,1)} %get-tuple-element.97), channel_id=1, source_target_pairs={{0,4},{2,8},{4,0},{6,12},{8,2},{10,14},{12,6},{14,10},{1,5},{3,9},... | collective-permute-start | bytes 2359304 | tf_op jit(solution)/shard_map/ppermute | solution.py:40
  96.6 35.2 %collective-permute-start.2 = (bf16[384,1024]{1,0:T(8,128)(2,1)}, bf16[384,1024]{1,0:T(8,128)(2,1)S(1)}, u32[]{:S(2)}, u32[]{:S(2)}) collective-permute-start(bf16[384,1024]{1,0:T(8,128)(2,1)} %get-tuple-element.98), channel_id=1, source_target_pairs={{0,4},{2,8},{4,0},{6,12},{8,2},{10,14},{12,6},{14,10},{1,5},{3,9},... | collective-permute-start | bytes 2359304 | tf_op jit(solution)/shard_map/ppermute | solution.py:40
  96.7 33.3 %collective-permute-start.3 = (bf16[384,768]{1,0:T(8,128)(2,1)}, bf16[384,768]{1,0:T(8,128)(2,1)}, u32[]{:S(2)}, u32[]{:S(2)}) collective-permute-start(bf16[384,768]{1,0:T(8,128)(2,1)} %get-tuple-element.99), channel_id=1, source_target_pairs={{0,8},{4,0},{8,12},{12,4},{1,9},{5,1},{9,13},{13,5},{2,10},{6,2},{... | collective-permute-start | bytes 1769480 | tf_op jit(solution)/shard_map/ppermute | solution.py:1819
  98.9 31.2 %collective-permute-start.4 = (bf16[384,768]{1,0:T(8,128)(2,1)}, bf16[384,768]{1,0:T(8,128)(2,1)}, u32[]{:S(2)}, u32[]{:S(2)}) collective-permute-start(bf16[384,768]{1,0:T(8,128)(2,1)} %get-tuple-element.100), channel_id=1, source_target_pairs={{4,8},{8,4},{5,9},{9,5},{6,10},{10,6},{7,11},{11,7},{20,24},{24,20... | collective-permute-start | bytes 1769480 | tf_op jit(solution)/shard_map/ppermute | solution.py:1820
  101.1 28.9 %copy-start = (s32[1536,8]{1,0:T(8,128)}, s32[1536,8]{1,0:T(8,128)S(1)}, u32[]{:S(2)}) copy-start(s32[1536,8]{1,0:T(8,128)S(1)} %copy.44.kcol) | copy-start | bytes 147460
  130.0 8.0 %copy-start.3 = (f32[384,1536]{1,0:T(8,128)}, f32[384,1536]{1,0:T(8,128)S(1)}, u32[]{:S(2)}) copy-start(f32[384,1536]{1,0:T(8,128)S(1)} %get-tuple-element.135.ot_ref) | copy-start | bytes 7077892
  130.0 8.0 %copy-start.4 = (f32[1536,128]{1,0:T(8,128)}, f32[1536,128]{1,0:T(8,128)S(1)}, u32[]{:S(2)}) copy-start(f32[1536,128]{1,0:T(8,128)S(1)} %get-tuple-element.140.logit) | copy-start | bytes 2359300
  130.0 8.0 %copy-start.5 = (f32[8,1536]{1,0:T(8,128)}, f32[8,1536]{1,0:T(8,128)S(1)}, u32[]{:S(2)}) copy-start(f32[8,1536]{1,0:T(8,128)S(1)} %get-tuple-element.136.lse_ref) | copy-start | bytes 147460
  130.0 3.6 copy-start.31
  130.1 7.9 %copy-start.18 = (bf16[384,1024]{1,0:T(8,128)(2,1)}, bf16[384,1024]{1,0:T(8,128)(2,1)S(1)}, u32[]{:S(2)}) copy-start(bf16[384,1024]{1,0:T(8,128)(2,1)S(1)} %collective-permute-done.1.gate_got) | copy-start | bytes 2359300
  131.8 6.2 %copy-start.19 = (bf16[384,1024]{1,0:T(8,128)(2,1)}, bf16[384,1024]{1,0:T(8,128)(2,1)S(1)}, u32[]{:S(2)}) copy-start(bf16[384,1024]{1,0:T(8,128)(2,1)S(1)} %collective-permute-done.2.up_got) | copy-start | bytes 2359300
  133.5 79.2 %copy-start.8 = (bf16[384,1536]{1,0:T(8,128)(2,1)}, bf16[384,1536]{1,0:T(8,128)(2,1)S(1)}, u32[]{:S(2)}) copy-start(bf16[384,1536]{1,0:T(8,128)(2,1)S(1)} %pad_maximum_fusion.1.cot) | copy-start | bytes 3538948
  133.5 114.0 %collective-permute-start.5 = (bf16[384,1536]{1,0:T(8,128)(2,1)S(1)}, bf16[384,1536]{1,0:T(8,128)(2,1)S(1)}, u32[]{:S(2)}, u32[]{:S(2)}) collective-permute-start(bf16[384,1536]{1,0:T(8,128)(2,1)S(1)} %pad_maximum_fusion.1.cot), channel_id=1, source_target_pairs={{0,8},{8,0},{1,9},{9,1},{2,10},{10,2},{3,11},{11,3},{4,12},{12,4},... | collective-permute-start | bytes 3538952 | tf_op jit(solution)/shard_map/ppermute | solution.py:22
  212.7 28.7 %collective-permute-start.6 = (bf16[384,1536]{1,0:T(8,128)(2,1)S(1)}, bf16[384,1536]{1,0:T(8,128)(2,1)S(1)}, u32[]{:S(2)}, u32[]{:S(2)}) collective-permute-start(bf16[384,1536]{1,0:T(8,128)(2,1)S(1)} %pad_maximum_fusion.1.cot), channel_id=1, source_target_pairs={{0,1},{1,0},{2,3},{3,2},{4,5},{5,4},{6,7},{7,6},{8,9},{9,8},{10,11... | collective-permute-start | bytes 3538952 | tf_op jit(solution)/shard_map/ppermute | solution.py:26
  219.0 8.0 %copy-start.26 = (bf16[4,384,1536]{2,1,0:T(8,128)(2,1)S(1)}, bf16[4,384,1536]{2,1,0:T(8,128)(2,1)}, u32[]{:S(2)}) copy-start(bf16[4,384,1536]{2,1,0:T(8,128)(2,1)} %get-tuple-element.115) | copy-start | bytes 14155780
  219.0 8.0 %copy-start.27 = (bf16[2,768,1024]{2,1,0:T(8,128)(2,1)S(1)}, bf16[2,768,1024]{2,1,0:T(8,128)(2,1)}, u32[]{:S(2)}) copy-start(bf16[2,768,1024]{2,1,0:T(8,128)(2,1)} %get-tuple-element.118) | copy-start | bytes 9437188
  226.9 7.4 %copy-start.34 = (f32[1536,1024]{1,0:T(8,128)}, f32[1536,1024]{1,0:T(8,128)S(1)}, u32[]{:S(2)}) copy-start(f32[1536,1024]{1,0:T(8,128)S(1)} %fusion.18) | copy-start | bytes 18874372
  227.0 14.4 %copy-start.30 = (bf16[1024,1536]{1,0:T(8,128)(2,1)S(1)}, bf16[1024,1536]{1,0:T(8,128)(2,1)}, u32[]{:S(2)}) copy-start(bf16[1024,1536]{1,0:T(8,128)(2,1)} %get-tuple-element.120) | copy-start | bytes 9437188
  241.4 6.1 %collective-permute-start.7 = (bf16[384,1536]{1,0:T(8,128)(2,1)S(1)}, bf16[384,1536]{1,0:T(8,128)(2,1)S(1)}, u32[]{:S(2)}, u32[]{:S(2)}) collective-permute-start(bf16[384,1536]{1,0:T(8,128)(2,1)S(1)} %collective-permute-done.6), channel_id=1, source_target_pairs={{0,8},{8,0},{1,9},{9,1},{2,10},{10,2},{3,11},{11,3},{4,12},{12,4},... | collective-permute-start | bytes 3538952 | tf_op jit(solution)/shard_map/ppermute | solution.py:22
  246.9 13.4 %collective-permute-start.11 = (bf16[384,1536]{1,0:T(8,128)(2,1)S(1)}, bf16[384,1536]{1,0:T(8,128)(2,1)S(1)}, u32[]{:S(2)}, u32[]{:S(2)}) collective-permute-start(bf16[384,1536]{1,0:T(8,128)(2,1)S(1)} %get-tuple-element.220), channel_id=1, source_target_pairs={{0,8},{8,0},{1,9},{9,1},{2,10},{10,2},{3,11},{11,3},{4,12},{12,4},... | collective-permute-start | bytes 3538952 | tf_op jit(solution)/shard_map/ppermute | solution.py:22
  247.4 12.9 %collective-permute-start.8 = (bf16[384,1536]{1,0:T(8,128)(2,1)S(1)}, bf16[384,1536]{1,0:T(8,128)(2,1)S(1)}, u32[]{:S(2)}, u32[]{:S(2)}) collective-permute-start(bf16[384,1536]{1,0:T(8,128)(2,1)S(1)} %get-tuple-element.221), channel_id=1, source_target_pairs={{0,8},{8,0},{1,9},{9,1},{2,10},{10,2},{3,11},{11,3},{4,12},{12,4},... | collective-permute-start | bytes 3538952 | tf_op jit(solution)/shard_map/ppermute | solution.py:22
  255.7 64.7 %collective-permute-start.10 = (bf16[512,1536]{1,0:T(8,128)(2,1)S(1)}, bf16[512,1536]{1,0:T(8,128)(2,1)S(1)}, u32[]{:S(2)}, u32[]{:S(2)}) collective-permute-start(bf16[512,1536]{1,0:T(8,128)(2,1)S(1)} %broadcast_select_fusion), channel_id=1, source_target_pairs={{0,16},{16,0},{1,17},{17,1},{2,18},{18,2},{3,19},{19,3},{4,20},{20... | collective-permute-start | bytes 4718600 | tf_op jit(solution)/shard_map/ppermute | solution.py:26
  273.4 8.5 %copy-start.35 = (bf16[1536,1024]{1,0:T(8,128)(2,1)S(1)}, bf16[1536,1024]{1,0:T(8,128)(2,1)}, u32[]{:S(2)}) copy-start(bf16[1536,1024]{1,0:T(8,128)(2,1)} %get-tuple-element.122) | copy-start | bytes 9437188
  281.7 10.8 %copy-start.7 = (bf16[1536,1024]{1,0:T(8,128)(2,1)}, bf16[1536,1024]{1,0:T(8,128)(2,1)S(1)}, u32[]{:S(2)}) copy-start(bf16[1536,1024]{1,0:T(8,128)(2,1)S(1)} %convolution_convert_fusion.5) | copy-start | bytes 9437188
  281.7 3.0 copy-start.29
  284.7 9.4 %copy-start.28 = (bf16[2,768,1024]{2,1,0:T(8,128)(2,1)S(1)}, bf16[2,768,1024]{2,1,0:T(8,128)(2,1)}, u32[]{:S(2)}) copy-start(bf16[2,768,1024]{2,1,0:T(8,128)(2,1)} %get-tuple-element.118) | copy-start | bytes 9437188
  284.7 9.4 %copy-start.36 = (bf16[1536,1024]{1,0:T(8,128)(2,1)S(1)}, bf16[1536,1024]{1,0:T(8,128)(2,1)}, u32[]{:S(2)}) copy-start(bf16[1536,1024]{1,0:T(8,128)(2,1)} %get-tuple-element.123) | copy-start | bytes 9437188
  292.6 18.4 %collective-permute-start.9 = (bf16[384,1024]{1,0:T(8,128)(2,1)S(1)}, bf16[384,1024]{1,0:T(8,128)(2,1)S(1)}, u32[]{:S(2)}, u32[]{:S(2)}) collective-permute-start(bf16[384,1024]{1,0:T(8,128)(2,1)S(1)} %constant_dynamic-slice_fusion.2), channel_id=1, source_target_pairs={{0,16},{16,0},{1,17},{17,1},{2,18},{18,2},{3,19},{19,3},{4,20},{20... | collective-permute-start | bytes 2359304 | tf_op jit(solution)/shard_map/ppermute | solution.py:26
  293.9 9.5 %slice-start = ((s8[4718592]{0:T(1024)(128)(4,1)}), s8[4194304]{0:T(1024)(128)(4,1)S(1)}, s32[]{:S(2)}) async-start(s8[4718592]{0:T(1024)(128)(4,1)} %bitcast.101), calls=%async_computation | async-start | bytes 8388608
  293.9 9.5 %slice-start.1 = ((s8[4718592]{0:T(1024)(128)(4,1)}), s8[524288]{0:T(1024)(128)(4,1)S(1)}, s32[]{:S(2)}) async-start(s8[4718592]{0:T(1024)(128)(4,1)} %bitcast.101), calls=%async_computation.1 | async-start | bytes 1048576
  293.9 26.5 %collective-permute-start.12 = (bf16[384,1536]{1,0:T(8,128)(2,1)S(1)}, bf16[384,1536]{1,0:T(8,128)(2,1)S(1)}, u32[]{:S(2)}, u32[]{:S(2)}) collective-permute-start(bf16[384,1536]{1,0:T(8,128)(2,1)S(1)} %get-tuple-element.218), channel_id=1, source_target_pairs={{0,1},{1,0},{2,3},{3,2},{4,5},{5,4},{6,7},{7,6},{8,9},{9,8},{10,11... | collective-permute-start | bytes 3538952 | tf_op jit(solution)/shard_map/ppermute | solution.py:26
  303.4 17.0 %copy-start.6 = (f32[384,1536]{1,0:T(8,128)S(1)}, f32[384,1536]{1,0:T(8,128)}, u32[]{:S(2)}) copy-start(f32[384,1536]{1,0:T(8,128)} %get-tuple-element.125.resid) | copy-start | bytes 7077892
  311.0 11.0 %copy-start.17 = (bf16[384,1024]{1,0:T(8,128)(2,1)}, bf16[384,1024]{1,0:T(8,128)(2,1)S(1)}, u32[]{:S(2)}) copy-start(bf16[384,1024]{1,0:T(8,128)(2,1)S(1)} %collective-permute-done.9.gate_got) | copy-start | bytes 2359300
  400.2 5.4 copy-start.9
  400.2 5.4 copy-start.32
  405.6 3.7 copy-start.12
  409.3 49.9 %collective-permute-start.16 = (bf16[2,384,1024]{2,1,0:T(8,128)(2,1)S(1)}, bf16[2,384,1024]{2,1,0:T(8,128)(2,1)}, u32[]{:S(2)}, u32[]{:S(2)}) collective-permute-start(bf16[2,384,1024]{2,1,0:T(8,128)(2,1)S(1)} %copy-done.12), channel_id=1, source_target_pairs={{2,0},{8,10},{3,1},{9,11},{6,4},{12,14},{7,5},{13,15},{18,16},{24,... | collective-permute-start | bytes 4718600 | tf_op jit(solution)/shard_map/ppermute | solution.py:65
  414.1 45.0 %collective-permute-start.13 = (bf16[192,1536]{1,0:T(8,128)(2,1)}, bf16[192,1536]{1,0:T(8,128)(2,1)S(1)}, u32[]{:S(2)}, u32[]{:S(2)}) collective-permute-start(bf16[192,1536]{1,0:T(8,128)(2,1)} %get-tuple-element.143), channel_id=1, source_target_pairs={{0,16},{16,0},{1,17},{17,1},{2,18},{18,2},{3,19},{19,3},{4,20},{20... | collective-permute-start | bytes 1769480 | tf_op jit(solution)/shard_map/ppermute | solution.py:26
  415.1 44.0 %collective-permute-start.14 = (bf16[384,768]{1,0:T(8,128)(2,1)}, bf16[384,768]{1,0:T(8,128)(2,1)}, u32[]{:S(2)}, u32[]{:S(2)}) collective-permute-start(bf16[384,768]{1,0:T(8,128)(2,1)} %get-tuple-element.144), channel_id=1, source_target_pairs={{8,0},{0,4},{12,8},{4,12},{9,1},{1,5},{13,9},{5,13},{10,2},{2,6},{... | collective-permute-start | bytes 1769480 | tf_op jit(solution)/shard_map/ppermute | solution.py:131
  415.1 44.0 %collective-permute-start.15 = (bf16[384,768]{1,0:T(8,128)(2,1)}, bf16[384,768]{1,0:T(8,128)(2,1)}, u32[]{:S(2)}, u32[]{:S(2)}) collective-permute-start(bf16[384,768]{1,0:T(8,128)(2,1)} %get-tuple-element.145), channel_id=1, source_target_pairs={{8,4},{4,8},{9,5},{5,9},{10,6},{6,10},{11,7},{7,11},{24,20},{20,24... | collective-permute-start | bytes 1769480 | tf_op jit(solution)/shard_map/ppermute | solution.py:132
  418.2 40.8 %copy-start.21 = (f32[8,1536]{1,0:T(8,128)S(1)}, f32[8,1536]{1,0:T(8,128)}, u32[]{:S(2)}) copy-start(f32[8,1536]{1,0:T(8,128)} %get-tuple-element.151) | copy-start | bytes 147460
  459.1 4.4 copy-start.33
  463.6 10.2 %copy-start.25 = (pred[4]{0:T(512)(128)(4,1)S(1)}, pred[4]{0:T(512)(128)(4,1)}, u32[]{:S(2)}) copy-start(pred[4]{0:T(512)(128)(4,1)} %iota_compare_fusion.4) | copy-start | bytes 16
  474.1 10.8 %copy-start.22 = (f32[8]{0:T(128)S(1)}, f32[8]{0:T(128)}, u32[]{:S(2)}) copy-start(f32[8]{0:T(128)} %pad.15.clone) | copy-start | bytes 100
  474.1 10.8 %copy-start.23 = (f32[8]{0:T(128)S(1)}, f32[8]{0:T(128)}, u32[]{:S(2)}) copy-start(f32[8]{0:T(128)} %pad.12.clone) | copy-start | bytes 100
  570.6 6.3 %copy-start.14 = (bf16[2,384,1024]{2,1,0:T(8,128)(2,1)S(1)}, bf16[2,384,1024]{2,1,0:T(8,128)(2,1)}, u32[]{:S(2)}) copy-start(bf16[2,384,1024]{2,1,0:T(8,128)(2,1)} %get-tuple-element.163) | copy-start | bytes 4718596
  576.9 2.2 copy-start.13
  579.1 2.2 copy-start.20
  581.2 4.2 copy-start.16

commit v6 on v5

--- a/solution.py
+++ b/solution.py
@@ -848,26 +848,41 @@
         self.near, self.mid, self.far, self.spans = near, mid, far, spans
         self.near_copies, self.far_copies = {}, {}
 
+    def start_near(self, bit):
+        w = self.wires
+        for i, span in enumerate(self.spans):
+            self.near_copies[bit, i] = w.send(
+                self.part.at[2 * bit + 1, span], self.near.at[bit, span], {"k": 1 - w.k}
+            )
+
+    def start_far(self, bit):
+        w = self.wires
+        for i, span in enumerate(self.spans):
+            self.near_copies[bit, i].wait_recv()
+
+            def add(rows, bit=bit):
+                self.mid[bit - 1, rows] = (
+                    self.part[2 * bit, rows].astype(F32) + self.near[bit, rows].astype(F32)
+                ).astype(BF16)
+
+            by_chunks(span, add)
+            self.far_copies[bit, i] = w.send(
+                self.mid.at[bit - 1, span], self.far.at[bit - 1, span], {"p": w.p ^ bit}
+            )
+
     def start(self):
-        w = self.wires
         for bit in reversed(range(self.psize)):
-            for i, span in enumerate(self.spans):
-                self.near_copies[bit, i] = w.send(
-                    self.part.at[2 * bit + 1, span], self.near.at[bit, span], {"k": 1 - w.k}
-                )
+            self.start_near(bit)
         for bit in reversed(range(1, self.psize)):
-            for i, span in enumerate(self.spans):
-                self.near_copies[bit, i].wait_recv()
-
-                def add(rows, bit=bit):
-                    self.mid[bit - 1, rows] = (
-                        self.part[2 * bit, rows].astype(F32) + self.near[bit, rows].astype(F32)
-                    ).astype(BF16)
-
-                by_chunks(span, add)
-                self.far_copies[bit, i] = w.send(
-                    self.mid.at[bit - 1, span], self.far.at[bit - 1, span], {"p": w.p ^ bit}
-                )
+            self.start_far(bit)
+
+    def start_with(self, make):
+        for bit in reversed(range(self.psize)):
+            make(2 * bit + 1)
+            self.start_near(bit)
+            make(2 * bit)
+            if bit:
+                self.start_far(bit)
 
     def each(self, i, body):
         span = self.spans[i]
@@ -902,7 +917,7 @@
 
 
 def enter_kernel(
-    psize, x_ref, gain_own, codes_own, qkv_shard, forget_shard, out_shard, xin, g, proj, out, gain_ref, codes,
+    psize, x_ref, gain_own, codes_own, qkv_shard, forget_shard, out_shard, xin, g, proj, out, gain_ref, codes, far_gains,
     own, qkv_stage, forget_stage, out_stage, send_sem, recv_sem, local_sem,
 ):
     w = Wires(send_sem, recv_sem, local_sem)
@@ -988,6 +1003,7 @@
 
     gain_copy = w.send(gain_own, gain_ref.at[:, pl.ds(half, half)], {"x": 1 - w.x})
     code_copies = [
+        w.send(gain_own, far_gains, {"k": 1 - w.k, "h": 1 - w.h}),
         w.send(codes_own, codes.at[1], {"x": 1 - w.x}),
         w.send(codes_own, codes.at[2], {"k": 1 - w.k}),
         w.send(codes_own, codes.at[3], {"k": 1 - w.k, "x": 1 - w.x}),
@@ -1408,9 +1424,9 @@
 
 
 def leave_kernel(
-    psize, osize, pieces, part, stream, base, gain_ref, small_in, proj_in, out_own, out_other,
+    psize, osize, pieces, grad_in, weight_in, stream, base, gain_ref, small_in, proj_in, out_own, out_other,
     pair_in, down_in, block, small, first_sum, second_sum, out_sum, up_sum, gate_sum, down_sum,
-    near, mid, far, kept, first_val, second_val, out_val, up_val, gate_val, down_val, first_bufs,
+    near, mid, far, part, kept, first_val, second_val, out_val, up_val, gate_val, down_val, first_bufs,
     second_over, second_across, second_bufs, out_bufs, small_other, small_bufs, gain_acc,
     send_sem, recv_sem, local_sem,
 ):
@@ -1451,9 +1467,19 @@
     second.start(0)
     for load in loads:
         load.wait()
-    reduce.start()
     for spread in spreads:
         spread.start()
+    columns = D // TILE
+
+    def multiply(block):
+        def one(n, carry):
+            span = pl.ds(pl.multiple_of(n * TILE, TILE), TILE)
+            part[block, :, span] = dot_nt(grad_in[block], weight_in[span, :]).astype(BF16)
+            return carry
+
+        lax.fori_loop(0, columns, one, 0)
+
+    reduce.start_with(multiply)
 
     near_slots = [w.slot() for _ in spans]
     far_slots = [w.slot() for _ in spans]
@@ -1600,8 +1626,9 @@
             sds((out_weight.shape[0], 2 * half), BF16),
             sds((8, D), F32),
             sds((4,) + codes.shape, jnp.int32),
+            sds(gains.shape, F32),
         ),
-        (VMEM, ANY, ANY, ANY, VMEM, VMEM),
+        (VMEM, ANY, ANY, ANY, VMEM, VMEM, VMEM),
         [ANY, VMEM, VMEM, ANY, ANY, ANY],
         [pltpu.VMEM((rows, D), BF16)]
         + [pltpu.VMEM(value.shape, BF16) for value in (qkv_weight, forget_weight, out_weight)],
@@ -1668,7 +1695,7 @@
     )
 
 
-def leave(psize, osize, part, stream, base, gains, small, proj, out_own, out_other, pair, down):
+def leave(psize, osize, grad, weight, stream, base, gains, small, proj, out_own, out_other, pair, down):
     rows = stream.shape[0]
     bits = len(bits_of(osize))
     half = D // 2
@@ -1696,9 +1723,10 @@
             both(down.shape),
         ),
         (ANY, VMEM, ANY, ANY, ANY, ANY, ANY, ANY),
-        [VMEM] * 5 + [ANY] * 5,
+        [VMEM] * 6 + [ANY] * 5,
         sum_scratch(psize, rows)
         + [
+            scratch(2 * psize, rows, D),
             scratch(2, rows, half),
             scratch(split, columns),
             scratch(2, split // 2, columns),
@@ -1715,7 +1743,7 @@
             pltpu.VMEM((3 + len(bits_of(psize)) + bits, 8, half), F32),
             pltpu.VMEM((8, D), F32),
         ],
-        (part, stream, base, gains, small, proj, out_own, out_other, pair, down),
+        (grad, weight, stream, base, gains, small, proj, out_own, out_other, pair, down),
     )
 
 
@@ -1776,10 +1804,10 @@
         packed = jnp.concatenate([prompt_doc[0], branch_seg[0], branch_doc[0]])
         code_rows = -(-packed.shape[0] // (8 * LANES)) * 8
         packed = jnp.pad(packed, (0, code_rows * LANES - packed.shape[0])).reshape(code_rows, LANES)
-        own_gains = jnp.concatenate([jnp.stack([attn_gain, ffn_gain]), jnp.zeros((6, feat), F32)])
-        bias = jnp.where(home, forget_bias, lax.ppermute(forget_bias, ("k", "h"), [(1, 2), (2, 1)]))
-        bias = jnp.concatenate([bias, jnp.zeros((lane_pad,), F32)])
-
+        bias_row = jnp.pad(forget_bias, (0, feat - heads))
+        own_gains = jnp.concatenate(
+            [jnp.stack([attn_gain, ffn_gain, bias_row]), jnp.zeros((5, feat), F32)]
+        )
         forget_wide = jnp.concatenate(
             [forget_weight, jnp.zeros((forget_weight.shape[0], lane_pad), BF16)], axis=1
         )
@@ -1787,9 +1815,10 @@
         if width % LANES:
             spare = jnp.zeros((qkv_weight.shape[0], LANES - width % LANES), BF16)
             first_part = jnp.concatenate([qkv_weight, forget_wide, spare], axis=1)
-        xin, normed_a_all, w_proj, w_out, gains8, codes = enter(
+        xin, normed_a_all, w_proj, w_out, gains8, codes, far_gains = enter(
             psize, layer_input, own_gains, packed, first_part, second_part, out_weight
         )
+        bias = jnp.where(home, own_gains[2, :LANES], far_gains[2, :LANES])
         packed = lax.dynamic_index_in_dim(
             codes, (core ^ xpos) * 2 + (xpos ^ hpos), 0, keepdims=False
         ).reshape(-1)
@@ -1840,7 +1869,8 @@
         gate_sig = jax.nn.sigmoid(gate_pre)
         gate_act = gate_pre * gate_sig
         hidden = (gate_act * up_pre).astype(BF16)
-        hidden = tie(hidden, *cot_others)
+        out_part = matmul(hidden, w_down).astype(BF16)
+        out_part, *cot_others = lax.optimization_barrier((out_part, *cot_others))
         cot_all = all_blocks(cot, cot_others)
 
         def finish(total, axis_bits):
@@ -1852,18 +1882,20 @@
         down_part = contract_rows(hidden, cot_all).astype(BF16)
         down_keep, down_give = split_rows(down_part, high)
         down_moved = xor_swap(down_give, "o", osize, 1)
-        out_sums = near_sums(matmul(hidden, w_down).astype(BF16))
+        out_sums = near_sums(out_part)
         out_far = far_sums(out_sums)
         grad_hidden = contract_cols(tie(cot_all, out_sums[0]), w_down)
         grad_gate = (grad_hidden * up_pre * gate_sig * (1.0 + gate_pre * (1.0 - gate_sig))).astype(BF16)
         grad_up = (grad_hidden * gate_act).astype(BF16)
         gate_part = contract_rows(normed_b_all, grad_gate).astype(BF16).reshape(2, feat, -1)
         gate_got = xor_swap(take_half(gate_part[1], 1 - opos % 2), "o", osize, 1)
-        grad_gate, grad_up = lax.optimization_barrier((grad_gate, grad_up, gate_part))[:2]
+        grad_gate, grad_up, gate_part, *out_far = lax.optimization_barrier(
+            (grad_gate, grad_up, gate_part, *out_far)
+        )
         up_part = contract_rows(normed_b_all, grad_up).astype(BF16).reshape(2, feat, -1)
         part = (contract_cols(grad_gate, w_gate) + contract_cols(grad_up, w_up)).astype(BF16)
-        part, up_part, gate_got, down_moved, *out_far = lax.optimization_barrier(
-            (part, up_part, gate_got, down_moved, *out_far)
+        part, up_part, gate_got, down_moved = lax.optimization_barrier(
+            (part, up_part, gate_got, down_moved)
         )
         layer_output = (resid + total_of(out_sums[0], out_far)).astype(BF16)
         down_total = add_parts(down_keep, down_moved)
@@ -1899,7 +1931,6 @@
         layer_output = unspread_join(own_part, near_moved, far_moved, core, same)
         grad_proj = grad_proj.reshape(-1, width + LANES)
         proj_part = contract_rows(normed_a_all, grad_proj).astype(BF16)
-        part = contract_cols(grad_proj, w_proj).astype(BF16).reshape(count, -1, D)
         down_total = finish(down_total, obits[1:])
         pair_total = finish(add_parts(pair_total, pair_moved), obits[1:])
         out_total = add_parts(out_keep, out_moved)
@@ -1913,7 +1944,8 @@
         input_grad, small, first_rows, second_rows, out_both, up_both, gate_both, down_both = leave(
             psize,
             osize,
-            part,
+            grad_proj.reshape(count, -1, width + LANES),
+            w_proj,
             xin,
             grad_resid,
             gains8,

time: 592 us -> 575 us (0.971)
  starting transfers between devices: 31 us -> 24.6 us
  waiting for transfers between devices: 19.3 us -> 13.1 us
    ppermute x5, waiting for transfers between devices: 17.6 us -> 4.64 us  [xor_swap(): return lax.ppermute(value, axis, [(i, i ^ bit) for i in range(size)])]
    dot_general x5 -> x4, matrix products: 43.9 us -> 34.2 us  [contract_cols(): lax.dot_general(left, right, (((1,), (1,)), ((), ())), preferred_element_...]
    pallas_call x4, Pallas kernels: 296 us -> 303 us  [exchange_call(): pl.pallas_call(kernel, out_shape=outs, in_specs=in_specs, out_specs=out_s...]
    ppermute x2, waiting for transfers between devices: 1.7 us -> 8.42 us  [fetch_home_away(): return lax.ppermute(value, ('k', 'x', 'h'), pairs)]
  transfers between devices with their start and end apart: 17 -> 16, of which waited for: 4 -> 3; matrix products, arithmetic and copies ran while one was open for 18% -> 17% of each run, Pallas kernels for 35% -> 23%
where the time goes in v6:
time: 575 us; the launch traced here: 569 us
  Pallas kernels  363 us (63%)
  matrix products  112 us (19%)
  other arithmetic  34.7 us (6%)
  starting transfers between devices  24.6 us (4%)
  local copies, waits for them, and re-layouts  19.3 us (3%)
  waiting for transfers between devices  13.1 us (2%)
    pallas_call x4, Pallas kernels, exchange_call(): pl.pallas_call(kernel, out_shape=outs, in_specs=in_specs, out_specs=out_s...  303 us
    dot_general x5, matrix products, contract_rows(): lax.dot_general(left, right, (((0,), (0,)), ((), ())), preferred_element_...  40.2 us
    dot_general x5, matrix products, matmul(): return jnp.dot(left, right, preferred_element_type=F32)  37.8 us
    pallas_call x1, Pallas kernels, attention_backward(): pl.pallas_call(functools.partial(backward_kernel, heads, count, prompt_le...  36.2 us
    dot_general x4, matrix products, contract_cols(): lax.dot_general(left, right, (((1,), (1,)), ((), ())), preferred_element_...  34.2 us
    pallas_call x1, Pallas kernels, attention_forward(): pl.pallas_call(functools.partial(forward_kernel, heads, count, prompt_len...  23.8 us
  transfers between devices with their start and end apart: 16, of which 3 were waited for; matrix products, arithmetic and copies ran while one was open for 17% of the time, Pallas kernels for 23%

profile of v6, /device:TPU:1, one launch (start us, length us, event | category | flops | bytes accessed | tf_op | source)
XLA Modules:
  0.0 568.9 jit_solution(17734592359572164765)
XLA Ops:
  0.7 0.7 stack.54
  1.4 0.7 stack.55
  2.7 0.7 pad_add_fusion.2
  4.0 0.9 copy.43
  5.0 0.7 concatenate.46.forget_shard
  5.8 0.7 maximum_maximum_fusion.1.gain_own
  6.4 68.4 %enter.1 = (bf16[384,1536]{1,0:T(8,128)(2,1)}, bf16[4,384,1536]{2,1,0:T(8,128)(2,1)}, bf16[2,768,1280]{2,1,0:T(8,128)(2,1)}, bf16[384,1536]{1,0:T(8,128)(2,1)}, ...) custom-call(bf16[768,768]{1,0:T(8,128)(2,1)} %x_ref.1, f32[8,768]{1,0:T(8,128)} %maximum_maximum_fusion.1.gain_own, ...), custom_call_target="tpu_custom_call" | custom-call | tf_op jit(solution)/shard_map/enter/pallas_call | solution.py:1583
  74.8 0.7 dynamic-slice_bitcast_fusion.1
  75.5 0.7 dynamic-slice_bitcast_fusion
  77.7 11.4 %fusion.17.proj_hbm = f32[4,384,1280]{2,1,0:T(8,128)} fusion(bf16[4,384,1536]{2,1,0:T(8,128)(2,1)} %get-tuple-element.91, bf16[1536,1280,1]{1,0,2:T(8,128)(2,1)} %bitcast.88), kind=kOutput, calls=%fused_computation.85 | convolution fusion | flops 6039797760 | bytes 16515072 | tf_op jit(solution)/shard_map/dot_general | solution.py:157
  89.2 1.3 constant_dynamic-slice_fusion.5
  90.9 1.1 broadcast_select_fusion.8
  92.2 1.9 collective-permute-start.2
  94.1 1.9 collective-permute-start.3
  96.1 2.6 collective-permute-start.1
  99.0 0.7 broadcast_select_fusion.12.bias_ref
  99.7 23.8 %attention_forward.1 = (bf16[4,384,384]{2,1,0:T(8,128)(2,1)S(1)}, f32[384,1536]{1,0:T(8,128)S(1)}, f32[8,1536]{1,0:T(8,128)S(1)}, bf16[6,1536,128]{2,1,0:T(8,128...) custom-call(s32[36]{0:T(128)S(1)} %reshape.135.flags, ...), custom_call_target="tpu_custom_call" | custom-call | flops 20000000000 | bytes 30000000 | tf_op jit(solution)/shard_map/attention_forward/pallas_call | solution.py:343
  123.6 8.4 %collective-permute-done.1.up_got = bf16[384,1024]{1,0:T(8,128)(2,1)} collective-permute-done((bf16[384,1024]{1,0:T(8,128)(2,1)}, bf16[384,1024]{1,0:T(8,128)(2,1)}, u32[]{:S(2)}, u32[]{:S(2)}) %collective-permute-start.1) | collective-permute-done | bytes 786464 | tf_op jit(solution)/shard_map/ppermute | solution.py:40
  132.0 1.3 broadcast_select_fusion.7
  133.5 4.3 convolution_convert_fusion.1
  137.8 73.0 %forward_exchange.1 = (f32[384,1536]{1,0:T(8,128)}, bf16[4,384,1536]{2,1,0:T(8,128)(2,1)}, bf16[2,768,1024]{2,1,0:T(8,128)(2,1)}, bf16[2,768,1024]{2,1,0:T(8,128)(2,1)}, bf16[1024,1536]{1,0:T(8,128)(2,1)}) custom-call(bf16[4,384,1536]{2,1,0:T(8,128)(2,1)} %bitcast.85, bf16[384,1536]{1,0:T(8,128)(2,1)} %get-tuple-element.115.xin.stream, ...), custom_call_target="tpu_custom_call" | custom-call | tf_op jit(solution)/shard_map/forward_exchange/pallas_call | solution.py:1583
  210.9 6.6 %collective-permute-start.5 = (bf16[384,1536]{1,0:T(8,128)(2,1)S(1)}, bf16[384,1536]{1,0:T(8,128)(2,1)}, u32[]{:S(2)}, u32[]{:S(2)}) collective-permute-start(bf16[384,1536]{1,0:T(8,128)(2,1)S(1)} %pad_maximum_fusion.1.cot), channel_id=1, source_target_pairs={{0,1},{1,0},{2,3},{3,2},{4,5},{5,4},{6,7},{7,6},{8,9},{9,8},{10,11... | collective-permute-start | bytes 3538952 | tf_op jit(solution)/shard_map/ppermute | solution.py:26
  217.5 8.0 %fusion.18 = f32[1536,1024]{1,0:T(8,128)S(1)} fusion(bf16[1536,1536]{1,0:T(8,128)(2,1)} %bitcast.95, bf16[1536,1024]{1,0:T(8,128)(2,1)} %bitcast.101), kind=kOutput, calls=%fused_computation.86 | convolution fusion | flops 4831838208 | bytes 14155776 | tf_op jit(solution)/shard_map/dot_general | solution.py:157
  225.5 7.3 %multiply_convert_fusion.2 = (bf16[1536,1024]{1,0:T(8,128)(2,1)S(1)}, f32[1536,1024]{1,0:T(8,128)}) fusion(f32[1536,1024]{1,0:T(8,128)S(1)} %fusion.18, bf16[1536,1536]{1,0:T(8,128)(2,1)S(1)} %bitcast.97, bf16[1536,1024]{1,0:T(8,128)(2,1)S(1)} %bitcast.103), kind=kOutput, calls=%fused_computation.7 | convolution fusion | flops 4841275392 | bytes 23592960 | tf_op jit(solution)/shard_map/dot_general | solution.py:157
  232.7 6.8 %convolution_convert_fusion = bf16[1536,1536]{1,0:T(8,128)(2,1)} fusion(bf16[1536,1024]{1,0:T(8,128)(2,1)S(1)} %get-tuple-element.245, bf16[1024,1536]{1,0:T(8,128)(2,1)S(1)} %copy-done.28), kind=kOutput, calls=%fused_computation.2 | convolution fusion | flops 4834197504 | bytes 11010048 | tf_op jit(solution)/shard_map/dot_general | solution.py:157
  240.7 2.0 fusion.13
  243.4 9.5 %convolution_convert_fusion.2 = bf16[1024,1536]{1,0:T(8,128)(2,1)S(1)} fusion(bf16[1536,1024]{1,0:T(8,128)(2,1)S(1)} %copy-done.36, bf16[384,1536]{1,0:T(8,128)(2,1)} %collective-permute-done.6, bf16[384,1536]{1,0:T(8,128)(2,1)} %collective-permute-done.5, bf16[384,1536]{1,0:T(8,128)(2,1)} %collective-permute-done.4, ...), kind=kOutput, calls=%fused_computation.11 | convolution fusion | flops 4857004032 | bytes 11010048 | tf_op jit(solution)/shard_map/dot_general | solution.py:145
  253.1 1.2 collective-permute-start.11
  254.3 5.6 pad_maximum_fusion
  261.2 12.0 %multiply_convert_fusion = (bf16[1536,1024]{1,0:T(8,128)(2,1)}, bf16[1536,1024]{1,0:T(8,128)(2,1)S(1)}) fusion(f32[1536,1024]{1,0:T(8,128)} %copy-done.31, f32[1536,1024]{1,0:T(8,128)} %get-tuple-element.246, bf16[1536,1536]{1,0:T(8,128)(2,1)S(1)} %pad_maximum_fusion, bf16[1024,1536]{1,0:T(8,128)(2,1)} %get-tuple-element.122), kind=kOutput, calls=%fused_computation.5 | convolution fusion | flops 4852285440 | bytes 26738688 | tf_op jit(solution)/shard_map/dot_general | solution.py:151
  273.2 8.9 %convolution_convert_fusion.4 = bf16[1536,1024]{1,0:T(8,128)(2,1)S(1)} fusion(bf16[1536,1536]{1,0:T(8,128)(2,1)} %bitcast.96, bf16[1536,1024]{1,0:T(8,128)(2,1)S(1)} %get-tuple-element.127), kind=kOutput, calls=%fused_computation.13 | convolution fusion | flops 4833411072 | bytes 11010048 | tf_op jit(solution)/shard_map/dot_general | solution.py:145
  282.3 0.8 collective-permute-start.10
  283.0 4.5 collective-permute-done.9
  287.6 7.9 %fusion.19 = f32[1536,1536]{1,0:T(8,128)} fusion(bf16[1536,1024]{1,0:T(8,128)(2,1)S(1)} %copy-done.32, bf16[1536,1024]{1,0:T(8,128)(2,1)S(1)} %bitcast.104), kind=kOutput, calls=%fused_computation.87 | convolution fusion | flops 4831838208 | bytes 15728640 | tf_op jit(solution)/shard_map/dot_general | solution.py:151
  295.4 10.7 %add_convert_fusion = bf16[1536,1536]{1,0:T(8,128)(2,1)} fusion(f32[1536,1536]{1,0:T(8,128)} %fusion.19, bf16[1536,1024]{1,0:T(8,128)(2,1)} %copy-done.34, bf16[1536,1024]{1,0:T(8,128)(2,1)} %bitcast.102), kind=kOutput, calls=%fused_computation | convolution fusion | flops 4836556800 | bytes 20447232 | tf_op jit(solution)/shard_map/dot_general | solution.py:151
  306.6 1.2 fusion.15
  308.5 6.6 %convolution_convert_fusion.3 = bf16[1536,1024]{1,0:T(8,128)(2,1)} fusion(bf16[1536,1536]{1,0:T(8,128)(2,1)S(1)} %bitcast.100, bf16[1536,1024]{1,0:T(8,128)(2,1)S(1)} %copy-done.33), kind=kOutput, calls=%fused_computation.12 | convolution fusion | flops 4833411072 | bytes 11010048 | tf_op jit(solution)/shard_map/dot_general | solution.py:145
  315.9 1.2 fusion.14
  317.2 76.7 %backward_exchange.1 = (f32[384,1536]{1,0:T(8,128)}, bf16[4,384,1536]{2,1,0:T(8,128)(2,1)}, f32[8,1536]{1,0:T(8,128)}, bf16[512,768]{1,0:T(8,128)(2,1)}, bf16[2,384,1024]{2,1,0:T(8,128)(2,1)}) custom-call(bf16[4,384,1536]{2,1,0:T(8,128)(2,1)} %bitcast.81, f32[384,1536]{1,0:T(8,128)} %get-tuple-element.130.resid, bf16[384,1536]{1,0:T(8,128)(2,1)} %copy-done.8, ...), custom_call_target="tpu_custom_call" | custom-call | tf_op jit(solution)/shard_map/backward_exchange/pallas_call | solution.py:1583
  393.9 4.5 fusion.2
  398.4 0.9 broadcast_select_fusion.1
  399.3 3.7 convolution_convert_fusion.5
  403.0 0.8 collective-permute-start.12
  404.2 2.7 collective-permute-start.14
  407.0 4.4 collective-permute-start.15
  411.4 36.2 %attention_backward.1 = (bf16[4,384,1280]{2,1,0:T(8,128)(2,1)}, f32[8,128]{1,0:T(8,128)}) custom-call(s32[36]{0:T(128)} %copy-done.2, bf16[4,384,384]{2,1,0:T(8,128)(2,1)} %bitcast.105, f32[384,1536]{1,0:T(8,128)} %copy-done.3, f32[8,1536]{1,0:T(8,128)} %copy-done.5, bf16[6,1536,128]{2,1,0:T(8,128)(2,1)} %get-tuple-element.143.qp, ...), custom_call_target="tpu_custom_call" | custom-call | flops 49999998976 | bytes 30000000 | tf_op jit(solution)/shard_map/attention_backward/pallas_call | solution.py:534
  447.7 10.8 %fusion = bf16[1536,1280]{1,0:T(8,128)(2,1)} fusion(bf16[4,384,1536]{2,1,0:T(8,128)(2,1)} %get-tuple-element.91, bf16[4,384,1280]{2,1,0:T(8,128)(2,1)} %get-tuple-element.155.grad_in), kind=kOutput, calls=%fused_computation.3 | convolution fusion | flops 6041763840 | bytes 12582912 | tf_op jit(solution)/shard_map/dot_general | solution.py:145
  458.5 3.2 add_convert_fusion.1.pair_in
  461.9 0.9 fusion.16
  462.7 0.7 slice_bitcast_fusion
  463.7 0.7 maximum_maximum_fusion.small_in
  464.4 85.1 %leave.1 = (bf16[768,768]{1,0:T(8,128)(2,1)}, f32[8,768]{1,0:T(8,128)}, bf16[384,1280]{1,0:T(8,128)(2,1)}, bf16[2,192,1280]{2,1,0:T(8,128)(2,1)}, bf16[2,192,768...) custom-call(bf16[4,384,1280]{2,1,0:T(8,128)(2,1)} %get-tuple-element, ...), custom_call_target="tpu_custom_call" | custom-call | tf_op jit(solution)/shard_map/leave/pallas_call | solution.py:1583
  549.5 0.7 slice_reduce_fusion.2
  550.2 1.4 slice_reduce_fusion
  551.7 1.0 fusion.5
  552.7 3.6 fusion.4
  556.4 0.8 copy.48
  557.1 1.1 bitcast_convert_fusion.3
  558.2 2.2 bitcast_convert_fusion.2
  560.4 2.2 bitcast_convert_fusion.1
  562.6 2.0 bitcast_convert_fusion
  564.6 1.4 broadcast_select_fusion.10
  566.0 1.1 pad_maximum_fusion.2
  567.6 1.0 copy.52
  (156 shorter events, 10.8 us)
Async XLA Ops:
  5.0 84.1 %copy-start.21 = (f32[8]{0:T(128)}, f32[8]{0:T(128)S(1)}, u32[]{:S(2)}) copy-start(f32[8]{0:T(128)S(1)} %pad.39.clone) | copy-start | bytes 100
  77.7 22.0 %copy-start.2 = (s32[36]{0:T(128)}, s32[36]{0:T(128)S(1)}, u32[]{:S(2)}) copy-start(s32[36]{0:T(128)S(1)} %reshape.135.flags) | copy-start | bytes 436
  77.7 11.4 %copy-start.10 = (bf16[768,1024]{1,0:T(8,128)(2,1)S(1)}, bf16[768,1024]{1,0:T(8,128)(2,1)}, u32[]{:S(2)}) copy-start(bf16[768,1024]{1,0:T(8,128)(2,1)} %gate_shard.1) | copy-start | bytes 4718596
  77.7 11.4 %copy-start.11 = (bf16[768,1024]{1,0:T(8,128)(2,1)S(1)}, bf16[768,1024]{1,0:T(8,128)(2,1)}, u32[]{:S(2)}) copy-start(bf16[768,1024]{1,0:T(8,128)(2,1)} %up_shard.1) | copy-start | bytes 4718596
  89.1 1.8 copy-start.16
  92.1 31.4 %copy-start.1 = (s32[8,1536]{1,0:T(8,128)}, s32[8,1536]{1,0:T(8,128)S(1)}, u32[]{:S(2)}) copy-start(s32[8,1536]{1,0:T(8,128)S(1)} %stack.69.qrow) | copy-start | bytes 147460
  92.2 31.4 %collective-permute-start.2 = (bf16[384,768]{1,0:T(8,128)(2,1)}, bf16[384,768]{1,0:T(8,128)(2,1)}, u32[]{:S(2)}, u32[]{:S(2)}) collective-permute-start(bf16[384,768]{1,0:T(8,128)(2,1)} %get-tuple-element.103), channel_id=1, source_target_pairs={{0,8},{4,0},{8,12},{12,4},{1,9},{5,1},{9,13},{13,5},{2,10},{6,2},{... | collective-permute-start | bytes 1769480 | tf_op jit(solution)/shard_map/ppermute | solution.py:1848
  94.1 29.5 %collective-permute-start.3 = (bf16[384,768]{1,0:T(8,128)(2,1)S(1)}, bf16[384,768]{1,0:T(8,128)(2,1)}, u32[]{:S(2)}, u32[]{:S(2)}) collective-permute-start(bf16[384,768]{1,0:T(8,128)(2,1)S(1)} %get-tuple-element.104), channel_id=1, source_target_pairs={{4,8},{8,4},{5,9},{9,5},{6,10},{10,6},{7,11},{11,7},{20,24},{24,20... | collective-permute-start | bytes 1769480 | tf_op jit(solution)/shard_map/ppermute | solution.py:1849
  96.0 27.6 %collective-permute-start = (bf16[384,1024]{1,0:T(8,128)(2,1)}, bf16[384,1024]{1,0:T(8,128)(2,1)}, u32[]{:S(2)}, u32[]{:S(2)}) collective-permute-start(bf16[384,1024]{1,0:T(8,128)(2,1)} %get-tuple-element.101), channel_id=1, source_target_pairs={{0,4},{2,8},{4,0},{6,12},{8,2},{10,14},{12,6},{14,10},{1,5},{3,9},... | collective-permute-start | bytes 2359304 | tf_op jit(solution)/shard_map/ppermute | solution.py:40
  96.1 35.9 %collective-permute-start.1 = (bf16[384,1024]{1,0:T(8,128)(2,1)}, bf16[384,1024]{1,0:T(8,128)(2,1)}, u32[]{:S(2)}, u32[]{:S(2)}) collective-permute-start(bf16[384,1024]{1,0:T(8,128)(2,1)} %get-tuple-element.102), channel_id=1, source_target_pairs={{0,4},{2,8},{4,0},{6,12},{8,2},{10,14},{12,6},{14,10},{1,5},{3,9},... | collective-permute-start | bytes 2359304 | tf_op jit(solution)/shard_map/ppermute | solution.py:40
  99.0 24.5 %copy-start = (s32[1536,8]{1,0:T(8,128)}, s32[1536,8]{1,0:T(8,128)S(1)}, u32[]{:S(2)}) copy-start(s32[1536,8]{1,0:T(8,128)S(1)} %copy.44.kcol) | copy-start | bytes 147460
  123.5 14.3 %copy-start.3 = (f32[384,1536]{1,0:T(8,128)}, f32[384,1536]{1,0:T(8,128)S(1)}, u32[]{:S(2)}) copy-start(f32[384,1536]{1,0:T(8,128)S(1)} %get-tuple-element.141.ot_ref) | copy-start | bytes 7077892
  123.5 14.3 %copy-start.4 = (f32[1536,128]{1,0:T(8,128)}, f32[1536,128]{1,0:T(8,128)S(1)}, u32[]{:S(2)}) copy-start(f32[1536,128]{1,0:T(8,128)S(1)} %get-tuple-element.146.logit) | copy-start | bytes 2359300
  123.5 14.3 %copy-start.5 = (f32[8,1536]{1,0:T(8,128)}, f32[8,1536]{1,0:T(8,128)S(1)}, u32[]{:S(2)}) copy-start(f32[8,1536]{1,0:T(8,128)S(1)} %get-tuple-element.142.lse_ref) | copy-start | bytes 147460
  123.5 10.0 %copy-start.29 = (bf16[384,1536]{1,0:T(8,128)(2,1)S(1)}, bf16[384,1536]{1,0:T(8,128)(2,1)}, u32[]{:S(2)}) copy-start(bf16[384,1536]{1,0:T(8,128)(2,1)} %get-tuple-element.114) | copy-start | bytes 3538948
  133.4 77.4 %copy-start.8 = (bf16[384,1536]{1,0:T(8,128)(2,1)}, bf16[384,1536]{1,0:T(8,128)(2,1)S(1)}, u32[]{:S(2)}) copy-start(bf16[384,1536]{1,0:T(8,128)(2,1)S(1)} %pad_maximum_fusion.1.cot) | copy-start | bytes 3538948
  133.4 109.9 %collective-permute-start.4 = (bf16[384,1536]{1,0:T(8,128)(2,1)S(1)}, bf16[384,1536]{1,0:T(8,128)(2,1)}, u32[]{:S(2)}, u32[]{:S(2)}) collective-permute-start(bf16[384,1536]{1,0:T(8,128)(2,1)S(1)} %pad_maximum_fusion.1.cot), channel_id=1, source_target_pairs={{0,8},{8,0},{1,9},{9,1},{2,10},{10,2},{3,11},{11,3},{4,12},{12,4},... | collective-permute-start | bytes 3538952 | tf_op jit(solution)/shard_map/ppermute | solution.py:22
  210.9 28.8 %collective-permute-start.5 = (bf16[384,1536]{1,0:T(8,128)(2,1)S(1)}, bf16[384,1536]{1,0:T(8,128)(2,1)}, u32[]{:S(2)}, u32[]{:S(2)}) collective-permute-start(bf16[384,1536]{1,0:T(8,128)(2,1)S(1)} %pad_maximum_fusion.1.cot), channel_id=1, source_target_pairs={{0,1},{1,0},{2,3},{3,2},{4,5},{5,4},{6,7},{7,6},{8,9},{9,8},{10,11... | collective-permute-start | bytes 3538952 | tf_op jit(solution)/shard_map/ppermute | solution.py:26
  217.4 8.0 %copy-start.25 = (bf16[4,384,1536]{2,1,0:T(8,128)(2,1)S(1)}, bf16[4,384,1536]{2,1,0:T(8,128)(2,1)}, u32[]{:S(2)}) copy-start(bf16[4,384,1536]{2,1,0:T(8,128)(2,1)} %get-tuple-element.119) | copy-start | bytes 14155780
  217.4 8.0 %copy-start.26 = (bf16[2,768,1024]{2,1,0:T(8,128)(2,1)S(1)}, bf16[2,768,1024]{2,1,0:T(8,128)(2,1)}, u32[]{:S(2)}) copy-start(bf16[2,768,1024]{2,1,0:T(8,128)(2,1)} %get-tuple-element.121) | copy-start | bytes 9437188
  225.4 7.3 %copy-start.31 = (f32[1536,1024]{1,0:T(8,128)}, f32[1536,1024]{1,0:T(8,128)S(1)}, u32[]{:S(2)}) copy-start(f32[1536,1024]{1,0:T(8,128)S(1)} %fusion.18) | copy-start | bytes 18874372
  225.5 7.3 %copy-start.28 = (bf16[1024,1536]{1,0:T(8,128)(2,1)S(1)}, bf16[1024,1536]{1,0:T(8,128)(2,1)}, u32[]{:S(2)}) copy-start(bf16[1024,1536]{1,0:T(8,128)(2,1)} %get-tuple-element.122) | copy-start | bytes 9437188
  232.7 6.8 %copy-start.35 = (bf16[1536,1024]{1,0:T(8,128)(2,1)}, bf16[1536,1024]{1,0:T(8,128)(2,1)S(1)}, u32[]{:S(2)}) copy-start(bf16[1536,1024]{1,0:T(8,128)(2,1)S(1)} %get-tuple-element.245) | copy-start | bytes 9437188
  239.7 3.7 collective-permute-start.6
  240.2 3.2 copy-start.36
  242.7 17.2 %collective-permute-start.8 = (bf16[384,1536]{1,0:T(8,128)(2,1)S(1)}, bf16[384,1536]{1,0:T(8,128)(2,1)S(1)}, u32[]{:S(2)}, u32[]{:S(2)}) collective-permute-start(bf16[384,1536]{1,0:T(8,128)(2,1)S(1)} %get-tuple-element.226), channel_id=1, source_target_pairs={{0,8},{8,0},{1,9},{9,1},{2,10},{10,2},{3,11},{11,3},{4,12},{12,4},... | collective-permute-start | bytes 3538952 | tf_op jit(solution)/shard_map/ppermute | solution.py:22
  243.3 16.6 %collective-permute-start.7 = (bf16[384,1536]{1,0:T(8,128)(2,1)S(1)}, bf16[384,1536]{1,0:T(8,128)(2,1)S(1)}, u32[]{:S(2)}, u32[]{:S(2)}) collective-permute-start(bf16[384,1536]{1,0:T(8,128)(2,1)S(1)} %get-tuple-element.227), channel_id=1, source_target_pairs={{0,8},{8,0},{1,9},{9,1},{2,10},{10,2},{3,11},{11,3},{4,12},{12,4},... | collective-permute-start | bytes 3538952 | tf_op jit(solution)/shard_map/ppermute | solution.py:22
  252.9 7.1 %slice-start = ((s8[4718592]{0:T(1024)(128)(4,1)}), s8[4194304]{0:T(1024)(128)(4,1)S(1)}, s32[]{:S(2)}) async-start(s8[4718592]{0:T(1024)(128)(4,1)} %bitcast.82), calls=%async_computation | async-start | bytes 8388608
  253.1 6.9 %slice-start.1 = ((s8[4718592]{0:T(1024)(128)(4,1)}), s8[524288]{0:T(1024)(128)(4,1)S(1)}, s32[]{:S(2)}) async-start(s8[4718592]{0:T(1024)(128)(4,1)} %bitcast.82), calls=%async_computation.1 | async-start | bytes 1048576
  253.1 61.9 %collective-permute-start.11 = (bf16[512,1536]{1,0:T(8,128)(2,1)S(1)}, bf16[512,1536]{1,0:T(8,128)(2,1)S(1)}, u32[]{:S(2)}, u32[]{:S(2)}) collective-permute-start(bf16[512,1536]{1,0:T(8,128)(2,1)S(1)} %broadcast_select_fusion), channel_id=1, source_target_pairs={{0,16},{16,0},{1,17},{17,1},{2,18},{18,2},{3,19},{19,3},{4,20},{20... | collective-permute-start | bytes 4718600 | tf_op jit(solution)/shard_map/ppermute | solution.py:26
  260.7 26.9 %collective-permute-start.9 = (bf16[384,1536]{1,0:T(8,128)(2,1)S(1)}, bf16[384,1536]{1,0:T(8,128)(2,1)S(1)}, u32[]{:S(2)}, u32[]{:S(2)}) collective-permute-start(bf16[384,1536]{1,0:T(8,128)(2,1)S(1)} %get-tuple-element.224), channel_id=1, source_target_pairs={{0,1},{1,0},{2,3},{3,2},{4,5},{5,4},{6,7},{7,6},{8,9},{9,8},{10,11... | collective-permute-start | bytes 3538952 | tf_op jit(solution)/shard_map/ppermute | solution.py:26
  273.2 8.9 %copy-start.34 = (bf16[1536,1024]{1,0:T(8,128)(2,1)}, bf16[1536,1024]{1,0:T(8,128)(2,1)S(1)}, u32[]{:S(2)}) copy-start(bf16[1536,1024]{1,0:T(8,128)(2,1)S(1)} %get-tuple-element.127) | copy-start | bytes 9437188
  273.2 14.4 %copy-start.32 = (bf16[1536,1024]{1,0:T(8,128)(2,1)S(1)}, bf16[1536,1024]{1,0:T(8,128)(2,1)}, u32[]{:S(2)}) copy-start(bf16[1536,1024]{1,0:T(8,128)(2,1)} %get-tuple-element.128) | copy-start | bytes 9437188
  282.1 13.4 %copy-start.7 = (bf16[1536,1024]{1,0:T(8,128)(2,1)}, bf16[1536,1024]{1,0:T(8,128)(2,1)S(1)}, u32[]{:S(2)}) copy-start(bf16[1536,1024]{1,0:T(8,128)(2,1)S(1)} %convolution_convert_fusion.4) | copy-start | bytes 9437188
  282.1 5.5 copy-start.27
  282.3 32.8 %collective-permute-start.10 = (bf16[384,1024]{1,0:T(8,128)(2,1)S(1)}, bf16[384,1024]{1,0:T(8,128)(2,1)S(1)}, u32[]{:S(2)}, u32[]{:S(2)}) collective-permute-start(bf16[384,1024]{1,0:T(8,128)(2,1)S(1)} %constant_dynamic-slice_fusion.2), channel_id=1, source_target_pairs={{0,16},{16,0},{1,17},{17,1},{2,18},{18,2},{3,19},{19,3},{4,20},{20... | collective-permute-start | bytes 2359304 | tf_op jit(solution)/shard_map/ppermute | solution.py:26
  287.6 20.3 %slice-start.2 = ((s8[4718592]{0:T(1024)(128)(4,1)}), s8[4194304]{0:T(1024)(128)(4,1)S(1)}, s32[]{:S(2)}) async-start(s8[4718592]{0:T(1024)(128)(4,1)} %bitcast.98), calls=%async_computation.2 | async-start | bytes 8388608
  295.4 10.7 %copy-start.6 = (f32[384,1536]{1,0:T(8,128)S(1)}, f32[384,1536]{1,0:T(8,128)}, u32[]{:S(2)}) copy-start(f32[384,1536]{1,0:T(8,128)} %get-tuple-element.130.resid) | copy-start | bytes 7077892
  295.4 12.4 %slice-start.3 = ((s8[4718592]{0:T(1024)(128)(4,1)}), s8[524288]{0:T(1024)(128)(4,1)S(1)}, s32[]{:S(2)}) async-start(s8[4718592]{0:T(1024)(128)(4,1)} %bitcast.98), calls=%async_computation.3 | async-start | bytes 1048576
  306.2 2.3 copy-start.33
  315.1 0.9 copy-start.18
  393.9 5.4 copy-start.9
  393.9 5.4 copy-start.30
  399.3 7.6 %copy-start.12 = (bf16[2,384,1024]{2,1,0:T(8,128)(2,1)S(1)}, bf16[2,384,1024]{2,1,0:T(8,128)(2,1)}, u32[]{:S(2)}) copy-start(bf16[2,384,1024]{2,1,0:T(8,128)(2,1)} %get-tuple-element.152) | copy-start | bytes 4718596
  403.0 44.7 %collective-permute-start.12 = (bf16[192,1536]{1,0:T(8,128)(2,1)}, bf16[192,1536]{1,0:T(8,128)(2,1)S(1)}, u32[]{:S(2)}, u32[]{:S(2)}) collective-permute-start(bf16[192,1536]{1,0:T(8,128)(2,1)} %get-tuple-element.149), channel_id=1, source_target_pairs={{0,16},{16,0},{1,17},{17,1},{2,18},{18,2},{3,19},{19,3},{4,20},{20... | collective-permute-start | bytes 1769480 | tf_op jit(solution)/shard_map/ppermute | solution.py:26
  403.8 43.9 %collective-permute-start.13 = (bf16[384,768]{1,0:T(8,128)(2,1)}, bf16[384,768]{1,0:T(8,128)(2,1)}, u32[]{:S(2)}, u32[]{:S(2)}) collective-permute-start(bf16[384,768]{1,0:T(8,128)(2,1)} %get-tuple-element.150), channel_id=1, source_target_pairs={{8,0},{0,4},{12,8},{4,12},{9,1},{1,5},{13,9},{5,13},{10,2},{2,6},{... | collective-permute-start | bytes 1769480 | tf_op jit(solution)/shard_map/ppermute | solution.py:131
  404.2 43.5 %collective-permute-start.14 = (bf16[384,768]{1,0:T(8,128)(2,1)}, bf16[384,768]{1,0:T(8,128)(2,1)}, u32[]{:S(2)}, u32[]{:S(2)}) collective-permute-start(bf16[384,768]{1,0:T(8,128)(2,1)} %get-tuple-element.151), channel_id=1, source_target_pairs={{8,4},{4,8},{9,5},{5,9},{10,6},{6,10},{11,7},{7,11},{24,20},{20,24... | collective-permute-start | bytes 1769480 | tf_op jit(solution)/shard_map/ppermute | solution.py:132
  407.0 40.7 %collective-permute-start.15 = (bf16[2,384,1024]{2,1,0:T(8,128)(2,1)S(1)}, bf16[2,384,1024]{2,1,0:T(8,128)(2,1)}, u32[]{:S(2)}, u32[]{:S(2)}) collective-permute-start(bf16[2,384,1024]{2,1,0:T(8,128)(2,1)S(1)} %copy-done.12), channel_id=1, source_target_pairs={{2,0},{8,10},{3,1},{9,11},{6,4},{12,14},{7,5},{13,15},{18,16},{24,... | collective-permute-start | bytes 4718600 | tf_op jit(solution)/shard_map/ppermute | solution.py:65
  411.4 36.2 %copy-start.20 = (f32[8,1536]{1,0:T(8,128)S(1)}, f32[8,1536]{1,0:T(8,128)}, u32[]{:S(2)}) copy-start(f32[8,1536]{1,0:T(8,128)} %get-tuple-element.157) | copy-start | bytes 147460
  458.5 4.9 copy-start.24
  458.5 5.2 copy-start.22
  458.5 5.2 copy-start.23
  552.6 4.5 copy-start.19
  552.7 5.6 copy-start.15
  557.1 3.3 copy-start.14
  560.4 2.2 copy-start.13
  564.6 3.1 copy-start.17

commit v7 on v6

--- a/solution.py
+++ b/solution.py
@@ -1179,13 +1179,13 @@
 
 
 def backward_exchange_kernel(
-    psize, part, resid, cot, gain_ref, down_own, down_other, gate_part, gate_got, up_part,
+    psize, grad_gate, grad_up, w_gate, w_up, resid, cot, gain_ref, down_own, down_other, gate_part, up_part,
     grad_resid, g, gain_grad, down_sum, pair_sum,
-    near, mid, far, own, down_across, down_moved, gate_val, gate_over, gate_across, up_val, up_over, up_across,
+    near, mid, far, own, part, down_across, down_moved, gate_val, gate_over, gate_across, up_val, up_over, up_across,
     send_sem, recv_sem, local_sem,
 ):
     w = Wires(send_sem, recv_sem, local_sem)
-    gate = EarlySum(w, gate_part, gate_val, gate_over, gate_across, pair_sum.at[0], 2, got=gate_got)
+    gate = EarlySum(w, gate_part, gate_val, gate_over, gate_across, pair_sum.at[0], 2)
     up = EarlySum(w, up_part, up_val, up_over, up_across, pair_sum.at[1], 2)
     gate.load()
     up.load()
@@ -1193,12 +1193,23 @@
     spans = row_spans(own.shape[0], PIECES)
     reduce = Reduce(w, psize, part, near, mid, far, spans)
     down_copy = w.send(down_other, down_across, {"x": 1 - w.x})
+    gate.start(1)
+    up.start(1)
     gate.start(0)
-    up.start(1)
     up.start(0)
+
+    def multiply(block):
+        def one(n, carry):
+            span = pl.ds(pl.multiple_of(n * TILE, TILE), TILE)
+            sums = dot_nt(grad_gate[block], w_gate[span, :]) + dot_nt(grad_up[block], w_up[span, :])
+            part[block, :, span] = sums.astype(BF16)
+            return carry
+
+        lax.fori_loop(0, D // TILE, one, 0)
+
+    reduce.start_with(multiply)
     for i in range(2):
         gate.pass_on(i)
-    reduce.start()
     down_home = w.copy(down_sum, down_moved, {"h": 1 - w.h}, w.slot())
     down_copy.wait_recv()
 
@@ -1661,7 +1672,9 @@
     )
 
 
-def backward_exchange(psize, part, resid, cot, gains, down_own, down_other, gate_part, gate_got, up_part):
+def backward_exchange(
+    psize, grad_gate, grad_up, w_gate, w_up, resid, cot, gains, down_own, down_other, gate_part, up_part
+):
     rows = resid.shape[0]
 
     def early(value):
@@ -1685,13 +1698,13 @@
             sds((2, gate_part.shape[1] // 2, gate_part.shape[2]), BF16),
         ),
         (VMEM, ANY, VMEM, VMEM, ANY),
-        [VMEM, VMEM, VMEM, VMEM, VMEM, ANY, ANY, VMEM, ANY],
+        [VMEM] * 8 + [ANY, ANY, ANY],
         sum_scratch(psize, rows)
-        + [pltpu.VMEM((rows, D), BF16)]
+        + [pltpu.VMEM((rows, D), BF16), pltpu.VMEM((2 * psize, rows, D), BF16)]
         + [pltpu.VMEM(down_own.shape, BF16)] * 2
         + early(gate_part)
         + early(up_part),
-        (part, resid, cot, gains, down_own, down_other, gate_part, gate_got, up_part),
+        (grad_gate, grad_up, w_gate, w_up, resid, cot, gains, down_own, down_other, gate_part, up_part),
     )
 
 
@@ -1888,27 +1901,24 @@
         grad_gate = (grad_hidden * up_pre * gate_sig * (1.0 + gate_pre * (1.0 - gate_sig))).astype(BF16)
         grad_up = (grad_hidden * gate_act).astype(BF16)
         gate_part = contract_rows(normed_b_all, grad_gate).astype(BF16).reshape(2, feat, -1)
-        gate_got = xor_swap(take_half(gate_part[1], 1 - opos % 2), "o", osize, 1)
-        grad_gate, grad_up, gate_part, *out_far = lax.optimization_barrier(
-            (grad_gate, grad_up, gate_part, *out_far)
-        )
         up_part = contract_rows(normed_b_all, grad_up).astype(BF16).reshape(2, feat, -1)
-        part = (contract_cols(grad_gate, w_gate) + contract_cols(grad_up, w_up)).astype(BF16)
-        part, up_part, gate_got, down_moved = lax.optimization_barrier(
-            (part, up_part, gate_got, down_moved)
+        up_part, gate_part, down_moved, *out_far = lax.optimization_barrier(
+            (up_part, gate_part, down_moved, *out_far)
         )
         layer_output = (resid + total_of(out_sums[0], out_far)).astype(BF16)
         down_total = add_parts(down_keep, down_moved)
         grad_resid, grad_branch_all, ffn_gain_part, down_total, pair_total = backward_exchange(
             psize,
-            part.reshape(count, -1, D),
+            grad_gate.reshape(count, -1, grad_gate.shape[1]),
+            grad_up.reshape(count, -1, grad_up.shape[1]),
+            w_gate,
+            w_up,
             resid,
             cot,
             gains8,
             down_total[:, :feat],
             down_total[:, feat:],
             gate_part,
-            gate_got,
             up_part,
         )
         grad_branch_all = grad_branch_all.reshape(-1, D)

time: 575 us -> 560 us (0.974)
  matrix products: 112 us -> 96 us
  Pallas kernels: 363 us -> 372 us
  waiting for transfers between devices: 13.1 us -> 4.29 us
    dot_general x4 -> x2, matrix products: 34.2 us -> 14.5 us  [contract_cols(): lax.dot_general(left, right, (((1,), (1,)), ((), ())), preferred_element_...]
  transfers between devices with their start and end apart: 16 -> 15, of which waited for: 3 -> 2; matrix products, arithmetic and copies ran while one was open for 17% -> 14% of each run, Pallas kernels for 23% -> 25%
where the time goes in v7:
time: 560 us; the launch traced here: 553 us
  Pallas kernels  372 us (66%)
  matrix products  96 us (17%)
  other arithmetic  37.1 us (7%)
  starting transfers between devices  24.1 us (4%)
  local copies, waits for them, and re-layouts  17.7 us (3%)
    pallas_call x4, Pallas kernels, exchange_call(): pl.pallas_call(kernel, out_shape=outs, in_specs=in_specs, out_specs=out_s...  306 us
    dot_general x5, matrix products, contract_rows(): lax.dot_general(left, right, (((0,), (0,)), ((), ())), preferred_element_...  43.7 us
    pallas_call x1, Pallas kernels, attention_backward(): pl.pallas_call(functools.partial(backward_kernel, heads, count, prompt_le...  39.9 us
    dot_general x5, matrix products, matmul(): return jnp.dot(left, right, preferred_element_type=F32)  37.8 us
    pallas_call x1, Pallas kernels, attention_forward(): pl.pallas_call(functools.partial(forward_kernel, heads, count, prompt_len...  26.7 us
    dot_general x2, matrix products, contract_cols(): lax.dot_general(left, right, (((1,), (1,)), ((), ())), preferred_element_...  14.5 us
  transfers between devices with their start and end apart: 15, of which 2 were waited for; matrix products, arithmetic and copies ran while one was open for 14% of the time, Pallas kernels for 25%

profile of v7, /device:TPU:1, one launch (start us, length us, event | category | flops | bytes accessed | tf_op | source)
XLA Modules:
  0.0 553.2 jit_solution(2602614343712849306)
XLA Ops:
  0.7 0.7 pad.12
  1.3 0.7 stack.54
  2.0 0.7 stack.55
  2.7 0.9 copy.43
  3.6 0.7 pad_add_fusion.2
  5.0 0.7 concatenate.46.forget_shard
  5.7 0.7 maximum_maximum_fusion.1.gain_own
  6.4 68.4 %enter.1 = (bf16[384,1536]{1,0:T(8,128)(2,1)}, bf16[4,384,1536]{2,1,0:T(8,128)(2,1)}, bf16[2,768,1280]{2,1,0:T(8,128)(2,1)}, bf16[384,1536]{1,0:T(8,128)(2,1)}, ...) custom-call(bf16[768,768]{1,0:T(8,128)(2,1)} %x_ref.1, f32[8,768]{1,0:T(8,128)} %maximum_maximum_fusion.1.gain_own, ...), custom_call_target="tpu_custom_call" | custom-call | tf_op jit(solution)/shard_map/enter/pallas_call | solution.py:1594
  74.8 0.7 dynamic-slice_bitcast_fusion
  75.5 0.7 dynamic-slice_bitcast_fusion.1
  76.2 0.7 broadcast_add_fusion
  77.8 11.4 %fusion.15.proj_hbm = f32[4,384,1280]{2,1,0:T(8,128)} fusion(bf16[4,384,1536]{2,1,0:T(8,128)(2,1)} %get-tuple-element.87, bf16[1536,1280,1]{1,0,2:T(8,128)(2,1)} %bitcast.83), kind=kOutput, calls=%fused_computation.82 | convolution fusion | flops 6039797760 | bytes 16515072 | tf_op jit(solution)/shard_map/dot_general | solution.py:157
  89.2 1.3 constant_dynamic-slice_fusion.3
  90.9 1.1 broadcast_select_fusion.8
  92.2 1.4 collective-permute-start
  93.5 1.3 collective-permute-start.1
  94.9 1.9 collective-permute-start.2
  96.8 1.9 collective-permute-start.3
  99.0 0.7 broadcast_select_fusion.12.bias_ref
  99.7 26.7 %attention_forward.1 = (bf16[4,384,384]{2,1,0:T(8,128)(2,1)S(1)}, f32[384,1536]{1,0:T(8,128)S(1)}, f32[8,1536]{1,0:T(8,128)S(1)}, bf16[6,1536,128]{2,1,0:T(8,128...) custom-call(s32[36]{0:T(128)S(1)} %reshape.136.flags, ...), custom_call_target="tpu_custom_call" | custom-call | flops 20000000000 | bytes 30000000 | tf_op jit(solution)/shard_map/attention_forward/pallas_call | solution.py:343
  126.5 3.6 collective-permute-done.1.up_got
  130.2 1.3 broadcast_select_fusion.7
  131.7 4.3 convolution_convert_fusion.1
  136.0 72.9 %forward_exchange.1 = (f32[384,1536]{1,0:T(8,128)}, bf16[4,384,1536]{2,1,0:T(8,128)(2,1)}, bf16[2,768,1024]{2,1,0:T(8,128)(2,1)}, bf16[2,768,1024]{2,1,0:T(8,128)(2,1)}, bf16[1024,1536]{1,0:T(8,128)(2,1)}) custom-call(bf16[4,384,1536]{2,1,0:T(8,128)(2,1)} %bitcast.80, bf16[384,1536]{1,0:T(8,128)(2,1)} %get-tuple-element.111.xin.stream, ...), custom_call_target="tpu_custom_call" | custom-call | tf_op jit(solution)/shard_map/forward_exchange/pallas_call | solution.py:1594
  208.9 6.6 %collective-permute-start.5 = (bf16[384,1536]{1,0:T(8,128)(2,1)S(1)}, bf16[384,1536]{1,0:T(8,128)(2,1)}, u32[]{:S(2)}, u32[]{:S(2)}) collective-permute-start(bf16[384,1536]{1,0:T(8,128)(2,1)S(1)} %pad_maximum_fusion.1.cot), channel_id=1, source_target_pairs={{0,1},{1,0},{2,3},{3,2},{4,5},{5,4},{6,7},{7,6},{8,9},{9,8},{10,11... | collective-permute-start | bytes 3538952 | tf_op jit(solution)/shard_map/ppermute | solution.py:26
  215.5 8.0 %fusion.16 = f32[1536,1024]{1,0:T(8,128)S(1)} fusion(bf16[1536,1536]{1,0:T(8,128)(2,1)} %bitcast.97, bf16[1536,1024]{1,0:T(8,128)(2,1)} %bitcast.86), kind=kOutput, calls=%fused_computation.83 | convolution fusion | flops 4831838208 | bytes 14155776 | tf_op jit(solution)/shard_map/dot_general | solution.py:157
  223.5 7.3 %multiply_convert_fusion.2 = (bf16[1536,1024]{1,0:T(8,128)(2,1)S(1)}, f32[1536,1024]{1,0:T(8,128)}) fusion(f32[1536,1024]{1,0:T(8,128)S(1)} %fusion.16, bf16[1536,1536]{1,0:T(8,128)(2,1)S(1)} %bitcast.100, bf16[1536,1024]{1,0:T(8,128)(2,1)S(1)} %bitcast.89), kind=kOutput, calls=%fused_computation.6 | convolution fusion | flops 4841275392 | bytes 23592960 | tf_op jit(solution)/shard_map/dot_general | solution.py:157
  230.8 6.9 %convolution_convert_fusion = bf16[1536,1536]{1,0:T(8,128)(2,1)} fusion(bf16[1536,1024]{1,0:T(8,128)(2,1)S(1)} %get-tuple-element.237, bf16[1024,1536]{1,0:T(8,128)(2,1)S(1)} %copy-done.25), kind=kOutput, calls=%fused_computation.1 | convolution fusion | flops 4834197504 | bytes 11010048 | tf_op jit(solution)/shard_map/dot_general | solution.py:157
  237.8 1.9 fusion.11
  240.9 9.2 %convolution_convert_fusion.4 = bf16[1024,1536]{1,0:T(8,128)(2,1)S(1)} fusion(bf16[1536,1024]{1,0:T(8,128)(2,1)S(1)} %copy-done.30, bf16[384,1536]{1,0:T(8,128)(2,1)} %collective-permute-done.6, bf16[384,1536]{1,0:T(8,128)(2,1)} %collective-permute-done.5, bf16[384,1536]{1,0:T(8,128)(2,1)} %collective-permute-done.4, ...), kind=kOutput, calls=%fused_computation.12 | convolution fusion | flops 4857004032 | bytes 11010048 | tf_op jit(solution)/shard_map/dot_general | solution.py:145
  250.3 1.3 collective-permute-start.8
  251.6 5.6 %pad_maximum_fusion = bf16[1536,1536]{1,0:T(8,128)(2,1)S(1)} fusion(bf16[384,1536]{1,0:T(8,128)(2,1)} %collective-permute-done.6, bf16[384,1536]{1,0:T(8,128)(2,1)} %collective-permute-done.5, bf16[384,1536]{1,0:T(8,128)(2,1)} %collective-permute-done.4, bf16[384,768]{1,0:T(8,128)(2,1)S(1)} %get-tuple-element.232, bf16[384,768]{1,0:T(8,128)(2,1)S(1)} %get-tuple-element.231), kind=kLoop, calls=%fused_computation.9 | loop fusion | flops 23592960 | bytes 9437184 | tf_op jit(solution)/shard_map/concatenate | solution.py:1799
  257.3 0.7 add_convert_fusion.3
  258.3 10.8 %multiply_convert_fusion = (bf16[1536,1024]{1,0:T(8,128)(2,1)S(1)}, bf16[1536,1024]{1,0:T(8,128)(2,1)S(1)}) fusion(f32[1536,1024]{1,0:T(8,128)} %copy-done.28, f32[1536,1024]{1,0:T(8,128)} %get-tuple-element.238, bf16[1536,1536]{1,0:T(8,128)(2,1)S(1)} %pad_maximum_fusion, bf16[1024,1536]{1,0:T(8,128)(2,1)} %get-tuple-element.118), kind=kOutput, calls=%fused_computation.4 | convolution fusion | flops 4852285440 | bytes 26738688 | tf_op jit(solution)/shard_map/dot_general | solution.py:151
  269.1 11.1 %convolution_convert_fusion.2 = bf16[1536,1024]{1,0:T(8,128)(2,1)} fusion(bf16[1536,1536]{1,0:T(8,128)(2,1)} %bitcast.98, bf16[1536,1024]{1,0:T(8,128)(2,1)S(1)} %get-tuple-element.215), kind=kOutput, calls=%fused_computation.10 | convolution fusion | flops 4833411072 | bytes 11010048 | tf_op jit(solution)/shard_map/dot_general | solution.py:145
  280.3 9.2 %convolution_convert_fusion.3 = bf16[1536,1024]{1,0:T(8,128)(2,1)} fusion(bf16[1536,1536]{1,0:T(8,128)(2,1)} %bitcast.99, bf16[1536,1024]{1,0:T(8,128)(2,1)S(1)} %get-tuple-element.214), kind=kOutput, calls=%fused_computation.11 | convolution fusion | flops 4833411072 | bytes 11010048 | tf_op jit(solution)/shard_map/dot_general | solution.py:145
  290.0 1.2 fusion.13
  291.2 2.0 add_convert_fusion.1
  293.2 1.2 fusion.12
  294.4 83.8 %backward_exchange.1 = (f32[384,1536]{1,0:T(8,128)}, bf16[4,384,1536]{2,1,0:T(8,128)(2,1)}, f32[8,1536]{1,0:T(8,128)}, bf16[512,768]{1,0:T(8,128)(2,1)}, bf16[2,384,1024]{2,1,0:T(8,128)(2,1)}) custom-call(bf16[4,384,1024]{2,1,0:T(8,128)(2,1)} %bitcast.91, bf16[4,384,1024]{2,1,0:T(8,128)(2,1)} %bitcast.90, bf16[1536,1024]{1,0:T(8,128)(2,1)} %bitcast.87, ...), custom_call_target="tpu_custom_call" | custom-call | tf_op jit(solution)/shard_map/backward_exchange/pallas_call | solution.py:1594
  378.2 4.5 fusion.2
  382.9 3.7 convolution_convert_fusion.5
  386.6 4.2 collective-permute-start.14
  391.3 3.8 collective-permute-start.13
  395.2 39.9 %attention_backward.1 = (bf16[4,384,1280]{2,1,0:T(8,128)(2,1)}, f32[8,128]{1,0:T(8,128)}) custom-call(s32[36]{0:T(128)} %copy-done.2, bf16[4,384,384]{2,1,0:T(8,128)(2,1)} %bitcast.101, f32[384,1536]{1,0:T(8,128)} %copy-done.3, f32[8,1536]{1,0:T(8,128)} %copy-done.5, bf16[6,1536,128]{2,1,0:T(8,128)(2,1)} %get-tuple-element.135.qp, ...), custom_call_target="tpu_custom_call" | custom-call | flops 49999998976 | bytes 30000000 | tf_op jit(solution)/shard_map/attention_backward/pallas_call | solution.py:534
  435.2 3.4 add_convert_fusion.pair_in
  438.6 1.2 add_convert_fusion.5
  439.8 0.9 fusion.14
  440.6 9.6 %fusion = bf16[1536,1280]{1,0:T(8,128)(2,1)} fusion(bf16[4,384,1536]{2,1,0:T(8,128)(2,1)} %get-tuple-element.87, bf16[4,384,1280]{2,1,0:T(8,128)(2,1)S(1)} %copy-done.9), kind=kOutput, calls=%fused_computation.2 | convolution fusion | flops 6041763840 | bytes 12582912 | tf_op jit(solution)/shard_map/dot_general | solution.py:145
  450.3 0.7 slice_bitcast_fusion
  451.2 0.7 maximum_maximum_fusion.small_in
  451.9 80.6 %leave.1 = (bf16[768,768]{1,0:T(8,128)(2,1)}, f32[8,768]{1,0:T(8,128)}, bf16[384,1280]{1,0:T(8,128)(2,1)}, bf16[2,192,1280]{2,1,0:T(8,128)(2,1)}, bf16[2,192,768...) custom-call(bf16[4,384,1280]{2,1,0:T(8,128)(2,1)} %get-tuple-element, ...), custom_call_target="tpu_custom_call" | custom-call | tf_op jit(solution)/shard_map/leave/pallas_call | solution.py:1594
  532.5 1.0 fusion.5
  533.4 3.5 fusion.4
  536.9 0.8 slice_reduce_fusion.2
  537.7 1.4 slice_reduce_fusion
  539.1 0.8 copy.48
  539.9 3.3 bitcast_convert_fusion
  543.2 2.2 bitcast_convert_fusion.1
  545.4 2.2 bitcast_convert_fusion.2
  547.5 1.1 bitcast_convert_fusion.3
  549.3 1.3 broadcast_select_fusion.10
  550.6 1.1 pad_maximum_fusion.2
  551.7 1.0 copy.52
  (133 shorter events, 6.5 us)
Async XLA Ops:
  5.0 84.1 %copy-start.22 = (f32[8]{0:T(128)}, f32[8]{0:T(128)S(1)}, u32[]{:S(2)}) copy-start(f32[8]{0:T(128)S(1)} %pad.39.clone) | copy-start | bytes 100
  77.8 21.9 %copy-start.2 = (s32[36]{0:T(128)}, s32[36]{0:T(128)S(1)}, u32[]{:S(2)}) copy-start(s32[36]{0:T(128)S(1)} %reshape.136.flags) | copy-start | bytes 436
  77.8 11.4 %copy-start.10 = (bf16[768,1024]{1,0:T(8,128)(2,1)S(1)}, bf16[768,1024]{1,0:T(8,128)(2,1)}, u32[]{:S(2)}) copy-start(bf16[768,1024]{1,0:T(8,128)(2,1)} %gate_shard.1) | copy-start | bytes 4718596
  77.8 11.4 %copy-start.11 = (bf16[768,1024]{1,0:T(8,128)(2,1)S(1)}, bf16[768,1024]{1,0:T(8,128)(2,1)}, u32[]{:S(2)}) copy-start(bf16[768,1024]{1,0:T(8,128)(2,1)} %up_shard.1) | copy-start | bytes 4718596
  89.2 1.8 copy-start.18
  92.2 34.3 %copy-start.1 = (s32[8,1536]{1,0:T(8,128)}, s32[8,1536]{1,0:T(8,128)S(1)}, u32[]{:S(2)}) copy-start(s32[8,1536]{1,0:T(8,128)S(1)} %stack.69.qrow) | copy-start | bytes 147460
  92.2 34.3 %collective-permute-start = (bf16[384,1024]{1,0:T(8,128)(2,1)}, bf16[384,1024]{1,0:T(8,128)(2,1)}, u32[]{:S(2)}, u32[]{:S(2)}) collective-permute-start(bf16[384,1024]{1,0:T(8,128)(2,1)} %get-tuple-element.97), channel_id=1, source_target_pairs={{0,4},{2,8},{4,0},{6,12},{8,2},{10,14},{12,6},{14,10},{1,5},{3,9},... | collective-permute-start | bytes 2359304 | tf_op jit(solution)/shard_map/ppermute | solution.py:40
  93.5 36.6 %collective-permute-start.1 = (bf16[384,1024]{1,0:T(8,128)(2,1)}, bf16[384,1024]{1,0:T(8,128)(2,1)}, u32[]{:S(2)}, u32[]{:S(2)}) collective-permute-start(bf16[384,1024]{1,0:T(8,128)(2,1)} %get-tuple-element.98), channel_id=1, source_target_pairs={{0,4},{2,8},{4,0},{6,12},{8,2},{10,14},{12,6},{14,10},{1,5},{3,9},... | collective-permute-start | bytes 2359304 | tf_op jit(solution)/shard_map/ppermute | solution.py:40
  94.9 31.6 %collective-permute-start.2 = (bf16[384,768]{1,0:T(8,128)(2,1)}, bf16[384,768]{1,0:T(8,128)(2,1)}, u32[]{:S(2)}, u32[]{:S(2)}) collective-permute-start(bf16[384,768]{1,0:T(8,128)(2,1)} %get-tuple-element.99), channel_id=1, source_target_pairs={{0,8},{4,0},{8,12},{12,4},{1,9},{5,1},{9,13},{13,5},{2,10},{6,2},{... | collective-permute-start | bytes 1769480 | tf_op jit(solution)/shard_map/ppermute | solution.py:1861
  96.8 29.7 %collective-permute-start.3 = (bf16[384,768]{1,0:T(8,128)(2,1)S(1)}, bf16[384,768]{1,0:T(8,128)(2,1)}, u32[]{:S(2)}, u32[]{:S(2)}) collective-permute-start(bf16[384,768]{1,0:T(8,128)(2,1)S(1)} %get-tuple-element.100), channel_id=1, source_target_pairs={{4,8},{8,4},{5,9},{9,5},{6,10},{10,6},{7,11},{11,7},{20,24},{24,20... | collective-permute-start | bytes 1769480 | tf_op jit(solution)/shard_map/ppermute | solution.py:1862
  99.0 27.4 %copy-start = (s32[1536,8]{1,0:T(8,128)}, s32[1536,8]{1,0:T(8,128)S(1)}, u32[]{:S(2)}) copy-start(s32[1536,8]{1,0:T(8,128)S(1)} %copy.44.kcol) | copy-start | bytes 147460
  126.4 9.5 %copy-start.3 = (f32[384,1536]{1,0:T(8,128)}, f32[384,1536]{1,0:T(8,128)S(1)}, u32[]{:S(2)}) copy-start(f32[384,1536]{1,0:T(8,128)S(1)} %get-tuple-element.133.ot_ref) | copy-start | bytes 7077892
  126.5 9.5 %copy-start.4 = (f32[1536,128]{1,0:T(8,128)}, f32[1536,128]{1,0:T(8,128)S(1)}, u32[]{:S(2)}) copy-start(f32[1536,128]{1,0:T(8,128)S(1)} %get-tuple-element.138.logit) | copy-start | bytes 2359300
  126.5 9.5 %copy-start.5 = (f32[8,1536]{1,0:T(8,128)}, f32[8,1536]{1,0:T(8,128)S(1)}, u32[]{:S(2)}) copy-start(f32[8,1536]{1,0:T(8,128)S(1)} %get-tuple-element.134.lse_ref) | copy-start | bytes 147460
  126.5 5.2 copy-start.26
  131.6 77.3 %copy-start.7 = (bf16[384,1536]{1,0:T(8,128)(2,1)}, bf16[384,1536]{1,0:T(8,128)(2,1)S(1)}, u32[]{:S(2)}) copy-start(bf16[384,1536]{1,0:T(8,128)(2,1)S(1)} %pad_maximum_fusion.1.cot) | copy-start | bytes 3538948
  131.6 108.7 %collective-permute-start.4 = (bf16[384,1536]{1,0:T(8,128)(2,1)S(1)}, bf16[384,1536]{1,0:T(8,128)(2,1)}, u32[]{:S(2)}, u32[]{:S(2)}) collective-permute-start(bf16[384,1536]{1,0:T(8,128)(2,1)S(1)} %pad_maximum_fusion.1.cot), channel_id=1, source_target_pairs={{0,8},{8,0},{1,9},{9,1},{2,10},{10,2},{3,11},{11,3},{4,12},{12,4},... | collective-permute-start | bytes 3538952 | tf_op jit(solution)/shard_map/ppermute | solution.py:22
  208.9 28.8 %collective-permute-start.5 = (bf16[384,1536]{1,0:T(8,128)(2,1)S(1)}, bf16[384,1536]{1,0:T(8,128)(2,1)}, u32[]{:S(2)}, u32[]{:S(2)}) collective-permute-start(bf16[384,1536]{1,0:T(8,128)(2,1)S(1)} %pad_maximum_fusion.1.cot), channel_id=1, source_target_pairs={{0,1},{1,0},{2,3},{3,2},{4,5},{5,4},{6,7},{7,6},{8,9},{9,8},{10,11... | collective-permute-start | bytes 3538952 | tf_op jit(solution)/shard_map/ppermute | solution.py:26
  215.5 8.0 %copy-start.12 = (bf16[2,768,1024]{2,1,0:T(8,128)(2,1)S(1)}, bf16[2,768,1024]{2,1,0:T(8,128)(2,1)}, u32[]{:S(2)}) copy-start(bf16[2,768,1024]{2,1,0:T(8,128)(2,1)} %get-tuple-element.117) | copy-start | bytes 9437188
  215.5 8.0 %copy-start.24 = (bf16[4,384,1536]{2,1,0:T(8,128)(2,1)S(1)}, bf16[4,384,1536]{2,1,0:T(8,128)(2,1)}, u32[]{:S(2)}) copy-start(bf16[4,384,1536]{2,1,0:T(8,128)(2,1)} %get-tuple-element.115) | copy-start | bytes 14155780
  223.5 7.3 %copy-start.28 = (f32[1536,1024]{1,0:T(8,128)}, f32[1536,1024]{1,0:T(8,128)S(1)}, u32[]{:S(2)}) copy-start(f32[1536,1024]{1,0:T(8,128)S(1)} %fusion.16) | copy-start | bytes 18874372
  223.5 7.3 %copy-start.25 = (bf16[1024,1536]{1,0:T(8,128)(2,1)S(1)}, bf16[1024,1536]{1,0:T(8,128)(2,1)}, u32[]{:S(2)}) copy-start(bf16[1024,1536]{1,0:T(8,128)(2,1)} %get-tuple-element.118) | copy-start | bytes 9437188
  230.8 6.9 %copy-start.29 = (bf16[1536,1024]{1,0:T(8,128)(2,1)}, bf16[1536,1024]{1,0:T(8,128)(2,1)S(1)}, u32[]{:S(2)}) copy-start(bf16[1536,1024]{1,0:T(8,128)(2,1)S(1)} %get-tuple-element.237) | copy-start | bytes 9437188
  237.7 3.2 collective-permute-start.6
  237.7 3.2 copy-start.30
  239.7 17.5 %collective-permute-start.7 = (bf16[384,1536]{1,0:T(8,128)(2,1)S(1)}, bf16[384,1536]{1,0:T(8,128)(2,1)S(1)}, u32[]{:S(2)}, u32[]{:S(2)}) collective-permute-start(bf16[384,1536]{1,0:T(8,128)(2,1)S(1)} %get-tuple-element.219), channel_id=1, source_target_pairs={{0,8},{8,0},{1,9},{9,1},{2,10},{10,2},{3,11},{11,3},{4,12},{12,4},... | collective-permute-start | bytes 3538952 | tf_op jit(solution)/shard_map/ppermute | solution.py:22
  240.2 17.0 %collective-permute-start.9 = (bf16[384,1536]{1,0:T(8,128)(2,1)S(1)}, bf16[384,1536]{1,0:T(8,128)(2,1)S(1)}, u32[]{:S(2)}, u32[]{:S(2)}) collective-permute-start(bf16[384,1536]{1,0:T(8,128)(2,1)S(1)} %get-tuple-element.218), channel_id=1, source_target_pairs={{0,8},{8,0},{1,9},{9,1},{2,10},{10,2},{3,11},{11,3},{4,12},{12,4},... | collective-permute-start | bytes 3538952 | tf_op jit(solution)/shard_map/ppermute | solution.py:22
  250.1 7.1 %slice-start = ((s8[4718592]{0:T(1024)(128)(4,1)}), s8[4194304]{0:T(1024)(128)(4,1)S(1)}, s32[]{:S(2)}) async-start(s8[4718592]{0:T(1024)(128)(4,1)} %bitcast.77), calls=%async_computation | async-start | bytes 8388608
  250.3 6.9 %slice-start.1 = ((s8[4718592]{0:T(1024)(128)(4,1)}), s8[524288]{0:T(1024)(128)(4,1)S(1)}, s32[]{:S(2)}) async-start(s8[4718592]{0:T(1024)(128)(4,1)} %bitcast.77), calls=%async_computation.1 | async-start | bytes 1048576
  250.3 39.1 %collective-permute-start.8 = (bf16[512,1536]{1,0:T(8,128)(2,1)S(1)}, bf16[512,1536]{1,0:T(8,128)(2,1)}, u32[]{:S(2)}, u32[]{:S(2)}) collective-permute-start(bf16[512,1536]{1,0:T(8,128)(2,1)S(1)} %broadcast_select_fusion), channel_id=1, source_target_pairs={{0,16},{16,0},{1,17},{17,1},{2,18},{18,2},{3,19},{19,3},{4,20},{20... | collective-permute-start | bytes 4718600 | tf_op jit(solution)/shard_map/ppermute | solution.py:26
  258.0 31.5 %collective-permute-start.10 = (bf16[384,1536]{1,0:T(8,128)(2,1)S(1)}, bf16[384,1536]{1,0:T(8,128)(2,1)S(1)}, u32[]{:S(2)}, u32[]{:S(2)}) collective-permute-start(bf16[384,1536]{1,0:T(8,128)(2,1)S(1)} %get-tuple-element.216), channel_id=1, source_target_pairs={{0,1},{1,0},{2,3},{3,2},{4,5},{5,4},{6,7},{7,6},{8,9},{9,8},{10,11... | collective-permute-start | bytes 3538952 | tf_op jit(solution)/shard_map/ppermute | solution.py:26
  269.1 11.1 %copy-start.14 = (bf16[1536,1024]{1,0:T(8,128)(2,1)}, bf16[1536,1024]{1,0:T(8,128)(2,1)S(1)}, u32[]{:S(2)}) copy-start(bf16[1536,1024]{1,0:T(8,128)(2,1)S(1)} %get-tuple-element.215) | copy-start | bytes 9437188
  269.1 11.1 %copy-start.13 = (bf16[1536,1024]{1,0:T(8,128)(2,1)}, bf16[1536,1024]{1,0:T(8,128)(2,1)S(1)}, u32[]{:S(2)}) copy-start(bf16[1536,1024]{1,0:T(8,128)(2,1)S(1)} %get-tuple-element.214) | copy-start | bytes 9437188
  280.3 9.2 %copy-start.6 = (f32[384,1536]{1,0:T(8,128)S(1)}, f32[384,1536]{1,0:T(8,128)}, u32[]{:S(2)}) copy-start(f32[384,1536]{1,0:T(8,128)} %get-tuple-element.123.resid) | copy-start | bytes 7077892
  378.2 4.6 copy-start.8
  378.2 4.6 copy-start.27
  382.9 3.7 copy-start.15
  386.6 48.6 %collective-permute-start.14 = (bf16[2,384,1024]{2,1,0:T(8,128)(2,1)S(1)}, bf16[2,384,1024]{2,1,0:T(8,128)(2,1)}, u32[]{:S(2)}, u32[]{:S(2)}) collective-permute-start(bf16[2,384,1024]{2,1,0:T(8,128)(2,1)S(1)} %copy-done.15), channel_id=1, source_target_pairs={{2,0},{8,10},{3,1},{9,11},{6,4},{12,14},{7,5},{13,15},{18,16},{24,... | collective-permute-start | bytes 4718600 | tf_op jit(solution)/shard_map/ppermute | solution.py:65
  390.7 44.4 %collective-permute-start.11 = (bf16[192,1536]{1,0:T(8,128)(2,1)S(1)}, bf16[192,1536]{1,0:T(8,128)(2,1)}, u32[]{:S(2)}, u32[]{:S(2)}) collective-permute-start(bf16[192,1536]{1,0:T(8,128)(2,1)S(1)} %get-tuple-element.141), channel_id=1, source_target_pairs={{0,16},{16,0},{1,17},{17,1},{2,18},{18,2},{3,19},{19,3},{4,20},{20... | collective-permute-start | bytes 1769480 | tf_op jit(solution)/shard_map/ppermute | solution.py:26
  391.3 43.8 %collective-permute-start.12 = (bf16[384,768]{1,0:T(8,128)(2,1)}, bf16[384,768]{1,0:T(8,128)(2,1)}, u32[]{:S(2)}, u32[]{:S(2)}) collective-permute-start(bf16[384,768]{1,0:T(8,128)(2,1)} %get-tuple-element.142), channel_id=1, source_target_pairs={{8,0},{0,4},{12,8},{4,12},{9,1},{1,5},{13,9},{5,13},{10,2},{2,6},{... | collective-permute-start | bytes 1769480 | tf_op jit(solution)/shard_map/ppermute | solution.py:131
  391.3 43.8 %collective-permute-start.13 = (bf16[384,768]{1,0:T(8,128)(2,1)}, bf16[384,768]{1,0:T(8,128)(2,1)}, u32[]{:S(2)}, u32[]{:S(2)}) collective-permute-start(bf16[384,768]{1,0:T(8,128)(2,1)} %get-tuple-element.143), channel_id=1, source_target_pairs={{8,4},{4,8},{9,5},{5,9},{10,6},{6,10},{11,7},{7,11},{24,20},{20,24... | collective-permute-start | bytes 1769480 | tf_op jit(solution)/shard_map/ppermute | solution.py:132
  395.2 39.9 %copy-start.21 = (f32[8,1536]{1,0:T(8,128)S(1)}, f32[8,1536]{1,0:T(8,128)}, u32[]{:S(2)}) copy-start(f32[8,1536]{1,0:T(8,128)} %get-tuple-element.149) | copy-start | bytes 147460
  435.2 5.5 copy-start.9
  440.6 10.6 %copy-start.23 = (f32[8]{0:T(128)S(1)}, f32[8]{0:T(128)}, u32[]{:S(2)}) copy-start(f32[8]{0:T(128)} %copy-done.22) | copy-start | bytes 100
  536.9 6.3 %copy-start.17 = (bf16[2,384,1024]{2,1,0:T(8,128)(2,1)S(1)}, bf16[2,384,1024]{2,1,0:T(8,128)(2,1)}, u32[]{:S(2)}) copy-start(bf16[2,384,1024]{2,1,0:T(8,128)(2,1)} %get-tuple-element.161) | copy-start | bytes 4718596
  543.2 2.2 copy-start.16
  545.4 2.2 copy-start.20
  547.5 4.2 copy-start.19

commit v8 on v7

--- a/solution.py
+++ b/solution.py
@@ -1036,6 +1036,8 @@
         qkv.relay_over(i)
         if i < PIECES:
             share.relay(i)
+    for i in range(3, PIECES):
+        share.relay(i)
     forget.relay_over(0)
     out_fetch.relay(0)
     out_fetch.relay_over(0)
@@ -1048,8 +1050,8 @@
 
 
 def forward_exchange_kernel(
-    psize, part, xin, gain_ref, gate_shard, gate_got, up_shard, up_got, down_shard, resid, g, gate, up, down,
-    near, mid, far, own, gate_stage, gate_keep, up_stage, up_keep, down_stage, send_sem, recv_sem, local_sem,
+    psize, attended, w_out, xin, gain_ref, gate_shard, gate_got, up_shard, up_got, down_shard, resid, g, gate, up, down,
+    near, mid, far, own, part, gate_stage, gate_keep, up_stage, up_keep, down_stage, send_sem, recv_sem, local_sem,
 ):
     w = Wires(send_sem, recv_sem, local_sem)
     gate_fetch = Fetch(w, gate_shard, gate, gate_stage, 2, gate_got, gate_keep)
@@ -1062,7 +1064,16 @@
     spans = row_spans(own.shape[0], PIECES)
     reduce = Reduce(w, psize, part, near, mid, far, spans)
     gate_fetch.start()
-    reduce.start()
+
+    def multiply(block):
+        def one(n, carry):
+            span = pl.ds(pl.multiple_of(n * TILE, TILE), TILE)
+            part[block, :, span] = dot_nn(attended[block], w_out[:, span]).astype(BF16)
+            return carry
+
+        lax.fori_loop(0, D // TILE, one, 0)
+
+    reduce.start_with(multiply)
     up_fetch.start()
     down_fetch.start()
     for fetch in fetches:
@@ -1647,7 +1658,7 @@
     )
 
 
-def forward_exchange(psize, part, xin, gains, gate_weight, gate_got, up_weight, up_got, down_weight):
+def forward_exchange(psize, attended, w_out, xin, gains, gate_weight, gate_got, up_weight, up_got, down_weight):
     rows = xin.shape[0]
     return exchange_call(
         functools.partial(forward_exchange_kernel, psize),
@@ -1661,14 +1672,14 @@
             sds((down_weight.shape[0], D), BF16),
         ),
         (VMEM, ANY, ANY, ANY, ANY),
-        [VMEM, VMEM, VMEM, ANY, ANY, ANY, ANY, ANY],
+        [VMEM, VMEM, VMEM, VMEM, ANY, ANY, ANY, ANY, ANY],
         sum_scratch(psize, rows)
-        + [pltpu.VMEM((rows, D), BF16)]
+        + [pltpu.VMEM((rows, D), BF16), pltpu.VMEM((2 * psize, rows, D), BF16)]
         + [
             pltpu.VMEM(value.shape, BF16)
             for value in (gate_weight, gate_got, up_weight, up_got, down_weight)
         ],
-        (part, xin, gains, gate_weight, gate_got, up_weight, up_got, down_weight),
+        (attended, w_out, xin, gains, gate_weight, gate_got, up_weight, up_got, down_weight),
     )
 
 
@@ -1870,9 +1881,8 @@
         cot = jnp.concatenate(
             [jnp.where(same, cot_near, cot_first), jnp.where(same, cot_first, cot_second)], axis=1
         )
-        part = matmul(attended, w_out).astype(BF16).reshape(count, -1, D)
         resid, normed_b_all, w_gate, w_up, w_down = forward_exchange(
-            psize, part, xin, gains8, gate_weight, gate_got, up_weight, up_got, down_weight
+            psize, attended.reshape(count, -1, heads * DH), w_out, xin, gains8, gate_weight, gate_got, up_weight, up_got, down_weight
         )
         normed_b_all = normed_b_all.reshape(-1, D)
         w_gate, w_up = w_gate.reshape(D, -1), w_up.reshape(D, -1)

time: 560 us -> 557 us (level)
    pallas_call x4, Pallas kernels: 306 us -> 314 us  [exchange_call(): pl.pallas_call(kernel, out_shape=outs, in_specs=in_specs, out_specs=out_s...]
    dot_general x5 -> x4, matrix products: 37.8 us -> 33.5 us  [matmul(): return jnp.dot(left, right, preferred_element_type=F32)]
  transfers between devices with their start and end apart: 15 -> 15, of which waited for: 2 -> 3; matrix products, arithmetic and copies ran while one was open for 14% -> 13% of each run, Pallas kernels for 25% -> 25%
where the time goes in v8:
time: 557 us; the launch traced here: 552 us
  Pallas kernels  376 us (68%)
  matrix products  91.5 us (16%)
  other arithmetic  37.2 us (7%)
  local copies, waits for them, and re-layouts  21.6 us (4%)
  starting transfers between devices  20.7 us (4%)
    pallas_call x4, Pallas kernels, exchange_call(): pl.pallas_call(kernel, out_shape=outs, in_specs=in_specs, out_specs=out_s...  314 us
    dot_general x5, matrix products, contract_rows(): lax.dot_general(left, right, (((0,), (0,)), ((), ())), preferred_element_...  43.5 us
    pallas_call x1, Pallas kernels, attention_backward(): pl.pallas_call(functools.partial(backward_kernel, heads, count, prompt_le...  37.6 us
    dot_general x4, matrix products, matmul(): return jnp.dot(left, right, preferred_element_type=F32)  33.5 us
    pallas_call x1, Pallas kernels, attention_forward(): pl.pallas_call(functools.partial(forward_kernel, heads, count, prompt_len...  25 us
    dot_general x2, matrix products, contract_cols(): lax.dot_general(left, right, (((1,), (1,)), ((), ())), preferred_element_...  14.5 us
  transfers between devices with their start and end apart: 15, of which 3 were waited for; matrix products, arithmetic and copies ran while one was open for 13% of the time, Pallas kernels for 25%

profile of v8, /device:TPU:1, one launch (start us, length us, event | category | flops | bytes accessed | tf_op | source)
XLA Modules:
  0.0 552.2 jit_solution(17435860200257185624)
XLA Ops:
  1.3 0.7 stack.54
  2.0 0.7 stack.55
  2.7 0.9 copy.43
  3.6 0.7 pad_add_fusion.2
  5.0 0.7 concatenate.46.forget_shard
  6.4 68.4 %enter.1 = (bf16[384,1536]{1,0:T(8,128)(2,1)}, bf16[4,384,1536]{2,1,0:T(8,128)(2,1)}, bf16[2,768,1280]{2,1,0:T(8,128)(2,1)}, bf16[384,1536]{1,0:T(8,128)(2,1)}, ...) custom-call(bf16[768,768]{1,0:T(8,128)(2,1)} %x_ref.1, f32[8,768]{1,0:T(8,128)} %maximum_maximum_fusion.1.gain_own, ...), custom_call_target="tpu_custom_call" | custom-call | tf_op jit(solution)/shard_map/enter/pallas_call | solution.py:1605
  74.8 0.7 dynamic-slice_bitcast_fusion
  75.5 0.7 dynamic-slice_bitcast_fusion.1
  76.2 0.7 broadcast_add_fusion
  77.8 11.4 %fusion.15.proj_hbm = f32[4,384,1280]{2,1,0:T(8,128)} fusion(bf16[4,384,1536]{2,1,0:T(8,128)(2,1)} %get-tuple-element.87, bf16[1536,1280,1]{1,0,2:T(8,128)(2,1)} %bitcast.77), kind=kOutput, calls=%fused_computation.81 | convolution fusion | flops 6039797760 | bytes 16515072 | tf_op jit(solution)/shard_map/dot_general | solution.py:157
  89.2 1.3 constant_dynamic-slice_fusion.3
  90.9 1.3 broadcast_select_fusion.8
  92.4 1.3 collective-permute-start
  93.7 1.4 collective-permute-start.1
  95.1 1.9 collective-permute-start.2
  97.0 1.9 collective-permute-start.3
  99.2 0.7 broadcast_select_fusion.12.bias_ref
  99.9 25.0 %attention_forward.1 = (bf16[4,384,384]{2,1,0:T(8,128)(2,1)S(1)}, f32[384,1536]{1,0:T(8,128)S(1)}, f32[8,1536]{1,0:T(8,128)S(1)}, bf16[6,1536,128]{2,1,0:T(8,128...) custom-call(s32[36]{0:T(128)S(1)} %reshape.129.flags, ...), custom_call_target="tpu_custom_call" | custom-call | flops 20000000000 | bytes 30000000 | tf_op jit(solution)/shard_map/attention_forward/pallas_call | solution.py:343
  124.9 1.0 copy-done
  125.9 1.4 copy-done.5
  127.3 0.9 copy-done.6
  128.8 1.4 collective-permute-done.1.up_got
  130.2 1.6 broadcast_select_fusion.7
  132.1 77.3 %forward_exchange.1 = (f32[384,1536]{1,0:T(8,128)}, bf16[4,384,1536]{2,1,0:T(8,128)(2,1)}, bf16[2,768,1024]{2,1,0:T(8,128)(2,1)}, bf16[2,768,1024]{2,1,0:T(8,128)(2,1)}, bf16[1024,1536]{1,0:T(8,128)(2,1)}) custom-call(bf16[4,384,384]{2,1,0:T(8,128)(2,1)} %copy-done, bf16[384,1536]{1,0:T(8,128)(2,1)} %get-tuple-element.110.w_out, ...), custom_call_target="tpu_custom_call" | custom-call | tf_op jit(solution)/shard_map/forward_exchange/pallas_call | solution.py:1605
  209.4 5.8 %collective-permute-start.5 = (bf16[384,1536]{1,0:T(8,128)(2,1)S(1)}, bf16[384,1536]{1,0:T(8,128)(2,1)}, u32[]{:S(2)}, u32[]{:S(2)}) collective-permute-start(bf16[384,1536]{1,0:T(8,128)(2,1)S(1)} %pad_maximum_fusion.1.cot), channel_id=1, source_target_pairs={{0,1},{1,0},{2,3},{3,2},{4,5},{5,4},{6,7},{7,6},{8,9},{9,8},{10,11... | collective-permute-start | bytes 3538952 | tf_op jit(solution)/shard_map/ppermute | solution.py:26
  215.2 8.0 %fusion.16 = f32[1536,1024]{1,0:T(8,128)S(1)} fusion(bf16[1536,1536]{1,0:T(8,128)(2,1)} %bitcast.91, bf16[1536,1024]{1,0:T(8,128)(2,1)} %bitcast.80), kind=kOutput, calls=%fused_computation.82 | convolution fusion | flops 4831838208 | bytes 14155776 | tf_op jit(solution)/shard_map/dot_general | solution.py:157
  223.3 7.3 %multiply_convert_fusion.2 = (bf16[1536,1024]{1,0:T(8,128)(2,1)S(1)}, f32[1536,1024]{1,0:T(8,128)}) fusion(f32[1536,1024]{1,0:T(8,128)S(1)} %fusion.16, bf16[1536,1536]{1,0:T(8,128)(2,1)S(1)} %bitcast.94, bf16[1536,1024]{1,0:T(8,128)(2,1)S(1)} %bitcast.83), kind=kOutput, calls=%fused_computation.5 | convolution fusion | flops 4841275392 | bytes 23592960 | tf_op jit(solution)/shard_map/dot_general | solution.py:157
  230.5 6.9 %convolution_convert_fusion = bf16[1536,1536]{1,0:T(8,128)(2,1)} fusion(bf16[1536,1024]{1,0:T(8,128)(2,1)S(1)} %get-tuple-element.237, bf16[1024,1536]{1,0:T(8,128)(2,1)S(1)} %copy-done.30), kind=kOutput, calls=%fused_computation.1 | convolution fusion | flops 4834197504 | bytes 11010048 | tf_op jit(solution)/shard_map/dot_general | solution.py:157
  237.4 0.8 collective-permute-done.5
  238.2 1.9 fusion.11
  241.4 9.1 %convolution_convert_fusion.3 = bf16[1024,1536]{1,0:T(8,128)(2,1)S(1)} fusion(bf16[1536,1024]{1,0:T(8,128)(2,1)S(1)} %copy-done.33, bf16[384,1536]{1,0:T(8,128)(2,1)} %collective-permute-done.6, bf16[384,1536]{1,0:T(8,128)(2,1)} %collective-permute-done.5, bf16[384,1536]{1,0:T(8,128)(2,1)S(1)} %collective-permute-done.4, ...), kind=kOutput, calls=%fused_computation.11 | convolution fusion | flops 4857004032 | bytes 11010048 | tf_op jit(solution)/shard_map/dot_general | solution.py:145
  250.7 5.6 %pad_maximum_fusion = bf16[1536,1536]{1,0:T(8,128)(2,1)S(1)} fusion(bf16[384,1536]{1,0:T(8,128)(2,1)} %collective-permute-done.6, bf16[384,1536]{1,0:T(8,128)(2,1)} %collective-permute-done.5, bf16[384,1536]{1,0:T(8,128)(2,1)S(1)} %collective-permute-done.4, bf16[384,768]{1,0:T(8,128)(2,1)S(1)} %get-tuple-element.232, bf16[384,768]{1,0:T(8,128)(2,1)S(1)} %get-tuple-element.231), kind=kLoop, calls=%fused_computation.8 | loop fusion | flops 23592960 | bytes 9437184 | tf_op jit(solution)/shard_map/concatenate | solution.py:1810
  257.1 10.8 %multiply_convert_fusion = (bf16[1536,1024]{1,0:T(8,128)(2,1)S(1)}, bf16[1536,1024]{1,0:T(8,128)(2,1)S(1)}) fusion(f32[1536,1024]{1,0:T(8,128)} %copy-done.31, f32[1536,1024]{1,0:T(8,128)} %get-tuple-element.238, bf16[1536,1536]{1,0:T(8,128)(2,1)S(1)} %pad_maximum_fusion, bf16[1024,1536]{1,0:T(8,128)(2,1)} %get-tuple-element.118), kind=kOutput, calls=%fused_computation.3 | convolution fusion | flops 4852285440 | bytes 26738688 | tf_op jit(solution)/shard_map/dot_general | solution.py:151
  268.0 11.1 %convolution_convert_fusion.1 = bf16[1536,1024]{1,0:T(8,128)(2,1)} fusion(bf16[1536,1536]{1,0:T(8,128)(2,1)} %bitcast.92, bf16[1536,1024]{1,0:T(8,128)(2,1)S(1)} %get-tuple-element.215), kind=kOutput, calls=%fused_computation.9 | convolution fusion | flops 4833411072 | bytes 11010048 | tf_op jit(solution)/shard_map/dot_general | solution.py:145
  279.1 9.2 %convolution_convert_fusion.2 = bf16[1536,1024]{1,0:T(8,128)(2,1)} fusion(bf16[1536,1536]{1,0:T(8,128)(2,1)} %bitcast.93, bf16[1536,1024]{1,0:T(8,128)(2,1)S(1)} %get-tuple-element.214), kind=kOutput, calls=%fused_computation.10 | convolution fusion | flops 4833411072 | bytes 11010048 | tf_op jit(solution)/shard_map/dot_general | solution.py:145
  288.7 1.2 fusion.13
  289.9 2.0 add_convert_fusion.1
  291.9 1.2 fusion.12
  293.2 83.7 %backward_exchange.1 = (f32[384,1536]{1,0:T(8,128)}, bf16[4,384,1536]{2,1,0:T(8,128)(2,1)}, f32[8,1536]{1,0:T(8,128)}, bf16[512,768]{1,0:T(8,128)(2,1)}, bf16[2,384,1024]{2,1,0:T(8,128)(2,1)}) custom-call(bf16[4,384,1024]{2,1,0:T(8,128)(2,1)} %bitcast.85, bf16[4,384,1024]{2,1,0:T(8,128)(2,1)} %bitcast.84, bf16[1536,1024]{1,0:T(8,128)(2,1)} %bitcast.81, ...), custom_call_target="tpu_custom_call" | custom-call | tf_op jit(solution)/shard_map/backward_exchange/pallas_call | solution.py:1605
  376.9 4.5 fusion.2
  381.4 0.9 broadcast_select_fusion.1
  382.4 3.7 convolution_convert_fusion.4
  386.0 3.9 collective-permute-start.14
  390.0 1.6 collective-permute-start.11
  391.5 2.0 collective-permute-start.13
  393.6 37.6 %attention_backward.1 = (bf16[4,384,1280]{2,1,0:T(8,128)(2,1)}, f32[8,128]{1,0:T(8,128)}) custom-call(s32[36]{0:T(128)} %copy-done.4, bf16[4,384,384]{2,1,0:T(8,128)(2,1)} %bitcast.95, f32[384,1536]{1,0:T(8,128)} %copy-done.5, f32[8,1536]{1,0:T(8,128)} %copy-done.7, bf16[6,1536,128]{2,1,0:T(8,128)(2,1)} %get-tuple-element.135.qp, ...), custom_call_target="tpu_custom_call" | custom-call | flops 49999998976 | bytes 30000000 | tf_op jit(solution)/shard_map/attention_backward/pallas_call | solution.py:534
  431.3 3.4 add_convert_fusion.pair_in
  434.8 0.9 fusion.14
  435.7 9.6 %fusion = bf16[1536,1280]{1,0:T(8,128)(2,1)} fusion(bf16[4,384,1536]{2,1,0:T(8,128)(2,1)} %get-tuple-element.87, bf16[4,384,1280]{2,1,0:T(8,128)(2,1)S(1)} %copy-done.11), kind=kOutput, calls=%fused_computation.2 | convolution fusion | flops 6041763840 | bytes 12582912 | tf_op jit(solution)/shard_map/dot_general | solution.py:145
  445.3 0.7 slice_bitcast_fusion
  446.2 0.7 maximum_maximum_fusion.small_in
  446.9 84.5 %leave.1 = (bf16[768,768]{1,0:T(8,128)(2,1)}, f32[8,768]{1,0:T(8,128)}, bf16[384,1280]{1,0:T(8,128)(2,1)}, bf16[2,192,1280]{2,1,0:T(8,128)(2,1)}, bf16[2,192,768...) custom-call(bf16[4,384,1280]{2,1,0:T(8,128)(2,1)} %get-tuple-element, ...), custom_call_target="tpu_custom_call" | custom-call | tf_op jit(solution)/shard_map/leave/pallas_call | solution.py:1605
  531.4 1.0 fusion.5
  532.4 3.5 fusion.4
  535.8 0.8 slice_reduce_fusion.2
  536.7 1.4 slice_reduce_fusion
  538.1 0.8 copy.48
  538.8 3.3 bitcast_convert_fusion
  542.1 2.2 bitcast_convert_fusion.1
  544.3 2.2 bitcast_convert_fusion.2
  546.5 1.1 bitcast_convert_fusion.3
  548.2 1.3 broadcast_select_fusion.10
  549.6 1.1 pad_maximum_fusion.2
  550.7 1.0 copy.52
  (138 shorter events, 8.3 us)
Async XLA Ops:
  5.0 84.1 %copy-start.27 = (f32[8]{0:T(128)}, f32[8]{0:T(128)S(1)}, u32[]{:S(2)}) copy-start(f32[8]{0:T(128)S(1)} %pad.39.clone) | copy-start | bytes 100
  77.8 22.1 %copy-start.4 = (s32[36]{0:T(128)}, s32[36]{0:T(128)S(1)}, u32[]{:S(2)}) copy-start(s32[36]{0:T(128)S(1)} %reshape.129.flags) | copy-start | bytes 436
  77.8 11.4 %copy-start.12 = (bf16[768,1024]{1,0:T(8,128)(2,1)S(1)}, bf16[768,1024]{1,0:T(8,128)(2,1)}, u32[]{:S(2)}) copy-start(bf16[768,1024]{1,0:T(8,128)(2,1)} %gate_shard.1) | copy-start | bytes 4718596
  77.8 11.4 %copy-start.13 = (bf16[768,1024]{1,0:T(8,128)(2,1)S(1)}, bf16[768,1024]{1,0:T(8,128)(2,1)}, u32[]{:S(2)}) copy-start(bf16[768,1024]{1,0:T(8,128)(2,1)} %up_shard.1) | copy-start | bytes 4718596
  89.2 1.8 copy-start.21
  92.3 32.5 %copy-start.3 = (s32[8,1536]{1,0:T(8,128)}, s32[8,1536]{1,0:T(8,128)S(1)}, u32[]{:S(2)}) copy-start(s32[8,1536]{1,0:T(8,128)S(1)} %stack.69.qrow) | copy-start | bytes 147460
  92.4 36.5 %collective-permute-start = (bf16[384,1024]{1,0:T(8,128)(2,1)}, bf16[384,1024]{1,0:T(8,128)(2,1)S(1)}, u32[]{:S(2)}, u32[]{:S(2)}) collective-permute-start(bf16[384,1024]{1,0:T(8,128)(2,1)} %get-tuple-element.97), channel_id=1, source_target_pairs={{0,4},{2,8},{4,0},{6,12},{8,2},{10,14},{12,6},{14,10},{1,5},{3,9},... | collective-permute-start | bytes 2359304 | tf_op jit(solution)/shard_map/ppermute | solution.py:40
  93.7 36.5 %collective-permute-start.1 = (bf16[384,1024]{1,0:T(8,128)(2,1)}, bf16[384,1024]{1,0:T(8,128)(2,1)S(1)}, u32[]{:S(2)}, u32[]{:S(2)}) collective-permute-start(bf16[384,1024]{1,0:T(8,128)(2,1)} %get-tuple-element.98), channel_id=1, source_target_pairs={{0,4},{2,8},{4,0},{6,12},{8,2},{10,14},{12,6},{14,10},{1,5},{3,9},... | collective-permute-start | bytes 2359304 | tf_op jit(solution)/shard_map/ppermute | solution.py:40
  95.1 33.7 %collective-permute-start.2 = (bf16[384,768]{1,0:T(8,128)(2,1)}, bf16[384,768]{1,0:T(8,128)(2,1)}, u32[]{:S(2)}, u32[]{:S(2)}) collective-permute-start(bf16[384,768]{1,0:T(8,128)(2,1)} %get-tuple-element.99), channel_id=1, source_target_pairs={{0,8},{4,0},{8,12},{12,4},{1,9},{5,1},{9,13},{13,5},{2,10},{6,2},{... | collective-permute-start | bytes 1769480 | tf_op jit(solution)/shard_map/ppermute | solution.py:1872
  97.0 31.8 %collective-permute-start.3 = (bf16[384,768]{1,0:T(8,128)(2,1)}, bf16[384,768]{1,0:T(8,128)(2,1)}, u32[]{:S(2)}, u32[]{:S(2)}) collective-permute-start(bf16[384,768]{1,0:T(8,128)(2,1)} %get-tuple-element.100), channel_id=1, source_target_pairs={{4,8},{8,4},{5,9},{9,5},{6,10},{10,6},{7,11},{11,7},{20,24},{24,20... | collective-permute-start | bytes 1769480 | tf_op jit(solution)/shard_map/ppermute | solution.py:1873
  99.2 25.7 %copy-start.2 = (s32[1536,8]{1,0:T(8,128)}, s32[1536,8]{1,0:T(8,128)S(1)}, u32[]{:S(2)}) copy-start(s32[1536,8]{1,0:T(8,128)S(1)} %copy.44.kcol) | copy-start | bytes 147460
  124.9 1.0 copy-start
  125.9 1.4 copy-start.5
  127.3 0.9 copy-start.6
  128.2 0.6 copy-start.7
  128.8 3.0 copy-start.23
  130.2 1.6 copy-start.24
  132.0 77.4 %copy-start.9 = (bf16[384,1536]{1,0:T(8,128)(2,1)}, bf16[384,1536]{1,0:T(8,128)(2,1)S(1)}, u32[]{:S(2)}) copy-start(bf16[384,1536]{1,0:T(8,128)(2,1)S(1)} %pad_maximum_fusion.1.cot) | copy-start | bytes 3538948
  132.0 108.8 %collective-permute-start.4 = (bf16[384,1536]{1,0:T(8,128)(2,1)S(1)}, bf16[384,1536]{1,0:T(8,128)(2,1)S(1)}, u32[]{:S(2)}, u32[]{:S(2)}) collective-permute-start(bf16[384,1536]{1,0:T(8,128)(2,1)S(1)} %pad_maximum_fusion.1.cot), channel_id=1, source_target_pairs={{0,8},{8,0},{1,9},{9,1},{2,10},{10,2},{3,11},{11,3},{4,12},{12,4},... | collective-permute-start | bytes 3538952 | tf_op jit(solution)/shard_map/ppermute | solution.py:22
  209.4 28.8 %collective-permute-start.5 = (bf16[384,1536]{1,0:T(8,128)(2,1)S(1)}, bf16[384,1536]{1,0:T(8,128)(2,1)}, u32[]{:S(2)}, u32[]{:S(2)}) collective-permute-start(bf16[384,1536]{1,0:T(8,128)(2,1)S(1)} %pad_maximum_fusion.1.cot), channel_id=1, source_target_pairs={{0,1},{1,0},{2,3},{3,2},{4,5},{5,4},{6,7},{7,6},{8,9},{9,8},{10,11... | collective-permute-start | bytes 3538952 | tf_op jit(solution)/shard_map/ppermute | solution.py:26
  215.2 8.0 %copy-start.14 = (bf16[2,768,1024]{2,1,0:T(8,128)(2,1)S(1)}, bf16[2,768,1024]{2,1,0:T(8,128)(2,1)}, u32[]{:S(2)}) copy-start(bf16[2,768,1024]{2,1,0:T(8,128)(2,1)} %get-tuple-element.117) | copy-start | bytes 9437188
  215.2 8.0 %copy-start.29 = (bf16[4,384,1536]{2,1,0:T(8,128)(2,1)S(1)}, bf16[4,384,1536]{2,1,0:T(8,128)(2,1)}, u32[]{:S(2)}) copy-start(bf16[4,384,1536]{2,1,0:T(8,128)(2,1)} %get-tuple-element.115) | copy-start | bytes 14155780
  223.2 7.3 %copy-start.31 = (f32[1536,1024]{1,0:T(8,128)}, f32[1536,1024]{1,0:T(8,128)S(1)}, u32[]{:S(2)}) copy-start(f32[1536,1024]{1,0:T(8,128)S(1)} %fusion.16) | copy-start | bytes 18874372
  223.2 7.3 %copy-start.30 = (bf16[1024,1536]{1,0:T(8,128)(2,1)S(1)}, bf16[1024,1536]{1,0:T(8,128)(2,1)}, u32[]{:S(2)}) copy-start(bf16[1024,1536]{1,0:T(8,128)(2,1)} %get-tuple-element.118) | copy-start | bytes 9437188
  230.5 6.9 %copy-start.32 = (bf16[1536,1024]{1,0:T(8,128)(2,1)}, bf16[1536,1024]{1,0:T(8,128)(2,1)S(1)}, u32[]{:S(2)}) copy-start(bf16[1536,1024]{1,0:T(8,128)(2,1)S(1)} %get-tuple-element.237) | copy-start | bytes 9437188
  238.2 3.2 collective-permute-start.6
  238.2 3.2 copy-start.33
  240.1 16.1 %collective-permute-start.7 = (bf16[384,1536]{1,0:T(8,128)(2,1)S(1)}, bf16[384,1536]{1,0:T(8,128)(2,1)S(1)}, u32[]{:S(2)}, u32[]{:S(2)}) collective-permute-start(bf16[384,1536]{1,0:T(8,128)(2,1)S(1)} %get-tuple-element.219), channel_id=1, source_target_pairs={{0,8},{8,0},{1,9},{9,1},{2,10},{10,2},{3,11},{11,3},{4,12},{12,4},... | collective-permute-start | bytes 3538952 | tf_op jit(solution)/shard_map/ppermute | solution.py:22
  240.7 15.6 %collective-permute-start.9 = (bf16[384,1536]{1,0:T(8,128)(2,1)S(1)}, bf16[384,1536]{1,0:T(8,128)(2,1)S(1)}, u32[]{:S(2)}, u32[]{:S(2)}) collective-permute-start(bf16[384,1536]{1,0:T(8,128)(2,1)S(1)} %get-tuple-element.218), channel_id=1, source_target_pairs={{0,8},{8,0},{1,9},{9,1},{2,10},{10,2},{3,11},{11,3},{4,12},{12,4},... | collective-permute-start | bytes 3538952 | tf_op jit(solution)/shard_map/ppermute | solution.py:22
  250.4 5.9 %slice-start = ((s8[4718592]{0:T(1024)(128)(4,1)}), s8[4194304]{0:T(1024)(128)(4,1)S(1)}, s32[]{:S(2)}) async-start(s8[4718592]{0:T(1024)(128)(4,1)} %bitcast.72), calls=%async_computation | async-start | bytes 8388608
  250.6 5.7 %slice-start.1 = ((s8[4718592]{0:T(1024)(128)(4,1)}), s8[524288]{0:T(1024)(128)(4,1)S(1)}, s32[]{:S(2)}) async-start(s8[4718592]{0:T(1024)(128)(4,1)} %bitcast.72), calls=%async_computation.1 | async-start | bytes 1048576
  250.6 37.7 %collective-permute-start.8 = (bf16[512,1536]{1,0:T(8,128)(2,1)S(1)}, bf16[512,1536]{1,0:T(8,128)(2,1)}, u32[]{:S(2)}, u32[]{:S(2)}) collective-permute-start(bf16[512,1536]{1,0:T(8,128)(2,1)S(1)} %broadcast_select_fusion), channel_id=1, source_target_pairs={{0,16},{16,0},{1,17},{17,1},{2,18},{18,2},{3,19},{19,3},{4,20},{20... | collective-permute-start | bytes 4718600 | tf_op jit(solution)/shard_map/ppermute | solution.py:26
  257.0 31.3 %collective-permute-start.10 = (bf16[384,1536]{1,0:T(8,128)(2,1)S(1)}, bf16[384,1536]{1,0:T(8,128)(2,1)S(1)}, u32[]{:S(2)}, u32[]{:S(2)}) collective-permute-start(bf16[384,1536]{1,0:T(8,128)(2,1)S(1)} %get-tuple-element.216), channel_id=1, source_target_pairs={{0,1},{1,0},{2,3},{3,2},{4,5},{5,4},{6,7},{7,6},{8,9},{9,8},{10,11... | collective-permute-start | bytes 3538952 | tf_op jit(solution)/shard_map/ppermute | solution.py:26
  267.9 11.1 %copy-start.16 = (bf16[1536,1024]{1,0:T(8,128)(2,1)}, bf16[1536,1024]{1,0:T(8,128)(2,1)S(1)}, u32[]{:S(2)}) copy-start(bf16[1536,1024]{1,0:T(8,128)(2,1)S(1)} %get-tuple-element.215) | copy-start | bytes 9437188
  267.9 11.1 %copy-start.15 = (bf16[1536,1024]{1,0:T(8,128)(2,1)}, bf16[1536,1024]{1,0:T(8,128)(2,1)S(1)}, u32[]{:S(2)}) copy-start(bf16[1536,1024]{1,0:T(8,128)(2,1)S(1)} %get-tuple-element.214) | copy-start | bytes 9437188
  279.1 9.2 %copy-start.8 = (f32[384,1536]{1,0:T(8,128)S(1)}, f32[384,1536]{1,0:T(8,128)}, u32[]{:S(2)}) copy-start(f32[384,1536]{1,0:T(8,128)} %get-tuple-element.123.resid) | copy-start | bytes 7077892
  293.2 83.7 %copy-start.1 = (bf16[4,384,384]{2,1,0:T(8,128)(2,1)S(1)}, bf16[4,384,384]{2,1,0:T(8,128)(2,1)}, u32[]{:S(2)}) copy-start(bf16[4,384,384]{2,1,0:T(8,128)(2,1)} %copy-done) | copy-start | bytes 3538948
  376.9 5.4 copy-start.10
  376.9 5.4 copy-start.20
  382.4 3.7 copy-start.17
  386.0 45.2 %collective-permute-start.14 = (bf16[2,384,1024]{2,1,0:T(8,128)(2,1)S(1)}, bf16[2,384,1024]{2,1,0:T(8,128)(2,1)}, u32[]{:S(2)}, u32[]{:S(2)}) collective-permute-start(bf16[2,384,1024]{2,1,0:T(8,128)(2,1)S(1)} %copy-done.17), channel_id=1, source_target_pairs={{2,0},{8,10},{3,1},{9,11},{6,4},{12,14},{7,5},{13,15},{18,16},{24,... | collective-permute-start | bytes 4718600 | tf_op jit(solution)/shard_map/ppermute | solution.py:65
  390.0 41.3 %collective-permute-start.11 = (bf16[192,1536]{1,0:T(8,128)(2,1)}, bf16[192,1536]{1,0:T(8,128)(2,1)S(1)}, u32[]{:S(2)}, u32[]{:S(2)}) collective-permute-start(bf16[192,1536]{1,0:T(8,128)(2,1)} %get-tuple-element.141), channel_id=1, source_target_pairs={{0,16},{16,0},{1,17},{17,1},{2,18},{18,2},{3,19},{19,3},{4,20},{20... | collective-permute-start | bytes 1769480 | tf_op jit(solution)/shard_map/ppermute | solution.py:26
  391.5 39.7 %collective-permute-start.12 = (bf16[384,768]{1,0:T(8,128)(2,1)}, bf16[384,768]{1,0:T(8,128)(2,1)}, u32[]{:S(2)}, u32[]{:S(2)}) collective-permute-start(bf16[384,768]{1,0:T(8,128)(2,1)} %get-tuple-element.142), channel_id=1, source_target_pairs={{8,0},{0,4},{12,8},{4,12},{9,1},{1,5},{13,9},{5,13},{10,2},{2,6},{... | collective-permute-start | bytes 1769480 | tf_op jit(solution)/shard_map/ppermute | solution.py:131
  391.5 39.7 %collective-permute-start.13 = (bf16[384,768]{1,0:T(8,128)(2,1)}, bf16[384,768]{1,0:T(8,128)(2,1)}, u32[]{:S(2)}, u32[]{:S(2)}) collective-permute-start(bf16[384,768]{1,0:T(8,128)(2,1)} %get-tuple-element.143), channel_id=1, source_target_pairs={{8,4},{4,8},{9,5},{5,9},{10,6},{6,10},{11,7},{7,11},{24,20},{20,24... | collective-permute-start | bytes 1769480 | tf_op jit(solution)/shard_map/ppermute | solution.py:132
  393.6 37.6 %copy-start.26 = (f32[8,1536]{1,0:T(8,128)S(1)}, f32[8,1536]{1,0:T(8,128)}, u32[]{:S(2)}) copy-start(f32[8,1536]{1,0:T(8,128)} %get-tuple-element.149) | copy-start | bytes 147460
  431.3 4.4 copy-start.11
  435.7 10.6 %copy-start.28 = (f32[8]{0:T(128)S(1)}, f32[8]{0:T(128)}, u32[]{:S(2)}) copy-start(f32[8]{0:T(128)} %copy-done.27) | copy-start | bytes 100
  535.8 6.3 %copy-start.19 = (bf16[2,384,1024]{2,1,0:T(8,128)(2,1)S(1)}, bf16[2,384,1024]{2,1,0:T(8,128)(2,1)}, u32[]{:S(2)}) copy-start(bf16[2,384,1024]{2,1,0:T(8,128)(2,1)} %get-tuple-element.161) | copy-start | bytes 4718596
  542.1 2.2 copy-start.18
  544.3 2.2 copy-start.25
  546.5 4.2 copy-start.22

commit v9 on v8

--- a/solution.py
+++ b/solution.py
@@ -1454,7 +1454,7 @@
 ):
     w = Wires(send_sem, recv_sem, local_sem)
     split = first_val.shape[0]
-    second = EarlySum(w, proj_in, second_val, second_over, second_across, None, 2, split)
+    second = EarlySum(w, proj_in, second_val, second_over, second_across, None, 1, split)
     second.load()
     loads = [
         w.local(source, target)
@@ -1475,7 +1475,7 @@
     )
     first.other = proj_in.at[1, pl.ds(0, split)]
     late = Chain(
-        w, osize, second_val.at[0], ["h"] + bits[1:], [second_bufs.at[i] for i in range(len(bits))], None, 2
+        w, osize, second_val.at[0], ["h"] + bits[1:], [second_bufs.at[i] for i in range(len(bits))], None, 1
     )
     out = Chain(w, osize, out_val, ["x", "h"] + bits[1:], [out_bufs.at[i] for i in range(1 + len(bits))], None, 1)
     out.other = out_other
@@ -1523,8 +1523,7 @@
     def cross_far(i):
         return w.copy(kept.at[1, spans[i]], target(i), {"k": 1 - w.k, "x": 1 - w.x}, far_slots[i])
 
-    for i in range(2):
-        second.pass_on(i)
+    second.pass_on(0)
     first.step(0, 0)
     for i in range(1, pieces):
         first.step(0, i)
@@ -1553,10 +1552,6 @@
         def _():
             cross_near(i).start()
             cross_far(i).start()
-
-        if i == 0:
-            second.finish(1)
-            late.start(0, 1)
 
     gain_sum = jnp.sum(gain_acc[...], axis=0, keepdims=True)
     row = lax.broadcasted_iota(jnp.int32, (8, half), 0)
@@ -1724,7 +1719,8 @@
     bits = len(bits_of(osize))
     half = D // 2
     columns = proj.shape[2]
-    split = proj.shape[1] // 2
+    split = proj.shape[1] * 3 // 4
+    late = (proj.shape[1] - split) // 2
 
     def scratch(*shape):
         return pltpu.VMEM(shape, BF16)
@@ -1740,7 +1736,7 @@
             sds((2 * rows, half), BF16),
             sds((8, half), F32),
             sds((split, columns), BF16),
-            both((split // 2, columns)),
+            both((late, columns)),
             both(out_own.shape),
             both(pair.shape[1:]),
             both(pair.shape[1:]),
@@ -1753,15 +1749,15 @@
             scratch(2 * psize, rows, D),
             scratch(2, rows, half),
             scratch(split, columns),
-            scratch(2, split // 2, columns),
+            scratch(2, late, columns),
             scratch(*out_own.shape),
             scratch(*pair.shape[1:]),
             scratch(*pair.shape[1:]),
             scratch(*down.shape),
             scratch(2 + bits, split, columns),
-            scratch(2, split // 2, columns),
-            scratch(split // 2, columns),
-            scratch(bits, split // 2, columns),
+            scratch(2, late, columns),
+            scratch(late, columns),
+            scratch(bits, late, columns),
             scratch(1 + bits, *out_own.shape),
             pltpu.VMEM((8, half), F32),
             pltpu.VMEM((3 + len(bits_of(psize)) + bits, 8, half), F32),
@@ -1976,7 +1972,7 @@
             pair_total,
             down_total,
         )
-        proj_grad = jnp.concatenate([first_rows, second_rows.reshape(first_rows.shape)], axis=0)
+        proj_grad = jnp.concatenate([first_rows, second_rows.reshape(-1, first_rows.shape[1])], axis=0)
         qkv_grad = proj_grad[:, :width].astype(F32)
         forget_grad = proj_grad[:, width : width + heads].astype(F32)
         bias_all = small[2, : 2 * psize * heads].reshape(2 * psize, heads)

time: 557 us -> 567 us (1.018)
  Pallas kernels: 376 us -> 384 us
  transfers between devices with their start and end apart: 15 -> 15, of which waited for: 3 -> 2; matrix products, arithmetic and copies ran while one was open for 13% -> 13% of each run, Pallas kernels for 25% -> 25%
where the time goes in v9:
time: 567 us; the launch traced here: 561 us
  Pallas kernels  384 us (68%)
  matrix products  91.5 us (16%)
  other arithmetic  37.2 us (7%)
  starting transfers between devices  23 us (4%)
  local copies, waits for them, and re-layouts  22 us (4%)
    pallas_call x4, Pallas kernels, exchange_call(): pl.pallas_call(kernel, out_shape=outs, in_specs=in_specs, out_specs=out_s...  318 us
    dot_general x5, matrix products, contract_rows(): lax.dot_general(left, right, (((0,), (0,)), ((), ())), preferred_element_...  43.5 us
    pallas_call x1, Pallas kernels, attention_backward(): pl.pallas_call(functools.partial(backward_kernel, heads, count, prompt_le...  39.8 us
    dot_general x4, matrix products, matmul(): return jnp.dot(left, right, preferred_element_type=F32)  33.5 us
    pallas_call x1, Pallas kernels, attention_forward(): pl.pallas_call(functools.partial(forward_kernel, heads, count, prompt_len...  26.7 us
    dot_general x2, matrix products, contract_cols(): lax.dot_general(left, right, (((1,), (1,)), ((), ())), preferred_element_...  14.5 us
  transfers between devices with their start and end apart: 15, of which 2 were waited for; matrix products, arithmetic and copies ran while one was open for 13% of the time, Pallas kernels for 25%

profile of v9, /device:TPU:1, one launch (start us, length us, event | category | flops | bytes accessed | tf_op | source)
XLA Modules:
  0.0 561.3 jit_solution(10783990957698146286)
XLA Ops:
  1.3 0.7 stack.54
  2.0 0.7 stack.55
  2.7 0.9 copy.43
  3.6 0.7 pad_add_fusion.2
  5.0 0.7 concatenate.46.forget_shard
  5.7 0.7 maximum_maximum_fusion.1.gain_own
  6.4 68.4 %enter.1 = (bf16[384,1536]{1,0:T(8,128)(2,1)}, bf16[4,384,1536]{2,1,0:T(8,128)(2,1)}, bf16[2,768,1280]{2,1,0:T(8,128)(2,1)}, bf16[384,1536]{1,0:T(8,128)(2,1)}, ...) custom-call(bf16[768,768]{1,0:T(8,128)(2,1)} %x_ref.1, f32[8,768]{1,0:T(8,128)} %maximum_maximum_fusion.1.gain_own, ...), custom_call_target="tpu_custom_call" | custom-call | tf_op jit(solution)/shard_map/enter/pallas_call | solution.py:1600
  74.8 0.7 dynamic-slice_bitcast_fusion
  76.2 0.7 broadcast_add_fusion
  77.7 11.4 %fusion.15.proj_hbm = f32[4,384,1280]{2,1,0:T(8,128)} fusion(bf16[4,384,1536]{2,1,0:T(8,128)(2,1)} %get-tuple-element.87, bf16[1536,1280,1]{1,0,2:T(8,128)(2,1)} %bitcast.75), kind=kOutput, calls=%fused_computation.81 | convolution fusion | flops 6039797760 | bytes 16515072 | tf_op jit(solution)/shard_map/dot_general | solution.py:157
  89.1 1.3 constant_dynamic-slice_fusion.3
  90.9 1.3 broadcast_select_fusion.8
  92.3 1.3 collective-permute-start
  93.7 1.4 collective-permute-start.1
  95.0 1.9 collective-permute-start.2
  97.0 1.9 collective-permute-start.3
  99.2 0.7 broadcast_select_fusion.12.bias_ref
  99.8 26.7 %attention_forward.1 = (bf16[4,384,384]{2,1,0:T(8,128)(2,1)S(1)}, f32[384,1536]{1,0:T(8,128)S(1)}, f32[8,1536]{1,0:T(8,128)S(1)}, bf16[6,1536,128]{2,1,0:T(8,128...) custom-call(s32[36]{0:T(128)S(1)} %reshape.129.flags, ...), custom_call_target="tpu_custom_call" | custom-call | flops 20000000000 | bytes 30000000 | tf_op jit(solution)/shard_map/attention_forward/pallas_call | solution.py:343
  126.5 1.0 copy-done
  127.6 1.4 copy-done.5
  128.9 0.9 copy-done.6
  130.5 1.9 broadcast_select_fusion.7
  132.6 74.4 %forward_exchange.1 = (f32[384,1536]{1,0:T(8,128)}, bf16[4,384,1536]{2,1,0:T(8,128)(2,1)}, bf16[2,768,1024]{2,1,0:T(8,128)(2,1)}, bf16[2,768,1024]{2,1,0:T(8,128)(2,1)}, bf16[1024,1536]{1,0:T(8,128)(2,1)}) custom-call(bf16[4,384,384]{2,1,0:T(8,128)(2,1)} %copy-done, bf16[384,1536]{1,0:T(8,128)(2,1)} %get-tuple-element.110.w_out, ...), custom_call_target="tpu_custom_call" | custom-call | tf_op jit(solution)/shard_map/forward_exchange/pallas_call | solution.py:1600
  207.0 5.9 %collective-permute-start.5 = (bf16[384,1536]{1,0:T(8,128)(2,1)S(1)}, bf16[384,1536]{1,0:T(8,128)(2,1)}, u32[]{:S(2)}, u32[]{:S(2)}) collective-permute-start(bf16[384,1536]{1,0:T(8,128)(2,1)S(1)} %pad_maximum_fusion.1.cot), channel_id=1, source_target_pairs={{0,1},{1,0},{2,3},{3,2},{4,5},{5,4},{6,7},{7,6},{8,9},{9,8},{10,11... | collective-permute-start | bytes 3538952 | tf_op jit(solution)/shard_map/ppermute | solution.py:26
  212.9 8.0 %fusion.16 = f32[1536,1024]{1,0:T(8,128)S(1)} fusion(bf16[1536,1536]{1,0:T(8,128)(2,1)} %bitcast.91, bf16[1536,1024]{1,0:T(8,128)(2,1)} %bitcast.78), kind=kOutput, calls=%fused_computation.82 | convolution fusion | flops 4831838208 | bytes 14155776 | tf_op jit(solution)/shard_map/dot_general | solution.py:157
  220.9 7.3 %multiply_convert_fusion.2 = (bf16[1536,1024]{1,0:T(8,128)(2,1)S(1)}, f32[1536,1024]{1,0:T(8,128)}) fusion(f32[1536,1024]{1,0:T(8,128)S(1)} %fusion.16, bf16[1536,1536]{1,0:T(8,128)(2,1)S(1)} %bitcast.94, bf16[1536,1024]{1,0:T(8,128)(2,1)S(1)} %bitcast.81), kind=kOutput, calls=%fused_computation.5 | convolution fusion | flops 4841275392 | bytes 23592960 | tf_op jit(solution)/shard_map/dot_general | solution.py:157
  228.2 6.8 %convolution_convert_fusion = bf16[1536,1536]{1,0:T(8,128)(2,1)} fusion(bf16[1536,1024]{1,0:T(8,128)(2,1)S(1)} %get-tuple-element.237, bf16[1024,1536]{1,0:T(8,128)(2,1)S(1)} %copy-done.31), kind=kOutput, calls=%fused_computation.1 | convolution fusion | flops 4834197504 | bytes 11010048 | tf_op jit(solution)/shard_map/dot_general | solution.py:157
  235.1 0.7 collective-permute-done.5
  235.8 1.9 fusion.11
  239.0 9.1 %convolution_convert_fusion.3 = bf16[1024,1536]{1,0:T(8,128)(2,1)S(1)} fusion(bf16[1536,1024]{1,0:T(8,128)(2,1)S(1)} %copy-done.34, bf16[384,1536]{1,0:T(8,128)(2,1)} %collective-permute-done.6, bf16[384,1536]{1,0:T(8,128)(2,1)} %collective-permute-done.5, bf16[384,1536]{1,0:T(8,128)(2,1)S(1)} %collective-permute-done.4, ...), kind=kOutput, calls=%fused_computation.11 | convolution fusion | flops 4857004032 | bytes 11010048 | tf_op jit(solution)/shard_map/dot_general | solution.py:145
  248.2 1.0 collective-permute-start.8
  249.2 5.6 %pad_maximum_fusion = bf16[1536,1536]{1,0:T(8,128)(2,1)S(1)} fusion(bf16[384,1536]{1,0:T(8,128)(2,1)} %collective-permute-done.6, bf16[384,1536]{1,0:T(8,128)(2,1)} %collective-permute-done.5, bf16[384,1536]{1,0:T(8,128)(2,1)S(1)} %collective-permute-done.4, bf16[384,768]{1,0:T(8,128)(2,1)S(1)} %get-tuple-element.232, bf16[384,768]{1,0:T(8,128)(2,1)S(1)} %get-tuple-element.231), kind=kLoop, calls=%fused_computation.8 | loop fusion | flops 23592960 | bytes 9437184 | tf_op jit(solution)/shard_map/concatenate | solution.py:1806
  256.3 10.8 %multiply_convert_fusion = (bf16[1536,1024]{1,0:T(8,128)(2,1)S(1)}, bf16[1536,1024]{1,0:T(8,128)(2,1)S(1)}) fusion(f32[1536,1024]{1,0:T(8,128)} %copy-done.32, f32[1536,1024]{1,0:T(8,128)} %get-tuple-element.238, bf16[1536,1536]{1,0:T(8,128)(2,1)S(1)} %pad_maximum_fusion, bf16[1024,1536]{1,0:T(8,128)(2,1)} %get-tuple-element.118), kind=kOutput, calls=%fused_computation.3 | convolution fusion | flops 4852285440 | bytes 26738688 | tf_op jit(solution)/shard_map/dot_general | solution.py:151
  267.1 11.1 %convolution_convert_fusion.1 = bf16[1536,1024]{1,0:T(8,128)(2,1)} fusion(bf16[1536,1536]{1,0:T(8,128)(2,1)} %bitcast.92, bf16[1536,1024]{1,0:T(8,128)(2,1)S(1)} %get-tuple-element.215), kind=kOutput, calls=%fused_computation.9 | convolution fusion | flops 4833411072 | bytes 11010048 | tf_op jit(solution)/shard_map/dot_general | solution.py:145
  278.2 9.2 %convolution_convert_fusion.2 = bf16[1536,1024]{1,0:T(8,128)(2,1)} fusion(bf16[1536,1536]{1,0:T(8,128)(2,1)} %bitcast.93, bf16[1536,1024]{1,0:T(8,128)(2,1)S(1)} %get-tuple-element.214), kind=kOutput, calls=%fused_computation.10 | convolution fusion | flops 4833411072 | bytes 11010048 | tf_op jit(solution)/shard_map/dot_general | solution.py:145
  287.9 1.2 fusion.13
  289.1 2.0 add_convert_fusion.1
  291.1 1.2 fusion.12
  292.3 83.1 %backward_exchange.1 = (f32[384,1536]{1,0:T(8,128)}, bf16[4,384,1536]{2,1,0:T(8,128)(2,1)}, f32[8,1536]{1,0:T(8,128)}, bf16[512,768]{1,0:T(8,128)(2,1)}, bf16[2,384,1024]{2,1,0:T(8,128)(2,1)}) custom-call(bf16[4,384,1024]{2,1,0:T(8,128)(2,1)} %bitcast.83, bf16[4,384,1024]{2,1,0:T(8,128)(2,1)} %bitcast.82, bf16[1536,1024]{1,0:T(8,128)(2,1)} %bitcast.79, ...), custom_call_target="tpu_custom_call" | custom-call | tf_op jit(solution)/shard_map/backward_exchange/pallas_call | solution.py:1600
  375.5 4.5 fusion.2
  380.0 0.9 broadcast_select_fusion.1
  380.9 3.7 convolution_convert_fusion.4
  384.6 4.0 collective-permute-start.14
  388.6 0.8 collective-permute-start.11
  389.4 3.3 collective-permute-start.13
  392.8 39.8 %attention_backward.1 = (bf16[4,384,1280]{2,1,0:T(8,128)(2,1)}, f32[8,128]{1,0:T(8,128)}) custom-call(s32[36]{0:T(128)} %copy-done.4, bf16[4,384,384]{2,1,0:T(8,128)(2,1)} %bitcast.95, f32[384,1536]{1,0:T(8,128)} %copy-done.5, f32[8,1536]{1,0:T(8,128)} %copy-done.7, bf16[6,1536,128]{2,1,0:T(8,128)(2,1)} %get-tuple-element.135.qp, ...), custom_call_target="tpu_custom_call" | custom-call | flops 49999998976 | bytes 30000000 | tf_op jit(solution)/shard_map/attention_backward/pallas_call | solution.py:534
  432.7 3.4 add_convert_fusion.pair_in
  436.2 0.9 fusion.14
  437.1 9.6 %fusion = bf16[1536,1280]{1,0:T(8,128)(2,1)} fusion(bf16[4,384,1536]{2,1,0:T(8,128)(2,1)} %get-tuple-element.87, bf16[4,384,1280]{2,1,0:T(8,128)(2,1)S(1)} %copy-done.12), kind=kOutput, calls=%fused_computation.2 | convolution fusion | flops 6041763840 | bytes 12582912 | tf_op jit(solution)/shard_map/dot_general | solution.py:145
  446.7 0.7 slice_bitcast_fusion
  447.7 0.7 maximum_maximum_fusion.small_in
  448.4 92.1 %leave.1 = (bf16[768,768]{1,0:T(8,128)(2,1)}, f32[8,768]{1,0:T(8,128)}, bf16[576,1280]{1,0:T(8,128)(2,1)}, bf16[2,96,1280]{2,1,0:T(8,128)(2,1)}, bf16[2,192,768]...) custom-call(bf16[4,384,1280]{2,1,0:T(8,128)(2,1)} %get-tuple-element, ...), custom_call_target="tpu_custom_call" | custom-call | tf_op jit(solution)/shard_map/leave/pallas_call | solution.py:1600
  540.5 1.1 fusion.5
  541.9 3.0 fusion.4
  545.0 0.8 slice_reduce_fusion.2
  545.8 1.4 slice_reduce_fusion
  547.2 0.8 copy.48
  548.0 3.3 bitcast_convert_fusion
  551.3 2.2 bitcast_convert_fusion.1
  553.4 2.2 bitcast_convert_fusion.2
  555.6 1.1 bitcast_convert_fusion.3
  557.3 1.3 broadcast_select_fusion.10
  558.7 1.1 pad_maximum_fusion.2
  559.8 1.0 copy.52
  (140 shorter events, 9.2 us)
Async XLA Ops:
  5.0 84.1 %copy-start.28 = (f32[8]{0:T(128)}, f32[8]{0:T(128)S(1)}, u32[]{:S(2)}) copy-start(f32[8]{0:T(128)S(1)} %pad.39.clone) | copy-start | bytes 100
  77.7 22.1 %copy-start.4 = (s32[36]{0:T(128)}, s32[36]{0:T(128)S(1)}, u32[]{:S(2)}) copy-start(s32[36]{0:T(128)S(1)} %reshape.129.flags) | copy-start | bytes 436
  77.7 11.4 %copy-start.13 = (bf16[768,1024]{1,0:T(8,128)(2,1)S(1)}, bf16[768,1024]{1,0:T(8,128)(2,1)}, u32[]{:S(2)}) copy-start(bf16[768,1024]{1,0:T(8,128)(2,1)} %gate_shard.1) | copy-start | bytes 4718596
  77.7 11.4 %copy-start.14 = (bf16[768,1024]{1,0:T(8,128)(2,1)S(1)}, bf16[768,1024]{1,0:T(8,128)(2,1)}, u32[]{:S(2)}) copy-start(bf16[768,1024]{1,0:T(8,128)(2,1)} %up_shard.1) | copy-start | bytes 4718596
  89.1 1.8 copy-start.22
  92.3 34.2 %copy-start.3 = (s32[8,1536]{1,0:T(8,128)}, s32[8,1536]{1,0:T(8,128)S(1)}, u32[]{:S(2)}) copy-start(s32[8,1536]{1,0:T(8,128)S(1)} %stack.69.qrow) | copy-start | bytes 147460
  92.3 38.1 %collective-permute-start = (bf16[384,1024]{1,0:T(8,128)(2,1)}, bf16[384,1024]{1,0:T(8,128)(2,1)S(1)}, u32[]{:S(2)}, u32[]{:S(2)}) collective-permute-start(bf16[384,1024]{1,0:T(8,128)(2,1)} %get-tuple-element.97), channel_id=1, source_target_pairs={{0,4},{2,8},{4,0},{6,12},{8,2},{10,14},{12,6},{14,10},{1,5},{3,9},... | collective-permute-start | bytes 2359304 | tf_op jit(solution)/shard_map/ppermute | solution.py:40
  93.7 36.8 %collective-permute-start.1 = (bf16[384,1024]{1,0:T(8,128)(2,1)}, bf16[384,1024]{1,0:T(8,128)(2,1)S(1)}, u32[]{:S(2)}, u32[]{:S(2)}) collective-permute-start(bf16[384,1024]{1,0:T(8,128)(2,1)} %get-tuple-element.98), channel_id=1, source_target_pairs={{0,4},{2,8},{4,0},{6,12},{8,2},{10,14},{12,6},{14,10},{1,5},{3,9},... | collective-permute-start | bytes 2359304 | tf_op jit(solution)/shard_map/ppermute | solution.py:40
  95.0 35.4 %collective-permute-start.2 = (bf16[384,768]{1,0:T(8,128)(2,1)}, bf16[384,768]{1,0:T(8,128)(2,1)}, u32[]{:S(2)}, u32[]{:S(2)}) collective-permute-start(bf16[384,768]{1,0:T(8,128)(2,1)} %get-tuple-element.99), channel_id=1, source_target_pairs={{0,8},{4,0},{8,12},{12,4},{1,9},{5,1},{9,13},{13,5},{2,10},{6,2},{... | collective-permute-start | bytes 1769480 | tf_op jit(solution)/shard_map/ppermute | solution.py:1868
  97.0 33.5 %collective-permute-start.3 = (bf16[384,768]{1,0:T(8,128)(2,1)}, bf16[384,768]{1,0:T(8,128)(2,1)}, u32[]{:S(2)}, u32[]{:S(2)}) collective-permute-start(bf16[384,768]{1,0:T(8,128)(2,1)} %get-tuple-element.100), channel_id=1, source_target_pairs={{4,8},{8,4},{5,9},{9,5},{6,10},{10,6},{7,11},{11,7},{20,24},{24,20... | collective-permute-start | bytes 1769480 | tf_op jit(solution)/shard_map/ppermute | solution.py:1869
  99.1 27.4 %copy-start.2 = (s32[1536,8]{1,0:T(8,128)}, s32[1536,8]{1,0:T(8,128)S(1)}, u32[]{:S(2)}) copy-start(s32[1536,8]{1,0:T(8,128)S(1)} %copy.44.kcol) | copy-start | bytes 147460
  126.5 1.0 copy-start
  127.6 1.4 copy-start.5
  128.9 0.9 copy-start.6
  129.9 0.6 copy-start.7
  130.5 1.9 copy-start.24
  130.5 1.9 copy-start.25
  132.5 74.5 %copy-start.10 = (bf16[384,1536]{1,0:T(8,128)(2,1)}, bf16[384,1536]{1,0:T(8,128)(2,1)S(1)}, u32[]{:S(2)}) copy-start(bf16[384,1536]{1,0:T(8,128)(2,1)S(1)} %pad_maximum_fusion.1.cot) | copy-start | bytes 3538948
  132.5 105.8 %collective-permute-start.4 = (bf16[384,1536]{1,0:T(8,128)(2,1)S(1)}, bf16[384,1536]{1,0:T(8,128)(2,1)S(1)}, u32[]{:S(2)}, u32[]{:S(2)}) collective-permute-start(bf16[384,1536]{1,0:T(8,128)(2,1)S(1)} %pad_maximum_fusion.1.cot), channel_id=1, source_target_pairs={{0,8},{8,0},{1,9},{9,1},{2,10},{10,2},{3,11},{11,3},{4,12},{12,4},... | collective-permute-start | bytes 3538952 | tf_op jit(solution)/shard_map/ppermute | solution.py:22
  207.0 28.8 %collective-permute-start.5 = (bf16[384,1536]{1,0:T(8,128)(2,1)S(1)}, bf16[384,1536]{1,0:T(8,128)(2,1)}, u32[]{:S(2)}, u32[]{:S(2)}) collective-permute-start(bf16[384,1536]{1,0:T(8,128)(2,1)S(1)} %pad_maximum_fusion.1.cot), channel_id=1, source_target_pairs={{0,1},{1,0},{2,3},{3,2},{4,5},{5,4},{6,7},{7,6},{8,9},{9,8},{10,11... | collective-permute-start | bytes 3538952 | tf_op jit(solution)/shard_map/ppermute | solution.py:26
  212.9 8.0 %copy-start.15 = (bf16[2,768,1024]{2,1,0:T(8,128)(2,1)S(1)}, bf16[2,768,1024]{2,1,0:T(8,128)(2,1)}, u32[]{:S(2)}) copy-start(bf16[2,768,1024]{2,1,0:T(8,128)(2,1)} %get-tuple-element.117) | copy-start | bytes 9437188
  212.9 8.0 %copy-start.30 = (bf16[4,384,1536]{2,1,0:T(8,128)(2,1)S(1)}, bf16[4,384,1536]{2,1,0:T(8,128)(2,1)}, u32[]{:S(2)}) copy-start(bf16[4,384,1536]{2,1,0:T(8,128)(2,1)} %get-tuple-element.115) | copy-start | bytes 14155780
  220.9 7.3 %copy-start.32 = (f32[1536,1024]{1,0:T(8,128)}, f32[1536,1024]{1,0:T(8,128)S(1)}, u32[]{:S(2)}) copy-start(f32[1536,1024]{1,0:T(8,128)S(1)} %fusion.16) | copy-start | bytes 18874372
  220.9 7.3 %copy-start.31 = (bf16[1024,1536]{1,0:T(8,128)(2,1)S(1)}, bf16[1024,1536]{1,0:T(8,128)(2,1)}, u32[]{:S(2)}) copy-start(bf16[1024,1536]{1,0:T(8,128)(2,1)} %get-tuple-element.118) | copy-start | bytes 9437188
  228.2 6.9 %copy-start.33 = (bf16[1536,1024]{1,0:T(8,128)(2,1)}, bf16[1536,1024]{1,0:T(8,128)(2,1)S(1)}, u32[]{:S(2)}) copy-start(bf16[1536,1024]{1,0:T(8,128)(2,1)S(1)} %get-tuple-element.237) | copy-start | bytes 9437188
  235.8 3.2 collective-permute-start.6
  235.8 3.2 copy-start.34
  237.7 17.1 %collective-permute-start.7 = (bf16[384,1536]{1,0:T(8,128)(2,1)S(1)}, bf16[384,1536]{1,0:T(8,128)(2,1)S(1)}, u32[]{:S(2)}, u32[]{:S(2)}) collective-permute-start(bf16[384,1536]{1,0:T(8,128)(2,1)S(1)} %get-tuple-element.219), channel_id=1, source_target_pairs={{0,8},{8,0},{1,9},{9,1},{2,10},{10,2},{3,11},{11,3},{4,12},{12,4},... | collective-permute-start | bytes 3538952 | tf_op jit(solution)/shard_map/ppermute | solution.py:22
  238.3 16.6 %collective-permute-start.9 = (bf16[384,1536]{1,0:T(8,128)(2,1)S(1)}, bf16[384,1536]{1,0:T(8,128)(2,1)S(1)}, u32[]{:S(2)}, u32[]{:S(2)}) collective-permute-start(bf16[384,1536]{1,0:T(8,128)(2,1)S(1)} %get-tuple-element.218), channel_id=1, source_target_pairs={{0,8},{8,0},{1,9},{9,1},{2,10},{10,2},{3,11},{11,3},{4,12},{12,4},... | collective-permute-start | bytes 3538952 | tf_op jit(solution)/shard_map/ppermute | solution.py:22
  248.0 6.9 %slice-start = ((s8[4718592]{0:T(1024)(128)(4,1)}), s8[4194304]{0:T(1024)(128)(4,1)S(1)}, s32[]{:S(2)}) async-start(s8[4718592]{0:T(1024)(128)(4,1)} %bitcast.72), calls=%async_computation | async-start | bytes 8388608
  248.2 6.7 %slice-start.1 = ((s8[4718592]{0:T(1024)(128)(4,1)}), s8[524288]{0:T(1024)(128)(4,1)S(1)}, s32[]{:S(2)}) async-start(s8[4718592]{0:T(1024)(128)(4,1)} %bitcast.72), calls=%async_computation.1 | async-start | bytes 1048576
  248.2 39.2 %collective-permute-start.8 = (bf16[512,1536]{1,0:T(8,128)(2,1)S(1)}, bf16[512,1536]{1,0:T(8,128)(2,1)}, u32[]{:S(2)}, u32[]{:S(2)}) collective-permute-start(bf16[512,1536]{1,0:T(8,128)(2,1)S(1)} %broadcast_select_fusion), channel_id=1, source_target_pairs={{0,16},{16,0},{1,17},{17,1},{2,18},{18,2},{3,19},{19,3},{4,20},{20... | collective-permute-start | bytes 4718600 | tf_op jit(solution)/shard_map/ppermute | solution.py:26
  255.6 31.8 %collective-permute-start.10 = (bf16[384,1536]{1,0:T(8,128)(2,1)S(1)}, bf16[384,1536]{1,0:T(8,128)(2,1)S(1)}, u32[]{:S(2)}, u32[]{:S(2)}) collective-permute-start(bf16[384,1536]{1,0:T(8,128)(2,1)S(1)} %get-tuple-element.216), channel_id=1, source_target_pairs={{0,1},{1,0},{2,3},{3,2},{4,5},{5,4},{6,7},{7,6},{8,9},{9,8},{10,11... | collective-permute-start | bytes 3538952 | tf_op jit(solution)/shard_map/ppermute | solution.py:26
  267.1 11.1 %copy-start.17 = (bf16[1536,1024]{1,0:T(8,128)(2,1)}, bf16[1536,1024]{1,0:T(8,128)(2,1)S(1)}, u32[]{:S(2)}) copy-start(bf16[1536,1024]{1,0:T(8,128)(2,1)S(1)} %get-tuple-element.215) | copy-start | bytes 9437188
  267.1 11.1 %copy-start.16 = (bf16[1536,1024]{1,0:T(8,128)(2,1)}, bf16[1536,1024]{1,0:T(8,128)(2,1)S(1)}, u32[]{:S(2)}) copy-start(bf16[1536,1024]{1,0:T(8,128)(2,1)S(1)} %get-tuple-element.214) | copy-start | bytes 9437188
  278.2 9.2 %copy-start.8 = (f32[384,1536]{1,0:T(8,128)S(1)}, f32[384,1536]{1,0:T(8,128)}, u32[]{:S(2)}) copy-start(f32[384,1536]{1,0:T(8,128)} %get-tuple-element.123.resid) | copy-start | bytes 7077892
  292.3 83.1 %copy-start.1 = (bf16[4,384,384]{2,1,0:T(8,128)(2,1)S(1)}, bf16[4,384,384]{2,1,0:T(8,128)(2,1)}, u32[]{:S(2)}) copy-start(bf16[4,384,384]{2,1,0:T(8,128)(2,1)} %copy-done) | copy-start | bytes 3538948
  375.4 5.4 copy-start.11
  375.5 5.4 copy-start.21
  380.9 3.7 copy-start.18
  384.6 48.1 %collective-permute-start.14 = (bf16[2,384,1024]{2,1,0:T(8,128)(2,1)S(1)}, bf16[2,384,1024]{2,1,0:T(8,128)(2,1)}, u32[]{:S(2)}, u32[]{:S(2)}) collective-permute-start(bf16[2,384,1024]{2,1,0:T(8,128)(2,1)S(1)} %copy-done.18), channel_id=1, source_target_pairs={{2,0},{8,10},{3,1},{9,11},{6,4},{12,14},{7,5},{13,15},{18,16},{24,... | collective-permute-start | bytes 4718600 | tf_op jit(solution)/shard_map/ppermute | solution.py:65
  388.6 44.1 %collective-permute-start.11 = (bf16[192,1536]{1,0:T(8,128)(2,1)}, bf16[192,1536]{1,0:T(8,128)(2,1)S(1)}, u32[]{:S(2)}, u32[]{:S(2)}) collective-permute-start(bf16[192,1536]{1,0:T(8,128)(2,1)} %get-tuple-element.141), channel_id=1, source_target_pairs={{0,16},{16,0},{1,17},{17,1},{2,18},{18,2},{3,19},{19,3},{4,20},{20... | collective-permute-start | bytes 1769480 | tf_op jit(solution)/shard_map/ppermute | solution.py:26
  389.4 43.2 %collective-permute-start.12 = (bf16[384,768]{1,0:T(8,128)(2,1)}, bf16[384,768]{1,0:T(8,128)(2,1)}, u32[]{:S(2)}, u32[]{:S(2)}) collective-permute-start(bf16[384,768]{1,0:T(8,128)(2,1)} %get-tuple-element.142), channel_id=1, source_target_pairs={{8,0},{0,4},{12,8},{4,12},{9,1},{1,5},{13,9},{5,13},{10,2},{2,6},{... | collective-permute-start | bytes 1769480 | tf_op jit(solution)/shard_map/ppermute | solution.py:131
  389.4 43.2 %collective-permute-start.13 = (bf16[384,768]{1,0:T(8,128)(2,1)}, bf16[384,768]{1,0:T(8,128)(2,1)}, u32[]{:S(2)}, u32[]{:S(2)}) collective-permute-start(bf16[384,768]{1,0:T(8,128)(2,1)} %get-tuple-element.143), channel_id=1, source_target_pairs={{8,4},{4,8},{9,5},{5,9},{10,6},{6,10},{11,7},{7,11},{24,20},{20,24... | collective-permute-start | bytes 1769480 | tf_op jit(solution)/shard_map/ppermute | solution.py:132
  392.8 39.8 %copy-start.27 = (f32[8,1536]{1,0:T(8,128)S(1)}, f32[8,1536]{1,0:T(8,128)}, u32[]{:S(2)}) copy-start(f32[8,1536]{1,0:T(8,128)} %get-tuple-element.149) | copy-start | bytes 147460
  432.7 4.4 copy-start.12
  437.1 10.6 %copy-start.29 = (f32[8]{0:T(128)S(1)}, f32[8]{0:T(128)}, u32[]{:S(2)}) copy-start(f32[8]{0:T(128)} %copy-done.28) | copy-start | bytes 100
  540.5 1.5 copy-start.9
  545.0 6.3 %copy-start.20 = (bf16[2,384,1024]{2,1,0:T(8,128)(2,1)S(1)}, bf16[2,384,1024]{2,1,0:T(8,128)(2,1)}, u32[]{:S(2)}) copy-start(bf16[2,384,1024]{2,1,0:T(8,128)(2,1)} %get-tuple-element.161) | copy-start | bytes 4718596
  551.3 2.2 copy-start.19
  553.4 2.2 copy-start.26
  555.6 4.2 copy-start.23
